TPU v7x, 32 devices: a whole 2x2x4 slice. The times are simulated.
32 devices in a mesh: dp: 8 (over y, x, core), fsdp: 4 (over z).
Axes of the slice: x: 2, y: 2, z: 4, core: 2. Of those that a mesh axis runs over, the one named last changes fastest.
Arguments:
- tokens: bfloat16 [6144, 2048], P(('dp', 'fsdp')), may hold values from -6 to 6
- cotangent: bfloat16 [6144, 2048], P(('dp', 'fsdp')), may hold values from -6 to 6
- segments: int32 [64, 96], P(('dp', 'fsdp')), may hold values from 0 to 2, never falling along the last dimension, each value on 1 to 48 neighbouring positions
- routes: int32 [6144, 8], P(('dp', 'fsdp')), may hold values from 0 to 15, all different within a row; in each aligned block of 96 rows (0 to 95, 96 to 191, ...) at most 72 rows name the same one
- w_qkv: bfloat16 [6144, 2048], P(('dp', 'fsdp')), may hold values from -0.125 to 0.125
- w_out: bfloat16 [2048, 2048], P(('dp', 'fsdp')), may hold values from -0.75 to 0.75
- norm_gains: bfloat16 [2048, 4], P(('dp', 'fsdp')), may hold values from 0.099609375 to 1.8984375
- w_router: bfloat16 [2048, 16], P(('dp', 'fsdp')), may hold values from -0.0625 to 0.0625
- w_gate_up: bfloat16 [16, 2048, 2048], P('fsdp', 'dp'), may hold values from -0.125 to 0.125
- w_down: bfloat16 [16, 2048, 1024], P('fsdp', 'dp'), may hold values from -1.5 to 1.5
Outputs:
- output: bfloat16 [6144, 2048], P(('dp', 'fsdp'))
- grad_tokens: float32 [6144, 2048], P(('dp', 'fsdp'))
- grad_qkv: float32 [6144, 2048], P(('dp', 'fsdp'))
- grad_out: float32 [2048, 2048], P(('dp', 'fsdp'))
- grad_gains: float32 [2048, 4], P(('dp', 'fsdp'))
- grad_router: float32 [2048, 16], P(('dp', 'fsdp'))
- grad_gate_up: float32 [16, 2048, 2048], P('fsdp', 'dp')
- grad_down: float32 [16, 2048, 1024], P('fsdp', 'dp')
Inputs may be any that keep to these rules, and one draw needn't show every extreme that they name: Each row names 8 different experts. In each sequence (96 rows of routes, aligned) at most 72 rows name one expert, a bound that some block reaches there. `segments`: along each sequence the ids start at 0 and never fall; a document has at most 48 tokens.
All inputs are finite; a program needn't handle non-finite values.
Results may differ from a plain program's by a relative error of at most 0.015.
Values may be sent and summed in bfloat16 or wider, within the bound.
No kernel may reach another device: no remote copies, remote signals or barrier semaphores. Data moves between devices by JAX's collectives and lax.ppermute only.
A program may use at most 320 MiB of HBM per device.

v0:
```python
import jax
import jax.numpy as jnp
from jax import lax
from jax.sharding import PartitionSpec as P

D = 2048
H = 16
HD = 128
FF = 1024
TOP = 8
E = 16
MB = 2
LEN = 96
CAP = 72


NORM_EPS = 1e-05
ROPE_BASE = 10000.0
PRECISE = lax.Precision.HIGHEST


def inverse_rms(field_in):
    return lax.rsqrt(jnp.mean(field_in * field_in, axis=-1, keepdims=True) + NORM_EPS)


def rotate(field_in, cos_table, sin_table):
    half_dim = field_in.shape[-1] // 2
    first_half = field_in[..., :half_dim]
    second_half = field_in[..., half_dim:]
    return jnp.concatenate(
        [
            first_half * cos_table - second_half * sin_table,
            second_half * cos_table + first_half * sin_table,
        ],
        axis=-1,
    )


def rotate_back(field_in, cos_table, sin_table):
    half_dim = field_in.shape[-1] // 2
    first_half = field_in[..., :half_dim]
    second_half = field_in[..., half_dim:]
    return jnp.concatenate(
        [
            first_half * cos_table + second_half * sin_table,
            second_half * cos_table - first_half * sin_table,
        ],
        axis=-1,
    )


def rope_tables(length, head_dim):
    half_dim = head_dim // 2
    frequency = ROPE_BASE ** (-(jnp.arange(half_dim).astype(jnp.float32) * 2.0) / head_dim)
    angles = jnp.arange(length).astype(jnp.float32)[:, None] * frequency[None, :]
    return (jnp.cos(angles)[:, None, :], jnp.sin(angles)[:, None, :])


def norm_back(grad_normed, normed, inverse):
    return inverse * (grad_normed - normed * jnp.mean(grad_normed * normed, axis=-1, keepdims=True))


def per_device(
    tokens, cotangent, segments, routes, w_qkv, w_out, norm_gains, w_router, w_gate_up, w_down
):
    groups = lax.axis_size("fsdp")
    local_experts = E // groups
    score_scale = HD ** (-0.5)
    cos_table, sin_table = rope_tables(LEN, HD)
    position = jnp.arange(LEN)
    causal = position[:, None] >= position[None, :]
    expert_ids = jnp.arange(E, dtype=jnp.int32)
    head_shape = (LEN, H, HD)
    f32 = jnp.float32
    bf16 = jnp.bfloat16
    contract_last = (((1,), (1,)), ((), ()))
    contract_first = (((0,), (0,)), ((), ()))

    def fetch_attention():
        return (
            lax.all_gather(w_qkv, ("dp", "fsdp"), axis=0, tiled=True),
            lax.all_gather(w_out, ("dp", "fsdp"), axis=0, tiled=True),
            lax.all_gather(norm_gains, ("dp", "fsdp"), axis=0, tiled=True),
            lax.all_gather(w_router, ("dp", "fsdp"), axis=0, tiled=True),
        )

    def fetch_experts():
        return (
            lax.all_gather(w_gate_up, "dp", axis=1, tiled=True),
            lax.all_gather(w_down, "dp", axis=1, tiled=True),
        )

    attn_total = (
        jnp.zeros((3 * D, D), f32),
        jnp.zeros((D, D), f32),
        jnp.zeros((D, 4), f32),
        jnp.zeros((D, E), f32),
    )
    expert_total = (
        jnp.zeros((local_experts, 2 * FF, D), f32),
        jnp.zeros((local_experts, D, FF), f32),
    )
    outputs_list = []
    grads_list = []
    for micro_batch in range(MB):
        attn_w = fetch_attention()
        exp_w = fetch_experts()
        qkv_full, out_full, gains_full, router_full = attn_w
        gate_up_full, down_full = exp_w
        gains_f = gains_full.astype(f32)
        router_f = router_full.astype(f32)
        row_start = micro_batch * LEN
        x_float = tokens[row_start : row_start + LEN].astype(f32)
        seg_row = segments[micro_batch]
        route_rows = routes[row_start : row_start + LEN]
        inverse_one = inverse_rms(x_float)
        normed_one = x_float * inverse_one
        hidden_one = (normed_one * gains_f[:, 0]).astype(bf16)
        projected = lax.dot_general(hidden_one, qkv_full, contract_last, preferred_element_type=f32)
        raw_q = projected[:, :D]
        raw_k = projected[:, D : 2 * D]
        raw_v = projected[:, 2 * D :]
        inverse_q = inverse_rms(raw_q)
        normed_q = raw_q * inverse_q
        inverse_k = inverse_rms(raw_k)
        normed_k = raw_k * inverse_k
        queries = rotate(
            (normed_q * gains_f[:, 1]).reshape(head_shape), cos_table, sin_table
        ).astype(bf16)
        keys_all = rotate(
            (normed_k * gains_f[:, 2]).reshape(head_shape), cos_table, sin_table
        ).astype(bf16)
        values_all = raw_v.reshape(head_shape).astype(bf16)
        allowed = causal & (seg_row[:, None] == seg_row[None, :])
        scores = (
            jnp.einsum("qhd,khd->hqk", queries, keys_all, preferred_element_type=f32) * score_scale
        )
        scores = jnp.where(allowed[None], scores, -1e30)
        attn_probs = jax.nn.softmax(scores, axis=-1)
        probs_low = attn_probs.astype(bf16)
        attended = (
            jnp.einsum("hqk,khd->qhd", probs_low, values_all, preferred_element_type=f32)
            .astype(bf16)
            .reshape(LEN, D)
        )
        residual = x_float + lax.dot_general(
            attended, out_full, contract_last, preferred_element_type=f32
        )
        inverse_two = inverse_rms(residual)
        normed_two = residual * inverse_two
        hidden_two = (normed_two * gains_f[:, 3]).astype(bf16)
        hidden_float = hidden_two.astype(f32)
        router_probs = jax.nn.softmax(jnp.dot(hidden_float, router_f, precision=PRECISE), axis=-1)
        route_picks = (route_rows[:, :, None] == expert_ids[None, None, :]).astype(f32)
        gate_vals = jnp.einsum("tke,te->tk", route_picks, router_probs, precision=PRECISE)
        route_flat = route_rows.reshape(-1)
        onehot = (route_flat[:, None] == expert_ids[None, :]).astype(jnp.int32)
        earlier = jnp.cumsum(onehot, axis=0) - onehot
        slot_index = jnp.sum(earlier * onehot, axis=1)
        token_rows = jnp.repeat(hidden_two, TOP, axis=0)
        dispatch_buf = jnp.zeros((E, CAP, D), bf16).at[route_flat, slot_index].set(token_rows)
        received = lax.all_to_all(dispatch_buf, "fsdp", split_axis=0, concat_axis=1, tiled=True)
        gate_and_up = jnp.einsum("ecd,efd->ecf", received, gate_up_full, preferred_element_type=f32)
        gate_part = gate_and_up[..., :FF]
        up_part = gate_and_up[..., FF:]
        silu_gate = jax.nn.silu(gate_part)
        activation = (silu_gate * up_part).astype(bf16)
        expert_out = jnp.einsum(
            "ecf,edf->ecd", activation, down_full, preferred_element_type=f32
        ).astype(bf16)
        returned = lax.all_to_all(expert_out, "fsdp", split_axis=1, concat_axis=0, tiled=True)
        chosen = returned[route_flat, slot_index].astype(f32).reshape(LEN, TOP, D)
        result_rows = residual + jnp.sum(gate_vals[:, :, None] * chosen, axis=1)
        outputs_list.append(result_rows.astype(bf16))
        attn_w = fetch_attention()
        exp_w = fetch_experts()
        qkv_full = attn_w[0]
        out_full = attn_w[1]
        gate_up_full, down_full = exp_w
        grad_rows_out = cotangent[row_start : row_start + LEN].astype(f32)
        grad_chosen = gate_vals[:, :, None] * grad_rows_out[:, None, :]
        grad_gates = jnp.sum(chosen * grad_rows_out[:, None, :], axis=2)
        grad_buf = (
            jnp.zeros((E, CAP, D), bf16)
            .at[route_flat, slot_index]
            .set(grad_chosen.reshape(LEN * TOP, D).astype(bf16))
        )
        grad_received = lax.all_to_all(grad_buf, "fsdp", split_axis=0, concat_axis=1, tiled=True)
        grad_act = jnp.einsum("ecd,edf->ecf", grad_received, down_full, preferred_element_type=f32)
        grad_down_batch = jnp.einsum(
            "ecd,ecf->edf", grad_received, activation, preferred_element_type=f32
        )
        sigmoid_gate = jax.nn.sigmoid(gate_part)
        grad_gate = grad_act * up_part * sigmoid_gate * (1.0 + gate_part * (1.0 - sigmoid_gate))
        grad_up = grad_act * silu_gate
        grad_both = jnp.concatenate([grad_gate, grad_up], axis=-1).astype(bf16)
        grad_gate_up_batch = jnp.einsum(
            "ecf,ecd->efd", grad_both, received, preferred_element_type=f32
        )
        grad_rows = jnp.einsum(
            "ecf,efd->ecd", grad_both, gate_up_full, preferred_element_type=f32
        ).astype(bf16)
        grad_returned = lax.all_to_all(grad_rows, "fsdp", split_axis=1, concat_axis=0, tiled=True)
        grad_hidden = jnp.sum(
            grad_returned[route_flat, slot_index].astype(f32).reshape(LEN, TOP, D), axis=1
        )
        grad_probs_router = jnp.einsum("tk,tke->te", grad_gates, route_picks, precision=PRECISE)
        grad_logits = router_probs * (
            grad_probs_router - jnp.sum(router_probs * grad_probs_router, axis=-1, keepdims=True)
        )
        grad_router_batch = jnp.dot(hidden_float.T, grad_logits, precision=PRECISE)
        grad_hidden = grad_hidden + jnp.dot(grad_logits, router_f.T, precision=PRECISE)
        grad_gain_two = jnp.sum(grad_hidden * normed_two, axis=0)
        grad_residual = grad_rows_out + norm_back(
            grad_hidden * gains_f[:, 3], normed_two, inverse_two
        )
        grad_attn = grad_residual.astype(bf16)
        grad_attended = jnp.dot(grad_attn, out_full, preferred_element_type=f32).astype(bf16)
        grad_out_batch = lax.dot_general(
            grad_attn, attended, contract_first, preferred_element_type=f32
        )
        grad_heads = grad_attended.reshape(head_shape)
        grad_probs = jnp.einsum("qhd,khd->hqk", grad_heads, values_all, preferred_element_type=f32)
        grad_values = jnp.einsum("hqk,qhd->khd", probs_low, grad_heads, preferred_element_type=f32)
        row_delta = jnp.sum(attn_probs * grad_probs, axis=-1, keepdims=True)
        grad_scores = (attn_probs * (grad_probs - row_delta)).astype(bf16)
        grad_queries = (
            jnp.einsum("hqk,khd->qhd", grad_scores, keys_all, preferred_element_type=f32)
            * score_scale
        )
        grad_keys = (
            jnp.einsum("hqk,qhd->khd", grad_scores, queries, preferred_element_type=f32)
            * score_scale
        )
        grad_normed_q = rotate_back(grad_queries, cos_table, sin_table).reshape(LEN, D)
        grad_normed_k = rotate_back(grad_keys, cos_table, sin_table).reshape(LEN, D)
        grad_gain_q = jnp.sum(grad_normed_q * normed_q, axis=0)
        grad_gain_k = jnp.sum(grad_normed_k * normed_k, axis=0)
        grad_raw_q = norm_back(grad_normed_q * gains_f[:, 1], normed_q, inverse_q)
        grad_raw_k = norm_back(grad_normed_k * gains_f[:, 2], normed_k, inverse_k)
        grad_projected = jnp.concatenate(
            [grad_raw_q, grad_raw_k, grad_values.reshape(LEN, D)], axis=1
        ).astype(bf16)
        grad_qkv_batch = lax.dot_general(
            grad_projected, hidden_one, contract_first, preferred_element_type=f32
        )
        grad_hidden_one = jnp.dot(grad_projected, qkv_full, preferred_element_type=f32)
        grad_gain_one = jnp.sum(grad_hidden_one * normed_one, axis=0)
        grad_token_rows = grad_residual + norm_back(
            grad_hidden_one * gains_f[:, 0], normed_one, inverse_one
        )
        grads_list.append(grad_token_rows)
        grad_gains_batch = jnp.stack(
            [grad_gain_one, grad_gain_q, grad_gain_k, grad_gain_two], axis=1
        )
        batch_attn = (grad_qkv_batch, grad_out_batch, grad_gains_batch, grad_router_batch)
        batch_expert = (grad_gate_up_batch, grad_down_batch)
        attn_total = tuple(
            (running + part_sum for running, part_sum in zip(attn_total, batch_attn))
        )
        expert_total = tuple(
            (running + part_sum for running, part_sum in zip(expert_total, batch_expert))
        )
    attn_total = (
        lax.psum_scatter(attn_total[0], ("dp", "fsdp"), scatter_dimension=0, tiled=True),
        lax.psum_scatter(attn_total[1], ("dp", "fsdp"), scatter_dimension=0, tiled=True),
        lax.psum_scatter(attn_total[2], ("dp", "fsdp"), scatter_dimension=0, tiled=True),
        lax.psum_scatter(attn_total[3], ("dp", "fsdp"), scatter_dimension=0, tiled=True),
    )
    expert_total = (
        lax.psum_scatter(
            expert_total[0].astype(jnp.bfloat16), "dp", scatter_dimension=1, tiled=True
        ).astype(jnp.float32),
        lax.psum_scatter(
            expert_total[1].astype(jnp.bfloat16), "dp", scatter_dimension=1, tiled=True
        ).astype(jnp.float32),
    )
    return (
        jnp.concatenate(outputs_list, axis=0),
        jnp.concatenate(grads_list, axis=0),
        attn_total[0],
        attn_total[1],
        attn_total[2],
        attn_total[3],
        expert_total[0],
        expert_total[1],
    )


def solution(mesh):
    in_specs = (
        P(("dp", "fsdp"), None),
        P(("dp", "fsdp"), None),
        P(("dp", "fsdp"), None),
        P(("dp", "fsdp"), None),
        P(("dp", "fsdp"), None),
        P(("dp", "fsdp"), None),
        P(("dp", "fsdp"), None),
        P(("dp", "fsdp"), None),
        P("fsdp", "dp", None),
        P("fsdp", "dp", None),
    )
    out_specs = (
        P(("dp", "fsdp"), None),
        P(("dp", "fsdp"), None),
        P(("dp", "fsdp"), None),
        P(("dp", "fsdp"), None),
        P(("dp", "fsdp"), None),
        P(("dp", "fsdp"), None),
        P("fsdp", "dp", None),
        P("fsdp", "dp", None),
    )
    return jax.shard_map(
        per_device, mesh=mesh, in_specs=in_specs, out_specs=out_specs, check_vma=False
    )
```

profile of v0, /device:TPU:0, one launch (start us, length us, event | category | flops | bytes accessed | tf_op | source)
XLA Modules:
  0.0 3112.2 jit_solution(12554293099472933991)
XLA Ops:
  11.1 72.5 %all-gather = bf16[32,64,4]{1,2,0:T(4,128)(2,1)S(1)} all-gather(bf16[1,64,4]{1,2,0:T(4,128)(2,1)S(1)} %bitcast.410), channel_id=1, replica_groups=mesh['dp'=8,'fsdp'=4] {'dp','fsdp'}, dimensions={0}, use_global_device_ids=true | all-gather | bytes 16896 | tf_op jit(solution)/shard_map/all_gather | solution.py:83
  87.8 68.3 %all-gather.1 = bf16[32,64,16]{1,2,0:T(8,128)(2,1)S(1)} all-gather(bf16[1,64,16]{1,2,0:T(8,128)(2,1)S(1)} %bitcast.409), channel_id=1, replica_groups=mesh['dp'=8,'fsdp'=4] {'dp','fsdp'}, dimensions={0}, use_global_device_ids=true | all-gather | bytes 67584 | tf_op jit(solution)/shard_map/all_gather | solution.py:84
  159.6 8.9 all-gather.7.cloned.1.call-done
  168.5 12.7 fusion.102
  181.4 14.8 fusion.105
  209.6 37.5 %all-gather.9.cloned.1.call-done = bf16[2048,2048]{1,0:T(8,128)(2,1)} async-done(((bf16[64,2048]{1,0:T(8,128)(2,1)}), bf16[2048,2048]{1,0:T(8,128)(2,1)}) %all-gather.9.cloned.1.call-update) | async-done | bytes 8388624 | tf_op jit(solution)/shard_map/all_gather | solution.py:82
  247.2 6.2 multiply_reduce_fusion.13
  261.3 139.7 %scatter_fusion.2 = bf16[16,72,2048]{2,1,0:T(8,128)(2,1)} fusion(bf16[16,72,2048]{2,1,0:T(8,128)(2,1)} %broadcast.373.clone.1, s32[768]{0:T(1024)S(1)} %get-tuple-element.41, bf16[768,2048]{1,0:T(8,128)(2,1)} %fusion.7), kind=kCustom, calls=%fused_computation.6 | custom fusion | bytes 9443328 | tf_op jit(solution)/shard_map/scatter | solution.py:186
  401.0 5.4 all-to-all-start.4
  411.3 138.1 %scatter_fusion = bf16[16,72,2048]{2,1,0:T(8,128)(2,1)} fusion(bf16[16,72,2048]{2,1,0:T(8,128)(2,1)} %broadcast.373.clone, s32[768]{0:T(1024)S(1)} %get-tuple-element.41, bf16[768,2048]{1,0:T(8,128)(2,1)} %broadcast_bitcast_fusion.1), kind=kCustom, calls=%fused_computation.4 | custom fusion | bytes 9443328 | tf_op jit(solution)/shard_map/scatter | solution.py:161
  549.4 5.3 all-to-all-start
  554.7 5.2 copy.182
  559.9 99.8 %all-to-all-done = bf16[16,72,2048]{2,1,0:T(8,128)(2,1)} async-done(((bf16[16,72,2048]{2,1,0:T(8,128)(2,1)}), bf16[16,72,2048]{2,1,0:T(8,128)(2,1)}, u32[]{:S(2)}, u32[]{:S(2)}) %all-to-all-start) | async-done | bytes 4718624 | tf_op jit(solution)/shard_map/all_to_all | solution.py:162
  659.7 5.2 copy.164
  665.0 19.3 fusion.176
  684.3 14.7 multiply_convert_fusion.3
  698.9 19.0 convolution_convert_fusion.1
  718.0 8.3 copy.183
  726.3 5.1 all-to-all-start.5
  731.3 8.7 convolution_convert_fusion.3
  740.1 5.9 copy.165
  746.0 89.5 %all-to-all-done.5 = bf16[4,288,2048]{2,0,1:T(4,128)(2,1)} async-done(((bf16[4,288,2048]{2,0,1:T(4,128)(2,1)}), bf16[4,288,2048]{2,0,1:T(4,128)(2,1)}, u32[]{:S(2)}, u32[]{:S(2)}) %all-to-all-start.5) | async-done | bytes 4718624 | tf_op jit(solution)/shard_map/all_to_all | solution.py:203
  835.5 5.2 all-to-all-start.1
  843.2 7.2 multiply_reduce_fusion.10
  851.0 7.1 copy.184
  858.1 12.3 gather_fusion.2
  873.4 71.3 %all-to-all-done.1 = bf16[4,288,2048]{2,0,1:T(4,128)(2,1)} async-done(((bf16[4,288,2048]{2,0,1:T(4,128)(2,1)}), bf16[4,288,2048]{2,0,1:T(4,128)(2,1)}, u32[]{:S(2)}, u32[]{:S(2)}) %all-to-all-start.1) | async-done | bytes 4718624 | tf_op jit(solution)/shard_map/all_to_all | solution.py:171
  944.6 7.2 copy.166
  951.8 12.0 gather_fusion
  963.9 5.1 fusion.3
  980.8 133.6 %scatter_fusion.3 = bf16[16,72,2048]{2,1,0:T(8,128)(2,1)} fusion(bf16[16,72,2048]{2,1,0:T(8,128)(2,1)} %broadcast.373.clone.3, s32[768]{0:T(1024)S(1)} %copy-done.2, bf16[768,2048]{1,0:T(8,128)(2,1)S(1)} %fusion.6), kind=kCustom, calls=%fused_computation.7 | custom fusion | bytes 9443328 | tf_op jit(solution)/shard_map/scatter | solution.py:186
  1122.7 134.5 %scatter_fusion.1 = bf16[16,72,2048]{2,1,0:T(8,128)(2,1)} fusion(bf16[16,72,2048]{2,1,0:T(8,128)(2,1)} %broadcast.373.clone.2, s32[768]{0:T(1024)S(1)} %copy-done.2, bf16[768,2048]{1,0:T(8,128)(2,1)S(1)} %broadcast_bitcast_fusion), kind=kCustom, calls=%fused_computation.5 | custom fusion | bytes 9443328 | tf_op jit(solution)/shard_map/scatter | solution.py:161
  1257.2 5.1 all-to-all-start.2
  1262.3 5.3 copy.192
  1267.7 98.7 %all-to-all-done.2 = bf16[16,72,2048]{2,1,0:T(8,128)(2,1)} async-done(((bf16[16,72,2048]{2,1,0:T(8,128)(2,1)}), bf16[16,72,2048]{2,1,0:T(8,128)(2,1)}, u32[]{:S(2)}, u32[]{:S(2)}) %all-to-all-start.2) | async-done | bytes 4718624 | tf_op jit(solution)/shard_map/all_to_all | solution.py:162
  1369.1 20.3 fusion.177
  1389.4 14.7 multiply_convert_fusion.1
  1404.2 10.0 convolution_convert_fusion.2
  1414.2 5.7 copy.180
  1419.9 5.1 all-to-all-start.3
  1425.0 18.1 convolution_convert_fusion
  1443.1 8.1 copy.193
  1451.2 77.6 %all-to-all-done.3 = bf16[4,288,2048]{2,0,1:T(4,128)(2,1)} async-done(((bf16[4,288,2048]{2,0,1:T(4,128)(2,1)}), bf16[4,288,2048]{2,0,1:T(4,128)(2,1)}, u32[]{:S(2)}, u32[]{:S(2)}) %all-to-all-start.3) | async-done | bytes 4718624 | tf_op jit(solution)/shard_map/all_to_all | solution.py:171
  1528.8 5.2 all-to-all-start.7
  1534.0 17.7 fusion.178
  1552.8 7.1 copy.181
  1559.9 12.0 gather_fusion.1
  1577.2 60.7 %all-to-all-done.7 = bf16[4,288,2048]{2,0,1:T(4,128)(2,1)} async-done(((bf16[4,288,2048]{2,0,1:T(4,128)(2,1)}), bf16[4,288,2048]{2,0,1:T(4,128)(2,1)}, u32[]{:S(2)}, u32[]{:S(2)}) %all-to-all-start.7) | async-done | bytes 4718624 | tf_op jit(solution)/shard_map/all_to_all | solution.py:203
  1637.9 7.0 copy.194
  1644.9 12.4 gather_fusion.3
  1679.3 10.6 fusion.53
  1690.0 14.2 fusion.40
  1711.3 20.7 add_convert_fusion.1
  1732.1 29.3 fusion.10
  1761.4 41.0 %add_convert_fusion = bf16[4,2048,2048]{2,1,0:T(8,128)(2,1)} fusion(f32[4,2048,2048]{2,1,0:T(8,128)} %fusion.10, bf16[4,288,2048]{2,1,0:T(8,128)(2,1)} %bitcast.360, bf16[4,288,1024]{2,1,0:T(8,128)(2,1)} %get-tuple-element.47, bf16[4,288,1024]{2,1,0:T(8,128)(2,1)} %get-tuple-element.46), kind=kOutput, calls=%fused_computation.10 | convolution fusion | flops 9706668032 | bytes 110100480 | tf_op jit(solution)/shard_map/ecf,ecd->efd/dot_general | solution.py:197
  1805.9 8.1 convolution_add_fusion.1
  1815.0 19.8 fusion.54
  1834.7 32.7 %convolution_add_fusion = f32[6144,2048]{1,0:T(8,128)} fusion(f32[6144,2048]{1,0:T(8,128)} %fusion.54, bf16[96,2048]{1,0:T(8,128)(2,1)} %bitcast.376, bf16[96,2048]{1,0:T(8,128)(2,1)} %copy-done.22, bf16[96,2048]{1,0:T(8,128)(2,1)} %copy-done.21, f32[96]{0:T(128)S(1)} %copy-done.101, f32[2048]{0:T(1024)S(1)} %bitcast.381, bf16[192,2048]{1,0:T(8,128)(2,1)S(1)} %copy-done.8), kind=kOutput, calls=%fused_computation.12 | convolution fusion | flops 2432827392 | bytes 102244864 | tf_op jit(solution)/shard_map/dot_general | solution.py:244
  1875.1 103.6 %reduce-scatter.21.cloned.1.call-done = f32[64,16]{1,0:T(8,128)} async-done(((f32[2048,16]{1,0:T(8,128)}), f32[64,16]{1,0:T(8,128)}) %reduce-scatter.21.cloned.1.call-update) | async-done | bytes 4112
  1980.1 114.8 %reduce-scatter.17.cloned.1.call-done = bf16[4,256,1024]{2,1,0:T(8,128)(2,1)} async-done(((bf16[4,2048,1024]{2,1,0:T(8,128)(2,1)}), bf16[4,256,1024]{2,1,0:T(8,128)(2,1)}) %reduce-scatter.17.cloned.1.call-update) | async-done | bytes 2097168 | tf_op jit(solution)/shard_map/reduce_scatter | solution.py:274
  2099.0 205.0 %reduce-scatter.15.cloned.1.call-done = bf16[4,256,2048]{2,1,0:T(8,128)(2,1)} async-done(((bf16[4,2048,2048]{2,1,0:T(8,128)(2,1)}), bf16[4,256,2048]{2,1,0:T(8,128)(2,1)}) %reduce-scatter.15.cloned.1.call-update) | async-done | bytes 4194320 | tf_op jit(solution)/shard_map/reduce_scatter | solution.py:271
  2304.0 6.7 convert_element_type.364
  2310.7 356.9 %reduce-scatter.13.cloned.1.call-done = f32[64,2048]{1,0:T(8,128)} async-done(((f32[2048,2048]{1,0:T(8,128)}), f32[64,2048]{1,0:T(8,128)}) %reduce-scatter.13.cloned.1.call-update) | async-done | bytes 524304 | tf_op jit(solution)/shard_map/reduce_scatter | solution.py:266
  2667.5 437.4 %reduce-scatter.11.cloned.1.call-done = f32[192,2048]{1,0:T(8,128)} async-done(((f32[6144,2048]{1,0:T(8,128)}), f32[192,2048]{1,0:T(8,128)}) %reduce-scatter.11.cloned.1.call-update) | async-done | bytes 1572880 | tf_op jit(solution)/shard_map/reduce_scatter | solution.py:265
  (408 shorter events, 118.2 us)
Async XLA Ops:
  7.2 80.6 %copy-start.122 = (bf16[64,16]{0,1:T(8,128)(2,1)S(1)}, bf16[64,16]{0,1:T(8,128)(2,1)}, u32[]{:S(2)}) copy-start(bf16[64,16]{0,1:T(8,128)(2,1)} %param.17) | copy-start | bytes 6148
  7.2 161.3 %all-gather.7.cloned.1.call-start = ((), (), s32[]{:S(2)}) async-start(), calls=%async_computation.14 | async-start | bytes 25952256 | tf_op jit(solution)/shard_map/all_gather | solution.py:81
  7.9 149.2 %copy-start.124 = (s32[2,96]{1,0:T(2,128)S(1)}, s32[2,96]{1,0:T(2,128)}, u32[]{:S(2)}) copy-start(s32[2,96]{1,0:T(2,128)} %param.12) | copy-start | bytes 2308
  8.0 150.3 %copy-start.26 = (bf16[192,2048]{1,0:T(8,128)(2,1)S(1)}, bf16[192,2048]{1,0:T(8,128)(2,1)}, u32[]{:S(2)}) copy-start(bf16[192,2048]{1,0:T(8,128)(2,1)} %param.11) | copy-start | bytes 2359300
  8.0 239.2 %all-gather.9.cloned.1.call-start = ((), (), s32[]{:S(2)}) async-start(), calls=%async_computation.15 | async-start | bytes 8650752 | tf_op jit(solution)/shard_map/all_gather | solution.py:82
  8.7 656.3 %all-gather.11.cloned.1.call-start = ((), (), s32[]{:S(2)}) async-start(), calls=%async_computation.16 | async-start | bytes 37748736 | tf_op jit(solution)/shard_map/all_gather | solution.py:89
  9.5 674.8 %all-gather.13.cloned.1.call-start = ((), (), s32[]{:S(2)}) async-start(), calls=%async_computation.17 | async-start | bytes 18874368 | tf_op jit(solution)/shard_map/all_gather | solution.py:90
  10.2 245.4 %copy-start.59 = (s32[96,8]{1,0:T(8,128)}, s32[96,8]{1,0:T(8,128)S(1)}, u32[]{:S(2)}) copy-start(s32[96,8]{1,0:T(8,128)S(1)} %copy.158) | copy-start | bytes 9220
  10.6 157.9 %copy-start.56 = (s32[96,8]{1,0:T(8,128)}, s32[96,8]{1,0:T(8,128)S(1)}, u32[]{:S(2)}) copy-start(s32[96,8]{1,0:T(8,128)S(1)} %copy.174) | copy-start | bytes 9220
  156.3 97.8 %copy-start.34 = (bf16[2048,16]{0,1:T(8,128)(2,1)}, bf16[2048,16]{0,1:T(8,128)(2,1)S(1)}, u32[]{:S(2)}) copy-start(bf16[2048,16]{0,1:T(8,128)(2,1)S(1)} %reshape.569) | copy-start | bytes 196612
  157.2 24.2 copy-start.96
  157.2 24.0 copy-start.99
  158.1 43.2 %copy-start.65 = (f32[96,64]{1,0:T(8,128)}, f32[96,64]{1,0:T(8,128)S(1)}, u32[]{:S(2)}) copy-start(f32[96,64]{1,0:T(8,128)S(1)} %get-tuple-element.119) | copy-start | bytes 73732
  158.2 43.2 %copy-start.67 = (f32[96,64]{1,0:T(8,128)}, f32[96,64]{1,0:T(8,128)S(1)}, u32[]{:S(2)}) copy-start(f32[96,64]{1,0:T(8,128)S(1)} %get-tuple-element.120) | copy-start | bytes 73732
  158.2 23.2 copy-start.54
  158.2 39.6 %copy-start.82 = (f32[2048,1]{0,1:T(1,128)}, f32[2048,1]{0,1:T(1,128)S(1)}, u32[]{:S(2)}) copy-start(f32[2048,1]{0,1:T(1,128)S(1)} %get-tuple-element.103) | copy-start | bytes 24580
  158.2 39.6 %copy-start.84 = (f32[2048,1]{0,1:T(1,128)}, f32[2048,1]{0,1:T(1,128)S(1)}, u32[]{:S(2)}) copy-start(f32[2048,1]{0,1:T(1,128)S(1)} %get-tuple-element.104) | copy-start | bytes 24580
  158.2 95.2 %copy-start.73 = (f32[2048,1]{0,1:T(1,128)}, f32[2048,1]{0,1:T(1,128)S(1)}, u32[]{:S(2)}) copy-start(f32[2048,1]{0,1:T(1,128)S(1)} %get-tuple-element.102) | copy-start | bytes 24580
  181.2 16.7 copy-start.4
  207.2 46.2 %copy-start.103 = (f32[16,96]{1,0:T(8,128)}, f32[16,96]{1,0:T(8,128)S(1)}, u32[]{:S(2)}) copy-start(f32[16,96]{1,0:T(8,128)S(1)} %get-tuple-element.121) | copy-start | bytes 18436
  209.6 43.8 %copy-start.53 = (bf16[16,12,8,128]{3,2,1,0:T(8,128)(2,1)}, bf16[16,12,8,128]{3,2,1,0:T(8,128)(2,1)S(1)}, u32[]{:S(2)}) copy-start(bf16[16,12,8,128]{3,2,1,0:T(8,128)(2,1)S(1)} %fusion.21) | copy-start | bytes 1179652
  209.6 46.6 %copy-start.12 = (f32[96,2048]{1,0:T(8,128)S(1)}, f32[96,2048]{1,0:T(8,128)}, u32[]{:S(2)}) copy-start(f32[96,2048]{1,0:T(8,128)} %get-tuple-element.80) | copy-start | bytes 2359300
  254.2 152.2 %copy-start.15 = (bf16[96,2048]{1,0:T(8,128)(2,1)}, bf16[96,2048]{1,0:T(8,128)(2,1)S(1)}, u32[]{:S(2)}) copy-start(bf16[96,2048]{1,0:T(8,128)(2,1)S(1)} %multiply_convert_fusion.13) | copy-start | bytes 1179652
  256.1 144.9 %copy-start.75 = (f32[96,1,8]{2,1,0:T(1,128)}, f32[96,1,8]{2,1,0:T(1,128)S(1)}, u32[]{:S(2)}) copy-start(f32[96,1,8]{2,1,0:T(1,128)S(1)} %fusion.76) | copy-start | bytes 9220
  401.0 148.4 %all-to-all-start.4 = ((bf16[16,72,2048]{2,1,0:T(8,128)(2,1)}), bf16[16,72,2048]{2,1,0:T(8,128)(2,1)}, u32[]{:S(2)}, u32[]{:S(2)}) async-start(bf16[16,72,2048]{2,1,0:T(8,128)(2,1)} %scatter_fusion.2), calls=%async_computation.4 | async-start | bytes 9437184 | tf_op jit(solution)/shard_map/all_to_all | solution.py:188
  549.4 110.3 %all-to-all-start = ((bf16[16,72,2048]{2,1,0:T(8,128)(2,1)}), bf16[16,72,2048]{2,1,0:T(8,128)(2,1)}, u32[]{:S(2)}, u32[]{:S(2)}) async-start(bf16[16,72,2048]{2,1,0:T(8,128)(2,1)} %scatter_fusion), calls=%async_computation | async-start | bytes 9437184 | tf_op jit(solution)/shard_map/all_to_all | solution.py:162
  698.9 19.0 copy-start.30
  726.3 109.2 %all-to-all-start.5 = ((bf16[4,288,2048]{2,0,1:T(4,128)(2,1)}), bf16[4,288,2048]{2,0,1:T(4,128)(2,1)}, u32[]{:S(2)}, u32[]{:S(2)}) async-start(bf16[4,288,2048]{2,0,1:T(4,128)(2,1)} %copy.183), calls=%async_computation.5 | async-start | bytes 9437184 | tf_op jit(solution)/shard_map/all_to_all | solution.py:203
  746.0 94.7 %copy-start.39 = (bf16[96,16,64]{2,0,1:T(8,128)(2,1)S(1)}, bf16[96,16,64]{2,0,1:T(8,128)(2,1)}, u32[]{:S(2)}) copy-start(bf16[96,16,64]{2,0,1:T(8,128)(2,1)} %get-tuple-element.100) | copy-start | bytes 589828
  746.0 94.7 %copy-start.41 = (bf16[96,16,64]{2,0,1:T(8,128)(2,1)S(1)}, bf16[96,16,64]{2,0,1:T(8,128)(2,1)}, u32[]{:S(2)}) copy-start(bf16[96,16,64]{2,0,1:T(8,128)(2,1)} %get-tuple-element.101) | copy-start | bytes 589828
  746.0 94.7 %copy-start.43 = (bf16[96,16,64]{2,0,1:T(8,128)(2,1)S(1)}, bf16[96,16,64]{2,0,1:T(8,128)(2,1)}, u32[]{:S(2)}) copy-start(bf16[96,16,64]{2,0,1:T(8,128)(2,1)} %get-tuple-element.98) | copy-start | bytes 589828
  746.0 94.7 %copy-start.45 = (bf16[96,16,64]{2,0,1:T(8,128)(2,1)S(1)}, bf16[96,16,64]{2,0,1:T(8,128)(2,1)}, u32[]{:S(2)}) copy-start(bf16[96,16,64]{2,0,1:T(8,128)(2,1)} %get-tuple-element.99) | copy-start | bytes 589828
  746.0 94.7 %copy-start.102 = (pred[96,96]{0,1:T(8,128)(4,1)S(1)}, pred[96,96]{0,1:T(8,128)(4,1)}, u32[]{:S(2)}) copy-start(pred[96,96]{0,1:T(8,128)(4,1)} %get-tuple-element.140) | copy-start | bytes 27652
  835.5 109.2 %all-to-all-start.1 = ((bf16[4,288,2048]{2,0,1:T(4,128)(2,1)}), bf16[4,288,2048]{2,0,1:T(4,128)(2,1)}, u32[]{:S(2)}, u32[]{:S(2)}) async-start(bf16[4,288,2048]{2,0,1:T(4,128)(2,1)} %copy.165), calls=%async_computation.1 | async-start | bytes 9437184 | tf_op jit(solution)/shard_map/all_to_all | solution.py:171
  951.8 12.0 copy-start.76
  973.5 145.9 %copy-start.17 = (bf16[96,2048]{1,0:T(8,128)(2,1)}, bf16[96,2048]{1,0:T(8,128)(2,1)S(1)}, u32[]{:S(2)}) copy-start(bf16[96,2048]{1,0:T(8,128)(2,1)S(1)} %get-tuple-element.114) | copy-start | bytes 1179652
  1114.5 142.7 %all-to-all-start.6 = ((bf16[16,72,2048]{2,1,0:T(8,128)(2,1)}), bf16[16,72,2048]{2,1,0:T(8,128)(2,1)}, u32[]{:S(2)}, u32[]{:S(2)}) async-start(bf16[16,72,2048]{2,1,0:T(8,128)(2,1)} %scatter_fusion.3), calls=%async_computation.6 | async-start | bytes 9437184 | tf_op jit(solution)/shard_map/all_to_all | solution.py:188
  1257.2 109.2 %all-to-all-start.2 = ((bf16[16,72,2048]{2,1,0:T(8,128)(2,1)}), bf16[16,72,2048]{2,1,0:T(8,128)(2,1)}, u32[]{:S(2)}, u32[]{:S(2)}) async-start(bf16[16,72,2048]{2,1,0:T(8,128)(2,1)} %scatter_fusion.1), calls=%async_computation.2 | async-start | bytes 9437184 | tf_op jit(solution)/shard_map/all_to_all | solution.py:162
  1369.1 20.3 copy-start
  1419.9 108.9 %all-to-all-start.3 = ((bf16[4,288,2048]{2,0,1:T(4,128)(2,1)}), bf16[4,288,2048]{2,0,1:T(4,128)(2,1)}, u32[]{:S(2)}, u32[]{:S(2)}) async-start(bf16[4,288,2048]{2,0,1:T(4,128)(2,1)} %copy.180), calls=%async_computation.3 | async-start | bytes 9437184 | tf_op jit(solution)/shard_map/all_to_all | solution.py:171
  1451.2 82.8 %copy-start.32 = (bf16[4,288,1024]{2,1,0:T(8,128)(2,1)S(1)}, bf16[4,288,1024]{2,1,0:T(8,128)(2,1)}, u32[]{:S(2)}) copy-start(bf16[4,288,1024]{2,1,0:T(8,128)(2,1)} %get-tuple-element.48) | copy-start | bytes 7077892
  1528.8 109.2 %all-to-all-start.7 = ((bf16[4,288,2048]{2,0,1:T(4,128)(2,1)}), bf16[4,288,2048]{2,0,1:T(4,128)(2,1)}, u32[]{:S(2)}, u32[]{:S(2)}) async-start(bf16[4,288,2048]{2,0,1:T(4,128)(2,1)} %copy.193), calls=%async_computation.7 | async-start | bytes 9437184 | tf_op jit(solution)/shard_map/all_to_all | solution.py:203
  1533.9 17.8 copy-start.125
  1533.9 17.8 copy-start.16
  1534.0 17.8 copy-start.81
  1534.0 17.8 copy-start.95
  1534.0 17.8 copy-start.121
  1534.0 339.7 %reduce-scatter.19.cloned.1.call-start = ((), (), s32[]{:S(2)}) async-start(), calls=%async_computation.22 | async-start | bytes 1081344
  1559.9 12.0 copy-start.78
  1577.2 82.5 %copy-start.79 = (f32[96,1,16]{0,2,1:T(8,128)}, f32[96,1,16]{0,2,1:T(8,128)S(1)}, u32[]{:S(2)}) copy-start(f32[96,1,16]{0,2,1:T(8,128)S(1)} %copy.212) | copy-start | bytes 18436
  1577.2 82.5 %copy-start.116 = (f32[96]{0:T(128)}, f32[96]{0:T(128)S(1)}, u32[]{:S(2)}) copy-start(f32[96]{0:T(128)S(1)} %fusion.117) | copy-start | bytes 1156
  1644.9 14.7 copy-start.35
  1644.9 14.7 copy-start.74
  1644.9 14.7 copy-start.119
  1674.7 15.2 copy-start.19
  1689.9 14.3 copy-start.13
  1690.0 14.2 copy-start.86
  1690.0 17.1 copy-start.18
  1707.1 271.6 %reduce-scatter.21.cloned.1.call-start = ((), (), s32[]{:S(2)}) async-start(), calls=%async_computation.23 | async-start | bytes 1081344
  1711.3 383.6 %reduce-scatter.17.cloned.1.call-start = ((), (), s32[]{:S(2)}) async-start(), calls=%async_computation.21 | async-start | bytes 18874368 | tf_op jit(solution)/shard_map/reduce_scatter | solution.py:274
  1732.1 571.9 %reduce-scatter.15.cloned.1.call-start = ((), (), s32[]{:S(2)}) async-start(), calls=%async_computation.20 | async-start | bytes 37748736 | tf_op jit(solution)/shard_map/reduce_scatter | solution.py:271
  1802.4 865.1 %reduce-scatter.13.cloned.1.call-start = ((), (), s32[]{:S(2)}) async-start(), calls=%async_computation.19 | async-start | bytes 17301504 | tf_op jit(solution)/shard_map/reduce_scatter | solution.py:266
  1814.0 20.7 copy-start.101
  1814.0 1290.9 %reduce-scatter.11.cloned.1.call-start = ((), (), s32[]{:S(2)}) async-start(), calls=%async_computation.18 | async-start | bytes 51904512 | tf_op jit(solution)/shard_map/reduce_scatter | solution.py:265
  (82 other events, 338.0 us)
Sparse Core Ops, SparseCore 0:
  10.9 157.5 all-gather.6
  171.4 75.7 all-gather.8
  249.1 159.2 all-gather.10
  410.2 89.7 all-gather.12
  1707.2 135.5 reduce-scatter.18
  1844.9 133.7 reduce-scatter.20
  1982.2 112.6 reduce-scatter.16
  2098.5 205.4 reduce-scatter.14
  2306.9 360.5 reduce-scatter.12
  2674.4 430.4 reduce-scatter.10
where the time goes:
time: 3140 us; the launch traced here: 3110 us
  waiting for transfers between devices  1760 us (56%)
  local copies, waits for them, and re-layouts  701 us (22%)
  matrix products  391 us (12%)
  blocking collectives  141 us (4%)
  other arithmetic  57.1 us (2%)
  starting transfers between devices  41.5 us (1%)
    reduce_scatter x1, waiting for transfers between devices, per_device(): lax.psum_scatter(attn_total[0], ('dp', 'fsdp'), scatter_dimension=0, tile...  437 us
    reduce_scatter x1, waiting for transfers between devices, per_device(): lax.psum_scatter(attn_total[1], ('dp', 'fsdp'), scatter_dimension=0, tile...  357 us
    scatter x2, local copies, waits for them, and re-layouts, per_device(): grad_buf = jnp.zeros((E, CAP, D), bf16).at[route_flat, slot_index].set(gr...  273 us
    scatter x2, local copies, waits for them, and re-layouts, per_device(): jnp.zeros((E, CAP, D), bf16).at[route_flat, slot_index].set(token_rows)  273 us
    reduce_scatter x1, waiting for transfers between devices, per_device(): lax.psum_scatter(expert_total[0].astype(jnp.bfloat16), 'dp', scatter_dime...  205 us
    all_to_all x2, waiting for transfers between devices, per_device(): lax.all_to_all(dispatch_buf, 'fsdp', split_axis=0, concat_axis=1, tiled=T...  199 us
    all_to_all x2, waiting for transfers between devices, per_device(): lax.all_to_all(grad_rows, 'fsdp', split_axis=1, concat_axis=0, tiled=True)  150 us
    all_to_all x2, waiting for transfers between devices, per_device(): lax.all_to_all(expert_out, 'fsdp', split_axis=1, concat_axis=0, tiled=True)  149 us
  transfers between devices with their start and end apart: 18, of which 13 were waited for; matrix products, arithmetic and copies ran while one was open for 26% of the time, Pallas kernels for 0%

commit v1 on v0

v1 whole, which is shorter than its diff:
```python
import jax
import jax.numpy as jnp
from jax import lax
from jax.sharding import Mesh
from jax.sharding import PartitionSpec as P

D = 2048
H = 16
HD = 128
FF = 1024
TOP = 8
E = 16
LEN = 96

NORM_EPS = 1e-05
ROPE_BASE = 10000.0
PRECISE = lax.Precision.HIGHEST
DP = ("q", "c")
ALL = ("q", "c", "z")
f32 = jnp.float32
bf16 = jnp.bfloat16


def inverse_rms(field_in):
    return lax.rsqrt(jnp.mean(field_in * field_in, axis=-1, keepdims=True) + NORM_EPS)


def rotate(field_in, cos_table, sin_table):
    half_dim = field_in.shape[-1] // 2
    first_half = field_in[..., :half_dim]
    second_half = field_in[..., half_dim:]
    return jnp.concatenate(
        [
            first_half * cos_table - second_half * sin_table,
            second_half * cos_table + first_half * sin_table,
        ],
        axis=-1,
    )


def rope_tables(length, head_dim):
    half_dim = head_dim // 2
    frequency = ROPE_BASE ** (-(jnp.arange(half_dim).astype(f32) * 2.0) / head_dim)
    angles = jnp.arange(length).astype(f32)[:, None] * frequency[None, :]
    return (jnp.cos(angles)[:, None, :], jnp.sin(angles)[:, None, :])


def norm_back(grad_normed, normed, inverse):
    return inverse * (grad_normed - normed * jnp.mean(grad_normed * normed, axis=-1, keepdims=True))


def mm(a, b, ca, cb):
    return lax.dot_general(a, b, (((ca,), (cb,)), ((), ())), preferred_element_type=f32)


def flip(value, size, bit):
    return lax.ppermute(value, DP, [(i, i ^ (1 << bit)) for i in range(size)])


def gather_xor(value, size, bits):
    lead = 0
    for bit in bits:
        other = flip(value, size, bit)
        value = jnp.stack([value, other], axis=lead)
        lead += 1
    return value


def bit_lists(size):
    high = list(range(1, size.bit_length() - 1))
    return high, high[::-1]


def gather_dp(value, size):
    width = value.shape[-1] // 2
    pieces = []
    for part, order in zip((value[:, :width], value[:, width:]), bit_lists(size)):
        out = part
        for k, bit in enumerate(order):
            out = jnp.stack([out, flip(out, size, bit)], axis=k)
        perm = [order.index(bit) for bit in range(len(order), 0, -1)]
        out = out.transpose(perm + [len(order), len(order) + 1])
        pieces.append(out.reshape((-1,) + part.shape))
    both = jnp.concatenate(pieces, axis=-1)
    other = flip(both, size, 0)
    return jnp.stack([both, other], axis=1).reshape((size,) + value.shape)


def scatter_dp(parts, size):
    rows, width = parts.shape[1], parts.shape[2]
    pair = parts.reshape(size // 2, 2, rows, width)
    got = flip(pair[:, 1], size, 0)
    summed = (pair[:, 0].astype(f32) + got.astype(f32)).astype(bf16)
    highs = size.bit_length() - 2
    halves = []
    for half, order in enumerate(bit_lists(size)):
        cur = summed[:, :, half * (width // 2) : (half + 1) * (width // 2)]
        cur = cur.reshape([2] * highs + [rows, width // 2])
        left = list(range(highs, 0, -1))
        for k, bit in enumerate(order):
            axis = left.index(bit)
            left.remove(bit)
            keep = lax.index_in_dim(cur, 0, axis, keepdims=False)
            send = lax.index_in_dim(cur, 1, axis, keepdims=False)
            total = keep.astype(f32) + flip(send, size, bit).astype(f32)
            cur = total if k == len(order) - 1 else total.astype(bf16)
        halves.append(cur)
    return jnp.concatenate(halves, axis=-1)


def gather_z(value, zs):
    spread = jnp.broadcast_to(value[None], (zs,) + value.shape)
    return lax.all_to_all(spread, "z", 0, 0, tiled=True)


def scatter_z(parts):
    got = lax.all_to_all(parts, "z", 0, 0, tiled=True)
    return jnp.sum(got.astype(f32), axis=0)


def swap_core(value):
    return lax.ppermute(value, "c", [(0, 1), (1, 0)])


def psum_dp(value, size):
    spread = jnp.broadcast_to(value[None], (size,) + value.shape)
    return jnp.sum(lax.all_to_all(spread, DP, 0, 0, tiled=True), axis=0)


def per_device(
    tokens, cotangent, segments, routes, w_qkv, w_out, norm_gains, w_router, w_gate_up, w_down
):
    zs = lax.axis_size("z")
    dps = lax.axis_size("q") * 2
    qi, ci, zi = lax.axis_index("q"), lax.axis_index("c"), lax.axis_index("z")
    di = qi * 2 + ci
    rows = tokens.shape[0]
    seqs = rows // LEN
    width = D // dps
    heads = width // HD
    local_experts = E // zs
    mine = local_experts // 2
    score_scale = HD ** (-0.5)
    sub = w_qkv.shape[0] // 3
    orow = w_out.shape[0]

    small = lax.all_gather(
        jnp.concatenate([norm_gains, w_router], axis=1), ALL, axis=0, tiled=True
    ).astype(f32)
    gains_f = small[:, :4]
    router_f = small[:, 4:]

    def unit_perm(t, back):
        pairs = []
        for i in range(dps):
            for j in range(zs):
                dest = (3 * i + (3 * j + t) // zs) % dps
                src_dev, dst_dev = i * zs + j, dest * zs + j
                pairs.append((dst_dev, src_dev) if back else (src_dev, dst_dev))
        return pairs

    moved = [
        lax.ppermute(w_qkv[t * sub : (t + 1) * sub], ALL, unit_perm(t, False)) for t in range(3)
    ]
    inv3 = pow(3, -1, dps)
    slot_of = [[0, 0, 0] for _ in range(dps)]
    type_of = [[0, 0, 0] for _ in range(dps)]
    for i in range(dps):
        for s in range(3):
            src = (inv3 * (i - s)) % dps
            kind = (3 * src + s) // dps
            slot_of[i][kind] = s
            type_of[i][s] = kind
    slot_of = jnp.asarray(slot_of, jnp.int32)[di]
    type_of = jnp.asarray(type_of, jnp.int32)[di]
    qkv_slots = gather_z(jnp.concatenate(moved, axis=0), zs).reshape(3, width, D)
    w_three = jnp.concatenate(
        [lax.dynamic_index_in_dim(qkv_slots, slot_of[k], 0, keepdims=False) for k in range(3)],
        axis=0,
    )
    out_cols = lax.all_to_all(
        w_out.reshape(orow, dps, width).transpose(1, 0, 2), DP, 0, 0, tiled=True
    )
    w_out_c = gather_z(out_cols, zs).transpose(1, 0, 2, 3).reshape(D, width)

    tok_g = gather_dp(tokens, dps).reshape(dps * rows, D)
    seg_g = lax.all_gather(segments, DP, axis=0, tiled=True).reshape(dps, seqs, LEN)
    order = jnp.arange(dps) ^ di
    seg_g = seg_g[order].reshape(dps * seqs, LEN)
    all_seqs = dps * seqs
    all_rows = dps * rows

    def core_half(weight):
        swapped = lax.all_to_all(
            weight.reshape((2, mine) + weight.shape[1:]), "c", 0, 0, tiled=True
        )
        return [swapped[:, e].reshape((2 * weight.shape[1], weight.shape[2])) for e in range(mine)]

    gu_half = core_half(w_gate_up)
    down_half = core_half(w_down)
    expert_w = []
    for e in range(mine):
        expert_w.append(
            (
                lax.all_gather(gu_half[e], "q", axis=0, tiled=True),
                lax.all_gather(down_half[e], "q", axis=0, tiled=True),
            )
        )

    def gather_cz(value):
        got = gather_z(value, zs).reshape((zs * value.shape[0],) + value.shape[1:])
        return jnp.concatenate([got, swap_core(got)], axis=0)

    def scatter_cz(parts):
        half = parts.shape[0] // 2
        mixed = parts[:half].astype(f32) + swap_core(parts[half:].astype(bf16)).astype(f32)
        return scatter_z(mixed.astype(bf16).reshape((zs, half // zs) + parts.shape[1:]))

    dy_g = gather_cz(cotangent)
    routes_g = gather_cz(routes)

    cos_table, sin_table = rope_tables(LEN, HD)
    position = jnp.arange(LEN)
    causal = position[:, None] >= position[None, :]
    head_shape = (all_seqs, LEN, heads, HD)

    x_g = tok_g.astype(f32)
    inv_one_g = inverse_rms(x_g)
    hidden_one = (x_g * inv_one_g * gains_f[:, 0]).astype(bf16)
    projected = mm(hidden_one, w_three, 1, 1)
    raw_q = projected[:, :width]
    raw_k = projected[:, width : 2 * width]
    raw_v = projected[:, 2 * width :]
    squares = psum_dp_stack(raw_q * raw_q, raw_k * raw_k, dps, di)
    inv_q = lax.rsqrt(squares[0] / D + NORM_EPS)[:, None]
    inv_k = lax.rsqrt(squares[1] / D + NORM_EPS)[:, None]
    normed_q = raw_q * inv_q
    normed_k = raw_k * inv_k
    own_gains = lax.dynamic_slice(gains_f, (di * width, 0), (width, 4))
    gain_q, gain_k = own_gains[:, 1], own_gains[:, 2]
    queries = rotate((normed_q * gain_q).reshape(head_shape), cos_table, sin_table).astype(bf16)
    keys_all = rotate((normed_k * gain_k).reshape(head_shape), cos_table, sin_table).astype(bf16)
    values_all = raw_v.reshape(head_shape).astype(bf16)
    allowed = causal[None] & (seg_g[:, :, None] == seg_g[:, None, :])
    scores = (
        jnp.einsum("sqhd,skhd->shqk", queries, keys_all, preferred_element_type=f32) * score_scale
    )
    scores = jnp.where(allowed[:, None], scores, -1e30)
    attn_probs = jax.nn.softmax(scores, axis=-1)
    probs_low = attn_probs.astype(bf16)
    attended = (
        jnp.einsum("shqk,skhd->sqhd", probs_low, values_all, preferred_element_type=f32)
        .astype(bf16)
        .reshape(all_rows, width)
    )
    attn_out = scatter_dp(mm(attended, w_out_c, 1, 1).astype(bf16).reshape(dps, rows, D), dps)

    x_float = tokens.astype(f32)
    inverse_one = inverse_rms(x_float)
    normed_one = x_float * inverse_one
    residual = x_float + attn_out
    inverse_two = inverse_rms(residual)
    normed_two = residual * inverse_two
    hidden_two = (normed_two * gains_f[:, 3]).astype(bf16)

    hidden_g = gather_cz(hidden_two)
    router_low = router_f.astype(bf16)
    router_g = jax.nn.softmax(mm(hidden_g, router_low, 1, 0), axis=-1)
    router_probs = jax.nn.softmax(mm(hidden_two, router_low, 1, 0), axis=-1)
    dy_f = dy_g.astype(f32)
    first_expert = zi * local_experts + ci * mine
    out_part = None
    hid_part = None
    gate_cols = []
    grad_gu, grad_dn = [], []
    for e in range(mine):
        gate_up, down = expert_w[e]
        expert = first_expert + e
        picked = jnp.any(routes_g == expert, axis=1, keepdims=True)
        prob = jnp.sum(
            jnp.where(jnp.arange(E)[None] == expert, router_g, 0.0), axis=1, keepdims=True
        )
        gate_val = jnp.where(picked, prob, 0.0)
        gate_and_up = mm(hidden_g, gate_up, 1, 1)
        g_part = gate_and_up[:, :FF]
        u_part = gate_and_up[:, FF:]
        sig = jax.nn.sigmoid(g_part)
        silu = g_part * sig
        act = (silu * u_part).astype(bf16)
        expert_out = mm(act, down, 1, 1).astype(bf16).astype(f32)
        piece = gate_val * expert_out
        out_part = piece if out_part is None else out_part + piece
        gate_cols.append(jnp.where(picked[:, 0], jnp.sum(dy_f * expert_out, axis=1), 0.0))
        grad_eo = (gate_val * dy_f).astype(bf16)
        grad_act = mm(grad_eo, down, 1, 0)
        grad_g = grad_act * u_part * sig * (1.0 + g_part * (1.0 - sig))
        grad_u = grad_act * silu
        grad_both = jnp.concatenate([grad_g, grad_u], axis=-1).astype(bf16)
        grad_dn.append(
            lax.psum_scatter(
                mm(grad_eo, act, 0, 0).astype(bf16), "q", scatter_dimension=0, tiled=True
            )
        )
        grad_gu.append(
            lax.psum_scatter(
                mm(grad_both, hidden_g, 0, 0).astype(bf16), "q", scatter_dimension=0, tiled=True
            )
        )
        rows_back = mm(grad_both, gate_up, 1, 0).astype(bf16).astype(f32)
        hid_part = rows_back if hid_part is None else hid_part + rows_back

    cols = jnp.stack(gate_cols, axis=0).reshape(mine, 2, zs, rows)
    other_cols = swap_core(cols[:, 1])
    both_cols = jnp.stack([cols[:, 0], other_cols], axis=0)
    back_cols = lax.all_to_all(both_cols.transpose(2, 0, 1, 3), "z", 0, 0, tiled=True)
    back_cols = jnp.where(ci == 0, back_cols, back_cols[:, ::-1])
    gp = back_cols.reshape(E, rows).T

    grad_hidden = scatter_cz(hid_part)
    result = residual + scatter_cz(out_part)

    grad_logits = router_probs * (gp - jnp.sum(router_probs * gp, axis=-1, keepdims=True))
    grad_router = lax.dot_general(
        hidden_two.astype(f32), grad_logits, (((0,), (0,)), ((), ())), precision=PRECISE
    )
    grad_hidden = grad_hidden + jnp.dot(grad_logits, router_f.T, precision=PRECISE)
    grad_gain_two = jnp.sum(grad_hidden * normed_two, axis=0)
    grad_residual = cotangent.astype(f32) + norm_back(
        grad_hidden * gains_f[:, 3], normed_two, inverse_two
    )
    grad_attn = grad_residual.astype(bf16)

    grad_attn_g = gather_dp(grad_attn, dps).reshape(all_rows, D)
    grad_heads = mm(grad_attn_g, w_out_c, 1, 0).astype(bf16).reshape(head_shape)
    grad_out_c = mm(grad_attn_g, attended, 0, 0)
    grad_probs = jnp.einsum("sqhd,skhd->shqk", grad_heads, values_all, preferred_element_type=f32)
    grad_values = jnp.einsum("shqk,sqhd->skhd", probs_low, grad_heads, preferred_element_type=f32)
    row_delta = jnp.sum(attn_probs * grad_probs, axis=-1, keepdims=True)
    grad_scores = (attn_probs * (grad_probs - row_delta)).astype(bf16)
    grad_queries = (
        jnp.einsum("shqk,skhd->sqhd", grad_scores, keys_all, preferred_element_type=f32)
        * score_scale
    )
    grad_keys = (
        jnp.einsum("shqk,sqhd->skhd", grad_scores, queries, preferred_element_type=f32)
        * score_scale
    )
    grad_nq = rotate(grad_queries, cos_table, -sin_table).reshape(all_rows, width)
    grad_nk = rotate(grad_keys, cos_table, -sin_table).reshape(all_rows, width)
    grad_gain_q = jnp.sum(grad_nq * normed_q, axis=0)
    grad_gain_k = jnp.sum(grad_nk * normed_k, axis=0)
    a_q = grad_nq * gain_q
    a_k = grad_nk * gain_k
    means = psum_dp_stack(a_q * normed_q, a_k * normed_k, dps, di) / D
    grad_raw_q = inv_q * (a_q - normed_q * means[0][:, None])
    grad_raw_k = inv_k * (a_k - normed_k * means[1][:, None])
    grad_projected = jnp.concatenate(
        [grad_raw_q, grad_raw_k, grad_values.reshape(all_rows, width)], axis=1
    ).astype(bf16)
    grad_h1 = scatter_dp(
        mm(grad_projected, w_three, 1, 0).astype(bf16).reshape(dps, rows, D), dps
    )
    grad_gain_one = jnp.sum(grad_h1 * normed_one, axis=0)
    grad_tokens = grad_residual + norm_back(grad_h1 * gains_f[:, 0], normed_one, inverse_one)

    grad_three = mm(grad_projected, hidden_one, 0, 0).astype(bf16).reshape(3, width, D)
    grad_slots = jnp.concatenate(
        [lax.dynamic_index_in_dim(grad_three, type_of[s], 0, keepdims=True) for s in range(3)],
        axis=0,
    )
    own_slots = scatter_z(grad_slots.reshape(zs, 3 * sub, D)).astype(bf16)
    grad_qkv = jnp.concatenate(
        [
            lax.ppermute(own_slots[t * sub : (t + 1) * sub], ALL, unit_perm(t, True))
            for t in range(3)
        ],
        axis=0,
    ).astype(f32)
    grad_cols = scatter_z(
        grad_out_c.astype(bf16).reshape(dps, zs, orow, width).transpose(1, 0, 2, 3)
    ).astype(bf16)
    grad_out = (
        lax.all_to_all(grad_cols, DP, 0, 0, tiled=True)
        .transpose(1, 0, 2)
        .reshape(orow, D)
        .astype(f32)
    )

    shard_cols = jnp.zeros((D, 2), f32)
    shard_cols = lax.dynamic_update_slice(
        shard_cols, jnp.stack([grad_gain_q, grad_gain_k], axis=1), (di * width, 0)
    )
    small_grads = jnp.concatenate(
        [grad_gain_one[:, None], shard_cols, grad_gain_two[:, None], grad_router], axis=1
    )
    small_own = lax.psum_scatter(small_grads, ALL, scatter_dimension=0, tiled=True)

    def core_back(parts):
        stacked = jnp.stack(parts, axis=0)
        split = stacked.reshape((mine, 2, stacked.shape[1] // 2, stacked.shape[2]))
        got = lax.all_to_all(split.transpose(1, 0, 2, 3), "c", 0, 0, tiled=True)
        return got.reshape((local_experts,) + got.shape[2:]).astype(f32)

    return (
        result.astype(bf16),
        grad_tokens,
        grad_qkv,
        grad_out,
        small_own[:, :4],
        small_own[:, 4:],
        core_back(grad_gu),
        core_back(grad_dn),
    )


def psum_dp_stack(first, second, size, own):
    count = first.shape[0]
    sums = jnp.stack([jnp.sum(first, axis=1), jnp.sum(second, axis=1)], axis=0)
    rel = sums.reshape(2, size, count // size)
    index = jnp.arange(size) ^ own
    true = rel[:, index].reshape(2, count)
    total = psum_dp(true, size).reshape(2, size, count // size)
    return total[:, index].reshape(2, count)


def solution(mesh):
    dps, zs = mesh.shape["dp"], mesh.shape["fsdp"]
    inner = Mesh(mesh.devices.reshape(dps // 2, 2, zs), ALL)
    rows = P(ALL, None)
    experts = P("z", DP, None)
    in_specs = (rows,) * 8 + (experts,) * 2
    out_specs = (rows,) * 6 + (experts,) * 2
    return jax.shard_map(
        per_device, mesh=inner, in_specs=in_specs, out_specs=out_specs, check_vma=False
    )
```

time: 3140 us -> 1310 us (0.42)
  waiting for transfers between devices: 1760 us -> 465 us
  local copies, waits for them, and re-layouts: 701 us -> 130 us
  matrix products: 391 us -> 236 us
  blocking collectives: 141 us -> 219 us
  other arithmetic: 57.1 us -> 127 us
  starting transfers between devices: 41.5 us -> 105 us
    reduce_scatter x4, waiting for transfers between devices: 1110 us -> 0.03 us  [the longest x2 0.02 us: per_device(): lax.psum_scatter(mm(grad_eo, act, 0, 0).astype(bf16), 'q', scatter_dimens...]
    scatter x4 -> x0, local copies, waits for them, and re-layouts: 546 us -> none  [the longest x2 273 us: per_device(): grad_buf = jnp.zeros((E, CAP, D), bf16).at[route_flat, slot_index].set(gr...]
    all_to_all x8 -> x15, waiting for transfers between devices: 498 us -> 239 us  [the longest x4 148 us: scatter_z(): got = lax.all_to_all(parts, 'z', 0, 0, tiled=True)]
    dot_general x42 -> x26, matrix products: 382 us -> 231 us  [the longest x20 225 us: mm(): lax.dot_general(a, b, (((ca,), (cb,)), ((), ())), preferred_element_type=...]
    ppermute x0 -> x32, waiting for transfers between devices: none -> 136 us  [the longest x20 130 us: flip(): return lax.ppermute(value, DP, [(i, i ^ 1 << bit) for i in range(size)])]
    all_to_all x0 -> x3, blocking collectives: none -> 91.1 us  [the longest x1 74 us: gather_z(): return lax.all_to_all(spread, 'z', 0, 0, tiled=True)]
    all_gather x4, waiting for transfers between devices: 46.4 us -> 0.05 us  [the longest x2 0.02 us: per_device(): lax.all_gather(gu_half[e], 'q', axis=0, tiled=True)]
    all_to_all x8 -> x2, local copies, waits for them, and re-layouts: 46.9 us -> 1.07 us  [gather_z(): return lax.all_to_all(spread, 'z', 0, 0, tiled=True)]
  transfers between devices with their start and end apart: 18 -> 56, of which waited for: 13 -> 28; matrix products, arithmetic and copies ran while one was open for 26% -> 35% of each run, Pallas kernels for 0% -> 0%
where the time goes in v1:
time: 1310 us; the launch traced here: 1300 us
  waiting for transfers between devices  465 us (35%)
  matrix products  236 us (18%)
  blocking collectives  219 us (17%)
  local copies, waits for them, and re-layouts  130 us (10%)
  other arithmetic  127 us (10%)
  starting transfers between devices  105 us (8%)
  between operations  21.9 us (2%)
    dot_general x20, matrix products, mm(): lax.dot_general(a, b, (((ca,), (cb,)), ((), ())), preferred_element_type=...  225 us
    all_to_all x4, waiting for transfers between devices, scatter_z(): got = lax.all_to_all(parts, 'z', 0, 0, tiled=True)  148 us
    ppermute x20, waiting for transfers between devices, flip(): return lax.ppermute(value, DP, [(i, i ^ 1 << bit) for i in range(size)])  130 us
    all_gather x1, blocking collectives, per_device(): lax.all_gather(jnp.concatenate([norm_gains, w_router], axis=1), ALL, axis...  121 us
    unnamed x10, waiting for transfers between devices  89.4 us
    all_to_all x4, waiting for transfers between devices, gather_z(): return lax.all_to_all(spread, 'z', 0, 0, tiled=True)  76.9 us
    all_to_all x1, blocking collectives, gather_z(): return lax.all_to_all(spread, 'z', 0, 0, tiled=True)  74 us
    unnamed x205, local copies, waits for them, and re-layouts  42.9 us
  transfers between devices with their start and end apart: 56, of which 28 were waited for; matrix products, arithmetic and copies ran while one was open for 35% of the time, Pallas kernels for 0%

profile of v1, /device:TPU:0, one launch (start us, length us, event | category | flops | bytes accessed | tf_op | source)
XLA Modules:
  0.0 1303.0 jit_solution(6000037747396314500)
XLA Ops:
  7.2 8.5 all_to_all.90
  23.0 7.9 collective-permute-done.2
  34.5 33.4 %collective-permute-done.3 = bf16[2,192,1024]{2,1,0:T(8,128)(2,1)S(1)} collective-permute-done((bf16[2,192,1024]{2,1,0:T(8,128)(2,1)S(1)}, bf16[2,192,1024]{2,1,0:T(8,128)(2,1)S(1)}, u32[]{:S(2)}, u32[]{:S(2)}) %collective-permute-start.3) | collective-permute-done | bytes 786464 | tf_op jit(solution)/shard_map/ppermute | solution.py:57
  84.0 4.8 all-to-all-start.7
  97.3 9.1 all-to-all-done.2
  109.6 7.7 all-to-all-start
  125.6 120.7 %all-gather = bf16[32,64,20]{1,2,0:T(8,128)(2,1)S(1)} all-gather(bf16[1,64,20]{1,2,0:T(8,128)(2,1)S(1)} %maximum_bitcast_fusion.3), channel_id=1, replica_groups=mesh['q'=4,'c'=2,'z'=4] {'q','c','z'}, dimensions={0}, use_global_device_ids=true | all-gather | bytes 84480 | tf_op jit(solution)/shard_map/all_gather | solution.py:147
  250.7 6.8 all-gather.1
  262.0 7.3 maximum_convert_fusion
  269.3 11.3 copy.303
  283.9 8.3 fusion.7
  301.9 5.1 fusion.35
  310.4 13.1 %all-to-all-done.3 = bf16[4,8,64,256]{3,2,1,0:T(8,128)(2,1)S(1)} async-done(((bf16[4,8,64,256]{3,2,1,0:T(8,128)(2,1)}), bf16[4,8,64,256]{3,2,1,0:T(8,128)(2,1)S(1)}, u32[]{:S(2)}, u32[]{:S(2)}) %all-to-all-start.3) | async-done | bytes 1048608 | tf_op jit(solution)/shard_map/all_to_all | solution.py:113
  324.1 3.9 all-to-all-start.1
  335.0 3.9 fusion.36
  356.3 4.4 subtract_convert_fusion.1
  370.9 5.4 collective-permute-done.8
  376.3 5.2 fusion.11
  385.3 33.5 %collective-permute-done.11 = bf16[2,192,1024]{2,1,0:T(8,128)(2,1)S(1)} collective-permute-done((bf16[2,192,1024]{2,1,0:T(8,128)(2,1)S(1)}, bf16[2,192,1024]{2,1,0:T(8,128)(2,1)S(1)}, u32[]{:S(2)}, u32[]{:S(2)}) %collective-permute-start.11) | collective-permute-done | bytes 786464 | tf_op jit(solution)/shard_map/ppermute | solution.py:57
  436.0 74.0 %all_to_all.91 = bf16[4,192,2048]{2,1,0:T(8,128)(2,1)} all-to-all(bf16[4,192,2048]{2,1,0:T(8,128)(2,1)S(1)} %broadcast_in_dim.70), channel_id=1, replica_groups=mesh['q'=4,'c'=2,'z'=4] {'z'}, dimensions={0} | all-to-all | bytes 6291456 | tf_op jit(solution)/shard_map/all_to_all | solution.py:113
  512.1 4.9 all-to-all-start.9
  517.9 5.0 collective-permute-done.13
  523.0 63.8 %all-to-all-done.9 = bf16[4,192,2048]{2,1,0:T(8,128)(2,1)} async-done(((bf16[4,192,2048]{2,1,0:T(8,128)(2,1)}), bf16[4,192,2048]{2,1,0:T(8,128)(2,1)}, u32[]{:S(2)}, u32[]{:S(2)}) %all-to-all-start.9) | async-done | bytes 3145760 | tf_op jit(solution)/shard_map/all_to_all | solution.py:113
  586.8 18.4 %fusion.96 = f32[1536,2048]{1,0:T(8,128)} fusion(bf16[2048,2048]{1,0:T(8,128)(2,1)} %all-gather.11.cloned.1.call-done, bf16[768,2048]{1,0:T(8,128)(2,1)} %collective-permute-done.14, bf16[768,2048]{1,0:T(8,128)(2,1)S(1)} %bitcast.314), kind=kOutput, calls=%fused_computation.279 | convolution fusion | flops 12897484800 | bytes 27262976 | tf_op jit(solution)/shard_map/dot_general | solution.py:53
  608.7 16.5 %multiply_convert_fusion.1 = (bf16[1536,1024]{1,0:T(8,128)(2,1)}, bf16[1536,1024]{1,0:T(8,128)(2,1)}, bf16[1536,1024]{1,0:T(8,128)(2,1)S(1)}) fusion(f32[1536,2048]{1,0:T(8,128)} %fusion.96, bf16[2048,1024]{1,0:T(8,128)(2,1)} %all-gather.13.cloned.1.call-done, f32[1536]{0:T(1024)S(1)} %broadcast_select_fusion.2, ...), kind=kOutput, calls=%fused_computation.48 | convolution fusion | flops 6484918272 | bytes 32512000 | tf_op jit(solution)/shard_map/dot_general | solution.py:53
  627.0 10.6 convolution_convert_fusion.8
  637.8 18.4 %fusion.97 = f32[1536,2048]{1,0:T(8,128)} fusion(bf16[2048,2048]{1,0:T(8,128)(2,1)} %all-gather.7.cloned.1.call-done, bf16[768,2048]{1,0:T(8,128)(2,1)} %collective-permute-done.14, bf16[768,2048]{1,0:T(8,128)(2,1)S(1)} %bitcast.316), kind=kOutput, calls=%fused_computation.280 | convolution fusion | flops 12897484800 | bytes 27262976 | tf_op jit(solution)/shard_map/dot_general | solution.py:53
  656.2 16.9 %multiply_convert_fusion.3 = (bf16[1536,1024]{1,0:T(8,128)(2,1)}, bf16[1536,1024]{1,0:T(8,128)(2,1)}, bf16[1536,1024]{1,0:T(8,128)(2,1)S(1)}) fusion(f32[1536,2048]{1,0:T(8,128)} %fusion.97, bf16[2048,1024]{1,0:T(8,128)(2,1)} %all-gather.9.cloned.1.call-done, f32[1536]{0:T(1024)S(1)} %broadcast_select_fusion.3, ...), kind=kOutput, calls=%fused_computation.50 | convolution fusion | flops 6484918272 | bytes 32512000 | tf_op jit(solution)/shard_map/dot_general | solution.py:53
  674.7 10.6 convolution_convert_fusion.9
  685.4 19.4 %convolution_convert_fusion.2 = bf16[2048,2048]{1,0:T(8,128)(2,1)} fusion(bf16[1536,1024]{1,0:T(8,128)(2,1)} %get-tuple-element.35, bf16[1536,1024]{1,0:T(8,128)(2,1)} %get-tuple-element.34, bf16[768,2048]{1,0:T(8,128)(2,1)} %collective-permute-done.14, bf16[768,2048]{1,0:T(8,128)(2,1)S(1)} %bitcast.317), kind=kOutput, calls=%fused_computation.24 | convolution fusion | flops 12914262016 | bytes 20971520 | tf_op jit(solution)/shard_map/dot_general | solution.py:53
  706.8 18.6 %convolution_convert_fusion.4 = bf16[1536,2048]{1,0:T(8,128)(2,1)} fusion(bf16[2048,2048]{1,0:T(8,128)(2,1)} %all-gather.11.cloned.1.call-done, bf16[1536,1024]{1,0:T(8,128)(2,1)} %get-tuple-element.35, bf16[1536,1024]{1,0:T(8,128)(2,1)S(1)} %copy-done.95), kind=kOutput, calls=%fused_computation.26 | convolution fusion | flops 12900630528 | bytes 20971520 | tf_op jit(solution)/shard_map/dot_general | solution.py:53
  725.4 16.8 %convert_add_fusion = f32[1536,2048]{1,0:T(8,128)S(1)} fusion(bf16[1536,2048]{1,0:T(8,128)(2,1)} %convolution_convert_fusion.4, bf16[2048,2048]{1,0:T(8,128)(2,1)} %all-gather.7.cloned.1.call-done, bf16[1536,1024]{1,0:T(8,128)(2,1)S(1)} %copy-done.94, bf16[1536,1024]{1,0:T(8,128)(2,1)S(1)} %copy-done.92), kind=kOutput, calls=%fused_computation.20 | convolution fusion | flops 12910067712 | bytes 33554432 | tf_op jit(solution)/shard_map/dot_general | solution.py:53
  742.2 4.6 copy-done.12
  748.9 10.8 convolution_convert_fusion.6
  759.8 16.3 %fusion.4 = (f32[1536]{0:T(1024)S(1)}, f32[1536]{0:T(1024)S(1)}, f32[1536,2048]{1,0:T(8,128)}) fusion(bf16[768,2048]{1,0:T(8,128)(2,1)} %collective-permute-done.16, bf16[768,2048]{1,0:T(8,128)(2,1)} %bitcast.54, bf16[1536,2048]{1,0:T(8,128)(2,1)} %convolution_convert_fusion.6, f32[1536]{0:T(1024)S(1)} %copy-done.85, f32[1536]{0:T(1024)S(1)} %broadcast_select_fusion.3, ...), kind=kOutput, calls=%fused_computation.15 | convolution fusion | flops 6486488064 | bytes 32530432 | tf_op jit(solution)/shard_map/dot_general | solution.py:53
  781.8 6.9 fusion.8
  788.7 5.2 all-to-all-start.10
  794.5 70.4 %all-to-all-done.10 = bf16[4,192,2048]{2,1,0:T(8,128)(2,1)} async-done(((bf16[4,192,2048]{2,1,0:T(8,128)(2,1)}), bf16[4,192,2048]{2,1,0:T(8,128)(2,1)}, u32[]{:S(2)}, u32[]{:S(2)}) %all-to-all-start.10) | async-done | bytes 3145760 | tf_op jit(solution)/shard_map/all_to_all | solution.py:117
  872.6 7.8 collective-permute-done.21
  883.1 15.4 %collective-permute-done.22 = bf16[2,192,1024]{2,1,0:T(8,128)(2,1)S(1)} collective-permute-done((bf16[2,192,1024]{2,1,0:T(8,128)(2,1)S(1)}, bf16[2,192,1024]{2,1,0:T(8,128)(2,1)S(1)}, u32[]{:S(2)}, u32[]{:S(2)}) %collective-permute-start.22) | collective-permute-done | bytes 786464 | tf_op jit(solution)/shard_map/ppermute | solution.py:57
  899.4 4.0 fusion.94
  904.5 18.5 %convolution_convert_fusion.3 = bf16[2048,2048]{1,0:T(8,128)(2,1)} fusion(bf16[1536,1024]{1,0:T(8,128)(2,1)} %get-tuple-element.33, bf16[1536,1024]{1,0:T(8,128)(2,1)S(1)} %copy-done.93, bf16[768,2048]{1,0:T(8,128)(2,1)} %collective-permute-done.14, bf16[768,2048]{1,0:T(8,128)(2,1)S(1)} %bitcast.318), kind=kOutput, calls=%fused_computation.25 | convolution fusion | flops 12914262016 | bytes 20971520 | tf_op jit(solution)/shard_map/dot_general | solution.py:53
  923.0 5.1 slice.522
  975.0 5.0 convolution_convert_fusion.11
  981.0 4.4 all-to-all-start.14
  985.5 7.0 fusion.9
  1000.4 11.7 all-to-all-done.14
  1012.1 4.7 all-to-all-start.8
  1020.8 5.4 convolution_convert_fusion
  1034.1 9.3 convolution_convert_fusion.10
  1047.3 40.4 %all-to-all-done.8 = bf16[4,192,2048]{2,1,0:T(8,128)(2,1)} async-done(((bf16[4,192,2048]{2,1,0:T(8,128)(2,1)}), bf16[4,192,2048]{2,1,0:T(8,128)(2,1)}, u32[]{:S(2)}, u32[]{:S(2)}) %all-to-all-start.8) | async-done | bytes 3145760 | tf_op jit(solution)/shard_map/all_to_all | solution.py:117
  1087.7 8.6 all_to_all.92
  1099.7 3.9 pad_maximum_fusion.12
  1106.5 4.6 all-to-all-start.13
  1111.5 4.2 fusion.10
  1116.3 3.8 convert_reduce_fusion.1
  1124.4 10.2 collective-permute-done.27
  1136.1 4.7 collective-permute-done.25
  1151.6 4.6 fusion.27
  1156.2 4.6 maximum_bitcast_fusion
  1160.8 25.2 %all-to-all-done.13 = bf16[4,192,2048]{2,1,0:T(8,128)(2,1)} async-done(((bf16[4,192,2048]{2,1,0:T(8,128)(2,1)}), bf16[4,192,2048]{2,1,0:T(8,128)(2,1)}, u32[]{:S(2)}, u32[]{:S(2)}) %all-to-all-start.13) | async-done | bytes 3145760 | tf_op jit(solution)/shard_map/all_to_all | solution.py:117
  1186.0 5.6 all-to-all-start.16
  1196.3 6.7 bitcast_convert_fusion
  1203.0 88.8 %reduce-scatter.16.cloned.1.call-done = f32[64,20]{1,0:T(8,128)} async-done(((f32[2048,20]{1,0:T(8,128)}), f32[64,20]{1,0:T(8,128)}) %reduce-scatter.16.cloned.1.call-update) | async-done | bytes 5136
  (470 shorter events, 258.4 us)
Async XLA Ops:
  7.2 579.6 %all-gather.11.cloned.1.call-start = ((), (), s32[]{:S(2)}) async-start(), calls=%async_computation.25 | async-start | bytes 10485760 | tf_op jit(solution)/shard_map/all_gather | solution.py:205
  18.5 12.5 collective-permute-start.2
  21.5 11.4 collective-permute-start
  31.0 36.8 %collective-permute-start.3 = (bf16[2,192,1024]{2,1,0:T(8,128)(2,1)S(1)}, bf16[2,192,1024]{2,1,0:T(8,128)(2,1)S(1)}, u32[]{:S(2)}, u32[]{:S(2)}) collective-permute-start(bf16[2,192,1024]{2,1,0:T(8,128)(2,1)S(1)} %get-tuple-element.93), channel_id=1, source_target_pairs={{0,8},{4,12},{8,0},{12,4},{16,24},{20,28},{24,16},{28,20},{1,9},{5... | collective-permute-start | bytes 2359304 | tf_op jit(solution)/shard_map/ppermute | solution.py:57
  33.1 36.6 %collective-permute-start.1 = (bf16[2,192,1024]{2,1,0:T(8,128)(2,1)S(1)}, bf16[2,192,1024]{2,1,0:T(8,128)(2,1)S(1)}, u32[]{:S(2)}, u32[]{:S(2)}) collective-permute-start(bf16[2,192,1024]{2,1,0:T(8,128)(2,1)S(1)} %get-tuple-element.87), channel_id=1, source_target_pairs={{0,16},{4,20},{8,24},{12,28},{16,0},{20,4},{24,8},{28,12},{1,17},{... | collective-permute-start | bytes 2359304 | tf_op jit(solution)/shard_map/ppermute | solution.py:57
  72.3 189.7 %collective-permute-start.4 = (bf16[4,192,2048]{2,1,0:T(8,128)(2,1)}, bf16[4,192,2048]{2,1,0:T(8,128)(2,1)}, u32[]{:S(2)}, u32[]{:S(2)}) collective-permute-start(bf16[4,192,2048]{2,1,0:T(8,128)(2,1)} %get-tuple-element.58), channel_id=1, source_target_pairs={{0,4},{4,0},{8,12},{12,8},{16,20},{20,16},{24,28},{28,24},{1,5},{5... | collective-permute-start | bytes 9437192 | tf_op jit(solution)/shard_map/ppermute | solution.py:57
  73.2 22.0 %collective-permute-start.7 = (bf16[64,2048]{1,0:T(8,128)(2,1)}, bf16[64,2048]{1,0:T(8,128)(2,1)}, u32[]{:S(2)}, u32[]{:S(2)}) collective-permute-start(bf16[64,2048]{1,0:T(8,128)(2,1)} %get-tuple-element.84), channel_id=1, source_target_pairs={{0,0},{1,5},{2,10},{3,11},{4,12},{5,17},{6,22},{7,23},{8,24},{9,29... | collective-permute-start | bytes 786440 | tf_op jit(solution)/shard_map/ppermute | solution.py:163
  76.8 18.5 %collective-permute-start.6 = (bf16[64,2048]{1,0:T(8,128)(2,1)}, bf16[64,2048]{1,0:T(8,128)(2,1)}, u32[]{:S(2)}, u32[]{:S(2)}) collective-permute-start(bf16[64,2048]{1,0:T(8,128)(2,1)} %get-tuple-element.85), channel_id=1, source_target_pairs={{0,0},{1,5},{2,6},{3,11},{4,12},{5,17},{6,18},{7,23},{8,24},{9,29}... | collective-permute-start | bytes 786440 | tf_op jit(solution)/shard_map/ppermute | solution.py:163
  80.4 14.8 %collective-permute-start.5 = (bf16[64,2048]{1,0:T(8,128)(2,1)}, bf16[64,2048]{1,0:T(8,128)(2,1)}, u32[]{:S(2)}, u32[]{:S(2)}) collective-permute-start(bf16[64,2048]{1,0:T(8,128)(2,1)} %get-tuple-element.83), channel_id=1, source_target_pairs={{0,0},{1,1},{2,6},{3,11},{4,12},{5,13},{6,18},{7,23},{8,24},{9,25}... | collective-permute-start | bytes 786440 | tf_op jit(solution)/shard_map/ppermute | solution.py:163
  84.0 7.8 all-to-all-start.7
  91.8 14.6 %all-to-all-start.2 = ((bf16[8,64,256]{2,1,0:T(8,128)(2,1)}), bf16[8,64,256]{2,1,0:T(8,128)(2,1)S(1)}, u32[]{:S(2)}, u32[]{:S(2)}) async-start(bf16[8,64,256]{2,1,0:T(8,128)(2,1)} %bitcast.324), calls=%async_computation.2 | async-start | bytes 524288 | tf_op jit(solution)/shard_map/all_to_all | solution.py:181
  109.6 182.6 %all-to-all-start = ((bf16[4,192,2048]{2,1,0:T(8,128)(2,1)}), bf16[4,192,2048]{2,1,0:T(8,128)(2,1)}, u32[]{:S(2)}, u32[]{:S(2)}) async-start(bf16[4,192,2048]{2,1,0:T(8,128)(2,1)} %broadcast_in_dim.56), calls=%async_computation | async-start | bytes 6291456 | tf_op jit(solution)/shard_map/all_to_all | solution.py:113
  117.3 133.4 %copy-start.88 = (s32[2,96]{1,0:T(2,128)S(1)}, s32[2,96]{1,0:T(2,128)}, u32[]{:S(2)}) copy-start(s32[2,96]{1,0:T(2,128)} %param.14) | copy-start | bytes 2308
  117.3 491.3 %all-gather.13.cloned.1.call-start = ((), (), s32[]{:S(2)}) async-start(), calls=%async_computation.26 | async-start | bytes 5242880 | tf_op jit(solution)/shard_map/all_gather | solution.py:206
  248.1 357.0 %copy-start.40 = (bf16[2048,20]{0,1:T(8,128)(2,1)}, bf16[2048,20]{0,1:T(8,128)(2,1)S(1)}, u32[]{:S(2)}) copy-start(bf16[2048,20]{0,1:T(8,128)(2,1)S(1)} %reshape.551) | copy-start | bytes 245764
  259.7 96.6 %copy-start.51 = (f32[96,64]{1,0:T(8,128)}, f32[96,64]{1,0:T(8,128)S(1)}, u32[]{:S(2)}) copy-start(f32[96,64]{1,0:T(8,128)S(1)} %get-tuple-element.106) | copy-start | bytes 73732
  293.3 30.2 %all-to-all-start.3 = ((bf16[4,8,64,256]{3,2,1,0:T(8,128)(2,1)}), bf16[4,8,64,256]{3,2,1,0:T(8,128)(2,1)S(1)}, u32[]{:S(2)}, u32[]{:S(2)}) async-start(bf16[4,8,64,256]{3,2,1,0:T(8,128)(2,1)} %broadcast_in_dim.66), calls=%async_computation.3 | async-start | bytes 2097152 | tf_op jit(solution)/shard_map/all_to_all | solution.py:113
  324.1 9.8 all-to-all-start.1
  328.0 309.7 %all-gather.7.cloned.1.call-start = ((), (), s32[]{:S(2)}) async-start(), calls=%async_computation.23 | async-start | bytes 10485760 | tf_op jit(solution)/shard_map/all_gather | solution.py:205
  370.4 5.9 collective-permute-start.8
  381.6 37.2 %collective-permute-start.11 = (bf16[2,192,1024]{2,1,0:T(8,128)(2,1)S(1)}, bf16[2,192,1024]{2,1,0:T(8,128)(2,1)S(1)}, u32[]{:S(2)}, u32[]{:S(2)}) collective-permute-start(bf16[2,192,1024]{2,1,0:T(8,128)(2,1)S(1)} %slice.357), channel_id=1, source_target_pairs={{0,16},{4,20},{8,24},{12,28},{16,0},{20,4},{24,8},{28,12},{1,17},{... | collective-permute-start | bytes 2359304 | tf_op jit(solution)/shard_map/ppermute | solution.py:57
  383.8 37.2 %collective-permute-start.9 = (bf16[2,192,1024]{2,1,0:T(8,128)(2,1)S(1)}, bf16[2,192,1024]{2,1,0:T(8,128)(2,1)S(1)}, u32[]{:S(2)}, u32[]{:S(2)}) collective-permute-start(bf16[2,192,1024]{2,1,0:T(8,128)(2,1)S(1)} %slice_bitcast_fusion.6), channel_id=1, source_target_pairs={{0,8},{4,12},{8,0},{12,4},{16,24},{20,28},{24,16},{28,20},{1,9},{5... | collective-permute-start | bytes 2359304 | tf_op jit(solution)/shard_map/ppermute | solution.py:57
  419.1 10.9 collective-permute-start.12
  421.4 10.7 collective-permute-start.10
  423.5 12.1 all-to-all-start.4
  435.6 74.5 %copy-start.8 = (bf16[192,2048]{1,0:T(8,128)(2,1)}, bf16[192,2048]{1,0:T(8,128)(2,1)S(1)}, u32[]{:S(2)}) copy-start(bf16[192,2048]{1,0:T(8,128)(2,1)S(1)} %multiply_convert_fusion.9) | copy-start | bytes 2359300
  436.0 74.0 %copy-start.15 = (bf16[192,2048]{1,0:T(8,128)(2,1)S(1)}, bf16[192,2048]{1,0:T(8,128)(2,1)}, u32[]{:S(2)}) copy-start(bf16[192,2048]{1,0:T(8,128)(2,1)} %param.13) | copy-start | bytes 2359300
  512.1 74.7 %all-to-all-start.9 = ((bf16[4,192,2048]{2,1,0:T(8,128)(2,1)}), bf16[4,192,2048]{2,1,0:T(8,128)(2,1)}, u32[]{:S(2)}, u32[]{:S(2)}) async-start(bf16[4,192,2048]{2,1,0:T(8,128)(2,1)} %broadcast_in_dim.74), calls=%async_computation.9 | async-start | bytes 6291456 | tf_op jit(solution)/shard_map/all_to_all | solution.py:113
  517.0 139.2 %all-gather.9.cloned.1.call-start = ((), (), s32[]{:S(2)}) async-start(), calls=%async_computation.24 | async-start | bytes 5242880 | tf_op jit(solution)/shard_map/all_gather | solution.py:206
  517.1 69.7 %collective-permute-start.14 = (bf16[768,2048]{1,0:T(8,128)(2,1)S(1)}, bf16[768,2048]{1,0:T(8,128)(2,1)}, u32[]{:S(2)}, u32[]{:S(2)}) collective-permute-start(bf16[768,2048]{1,0:T(8,128)(2,1)S(1)} %bitcast.313), channel_id=1, source_target_pairs={{0,4},{4,0},{1,5},{5,1},{2,6},{6,2},{3,7},{7,3},{8,12},{12,8},{9,1... | collective-permute-start | bytes 9437192 | tf_op jit(solution)/shard_map/ppermute | solution.py:122
  517.6 513.2 %reduce-scatter.14.cloned.1.call-start = ((), (), s32[]{:S(2)}) async-start(), calls=%async_computation.30 | async-start | bytes 5242880 | tf_op jit(solution)/shard_map/reduce_scatter | solution.py:300
  517.8 5.1 collective-permute-start.13
  523.0 85.6 %copy-start.70 = (pred[1536]{0:T(1024)(128)(4,1)}, pred[1536]{0:T(1024)(128)(4,1)S(1)}, u32[]{:S(2)}) copy-start(pred[1536]{0:T(1024)(128)(4,1)S(1)} %get-tuple-element.25) | copy-start | bytes 4612
  523.0 114.8 %copy-start.68 = (pred[1536]{0:T(1024)(128)(4,1)}, pred[1536]{0:T(1024)(128)(4,1)S(1)}, u32[]{:S(2)}) copy-start(pred[1536]{0:T(1024)(128)(4,1)S(1)} %get-tuple-element.24) | copy-start | bytes 4612
  586.8 21.9 %collective-permute-start.16 = (bf16[768,2048]{1,0:T(8,128)(2,1)}, bf16[768,2048]{1,0:T(8,128)(2,1)}, u32[]{:S(2)}, u32[]{:S(2)}) collective-permute-start(bf16[768,2048]{1,0:T(8,128)(2,1)} %bitcast.54), channel_id=1, source_target_pairs={{0,4},{4,0},{1,5},{5,1},{2,6},{6,2},{3,7},{7,3},{8,12},{12,8},{9,1... | collective-permute-start | bytes 9437192 | tf_op jit(solution)/shard_map/ppermute | solution.py:122
  637.7 393.1 %reduce-scatter.12.cloned.1.call-start = ((), (), s32[]{:S(2)}) async-start(), calls=%async_computation.29 | async-start | bytes 5242880 | tf_op jit(solution)/shard_map/reduce_scatter | solution.py:300
  685.4 470.7 %reduce-scatter.10.cloned.1.call-start = ((), (), s32[]{:S(2)}) async-start(), calls=%async_computation.28 | async-start | bytes 10485760 | tf_op jit(solution)/shard_map/reduce_scatter | solution.py:305
  747.2 34.6 %collective-permute-start.17 = (bf16[768,2048]{1,0:T(8,128)(2,1)S(1)}, bf16[768,2048]{1,0:T(8,128)(2,1)}, u32[]{:S(2)}, u32[]{:S(2)}) collective-permute-start(bf16[768,2048]{1,0:T(8,128)(2,1)S(1)} %slice.521), channel_id=1, source_target_pairs={{0,4},{4,0},{1,5},{5,1},{2,6},{6,2},{3,7},{7,3},{8,12},{12,8},{9,1... | collective-permute-start | bytes 9437192 | tf_op jit(solution)/shard_map/ppermute | solution.py:122
  776.3 1.4 collective-permute-start.18
  778.3 10.4 all-to-all-start.11
  788.7 76.2 %all-to-all-start.10 = ((bf16[4,192,2048]{2,1,0:T(8,128)(2,1)}), bf16[4,192,2048]{2,1,0:T(8,128)(2,1)}, u32[]{:S(2)}, u32[]{:S(2)}) async-start(bf16[4,192,2048]{2,1,0:T(8,128)(2,1)} %bitcast.55), calls=%async_computation.10 | async-start | bytes 6291456 | tf_op jit(solution)/shard_map/all_to_all | solution.py:117
  794.0 73.7 %copy-start.66 = (f32[192]{0:T(256)S(1)}, f32[192]{0:T(256)}, u32[]{:S(2)}) copy-start(f32[192]{0:T(256)} %copy-done.65) | copy-start | bytes 2308
  794.0 362.2 %reduce-scatter.8.cloned.1.call-start = ((), (), s32[]{:S(2)}) async-start(), calls=%async_computation.27 | async-start | bytes 10485760 | tf_op jit(solution)/shard_map/reduce_scatter | solution.py:305
  870.2 10.2 collective-permute-start.21
  871.7 10.0 collective-permute-start.19
  880.5 17.9 %collective-permute-start.22 = (bf16[2,192,1024]{2,1,0:T(8,128)(2,1)S(1)}, bf16[2,192,1024]{2,1,0:T(8,128)(2,1)S(1)}, u32[]{:S(2)}, u32[]{:S(2)}) collective-permute-start(bf16[2,192,1024]{2,1,0:T(8,128)(2,1)S(1)} %get-tuple-element.82), channel_id=1, source_target_pairs={{0,8},{4,12},{8,0},{12,4},{16,24},{20,28},{24,16},{28,20},{1,9},{5... | collective-permute-start | bytes 2359304 | tf_op jit(solution)/shard_map/ppermute | solution.py:57
  881.9 17.3 %collective-permute-start.20 = (bf16[2,192,1024]{2,1,0:T(8,128)(2,1)S(1)}, bf16[2,192,1024]{2,1,0:T(8,128)(2,1)S(1)}, u32[]{:S(2)}, u32[]{:S(2)}) collective-permute-start(bf16[2,192,1024]{2,1,0:T(8,128)(2,1)S(1)} %get-tuple-element.76), channel_id=1, source_target_pairs={{0,16},{4,20},{8,24},{12,28},{16,0},{20,4},{24,8},{28,12},{1,17},{... | collective-permute-start | bytes 2359304 | tf_op jit(solution)/shard_map/ppermute | solution.py:57
  903.3 24.7 %collective-permute-start.23 = (bf16[4,192,2048]{2,1,0:T(8,128)(2,1)}, bf16[4,192,2048]{2,1,0:T(8,128)(2,1)}, u32[]{:S(2)}, u32[]{:S(2)}) collective-permute-start(bf16[4,192,2048]{2,1,0:T(8,128)(2,1)} %get-tuple-element.53), channel_id=1, source_target_pairs={{0,4},{4,0},{8,12},{12,8},{16,20},{20,16},{24,28},{28,24},{1,5},{5... | collective-permute-start | bytes 9437192 | tf_op jit(solution)/shard_map/ppermute | solution.py:57
  928.1 57.4 %collective-permute-start.15 = (bf16[768,2048]{1,0:T(8,128)(2,1)}, bf16[768,2048]{1,0:T(8,128)(2,1)}, u32[]{:S(2)}, u32[]{:S(2)}) collective-permute-start(bf16[768,2048]{1,0:T(8,128)(2,1)} %slice.522), channel_id=1, source_target_pairs={{0,4},{4,0},{1,5},{5,1},{2,6},{6,2},{3,7},{7,3},{8,12},{12,8},{9,1... | collective-permute-start | bytes 9437192 | tf_op jit(solution)/shard_map/ppermute | solution.py:122
  971.4 9.6 all-to-all-start.12
  981.0 31.2 %all-to-all-start.14 = ((bf16[4,8,64,256]{3,2,1,0:T(8,128)(2,1)}), bf16[4,8,64,256]{3,2,1,0:T(8,128)(2,1)}, u32[]{:S(2)}, u32[]{:S(2)}) async-start(bf16[4,8,64,256]{3,2,1,0:T(8,128)(2,1)} %bitcast.310), calls=%async_computation.14 | async-start | bytes 2097152 | tf_op jit(solution)/shard_map/all_to_all | solution.py:117
  1012.1 75.5 %all-to-all-start.8 = ((bf16[4,192,2048]{2,1,0:T(8,128)(2,1)}), bf16[4,192,2048]{2,1,0:T(8,128)(2,1)}, u32[]{:S(2)}, u32[]{:S(2)}) async-start(bf16[4,192,2048]{2,1,0:T(8,128)(2,1)} %bitcast.290), calls=%async_computation.8 | async-start | bytes 6291456 | tf_op jit(solution)/shard_map/all_to_all | solution.py:117
  1029.8 81.7 %collective-permute-start.24 = (bf16[4,192,2048]{2,1,0:T(8,128)(2,1)}, bf16[4,192,2048]{2,1,0:T(8,128)(2,1)}, u32[]{:S(2)}, u32[]{:S(2)}) collective-permute-start(bf16[4,192,2048]{2,1,0:T(8,128)(2,1)} %slice_bitcast_fusion), channel_id=1, source_target_pairs={{0,4},{4,0},{8,12},{12,8},{16,20},{20,16},{24,28},{28,24},{1,5},{5... | collective-permute-start | bytes 9437192 | tf_op jit(solution)/shard_map/ppermute | solution.py:57
  1096.2 10.3 all-to-all-start.15
  1106.5 79.5 %all-to-all-start.13 = ((bf16[4,192,2048]{2,1,0:T(8,128)(2,1)}), bf16[4,192,2048]{2,1,0:T(8,128)(2,1)}, u32[]{:S(2)}, u32[]{:S(2)}) async-start(bf16[4,192,2048]{2,1,0:T(8,128)(2,1)} %bitcast.289), calls=%async_computation.13 | async-start | bytes 6291456 | tf_op jit(solution)/shard_map/all_to_all | solution.py:117
  1111.2 180.7 %reduce-scatter.16.cloned.1.call-start = ((), (), s32[]{:S(2)}) async-start(), calls=%async_computation.31 | async-start | bytes 1081344
  1115.7 18.8 %collective-permute-start.27 = (bf16[2,192,1024]{2,1,0:T(8,128)(2,1)S(1)}, bf16[2,192,1024]{2,1,0:T(8,128)(2,1)S(1)}, u32[]{:S(2)}, u32[]{:S(2)}) collective-permute-start(bf16[2,192,1024]{2,1,0:T(8,128)(2,1)S(1)} %slice.392), channel_id=1, source_target_pairs={{0,16},{4,20},{8,24},{12,28},{16,0},{20,4},{24,8},{28,12},{1,17},{... | collective-permute-start | bytes 2359304 | tf_op jit(solution)/shard_map/ppermute | solution.py:57
  1120.4 20.5 %collective-permute-start.25 = (bf16[2,192,1024]{2,1,0:T(8,128)(2,1)S(1)}, bf16[2,192,1024]{2,1,0:T(8,128)(2,1)S(1)}, u32[]{:S(2)}, u32[]{:S(2)}) collective-permute-start(bf16[2,192,1024]{2,1,0:T(8,128)(2,1)S(1)} %slice_bitcast_fusion.4), channel_id=1, source_target_pairs={{0,8},{4,12},{8,0},{12,4},{16,24},{20,28},{24,16},{28,20},{1,9},{5... | collective-permute-start | bytes 2359304 | tf_op jit(solution)/shard_map/ppermute | solution.py:57
  1134.9 12.4 collective-permute-start.28
  1141.2 7.8 collective-permute-start.26
  1186.0 10.3 all-to-all-start.16
  1194.3 100.5 %collective-permute-start.31 = (bf16[64,2048]{1,0:T(8,128)(2,1)S(1)}, bf16[64,2048]{1,0:T(8,128)(2,1)S(1)}, u32[]{:S(2)}, u32[]{:S(2)}) collective-permute-start(bf16[64,2048]{1,0:T(8,128)(2,1)S(1)} %get-tuple-element.72), channel_id=1, source_target_pairs={{0,0},{5,1},{10,2},{11,3},{12,4},{17,5},{22,6},{23,7},{24,8},{29,9... | collective-permute-start | bytes 786440 | tf_op jit(solution)/shard_map/ppermute | solution.py:374
  1194.9 99.8 %collective-permute-start.30 = (bf16[64,2048]{1,0:T(8,128)(2,1)S(1)}, bf16[64,2048]{1,0:T(8,128)(2,1)S(1)}, u32[]{:S(2)}, u32[]{:S(2)}) collective-permute-start(bf16[64,2048]{1,0:T(8,128)(2,1)S(1)} %get-tuple-element.73), channel_id=1, source_target_pairs={{0,0},{5,1},{6,2},{11,3},{12,4},{17,5},{18,6},{23,7},{24,8},{29,9}... | collective-permute-start | bytes 786440 | tf_op jit(solution)/shard_map/ppermute | solution.py:374
  1195.6 99.1 %collective-permute-start.29 = (bf16[64,2048]{1,0:T(8,128)(2,1)S(1)}, bf16[64,2048]{1,0:T(8,128)(2,1)S(1)}, u32[]{:S(2)}, u32[]{:S(2)}) collective-permute-start(bf16[64,2048]{1,0:T(8,128)(2,1)S(1)} %get-tuple-element.71), channel_id=1, source_target_pairs={{0,0},{1,1},{6,2},{11,3},{12,4},{13,5},{18,6},{23,7},{24,8},{25,9}... | collective-permute-start | bytes 786440 | tf_op jit(solution)/shard_map/ppermute | solution.py:374
  (90 other events, 647.0 us)
Sparse Core Ops, SparseCore 0:
  18.4 116.6 all-gather.10
  136.9 53.6 all-gather.12
  371.0 106.2 all-gather.6
  519.4 52.9 all-gather.8
  637.8 50.7 reduce-scatter.13
  691.4 52.5 reduce-scatter.11
  747.7 86.3 reduce-scatter.9
  923.1 84.7 reduce-scatter.7
  1151.7 140.1 reduce-scatter.15

commit v2 on v1

v2 whole, which is shorter than its diff:
```python
import functools

import jax
import jax.numpy as jnp
from jax import lax
from jax.experimental import pallas as pl
from jax.experimental.pallas import tpu as pltpu
from jax.sharding import Mesh
from jax.sharding import PartitionSpec as P

D = 2048
H = 16
HD = 128
FF = 1024
TOP = 8
E = 16
LEN = 96

NORM_EPS = 1e-05
ROPE_BASE = 10000.0
PRECISE = lax.Precision.HIGHEST
DP = ("q", "c")
ALL = ("q", "c", "z")
f32 = jnp.float32
bf16 = jnp.bfloat16


def inverse_rms(field_in):
    return lax.rsqrt(jnp.mean(field_in * field_in, axis=-1, keepdims=True) + NORM_EPS)


def rope_tables(length, head_dim):
    half_dim = head_dim // 2
    frequency = ROPE_BASE ** (-(jnp.arange(half_dim).astype(f32) * 2.0) / head_dim)
    angles = jnp.arange(length).astype(f32)[:, None] * frequency[None, :]
    return jnp.cos(angles), jnp.sin(angles)


def norm_back(grad_normed, normed, inverse):
    return inverse * (grad_normed - normed * jnp.mean(grad_normed * normed, axis=-1, keepdims=True))


def mm(a, b, ca, cb):
    return lax.dot_general(a, b, (((ca,), (cb,)), ((), ())), preferred_element_type=f32)


def flip(value, size, bit):
    return lax.ppermute(value, DP, [(i, i ^ (1 << bit)) for i in range(size)])


def relative(size):
    return [high * 2 + core for core in range(2) for high in range(size // 2)]


def bit_lists(size):
    high = list(range(1, size.bit_length() - 1))
    return high, high[::-1]


def gather_dp(value, size):
    width = value.shape[-1] // 2
    pieces = []
    for part, order in zip((value[:, :width], value[:, width:]), bit_lists(size)):
        out, have = part, []
        for bit in order:
            axis = sum(1 for other in have if other > bit)
            out = jnp.stack([out, flip(out, size, bit)], axis=axis)
            have.append(bit)
        pieces.append(out.reshape(-1, width))
    both = jnp.concatenate(pieces, axis=-1)
    return jnp.concatenate([both, flip(both, size, 0)], axis=0)


def scatter_dp(parts, size):
    rows, width = parts.shape[0] // size, parts.shape[1]
    half_rows = parts.shape[0] // 2
    got = flip(parts[half_rows:], size, 0)
    summed = (parts[:half_rows].astype(f32) + got.astype(f32)).astype(bf16)
    highs = size.bit_length() - 2
    halves = []
    for half, order in enumerate(bit_lists(size)):
        cur = summed[:, half * (width // 2) : (half + 1) * (width // 2)]
        cur = cur.reshape([2] * highs + [rows, width // 2])
        left = list(range(highs, 0, -1))
        for k, bit in enumerate(order):
            axis = left.index(bit)
            left.remove(bit)
            keep = lax.index_in_dim(cur, 0, axis, keepdims=False)
            send = lax.index_in_dim(cur, 1, axis, keepdims=False)
            total = keep.astype(f32) + flip(send, size, bit).astype(f32)
            cur = total if k == len(order) - 1 else total.astype(bf16)
        halves.append(cur)
    return jnp.concatenate(halves, axis=-1)


def sum_dp(value, size):
    count = size.bit_length() - 1
    shape = value.shape
    value = value[:2].reshape((2,) + (2,) * count + (-1,))
    for bit in range(count):
        value = value + jnp.flip(flip(value, size, bit), 1 if bit == 0 else count - bit + 1)
    return jnp.pad(value.reshape(2, shape[1]), ((0, 6), (0, 0)))


def line(value, zs, step):
    return lax.ppermute(value, "z", [(j, j + step) for j in range(zs) if 0 <= j + step < zs])


def gather_z(value, zs, zi):
    right, left = [value], [value]
    for _ in range(zs - 1):
        right.append(line(right[-1], zs, 1))
        left.append(line(left[-1], zs, -1))
    return [value] + [jnp.where(zi >= k, right[k], left[zs - k]) for k in range(1, zs)]


def gather_z_true(value, zs, zi):
    blocks = jnp.stack(gather_z(value, zs, zi)[::-1] * 2, axis=0)
    return lax.dynamic_slice_in_dim(blocks, zs - 1 - zi, zs, 0)


def scatter_z(parts):
    zs = len(parts)
    right, left = None, None
    for s in range(1, zs):
        go_right = parts[s] if right is None else (parts[s].astype(f32) + right).astype(bf16)
        go_left = parts[zs - s] if left is None else (parts[zs - s].astype(f32) + left).astype(bf16)
        right = line(go_right, zs, 1).astype(f32)
        left = line(go_left, zs, -1).astype(f32)
    return parts[0].astype(f32) + right + left


def swap_core(value):
    return lax.ppermute(value, "c", [(0, 1), (1, 0)])


def gather_cz(value, zs, zi):
    got = jnp.concatenate(gather_z(value, zs, zi), axis=0)
    return jnp.concatenate([got, swap_core(got)], axis=0)


def scatter_cz(parts, zs):
    half = parts.shape[0] // 2
    mixed = parts[:half].astype(f32) + swap_core(parts[half:].astype(bf16)).astype(f32)
    mixed = mixed.astype(bf16)
    block = half // zs
    return scatter_z([mixed[k * block : (k + 1) * block] for k in range(zs)])


BLOCK = 4 * LEN


def kdot(a, b, ca, cb):
    return lax.dot_general(a, b, (((ca,), (cb,)), ((), ())), preferred_element_type=f32)


def to_rows(first, second):
    lane = lax.broadcasted_iota(jnp.int32, (first.shape[0], 128), 1)
    both = jnp.where(lane == 0, first, jnp.where(lane == 1, second, 0.0))
    return both.T[:8]


def to_cols(block):
    cols = jnp.concatenate([block] * 16, axis=0).T
    return cols[:, 0:1], cols[:, 1:2]


def qkv_kernel(width, tok_ref, gain_ref, w_ref, hid_ref, raw_ref, sum_ref):
    x = tok_ref[...].astype(f32)
    inverse = lax.rsqrt(jnp.mean(x * x, axis=-1, keepdims=True) + NORM_EPS)
    hidden = (x * inverse * gain_ref[...]).astype(bf16)
    hid_ref[...] = hidden
    raw = kdot(hidden, w_ref[...], 1, 1)
    raw_ref[...] = raw
    q, k = raw[:, :width], raw[:, width : 2 * width]
    sum_ref[...] = to_rows(
        jnp.sum(q * q, axis=-1, keepdims=True), jnp.sum(k * k, axis=-1, keepdims=True)
    )


def spin(x, cos, sin):
    return x * cos + pltpu.roll(x, HD // 2, 1) * sin


def heads_of(raw, inv_q, inv_k, gain_ref, cos, sin, width, head):
    lo = head * HD
    normed_q = raw[:, lo : lo + HD] * inv_q
    normed_k = raw[:, width + lo : width + lo + HD] * inv_k
    query = spin(normed_q * gain_ref[0:1, lo : lo + HD], cos, sin).astype(bf16)
    key = spin(normed_k * gain_ref[1:2, lo : lo + HD], cos, sin).astype(bf16)
    value = raw[:, 2 * width + lo : 2 * width + lo + HD].astype(bf16)
    return normed_q, normed_k, query, key, value


def probs_of(query, key, mask):
    scores = jnp.where(mask > 0.5, kdot(query, key, 1, 1) * HD ** (-0.5), -1e30)
    scores = jnp.exp(scores - jnp.max(scores, axis=-1, keepdims=True))
    return scores / jnp.sum(scores, axis=-1, keepdims=True)


def inverses(sum_ref):
    ss_q, ss_k = to_cols(sum_ref[...])
    return lax.rsqrt(ss_q / D + NORM_EPS), lax.rsqrt(ss_k / D + NORM_EPS)


def attend_kernel(width, raw_ref, sum_ref, gain_ref, cos_ref, sin_ref, mask_ref, w_ref, att_ref, part_ref):
    inv_q, inv_k = inverses(sum_ref)
    raw = raw_ref[...]
    cos, sin = cos_ref[...], sin_ref[...]
    for head in range(width // HD):
        _, _, query, key, value = heads_of(raw, inv_q, inv_k, gain_ref, cos, sin, width, head)
        for s in range(BLOCK // LEN):
            at = slice(s * LEN, (s + 1) * LEN)
            probs = probs_of(query[at], key[at], mask_ref[s])
            att_ref[at, head * HD : (head + 1) * HD] = kdot(
                probs.astype(bf16), value[at], 1, 0
            ).astype(bf16)
    part_ref[...] = kdot(att_ref[...], w_ref[...], 1, 1).astype(bf16)


def attend_back_kernel(
    width, raw_ref, sum_ref, gain_ref, cos_ref, sin_ref, mask_ref, w_ref, grad_ref,
    back_ref, dv_ref, dot_ref, gsum_ref,
):
    inv_q, inv_k = inverses(sum_ref)
    raw = raw_ref[...]
    cos, sin = cos_ref[...], sin_ref[...]
    grad_heads = kdot(grad_ref[...], w_ref[...], 1, 0).astype(bf16)

    @pl.when(pl.program_id(0) == 0)
    def _():
        gsum_ref[...] = jnp.zeros_like(gsum_ref)

    dot_q = dot_k = 0.0
    for head in range(width // HD):
        lo = head * HD
        normed_q, normed_k, query, key, value = heads_of(
            raw, inv_q, inv_k, gain_ref, cos, sin, width, head
        )
        grads_q, grads_k = [], []
        for s in range(BLOCK // LEN):
            at = slice(s * LEN, (s + 1) * LEN)
            probs = probs_of(query[at], key[at], mask_ref[s])
            grad = grad_heads[at, lo : lo + HD]
            grad_probs = kdot(grad, value[at], 1, 1)
            dv_ref[at, lo : lo + HD] = kdot(probs.astype(bf16), grad, 0, 0).astype(bf16)
            delta = jnp.sum(probs * grad_probs, axis=-1, keepdims=True)
            grad_scores = (probs * (grad_probs - delta)).astype(bf16)
            grads_q.append(kdot(grad_scores, key[at], 1, 0))
            grads_k.append(kdot(grad_scores, query[at], 0, 0))
        grad_nq = spin(jnp.concatenate(grads_q, axis=0) * HD ** (-0.5), cos, -sin)
        grad_nk = spin(jnp.concatenate(grads_k, axis=0) * HD ** (-0.5), cos, -sin)
        prod_q, prod_k = grad_nq * normed_q, grad_nk * normed_k
        gsum_ref[0:1, lo : lo + HD] += jnp.sum(prod_q, axis=0, keepdims=True)
        gsum_ref[1:2, lo : lo + HD] += jnp.sum(prod_k, axis=0, keepdims=True)
        gain_q, gain_k = gain_ref[0:1, lo : lo + HD], gain_ref[1:2, lo : lo + HD]
        dot_q = dot_q + jnp.sum(prod_q * gain_q, axis=-1, keepdims=True)
        dot_k = dot_k + jnp.sum(prod_k * gain_k, axis=-1, keepdims=True)
        back_ref[:, lo : lo + HD] = grad_nq * gain_q
        back_ref[:, width + lo : width + lo + HD] = grad_nk * gain_k
    dot_ref[...] = to_rows(dot_q, dot_k)


def project_back_kernel(
    width, raw_ref, sum_ref, back_ref, dv_ref, dot_ref, w_ref, proj_ref, part_ref
):
    inv_q, inv_k = inverses(sum_ref)
    mean_q, mean_k = to_cols(dot_ref[...] / D)
    normed_q = raw_ref[:, :width] * inv_q
    normed_k = raw_ref[:, width : 2 * width] * inv_k
    proj_ref[:, :width] = (inv_q * (back_ref[:, :width] - normed_q * mean_q)).astype(bf16)
    proj_ref[:, width : 2 * width] = (
        inv_k * (back_ref[:, width:] - normed_k * mean_k)
    ).astype(bf16)
    proj_ref[:, 2 * width :] = dv_ref[...]
    part_ref[...] = kdot(proj_ref[...], w_ref[...], 1, 0).astype(bf16)


def by_rows(cols):
    return pl.BlockSpec((BLOCK, cols), lambda i: (i, 0))


def across(rows):
    return pl.BlockSpec((rows, BLOCK), lambda i: (0, i))


def whole(shape):
    return pl.BlockSpec(shape, lambda i: (0,) * len(shape))


def run_blocks(body, rows, in_specs, out_specs, out_shape, args, flops):
    nbytes = sum(arg.size * arg.dtype.itemsize for arg in args)
    nbytes += sum(out.size * out.dtype.itemsize for out in out_shape)
    return pl.pallas_call(
        body,
        grid=(rows // BLOCK,),
        in_specs=in_specs,
        out_specs=out_specs,
        out_shape=out_shape,
        cost_estimate=pl.CostEstimate(flops=flops, bytes_accessed=nbytes, transcendentals=0),
    )(*args)


def shape_of(rows, cols, dtype):
    return jax.ShapeDtypeStruct((rows, cols), dtype)


def per_device(
    tokens, cotangent, segments, routes, w_qkv, w_out, norm_gains, w_router, w_gate_up, w_down
):
    zs = lax.axis_size("z")
    dps = lax.axis_size("q") * 2
    world = dps * zs
    qi, ci, zi = lax.axis_index("q"), lax.axis_index("c"), lax.axis_index("z")
    di = qi * 2 + ci
    rows = tokens.shape[0]
    seqs = rows // LEN
    width = D // dps
    local_experts = E // zs
    mine = local_experts // 2
    sub = w_qkv.shape[0] // 3
    orow = w_out.shape[0]
    all_rows = dps * rows
    all_seqs = dps * seqs

    def unit_perm(t, back):
        pairs = []
        for i in range(dps):
            for j in range(zs):
                dest = (3 * i + (3 * j + t) // zs) % dps
                src_dev, dst_dev = i * zs + j, dest * zs + j
                pairs.append((dst_dev, src_dev) if back else (src_dev, dst_dev))
        return pairs

    moved = [
        lax.ppermute(w_qkv[t * sub : (t + 1) * sub], ALL, unit_perm(t, False)) for t in range(3)
    ]
    inv3 = pow(3, -1, dps)
    slot_of = [[0, 0, 0] for _ in range(dps)]
    type_of = [[0, 0, 0] for _ in range(dps)]
    for i in range(dps):
        for s in range(3):
            src = (inv3 * (i - s)) % dps
            kind = (3 * src + s) // dps
            slot_of[i][kind] = s
            type_of[i][s] = kind
    slot_of = jnp.asarray(slot_of, jnp.int32)[di]
    type_of = jnp.asarray(type_of, jnp.int32)[di]

    mini = jnp.concatenate(
        [
            norm_gains.reshape(-1),
            w_router.reshape(-1),
            segments.astype(bf16).reshape(-1),
            routes.astype(bf16).reshape(-1),
        ]
    )
    minis = lax.all_to_all(
        jnp.broadcast_to(mini[None], (world,) + mini.shape), ALL, 0, 0, tiled=True
    )
    at = 0
    split = []
    for part in (norm_gains, w_router, segments, routes):
        split.append(minis[:, at : at + part.size])
        at += part.size
    gains_f = split[0].reshape(D, 4).astype(f32)
    router_low = split[1].reshape(D, E)
    router_f = router_low.astype(f32)
    seg_all = split[2].reshape(dps, zs, seqs, LEN)
    seg_own = lax.dynamic_index_in_dim(seg_all, zi, 1, keepdims=False)
    seg_own = seg_own[jnp.asarray(relative(dps)) ^ di].reshape(all_seqs, LEN)
    routes_all = split[3].reshape(dps // 2, 2, zs, rows, TOP)
    routes_own = lax.dynamic_index_in_dim(routes_all, qi, 0, keepdims=False)
    routes_own = routes_own[jnp.stack([ci, 1 - ci])][:, (zi - jnp.arange(zs)) % zs]
    routes_g = routes_own.reshape(2 * zs * rows, TOP).astype(jnp.int32)
    position = jnp.arange(LEN)
    causal = position[:, None] >= position[None, :]
    mask = (causal[None] & (seg_own[:, :, None] == seg_own[:, None, :])).astype(f32)
    own_gains = lax.dynamic_slice(gains_f, (di * width, 0), (width, 4))
    gain_rows = jnp.pad(own_gains[:, 1:3].T, ((0, 6), (0, 0)))
    cos_table, sin_table = rope_tables(LEN, HD)
    cos_full = jnp.tile(jnp.concatenate([cos_table, cos_table], axis=1), (BLOCK // LEN, 1))
    sin_full = jnp.tile(jnp.concatenate([-sin_table, sin_table], axis=1), (BLOCK // LEN, 1))

    tok_g = gather_dp(tokens, dps)
    qkv_slots = gather_z_true(jnp.concatenate(moved, axis=0), zs, zi).reshape(3, width, D)
    w_three = jnp.concatenate(
        [lax.dynamic_index_in_dim(qkv_slots, slot_of[k], 0, keepdims=False) for k in range(3)],
        axis=0,
    )
    out_cols = lax.all_to_all(
        w_out.reshape(orow, dps, width).transpose(1, 0, 2), DP, 0, 0, tiled=True
    )
    w_out_c = gather_z_true(out_cols, zs, zi).transpose(1, 0, 2, 3).reshape(D, width)

    def core_half(weight):
        swapped = lax.all_to_all(
            weight.reshape((2, mine) + weight.shape[1:]), "c", 0, 0, tiled=True
        )
        return [swapped[:, e].reshape((2 * weight.shape[1], weight.shape[2])) for e in range(mine)]

    gu_half = core_half(w_gate_up)
    down_half = core_half(w_down)
    expert_w = []
    for e in range(mine):
        expert_w.append(
            (
                lax.all_gather(gu_half[e], "q", axis=0, tiled=True),
                lax.all_gather(down_half[e], "q", axis=0, tiled=True),
            )
        )

    hidden_one, raw, sums = run_blocks(
        functools.partial(qkv_kernel, width),
        all_rows,
        [by_rows(D), whole((1, D)), whole((3 * width, D))],
        [by_rows(D), by_rows(3 * width), across(8)],
        [
            shape_of(all_rows, D, bf16),
            shape_of(all_rows, 3 * width, f32),
            shape_of(8, all_rows, f32),
        ],
        (tok_g, gains_f[:, 0][None], w_three),
        6 * all_rows * width * D,
    )
    dy_g = gather_cz(cotangent, zs, zi)
    sums = sum_dp(sums, dps)
    mask_spec = pl.BlockSpec((BLOCK // LEN, LEN, LEN), lambda i: (i, 0, 0))
    table_specs = [whole((8, width)), whole((BLOCK, HD)), whole((BLOCK, HD)), mask_spec]
    tables = (gain_rows, cos_full, sin_full, mask)
    attended, part = run_blocks(
        functools.partial(attend_kernel, width),
        all_rows,
        [by_rows(3 * width), across(8)] + table_specs + [whole((D, width))],
        [by_rows(width), by_rows(D)],
        [shape_of(all_rows, width, bf16), shape_of(all_rows, D, bf16)],
        (raw, sums) + tables + (w_out_c,),
        3 * all_rows * width * D,
    )
    part, dy_g = lax.optimization_barrier((part, dy_g))
    attn_out = scatter_dp(part, dps)
    x_float = tokens.astype(f32)
    inverse_one = inverse_rms(x_float)
    normed_one = x_float * inverse_one
    residual = x_float + attn_out
    inverse_two = inverse_rms(residual)
    normed_two = residual * inverse_two
    hidden_two = (normed_two * gains_f[:, 3]).astype(bf16)
    router_probs = jax.nn.softmax(mm(hidden_two, router_low, 1, 0), axis=-1)

    hidden_g = gather_cz(hidden_two, zs, zi)
    router_g = jax.nn.softmax(mm(hidden_g, router_low, 1, 0), axis=-1)
    dy_f = dy_g.astype(f32)
    first_expert = zi * local_experts + ci * mine

    passes = []
    for e in range(mine):
        gate_up, down = expert_w[e]
        expert = first_expert + e
        picked = jnp.any(routes_g == expert, axis=1, keepdims=True)
        prob = jnp.sum(
            jnp.where(jnp.arange(E)[None] == expert, router_g, 0.0), axis=1, keepdims=True
        )
        gate_val = jnp.where(picked, prob, 0.0)
        gate_and_up = mm(hidden_g, gate_up, 1, 1)
        g_part = gate_and_up[:, :FF]
        u_part = gate_and_up[:, FF:]
        sig = jax.nn.sigmoid(g_part)
        silu = g_part * sig
        act = (silu * u_part).astype(bf16)
        expert_out = mm(act, down, 1, 1).astype(bf16).astype(f32)
        grad_gate = jnp.where(picked[:, 0], jnp.sum(dy_f * expert_out, axis=1), 0.0)
        grad_eo = (gate_val * dy_f).astype(bf16)
        grad_act = mm(grad_eo, down, 1, 0)
        grad_g = grad_act * u_part * sig * (1.0 + g_part * (1.0 - sig))
        grad_u = grad_act * silu
        grad_both = jnp.concatenate([grad_g, grad_u], axis=-1).astype(bf16)
        rows_back = mm(grad_both, gate_up, 1, 0).astype(bf16).astype(f32)
        dn = mm(grad_eo, act, 0, 0).astype(bf16)
        gu = mm(grad_both, hidden_g, 0, 0).astype(bf16)
        passes.append(
            dict(
                out=gate_val * expert_out,
                back=rows_back,
                gate=grad_gate,
                dn=lax.psum_scatter(dn, "q", scatter_dimension=0, tiled=True),
                gu=lax.psum_scatter(gu, "q", scatter_dimension=0, tiled=True),
            )
        )

    hid_part = sum([p["back"] for p in passes[1:]], passes[0]["back"])
    out_part = sum([p["out"] for p in passes[1:]], passes[0]["out"])
    grad_hidden = scatter_cz(hid_part, zs)
    cols = jnp.stack([p["gate"] for p in passes], axis=0).reshape(mine, 2, zs, rows)
    cols = jnp.where(ci == 0, cols, cols[:, ::-1])
    cols = cols[:, :, (zi - jnp.arange(zs)) % zs]
    got = lax.all_to_all(
        cols.transpose(1, 2, 0, 3).reshape(2 * zs, mine, rows), ("c", "z"), 0, 0, tiled=True
    )
    gp = got.reshape(2, zs, mine, rows).transpose(1, 0, 2, 3).reshape(E, rows).T

    grad_logits = router_probs * (gp - jnp.sum(router_probs * gp, axis=-1, keepdims=True))
    grad_router = lax.dot_general(
        hidden_two.astype(f32), grad_logits, (((0,), (0,)), ((), ())), precision=PRECISE
    )
    grad_hidden = grad_hidden + jnp.dot(grad_logits, router_f.T, precision=PRECISE)
    gain_two = jnp.sum(grad_hidden * normed_two, axis=0)
    grad_residual = cotangent.astype(f32) + norm_back(
        grad_hidden * gains_f[:, 3], normed_two, inverse_two
    )

    grad_attn_g = gather_dp(grad_residual.astype(bf16), dps)
    back, dv, dots, gain_sums = run_blocks(
        functools.partial(attend_back_kernel, width),
        all_rows,
        [by_rows(3 * width), across(8)] + table_specs + [whole((D, width)), by_rows(D)],
        [by_rows(2 * width), by_rows(width), across(8), whole((8, width))],
        [
            shape_of(all_rows, 2 * width, f32),
            shape_of(all_rows, width, bf16),
            shape_of(8, all_rows, f32),
            shape_of(8, width, f32),
        ],
        (raw, sums) + tables + (w_out_c, grad_attn_g),
        5 * all_rows * width * D,
    )
    dots = sum_dp(dots, dps)
    grad_projected, part = run_blocks(
        functools.partial(project_back_kernel, width),
        all_rows,
        [
            by_rows(3 * width), across(8), by_rows(2 * width), by_rows(width), across(8),
            whole((3 * width, D)),
        ],
        [by_rows(3 * width), by_rows(D)],
        [shape_of(all_rows, 3 * width, bf16), shape_of(all_rows, D, bf16)],
        (raw, sums, back, dv, dots, w_three),
        6 * all_rows * width * D,
    )
    grad_h1 = scatter_dp(part, dps)
    gain_one = jnp.sum(grad_h1 * normed_one, axis=0)
    grad_tokens = grad_residual + norm_back(grad_h1 * gains_f[:, 0], normed_one, inverse_one)
    result = residual + scatter_cz(out_part, zs)

    def z_parts(value):
        return [
            lax.dynamic_index_in_dim(value, (zi - k) % zs, 0, keepdims=False) for k in range(zs)
        ]

    grad_out_c = mm(grad_attn_g, attended, 0, 0)
    grad_cols = scatter_z(
        z_parts(grad_out_c.astype(bf16).reshape(dps, zs, orow, width).transpose(1, 0, 2, 3))
    ).astype(bf16)
    grad_out = (
        lax.all_to_all(grad_cols, DP, 0, 0, tiled=True)
        .transpose(1, 0, 2)
        .reshape(orow, D)
        .astype(f32)
    )
    grad_three = mm(grad_projected, hidden_one, 0, 0).astype(bf16).reshape(3, width, D)
    grad_slots = jnp.concatenate(
        [lax.dynamic_index_in_dim(grad_three, type_of[s], 0, keepdims=True) for s in range(3)],
        axis=0,
    )
    own_slots = scatter_z(z_parts(grad_slots.reshape(zs, 3 * sub, D))).astype(bf16)
    grad_qkv = jnp.concatenate(
        [
            lax.ppermute(own_slots[t * sub : (t + 1) * sub], ALL, unit_perm(t, True))
            for t in range(3)
        ],
        axis=0,
    ).astype(f32)

    shard_cols = lax.dynamic_update_slice(jnp.zeros((D, 2), f32), gain_sums[:2].T, (di * width, 0))
    small_grads = jnp.concatenate(
        [gain_one[:, None], shard_cols, gain_two[:, None], grad_router], axis=1
    )
    small_own = jnp.sum(
        lax.all_to_all(
            small_grads.reshape(world, D * (E + 4) // world), ALL, 0, 0, tiled=True
        ),
        axis=0,
    ).reshape(D // world, E + 4)

    def core_back(parts):
        stacked = jnp.stack(parts, axis=0)
        split = stacked.reshape((mine, 2, stacked.shape[1] // 2, stacked.shape[2]))
        got = lax.all_to_all(split.transpose(1, 0, 2, 3), "c", 0, 0, tiled=True)
        return got.reshape((local_experts,) + got.shape[2:]).astype(f32)

    return (
        result.astype(bf16),
        grad_tokens,
        grad_qkv,
        grad_out,
        small_own[:, :4],
        small_own[:, 4:],
        core_back([p["gu"] for p in passes]),
        core_back([p["dn"] for p in passes]),
    )


def solution(mesh):
    dps, zs = mesh.shape["dp"], mesh.shape["fsdp"]
    inner = Mesh(mesh.devices.reshape(dps // 2, 2, zs), ALL)
    rows = P(ALL, None)
    experts = P("z", DP, None)
    in_specs = (rows,) * 8 + (experts,) * 2
    out_specs = (rows,) * 6 + (experts,) * 2
    return jax.shard_map(
        per_device, mesh=inner, in_specs=in_specs, out_specs=out_specs, check_vma=False
    )
```

time: 1310 us -> 1040 us (0.79)
  blocking collectives: 219 us -> 15.6 us
  waiting for transfers between devices: 465 us -> 272 us
  starting transfers between devices: 105 us -> 224 us
  Pallas kernels: 0 us -> 66.1 us
  local copies, waits for them, and re-layouts: 130 us -> 84.5 us
  matrix products: 236 us -> 214 us
    all_to_all x11 -> x3, waiting for transfers between devices: 225 us -> 17.5 us  [the longest x1 12.8 us: per_device(): lax.all_to_all(cols.transpose(1, 2, 0, 3).reshape(2 * zs, mine, rows), ('...]
    ppermute x0 -> x48, waiting for transfers between devices: none -> 158 us  [line(): lax.ppermute(value, 'z', [(j, j + step) for j in range(zs) if 0 <= j + st...]
    ppermute x0 -> x48, starting transfers between devices: none -> 133 us  [line(): lax.ppermute(value, 'z', [(j, j + step) for j in range(zs) if 0 <= j + st...]
    all_gather x2 -> x0, blocking collectives: 127 us -> none  [the longest x1 121 us: per_device(): lax.all_gather(jnp.concatenate([norm_gains, w_router], axis=1), ALL, axis...]
    unnamed x10 -> x8, waiting for transfers between devices: 89.4 us -> 0.13 us
    all_to_all x1 -> x0, blocking collectives: 74 us -> none  [gather_z(): return lax.all_to_all(spread, 'z', 0, 0, tiled=True)]
    pallas_call x0 -> x4, Pallas kernels: none -> 66.1 us  [run_blocks(): pl.pallas_call(body, grid=(rows // BLOCK,), in_specs=in_specs, out_specs=...]
    ppermute x20 -> x26, waiting for transfers between devices: 130 us -> 94.4 us  [flip(): return lax.ppermute(value, DP, [(i, i ^ 1 << bit) for i in range(size)])]
  transfers between devices with their start and end apart: 56 -> 99, of which waited for: 28 -> 44; matrix products, arithmetic and copies ran while one was open for 35% -> 38% of each run, Pallas kernels for 0% -> 6%
where the time goes in v2:
time: 1040 us; the launch traced here: 1020 us
  waiting for transfers between devices  272 us (26%)
  starting transfers between devices  224 us (22%)
  matrix products  214 us (21%)
  other arithmetic  124 us (12%)
  local copies, waits for them, and re-layouts  84.5 us (8%)
  Pallas kernels  66.1 us (6%)
  between operations  22.6 us (2%)
  blocking collectives  15.6 us (2%)
    dot_general x16, matrix products, mm(): lax.dot_general(a, b, (((ca,), (cb,)), ((), ())), preferred_element_type=...  213 us
    ppermute x48, waiting for transfers between devices, line(): lax.ppermute(value, 'z', [(j, j + step) for j in range(zs) if 0 <= j + st...  158 us
    ppermute x48, starting transfers between devices, line(): lax.ppermute(value, 'z', [(j, j + step) for j in range(zs) if 0 <= j + st...  133 us
    ppermute x26, waiting for transfers between devices, flip(): return lax.ppermute(value, DP, [(i, i ^ 1 << bit) for i in range(size)])  94.4 us
    pallas_call x4, Pallas kernels, run_blocks(): pl.pallas_call(body, grid=(rows // BLOCK,), in_specs=in_specs, out_specs=...  66.1 us
    ppermute x26, starting transfers between devices, flip(): return lax.ppermute(value, DP, [(i, i ^ 1 << bit) for i in range(size)])  37.3 us
    concatenate x2, other arithmetic, gather_dp(): return jnp.concatenate([both, flip(both, size, 0)], axis=0)  27.1 us
    unnamed x155, local copies, waits for them, and re-layouts  23.9 us
  transfers between devices with their start and end apart: 99, of which 44 were waited for; matrix products, arithmetic and copies ran while one was open for 38% of the time, Pallas kernels for 6%

profile of v2, /device:TPU:0, one launch (start us, length us, event | category | flops | bytes accessed | tf_op | source)
XLA Modules:
  0.0 1023.1 jit_solution(10617443750928771081)
XLA Ops:
  7.2 8.5 all_to_all.54
  18.3 5.0 all-to-all-start.3
  62.7 15.0 %all-to-all-start = ((bf16[32,2,1504]{2,1,0:T(2,128)(2,1)}), bf16[32,2,1504]{2,1,0:T(2,128)(2,1)S(1)}, u32[]{:S(2)}, u32[]{:S(2)}) async-start(bf16[32,2,1504]{2,1,0:T(2,128)(2,1)} %reshape.537), calls=%async_computation | async-start | bytes 393216 | tf_op jit(solution)/shard_map/all_to_all | solution.py:358
  80.0 5.3 collective-permute-start.17
  90.6 5.1 collective-permute-start.18
  100.4 4.6 collective-permute-start.23
  112.8 13.3 %collective-permute-done.19 = bf16[8,64,256]{2,1,0:T(8,128)(2,1)S(1)} collective-permute-done((bf16[8,64,256]{2,1,0:T(8,128)(2,1)}, bf16[8,64,256]{2,1,0:T(8,128)(2,1)S(1)}, u32[]{:S(2)}, u32[]{:S(2)}) %collective-permute-start.19) | collective-permute-done | bytes 262176 | tf_op jit(solution)/shard_map/ppermute | solution.py:106
  139.3 5.6 collective-permute-start.27
  149.6 10.2 collective-permute-done.3
  166.5 4.6 collective-permute-start.28
  174.9 7.2 collective-permute-done.9
  192.9 6.0 collective-permute-done.28
  203.2 9.4 collective-permute-done.10
  216.9 15.7 %pad_maximum_fusion.tok_ref = bf16[1536,2048]{1,0:T(8,128)(2,1)} fusion(bf16[768,2048]{1,0:T(8,128)(2,1)} %collective-permute-done.4, bf16[768,1024]{1,0:T(8,128)(2,1)S(1)} %bitcast.287, bf16[768,1024]{1,0:T(8,128)(2,1)S(1)} %bitcast.289), kind=kLoop, calls=%fused_computation.28 | loop fusion | flops 18874368 | bytes 12582912 | tf_op jit(solution)/shard_map/concatenate | solution.py:71
  232.6 11.8 %shard_map.188 = (bf16[1536,2048]{1,0:T(8,128)(2,1)}, f32[1536,768]{1,0:T(8,128)}, f32[8,1536]{1,0:T(8,128)}) custom-call(bf16[1536,2048]{1,0:T(8,128)(2,1)} %pad_maximum_fusion.tok_ref, f32[1,2048]{1,0:T(1,128)} %bitcast.339, bf16[768,2048]{1,0:T(8,128)(2,1)} %pad_maximum_fusion.9.w_ref), custom_call_target="tpu_custom_call" | custom-call | flops 4831838208 | bytes 20504576 | tf_op jit(solution)/shard_map/pallas_call | solution.py:294
  256.5 17.8 %shard_map.189 = (bf16[1536,256]{1,0:T(8,128)(2,1)}, bf16[1536,2048]{1,0:T(8,128)(2,1)}) custom-call(f32[1536,768]{1,0:T(8,128)} %get-tuple-element.21.raw_ref, f32[8,1536]{1,0:T(8,128)} %pad.11.sum_ref, f32[8,256]{1,0:T(8,128)} %pad.12.gain_ref, f32[384,128]{1,0:T(8,128)} %bitcast.333, f32[384,128]{1,0:T(8,128)} %bitcast.335, ...), custom_call_target="tpu_custom_call" | custom-call | flops 2415919104 | bytes 13885440 | tf_op jit(solution)/shard_map/pallas_call | solution.py:294
  280.9 5.9 collective-permute-done.30
  294.4 33.0 %collective-permute-done.31 = bf16[2,192,1024]{2,1,0:T(8,128)(2,1)S(1)} collective-permute-done((bf16[2,192,1024]{2,1,0:T(8,128)(2,1)S(1)}, bf16[2,192,1024]{2,1,0:T(8,128)(2,1)S(1)}, u32[]{:S(2)}, u32[]{:S(2)}) %collective-permute-start.31) | collective-permute-done | bytes 786464 | tf_op jit(solution)/shard_map/ppermute | solution.py:48
  331.5 11.6 %collective-permute-done.32 = bf16[192,1024]{1,0:T(8,128)(2,1)S(1)} collective-permute-done((bf16[192,1024]{1,0:T(8,128)(2,1)S(1)}, bf16[192,1024]{1,0:T(8,128)(2,1)S(1)}, u32[]{:S(2)}, u32[]{:S(2)}) %collective-permute-start.32) | collective-permute-done | bytes 393248 | tf_op jit(solution)/shard_map/ppermute | solution.py:48
  347.0 4.6 collective-permute-start.35
  351.6 15.0 %collective-permute-done.36 = bf16[192,2048]{1,0:T(8,128)(2,1)S(1)} collective-permute-done((bf16[192,2048]{1,0:T(8,128)(2,1)S(1)}, bf16[192,2048]{1,0:T(8,128)(2,1)S(1)}, u32[]{:S(2)}, u32[]{:S(2)}) %collective-permute-start.36) | collective-permute-done | bytes 786464 | tf_op jit(solution)/shard_map/ppermute | solution.py:106
  367.9 4.6 collective-permute-start.39
  372.5 14.3 %collective-permute-done.37 = bf16[192,2048]{1,0:T(8,128)(2,1)S(1)} collective-permute-done((bf16[192,2048]{1,0:T(8,128)(2,1)S(1)}, bf16[192,2048]{1,0:T(8,128)(2,1)S(1)}, u32[]{:S(2)}, u32[]{:S(2)}) %collective-permute-start.37) | collective-permute-done | bytes 786464 | tf_op jit(solution)/shard_map/ppermute | solution.py:106
  388.0 4.6 collective-permute-start.40
  392.7 13.5 %collective-permute-done.38 = bf16[192,2048]{1,0:T(8,128)(2,1)S(1)} collective-permute-done((bf16[192,2048]{1,0:T(8,128)(2,1)S(1)}, bf16[192,2048]{1,0:T(8,128)(2,1)S(1)}, u32[]{:S(2)}, u32[]{:S(2)}) %collective-permute-start.38) | collective-permute-done | bytes 786464 | tf_op jit(solution)/shard_map/ppermute | solution.py:106
  426.5 19.2 %fusion.80 = f32[1536,2048]{1,0:T(8,128)} fusion(bf16[1536,2048]{1,0:T(8,128)(2,1)} %constant_dynamic-update-slice_fusion.8, bf16[2048,2048]{1,0:T(8,128)(2,1)} %all-gather.9.cloned.1.call-done), kind=kOutput, calls=%fused_computation.288 | convolution fusion | flops 12884901888 | bytes 27262976 | tf_op jit(solution)/shard_map/dot_general | solution.py:44
  445.9 18.7 %multiply_convert_fusion.1 = (bf16[1536,1024]{1,0:T(8,128)(2,1)}, bf16[1536,1024]{1,0:T(8,128)(2,1)}, bf16[1536,1024]{1,0:T(8,128)(2,1)S(1)}) fusion(f32[1536,2048]{1,0:T(8,128)} %fusion.80, bf16[2048,1024]{1,0:T(8,128)(2,1)} %all-gather.11.cloned.1.call-done, bf16[1536,2048]{1,0:T(8,128)(2,1)} %constant_dynamic-update-slice_fusion.3, ...), kind=kOutput, calls=%fused_computation.34 | convolution fusion | flops 6475481088 | bytes 32512000 | tf_op jit(solution)/shard_map/dot_general | solution.py:44
  466.4 11.7 %convolution_convert_fusion.6 = bf16[2048,1024]{1,0:T(8,128)(2,1)} fusion(bf16[1536,1024]{1,0:T(8,128)(2,1)S(1)} %get-tuple-element.96, bf16[1536,2048]{1,0:T(8,128)(2,1)} %constant_dynamic-update-slice_fusion.3, f32[1536]{0:T(1024)S(1)} %broadcast_select_fusion.13), kind=kOutput, calls=%fused_computation.46 | convolution fusion | flops 6453985280 | bytes 13637632 | tf_op jit(solution)/shard_map/dot_general | solution.py:44
  478.3 19.3 %fusion.79 = f32[1536,2048]{1,0:T(8,128)} fusion(bf16[1536,2048]{1,0:T(8,128)(2,1)} %constant_dynamic-update-slice_fusion.8, bf16[2048,2048]{1,0:T(8,128)(2,1)} %all-gather.5.cloned.1.call-done), kind=kOutput, calls=%fused_computation.287 | convolution fusion | flops 12884901888 | bytes 27262976 | tf_op jit(solution)/shard_map/dot_general | solution.py:44
  497.5 19.1 %multiply_convert_fusion.3 = (bf16[1536,1024]{1,0:T(8,128)(2,1)}, bf16[1536,1024]{1,0:T(8,128)(2,1)}, bf16[1536,1024]{1,0:T(8,128)(2,1)S(1)}) fusion(f32[1536,2048]{1,0:T(8,128)} %fusion.79, bf16[2048,1024]{1,0:T(8,128)(2,1)} %all-gather.7.cloned.1.call-done, bf16[1536,2048]{1,0:T(8,128)(2,1)} %constant_dynamic-update-slice_fusion.3, ...), kind=kOutput, calls=%fused_computation.36 | convolution fusion | flops 6475481088 | bytes 32512000 | tf_op jit(solution)/shard_map/dot_general | solution.py:44
  518.2 11.8 %convolution_convert_fusion.7 = bf16[2048,1024]{1,0:T(8,128)(2,1)} fusion(bf16[1536,1024]{1,0:T(8,128)(2,1)S(1)} %get-tuple-element.95, bf16[1536,2048]{1,0:T(8,128)(2,1)} %constant_dynamic-update-slice_fusion.3, f32[1536]{0:T(1024)S(1)} %broadcast_select_fusion.14), kind=kOutput, calls=%fused_computation.47 | convolution fusion | flops 6453985280 | bytes 13637632 | tf_op jit(solution)/shard_map/dot_general | solution.py:44
  530.1 19.6 %convolution_convert_fusion.2 = bf16[1536,2048]{1,0:T(8,128)(2,1)} fusion(bf16[2048,2048]{1,0:T(8,128)(2,1)} %all-gather.9.cloned.1.call-done, bf16[1536,1024]{1,0:T(8,128)(2,1)} %get-tuple-element.94, bf16[1536,1024]{1,0:T(8,128)(2,1)} %get-tuple-element.93), kind=kOutput, calls=%fused_computation.18 | convolution fusion | flops 12900630528 | bytes 20971520 | tf_op jit(solution)/shard_map/dot_general | solution.py:44
  549.7 16.7 %convert_add_fusion = f32[1536,2048]{1,0:T(8,128)S(1)} fusion(bf16[1536,2048]{1,0:T(8,128)(2,1)} %convolution_convert_fusion.2, bf16[2048,2048]{1,0:T(8,128)(2,1)} %all-gather.5.cloned.1.call-done, bf16[1536,1024]{1,0:T(8,128)(2,1)S(1)} %copy-done.63, bf16[1536,1024]{1,0:T(8,128)(2,1)S(1)} %copy-done.61), kind=kOutput, calls=%fused_computation.15 | convolution fusion | flops 12910067712 | bytes 33554432 | tf_op jit(solution)/shard_map/dot_general | solution.py:44
  566.4 4.6 copy-done.18
  575.2 17.6 %convolution_convert_fusion = bf16[2048,2048]{1,0:T(8,128)(2,1)} fusion(bf16[1536,2048]{1,0:T(8,128)(2,1)} %constant_dynamic-update-slice_fusion.8, bf16[1536,1024]{1,0:T(8,128)(2,1)S(1)} %copy-done.66, bf16[1536,1024]{1,0:T(8,128)(2,1)S(1)} %copy-done.65), kind=kOutput, calls=%fused_computation.16 | convolution fusion | flops 12901679104 | bytes 20971520 | tf_op jit(solution)/shard_map/dot_general | solution.py:44
  594.5 5.0 fusion.5
  604.9 8.7 convolution_convert_fusion.4
  613.6 7.1 collective-permute-done.50
  631.6 14.4 %fusion.3 = (f32[1536]{0:T(1024)S(1)}, f32[1536]{0:T(1024)S(1)}, f32[1536,2048]{1,0:T(8,128)}) fusion(bf16[1536,2048]{1,0:T(8,128)(2,1)S(1)} %bitcast.338, bf16[1536,2048]{1,0:T(8,128)(2,1)} %convolution_convert_fusion.4, f32[1536]{0:T(1024)S(1)} %copy-done.48, f32[1536]{0:T(1024)S(1)} %broadcast_select_fusion.14, bf16[1536,1024]{1,0:T(8,128)(2,1)S(1)} %copy-done.58, ...), kind=kOutput, calls=%fused_computation.13 | convolution fusion | flops 6477050880 | bytes 32530432 | tf_op jit(solution)/shard_map/dot_general | solution.py:44
  664.9 12.8 %all-to-all-done.4 = f32[8,2,192]{2,1,0:T(2,128)S(1)} async-done(((f32[8,2,192]{2,1,0:T(2,128)}), f32[8,2,192]{2,1,0:T(2,128)S(1)}, u32[]{:S(2)}, u32[]{:S(2)}) %all-to-all-start.4) | async-done | bytes 12320 | tf_op jit(solution)/shard_map/all_to_all | solution.py:497
  684.6 8.9 collective-permute-done.58
  696.4 16.5 %collective-permute-done.59 = bf16[2,192,1024]{2,1,0:T(8,128)(2,1)S(1)} collective-permute-done((bf16[2,192,1024]{2,1,0:T(8,128)(2,1)S(1)}, bf16[2,192,1024]{2,1,0:T(8,128)(2,1)S(1)}, u32[]{:S(2)}, u32[]{:S(2)}) %collective-permute-start.59) | collective-permute-done | bytes 786464 | tf_op jit(solution)/shard_map/ppermute | solution.py:48
  716.8 5.1 slice.428
  722.4 18.3 %convolution_convert_fusion.1 = bf16[2048,2048]{1,0:T(8,128)(2,1)} fusion(bf16[1536,2048]{1,0:T(8,128)(2,1)} %constant_dynamic-update-slice_fusion.8, bf16[1536,1024]{1,0:T(8,128)(2,1)S(1)} %copy-done.64, bf16[1536,1024]{1,0:T(8,128)(2,1)S(1)} %copy-done.62), kind=kOutput, calls=%fused_computation.17 | convolution fusion | flops 12901679104 | bytes 20971520 | tf_op jit(solution)/shard_map/dot_general | solution.py:44
  740.8 11.4 %pad_maximum_fusion.3.grad_ref = bf16[1536,2048]{1,0:T(8,128)(2,1)} fusion(bf16[768,2048]{1,0:T(8,128)(2,1)} %collective-permute-done.60, bf16[768,1024]{1,0:T(8,128)(2,1)S(1)} %bitcast.281, bf16[768,1024]{1,0:T(8,128)(2,1)} %bitcast.284), kind=kLoop, calls=%fused_computation.31 | loop fusion | flops 18874368 | bytes 12582912 | tf_op jit(solution)/shard_map/concatenate | solution.py:71
  752.1 25.2 %shard_map.190 = (f32[1536,512]{1,0:T(8,128)}, bf16[1536,256]{1,0:T(8,128)(2,1)}, f32[8,1536]{1,0:T(8,128)}, f32[8,256]{1,0:T(8,128)}) custom-call(f32[1536,768]{1,0:T(8,128)} %get-tuple-element.21.raw_ref, f32[8,1536]{1,0:T(8,128)} %pad.11.sum_ref, f32[8,256]{1,0:T(8,128)} %pad.12.gain_ref, f32[384,128]{1,0:T(8,128)} %bitcast.334, f32[384,128]{1,0:T(8,128)} %bitcast.336, ...), custom_call_target="tpu_custom_call" | custom-call | flops 4026531840 | bytes 17088512 | tf_op jit(solution)/shard_map/pallas_call | solution.py:294
  778.4 7.1 fusion.6
  786.1 4.8 convolution_convert_fusion.9
  795.6 11.2 %shard_map.191 = (bf16[1536,768]{1,0:T(8,128)(2,1)}, bf16[1536,2048]{1,0:T(8,128)(2,1)}) custom-call(f32[1536,768]{1,0:T(8,128)} %get-tuple-element.21.raw_ref, f32[8,1536]{1,0:T(8,128)} %pad.11.sum_ref, f32[1536,512]{1,0:T(8,128)} %get-tuple-element.26.back_ref, bf16[1536,256]{1,0:T(8,128)(2,1)} %get-tuple-element.27.dv_ref, f32[8,1536]{1,0:T(8,128)} %pad.13.dot_ref, ...), custom_call_target="tpu_custom_call" | custom-call | flops 4831838208 | bytes 20545536 | tf_op jit(solution)/shard_map/pallas_call | solution.py:294
  806.8 8.2 convolution_convert_fusion.8
  827.3 5.1 collective-permute-start.43
  836.4 5.3 collective-permute-done.69
  846.5 12.1 %collective-permute-done.43 = bf16[192,2048]{1,0:T(8,128)(2,1)S(1)} collective-permute-done((bf16[192,2048]{1,0:T(8,128)(2,1)S(1)}, bf16[192,2048]{1,0:T(8,128)(2,1)S(1)}, u32[]{:S(2)}, u32[]{:S(2)}) %collective-permute-start.43) | collective-permute-done | bytes 786464 | tf_op jit(solution)/shard_map/ppermute | solution.py:106
  867.3 5.2 collective-permute-start.80
  878.2 14.1 %collective-permute-done.44 = bf16[192,2048]{1,0:T(8,128)(2,1)S(1)} collective-permute-done((bf16[192,2048]{1,0:T(8,128)(2,1)S(1)}, bf16[192,2048]{1,0:T(8,128)(2,1)S(1)}, u32[]{:S(2)}, u32[]{:S(2)}) %collective-permute-start.44) | collective-permute-done | bytes 786464 | tf_op jit(solution)/shard_map/ppermute | solution.py:106
  895.4 5.9 collective-permute-start.45
  904.4 4.9 all-to-all-start.8
  926.6 4.6 collective-permute-start.71
  947.9 7.4 collective-permute-done.74
  963.6 8.9 collective-permute-start.68
  984.5 6.4 all-to-all-start.6
  991.0 4.9 fusion.27
  1004.0 7.1 all_to_all.55
  1011.1 4.7 bitcast_convert_fusion
  (525 shorter events, 328.9 us)
Async XLA Ops:
  7.2 419.3 %all-gather.9.cloned.1.call-start = ((), (), s32[]{:S(2)}) async-start(), calls=%async_computation.15 | async-start | bytes 10485760 | tf_op jit(solution)/shard_map/all_gather | solution.py:408
  24.1 55.9 %collective-permute-start.7 = (bf16[64,2048]{1,0:T(8,128)(2,1)}, bf16[64,2048]{1,0:T(8,128)(2,1)}, u32[]{:S(2)}, u32[]{:S(2)}) collective-permute-start(bf16[64,2048]{1,0:T(8,128)(2,1)} %get-tuple-element.138), channel_id=1, source_target_pairs={{0,0},{1,5},{2,10},{3,11},{4,12},{5,17},{6,22},{7,23},{8,24},{9,29... | collective-permute-start | bytes 786440 | tf_op jit(solution)/shard_map/ppermute | solution.py:336
  27.7 31.3 %collective-permute-start.5 = (bf16[64,2048]{1,0:T(8,128)(2,1)S(1)}, bf16[64,2048]{1,0:T(8,128)(2,1)S(1)}, u32[]{:S(2)}, u32[]{:S(2)}) collective-permute-start(bf16[64,2048]{1,0:T(8,128)(2,1)S(1)} %get-tuple-element.139), channel_id=1, source_target_pairs={{0,0},{1,1},{2,6},{3,11},{4,12},{5,13},{6,18},{7,23},{8,24},{9,25}... | collective-permute-start | bytes 786440 | tf_op jit(solution)/shard_map/ppermute | solution.py:336
  28.3 49.3 %collective-permute-start.6 = (bf16[64,2048]{1,0:T(8,128)(2,1)}, bf16[64,2048]{1,0:T(8,128)(2,1)}, u32[]{:S(2)}, u32[]{:S(2)}) collective-permute-start(bf16[64,2048]{1,0:T(8,128)(2,1)} %get-tuple-element.140), channel_id=1, source_target_pairs={{0,0},{1,5},{2,6},{3,11},{4,12},{5,17},{6,18},{7,23},{8,24},{9,29}... | collective-permute-start | bytes 786440 | tf_op jit(solution)/shard_map/ppermute | solution.py:336
  32.0 99.5 %collective-permute-start.24 = (bf16[192,2048]{1,0:T(8,128)(2,1)S(1)}, bf16[192,2048]{1,0:T(8,128)(2,1)}, u32[]{:S(2)}, u32[]{:S(2)}) collective-permute-start(bf16[192,2048]{1,0:T(8,128)(2,1)S(1)} %copy-done.11), channel_id=1, source_target_pairs={{1,0},{2,1},{3,2},{5,4},{6,5},{7,6},{9,8},{10,9},{11,10},{13,12},{... | collective-permute-start | bytes 2359304 | tf_op jit(solution)/shard_map/ppermute | solution.py:106
  34.5 74.6 %collective-permute-start.2 = (bf16[192,1024]{1,0:T(8,128)(2,1)}, bf16[192,1024]{1,0:T(8,128)(2,1)}, u32[]{:S(2)}, u32[]{:S(2)}) collective-permute-start(bf16[192,1024]{1,0:T(8,128)(2,1)} %get-tuple-element.145), channel_id=1, source_target_pairs={{0,16},{4,20},{8,24},{12,28},{16,0},{20,4},{24,8},{28,12},{1,17},{... | collective-permute-start | bytes 1179656 | tf_op jit(solution)/shard_map/ppermute | solution.py:48
  38.3 24.4 %all-to-all-start.1 = ((bf16[8,64,256]{2,1,0:T(8,128)(2,1)}), bf16[8,64,256]{2,1,0:T(8,128)(2,1)}, u32[]{:S(2)}, u32[]{:S(2)}) async-start(bf16[8,64,256]{2,1,0:T(8,128)(2,1)} %bitcast.271), calls=%async_computation.1 | async-start | bytes 524288 | tf_op jit(solution)/shard_map/all_to_all | solution.py:391
  42.4 403.5 %all-gather.11.cloned.1.call-start = ((), (), s32[]{:S(2)}) async-start(), calls=%async_computation.16 | async-start | bytes 5242880 | tf_op jit(solution)/shard_map/all_gather | solution.py:409
  59.7 40.7 %collective-permute-start = (bf16[192,1024]{1,0:T(8,128)(2,1)}, bf16[192,1024]{1,0:T(8,128)(2,1)}, u32[]{:S(2)}, u32[]{:S(2)}) collective-permute-start(bf16[192,1024]{1,0:T(8,128)(2,1)} %get-tuple-element.146), channel_id=1, source_target_pairs={{0,8},{4,12},{8,0},{12,4},{16,24},{20,28},{24,16},{28,20},{1,9},{5... | collective-permute-start | bytes 1179656 | tf_op jit(solution)/shard_map/ppermute | solution.py:48
  62.7 24.4 %all-to-all-start = ((bf16[32,2,1504]{2,1,0:T(2,128)(2,1)}), bf16[32,2,1504]{2,1,0:T(2,128)(2,1)S(1)}, u32[]{:S(2)}, u32[]{:S(2)}) async-start(bf16[32,2,1504]{2,1,0:T(2,128)(2,1)} %reshape.537), calls=%async_computation | async-start | bytes 393216 | tf_op jit(solution)/shard_map/all_to_all | solution.py:358
  77.6 400.6 %all-gather.5.cloned.1.call-start = ((), (), s32[]{:S(2)}) async-start(), calls=%async_computation.13 | async-start | bytes 10485760 | tf_op jit(solution)/shard_map/all_gather | solution.py:408
  100.4 35.3 %collective-permute-start.23 = (bf16[192,2048]{1,0:T(8,128)(2,1)S(1)}, bf16[192,2048]{1,0:T(8,128)(2,1)S(1)}, u32[]{:S(2)}, u32[]{:S(2)}) collective-permute-start(bf16[192,2048]{1,0:T(8,128)(2,1)S(1)} %copy-done.11), channel_id=1, source_target_pairs={{0,1},{1,2},{2,3},{4,5},{5,6},{6,7},{8,9},{9,10},{10,11},{12,13},{... | collective-permute-start | bytes 2359304 | tf_op jit(solution)/shard_map/ppermute | solution.py:106
  105.0 21.2 %collective-permute-start.19 = (bf16[8,64,256]{2,1,0:T(8,128)(2,1)}, bf16[8,64,256]{2,1,0:T(8,128)(2,1)S(1)}, u32[]{:S(2)}, u32[]{:S(2)}) collective-permute-start(bf16[8,64,256]{2,1,0:T(8,128)(2,1)} %collective-permute-done.18), channel_id=1, source_target_pairs={{0,1},{1,2},{2,3},{4,5},{5,6},{6,7},{8,9},{9,10},{10,11},{12,13},{... | collective-permute-start | bytes 786440 | tf_op jit(solution)/shard_map/ppermute | solution.py:106
  109.1 30.2 %collective-permute-start.11 = (bf16[192,2048]{1,0:T(8,128)(2,1)S(1)}, bf16[192,2048]{1,0:T(8,128)(2,1)S(1)}, u32[]{:S(2)}, u32[]{:S(2)}) collective-permute-start(bf16[192,2048]{1,0:T(8,128)(2,1)S(1)} %constant_dynamic-update-slice_fusion), channel_id=1, source_target_pairs={{1,0},{2,1},{3,2},{5,4},{6,5},{7,6},{9,8},{10,9},{11,10},{13,12},{... | collective-permute-start | bytes 2359304 | tf_op jit(solution)/shard_map/ppermute | solution.py:106
  110.4 23.8 %collective-permute-start.22 = (bf16[8,64,256]{2,1,0:T(8,128)(2,1)S(1)}, bf16[8,64,256]{2,1,0:T(8,128)(2,1)S(1)}, u32[]{:S(2)}, u32[]{:S(2)}) collective-permute-start(bf16[8,64,256]{2,1,0:T(8,128)(2,1)S(1)} %collective-permute-done.21), channel_id=1, source_target_pairs={{1,0},{2,1},{3,2},{5,4},{6,5},{7,6},{9,8},{10,9},{11,10},{13,12},{... | collective-permute-start | bytes 786440 | tf_op jit(solution)/shard_map/ppermute | solution.py:106
  126.1 22.2 %collective-permute-start.8 = (bf16[192,2048]{1,0:T(8,128)(2,1)S(1)}, bf16[192,2048]{1,0:T(8,128)(2,1)S(1)}, u32[]{:S(2)}, u32[]{:S(2)}) collective-permute-start(bf16[192,2048]{1,0:T(8,128)(2,1)S(1)} %constant_dynamic-update-slice_fusion), channel_id=1, source_target_pairs={{0,1},{1,2},{2,3},{4,5},{5,6},{6,7},{8,9},{9,10},{10,11},{12,13},{... | collective-permute-start | bytes 2359304 | tf_op jit(solution)/shard_map/ppermute | solution.py:106
  131.5 28.3 %collective-permute-start.3 = (bf16[2,192,1024]{2,1,0:T(8,128)(2,1)S(1)}, bf16[2,192,1024]{2,1,0:T(8,128)(2,1)S(1)}, u32[]{:S(2)}, u32[]{:S(2)}) collective-permute-start(bf16[2,192,1024]{2,1,0:T(8,128)(2,1)S(1)} %get-tuple-element.148), channel_id=1, source_target_pairs={{0,8},{4,12},{8,0},{12,4},{16,24},{20,28},{24,16},{28,20},{1,9},{5... | collective-permute-start | bytes 2359304 | tf_op jit(solution)/shard_map/ppermute | solution.py:48
  134.2 28.8 %collective-permute-start.25 = (bf16[192,2048]{1,0:T(8,128)(2,1)}, bf16[192,2048]{1,0:T(8,128)(2,1)S(1)}, u32[]{:S(2)}, u32[]{:S(2)}) collective-permute-start(bf16[192,2048]{1,0:T(8,128)(2,1)} %collective-permute-done.24), channel_id=1, source_target_pairs={{1,0},{2,1},{3,2},{5,4},{6,5},{7,6},{9,8},{10,9},{11,10},{13,12},{... | collective-permute-start | bytes 2359304 | tf_op jit(solution)/shard_map/ppermute | solution.py:106
  135.7 30.3 %collective-permute-start.1 = (bf16[2,192,1024]{2,1,0:T(8,128)(2,1)S(1)}, bf16[2,192,1024]{2,1,0:T(8,128)(2,1)S(1)}, u32[]{:S(2)}, u32[]{:S(2)}) collective-permute-start(bf16[2,192,1024]{2,1,0:T(8,128)(2,1)S(1)} %get-tuple-element.142), channel_id=1, source_target_pairs={{0,16},{4,20},{8,24},{12,28},{16,0},{20,4},{24,8},{28,12},{1,17},{... | collective-permute-start | bytes 2359304 | tf_op jit(solution)/shard_map/ppermute | solution.py:48
  139.3 27.2 %collective-permute-start.27 = (bf16[192,2048]{1,0:T(8,128)(2,1)S(1)}, bf16[192,2048]{1,0:T(8,128)(2,1)S(1)}, u32[]{:S(2)}, u32[]{:S(2)}) collective-permute-start(bf16[192,2048]{1,0:T(8,128)(2,1)S(1)} %collective-permute-done.23), channel_id=1, source_target_pairs={{0,1},{1,2},{2,3},{4,5},{5,6},{6,7},{8,9},{9,10},{10,11},{12,13},{... | collective-permute-start | bytes 2359304 | tf_op jit(solution)/shard_map/ppermute | solution.py:106
  148.3 25.2 %collective-permute-start.12 = (bf16[192,2048]{1,0:T(8,128)(2,1)S(1)}, bf16[192,2048]{1,0:T(8,128)(2,1)S(1)}, u32[]{:S(2)}, u32[]{:S(2)}) collective-permute-start(bf16[192,2048]{1,0:T(8,128)(2,1)S(1)} %collective-permute-done.11), channel_id=1, source_target_pairs={{1,0},{2,1},{3,2},{5,4},{6,5},{7,6},{9,8},{10,9},{11,10},{13,12},{... | collective-permute-start | bytes 2359304 | tf_op jit(solution)/shard_map/ppermute | solution.py:106
  159.8 22.3 %collective-permute-start.9 = (bf16[192,2048]{1,0:T(8,128)(2,1)S(1)}, bf16[192,2048]{1,0:T(8,128)(2,1)S(1)}, u32[]{:S(2)}, u32[]{:S(2)}) collective-permute-start(bf16[192,2048]{1,0:T(8,128)(2,1)S(1)} %collective-permute-done.8), channel_id=1, source_target_pairs={{0,1},{1,2},{2,3},{4,5},{5,6},{6,7},{8,9},{9,10},{10,11},{12,13},{... | collective-permute-start | bytes 2359304 | tf_op jit(solution)/shard_map/ppermute | solution.py:106
  163.0 27.4 %collective-permute-start.26 = (bf16[192,2048]{1,0:T(8,128)(2,1)S(1)}, bf16[192,2048]{1,0:T(8,128)(2,1)S(1)}, u32[]{:S(2)}, u32[]{:S(2)}) collective-permute-start(bf16[192,2048]{1,0:T(8,128)(2,1)S(1)} %collective-permute-done.25), channel_id=1, source_target_pairs={{1,0},{2,1},{3,2},{5,4},{6,5},{7,6},{9,8},{10,9},{11,10},{13,12},{... | collective-permute-start | bytes 2359304 | tf_op jit(solution)/shard_map/ppermute | solution.py:106
  166.4 50.5 %collective-permute-start.4 = (bf16[768,2048]{1,0:T(8,128)(2,1)S(1)}, bf16[768,2048]{1,0:T(8,128)(2,1)}, u32[]{:S(2)}, u32[]{:S(2)}) collective-permute-start(bf16[768,2048]{1,0:T(8,128)(2,1)S(1)} %pad_maximum_fusion.8), channel_id=1, source_target_pairs={{0,4},{4,0},{8,12},{12,8},{16,20},{20,16},{24,28},{28,24},{1,5},{5... | collective-permute-start | bytes 9437192 | tf_op jit(solution)/shard_map/ppermute | solution.py:48
  166.5 32.3 %collective-permute-start.28 = (bf16[192,2048]{1,0:T(8,128)(2,1)S(1)}, bf16[192,2048]{1,0:T(8,128)(2,1)S(1)}, u32[]{:S(2)}, u32[]{:S(2)}) collective-permute-start(bf16[192,2048]{1,0:T(8,128)(2,1)S(1)} %collective-permute-done.27), channel_id=1, source_target_pairs={{0,1},{1,2},{2,3},{4,5},{5,6},{6,7},{8,9},{9,10},{10,11},{12,13},{... | collective-permute-start | bytes 2359304 | tf_op jit(solution)/shard_map/ppermute | solution.py:106
  173.6 39.6 %collective-permute-start.13 = (bf16[192,2048]{1,0:T(8,128)(2,1)S(1)}, bf16[192,2048]{1,0:T(8,128)(2,1)S(1)}, u32[]{:S(2)}, u32[]{:S(2)}) collective-permute-start(bf16[192,2048]{1,0:T(8,128)(2,1)S(1)} %collective-permute-done.12), channel_id=1, source_target_pairs={{1,0},{2,1},{3,2},{5,4},{6,5},{7,6},{9,8},{10,9},{11,10},{13,12},{... | collective-permute-start | bytes 2359304 | tf_op jit(solution)/shard_map/ppermute | solution.py:106
  182.0 30.5 %collective-permute-start.10 = (bf16[192,2048]{1,0:T(8,128)(2,1)S(1)}, bf16[192,2048]{1,0:T(8,128)(2,1)S(1)}, u32[]{:S(2)}, u32[]{:S(2)}) collective-permute-start(bf16[192,2048]{1,0:T(8,128)(2,1)S(1)} %collective-permute-done.9), channel_id=1, source_target_pairs={{0,1},{1,2},{2,3},{4,5},{5,6},{6,7},{8,9},{9,10},{10,11},{12,13},{... | collective-permute-start | bytes 2359304 | tf_op jit(solution)/shard_map/ppermute | solution.py:106
  203.2 71.1 %collective-permute-start.29 = (bf16[768,2048]{1,0:T(8,128)(2,1)}, bf16[768,2048]{1,0:T(8,128)(2,1)}, u32[]{:S(2)}, u32[]{:S(2)}) collective-permute-start(bf16[768,2048]{1,0:T(8,128)(2,1)} %pad_maximum_fusion.10), channel_id=1, source_target_pairs={{0,4},{4,0},{1,5},{5,1},{2,6},{6,2},{3,7},{7,3},{8,12},{12,8},{9,1... | collective-permute-start | bytes 9437192 | tf_op jit(solution)/shard_map/ppermute | solution.py:134
  280.8 216.7 %all-gather.7.cloned.1.call-start = ((), (), s32[]{:S(2)}) async-start(), calls=%async_computation.14 | async-start | bytes 5242880 | tf_op jit(solution)/shard_map/all_gather | solution.py:409
  291.2 36.2 %collective-permute-start.31 = (bf16[2,192,1024]{2,1,0:T(8,128)(2,1)S(1)}, bf16[2,192,1024]{2,1,0:T(8,128)(2,1)S(1)}, u32[]{:S(2)}, u32[]{:S(2)}) collective-permute-start(bf16[2,192,1024]{2,1,0:T(8,128)(2,1)S(1)} %slice_bitcast_fusion.2), channel_id=1, source_target_pairs={{0,8},{4,12},{8,0},{12,4},{16,24},{20,28},{24,16},{28,20},{1,9},{5... | collective-permute-start | bytes 2359304 | tf_op jit(solution)/shard_map/ppermute | solution.py:48
  292.9 36.6 %collective-permute-start.33 = (bf16[2,192,1024]{2,1,0:T(8,128)(2,1)S(1)}, bf16[2,192,1024]{2,1,0:T(8,128)(2,1)S(1)}, u32[]{:S(2)}, u32[]{:S(2)}) collective-permute-start(bf16[2,192,1024]{2,1,0:T(8,128)(2,1)S(1)} %bitcast.326), channel_id=1, source_target_pairs={{0,16},{4,20},{8,24},{12,28},{16,0},{20,4},{24,8},{28,12},{1,17},{... | collective-permute-start | bytes 2359304 | tf_op jit(solution)/shard_map/ppermute | solution.py:48
  345.7 20.9 %collective-permute-start.36 = (bf16[192,2048]{1,0:T(8,128)(2,1)S(1)}, bf16[192,2048]{1,0:T(8,128)(2,1)S(1)}, u32[]{:S(2)}, u32[]{:S(2)}) collective-permute-start(bf16[192,2048]{1,0:T(8,128)(2,1)S(1)} %get-tuple-element.82), channel_id=1, source_target_pairs={{1,0},{2,1},{3,2},{5,4},{6,5},{7,6},{9,8},{10,9},{11,10},{13,12},{... | collective-permute-start | bytes 2359304 | tf_op jit(solution)/shard_map/ppermute | solution.py:106
  347.0 20.9 %collective-permute-start.35 = (bf16[192,2048]{1,0:T(8,128)(2,1)S(1)}, bf16[192,2048]{1,0:T(8,128)(2,1)S(1)}, u32[]{:S(2)}, u32[]{:S(2)}) collective-permute-start(bf16[192,2048]{1,0:T(8,128)(2,1)S(1)} %get-tuple-element.82), channel_id=1, source_target_pairs={{0,1},{1,2},{2,3},{4,5},{5,6},{6,7},{8,9},{9,10},{10,11},{12,13},{... | collective-permute-start | bytes 2359304 | tf_op jit(solution)/shard_map/ppermute | solution.py:106
  366.6 20.2 %collective-permute-start.37 = (bf16[192,2048]{1,0:T(8,128)(2,1)S(1)}, bf16[192,2048]{1,0:T(8,128)(2,1)S(1)}, u32[]{:S(2)}, u32[]{:S(2)}) collective-permute-start(bf16[192,2048]{1,0:T(8,128)(2,1)S(1)} %collective-permute-done.36), channel_id=1, source_target_pairs={{1,0},{2,1},{3,2},{5,4},{6,5},{7,6},{9,8},{10,9},{11,10},{13,12},{... | collective-permute-start | bytes 2359304 | tf_op jit(solution)/shard_map/ppermute | solution.py:106
  367.9 20.2 %collective-permute-start.39 = (bf16[192,2048]{1,0:T(8,128)(2,1)S(1)}, bf16[192,2048]{1,0:T(8,128)(2,1)S(1)}, u32[]{:S(2)}, u32[]{:S(2)}) collective-permute-start(bf16[192,2048]{1,0:T(8,128)(2,1)S(1)} %collective-permute-done.35), channel_id=1, source_target_pairs={{0,1},{1,2},{2,3},{4,5},{5,6},{6,7},{8,9},{9,10},{10,11},{12,13},{... | collective-permute-start | bytes 2359304 | tf_op jit(solution)/shard_map/ppermute | solution.py:106
  388.0 20.5 %collective-permute-start.40 = (bf16[192,2048]{1,0:T(8,128)(2,1)S(1)}, bf16[192,2048]{1,0:T(8,128)(2,1)S(1)}, u32[]{:S(2)}, u32[]{:S(2)}) collective-permute-start(bf16[192,2048]{1,0:T(8,128)(2,1)S(1)} %collective-permute-done.39), channel_id=1, source_target_pairs={{0,1},{1,2},{2,3},{4,5},{5,6},{6,7},{8,9},{9,10},{10,11},{12,13},{... | collective-permute-start | bytes 2359304 | tf_op jit(solution)/shard_map/ppermute | solution.py:106
  411.5 489.8 %reduce-scatter.11.cloned.1.call-start = ((), (), s32[]{:S(2)}) async-start(), calls=%async_computation.20 | async-start | bytes 5242880 | tf_op jit(solution)/shard_map/reduce_scatter | solution.py:486
  478.2 423.1 %reduce-scatter.9.cloned.1.call-start = ((), (), s32[]{:S(2)}) async-start(), calls=%async_computation.19 | async-start | bytes 5242880 | tf_op jit(solution)/shard_map/reduce_scatter | solution.py:486
  530.0 471.3 %reduce-scatter.7.cloned.1.call-start = ((), (), s32[]{:S(2)}) async-start(), calls=%async_computation.18 | async-start | bytes 10485760 | tf_op jit(solution)/shard_map/reduce_scatter | solution.py:487
  573.1 21.4 %collective-permute-start.49 = (bf16[768,2048]{1,0:T(8,128)(2,1)}, bf16[768,2048]{1,0:T(8,128)(2,1)}, u32[]{:S(2)}, u32[]{:S(2)}) collective-permute-start(bf16[768,2048]{1,0:T(8,128)(2,1)} %slice.427), channel_id=1, source_target_pairs={{0,4},{4,0},{1,5},{5,1},{2,6},{6,2},{3,7},{7,3},{8,12},{12,8},{9,1... | collective-permute-start | bytes 9437192 | tf_op jit(solution)/shard_map/ppermute | solution.py:134
  599.6 21.1 %collective-permute-start.50 = (bf16[192,2048]{1,0:T(8,128)(2,1)S(1)}, bf16[192,2048]{1,0:T(8,128)(2,1)S(1)}, u32[]{:S(2)}, u32[]{:S(2)}) collective-permute-start(bf16[192,2048]{1,0:T(8,128)(2,1)S(1)} %get-tuple-element.109), channel_id=1, source_target_pairs={{0,1},{1,2},{2,3},{4,5},{5,6},{6,7},{8,9},{9,10},{10,11},{12,13},{... | collective-permute-start | bytes 2359304 | tf_op jit(solution)/shard_map/ppermute | solution.py:106
  603.5 21.6 %collective-permute-start.53 = (bf16[192,2048]{1,0:T(8,128)(2,1)S(1)}, bf16[192,2048]{1,0:T(8,128)(2,1)S(1)}, u32[]{:S(2)}, u32[]{:S(2)}) collective-permute-start(bf16[192,2048]{1,0:T(8,128)(2,1)S(1)} %get-tuple-element.110), channel_id=1, source_target_pairs={{1,0},{2,1},{3,2},{5,4},{6,5},{7,6},{9,8},{10,9},{11,10},{13,12},{... | collective-permute-start | bytes 2359304 | tf_op jit(solution)/shard_map/ppermute | solution.py:106
  630.0 20.7 %collective-permute-start.54 = (bf16[192,2048]{1,0:T(8,128)(2,1)}, bf16[192,2048]{1,0:T(8,128)(2,1)}, u32[]{:S(2)}, u32[]{:S(2)}) collective-permute-start(bf16[192,2048]{1,0:T(8,128)(2,1)} %get-tuple-element.108), channel_id=1, source_target_pairs={{1,0},{2,1},{3,2},{5,4},{6,5},{7,6},{9,8},{10,9},{11,10},{13,12},{... | collective-permute-start | bytes 2359304 | tf_op jit(solution)/shard_map/ppermute | solution.py:106
  654.1 24.5 %collective-permute-start.52 = (bf16[192,2048]{1,0:T(8,128)(2,1)}, bf16[192,2048]{1,0:T(8,128)(2,1)}, u32[]{:S(2)}, u32[]{:S(2)}) collective-permute-start(bf16[192,2048]{1,0:T(8,128)(2,1)} %get-tuple-element.105), channel_id=1, source_target_pairs={{0,1},{1,2},{2,3},{4,5},{5,6},{6,7},{8,9},{9,10},{10,11},{12,13},{... | collective-permute-start | bytes 2359304 | tf_op jit(solution)/shard_map/ppermute | solution.py:106
  658.1 20.5 %collective-permute-start.55 = (bf16[192,2048]{1,0:T(8,128)(2,1)S(1)}, bf16[192,2048]{1,0:T(8,128)(2,1)}, u32[]{:S(2)}, u32[]{:S(2)}) collective-permute-start(bf16[192,2048]{1,0:T(8,128)(2,1)S(1)} %get-tuple-element.106), channel_id=1, source_target_pairs={{1,0},{2,1},{3,2},{5,4},{6,5},{7,6},{9,8},{10,9},{11,10},{13,12},{... | collective-permute-start | bytes 2359304 | tf_op jit(solution)/shard_map/ppermute | solution.py:106
  664.8 336.5 %reduce-scatter.5.cloned.1.call-start = ((), (), s32[]{:S(2)}) async-start(), calls=%async_computation.17 | async-start | bytes 10485760 | tf_op jit(solution)/shard_map/reduce_scatter | solution.py:487
  716.8 23.9 %collective-permute-start.60 = (bf16[768,2048]{1,0:T(8,128)(2,1)}, bf16[768,2048]{1,0:T(8,128)(2,1)}, u32[]{:S(2)}, u32[]{:S(2)}) collective-permute-start(bf16[768,2048]{1,0:T(8,128)(2,1)} %pad_maximum_fusion.12), channel_id=1, source_target_pairs={{0,4},{4,0},{8,12},{12,8},{16,20},{20,16},{24,28},{28,24},{1,5},{5... | collective-permute-start | bytes 9437192 | tf_op jit(solution)/shard_map/ppermute | solution.py:48
  721.9 56.5 %collective-permute-start.42 = (bf16[768,2048]{1,0:T(8,128)(2,1)}, bf16[768,2048]{1,0:T(8,128)(2,1)}, u32[]{:S(2)}, u32[]{:S(2)}) collective-permute-start(bf16[768,2048]{1,0:T(8,128)(2,1)} %slice.428), channel_id=1, source_target_pairs={{0,4},{4,0},{1,5},{5,1},{2,6},{6,2},{3,7},{7,3},{8,12},{12,8},{9,1... | collective-permute-start | bytes 9437192 | tf_op jit(solution)/shard_map/ppermute | solution.py:134
  793.2 22.1 %collective-permute-start.78 = (bf16[8,64,256]{2,1,0:T(8,128)(2,1)S(1)}, bf16[8,64,256]{2,1,0:T(8,128)(2,1)S(1)}, u32[]{:S(2)}, u32[]{:S(2)}) collective-permute-start(bf16[8,64,256]{2,1,0:T(8,128)(2,1)S(1)} %dynamic-slice_bitcast_fusion.6), channel_id=1, source_target_pairs={{0,1},{1,2},{2,3},{4,5},{5,6},{6,7},{8,9},{9,10},{10,11},{12,13},{... | collective-permute-start | bytes 786440 | tf_op jit(solution)/shard_map/ppermute | solution.py:106
  818.7 23.0 %collective-permute-start.69 = (bf16[192,2048]{1,0:T(8,128)(2,1)S(1)}, bf16[192,2048]{1,0:T(8,128)(2,1)S(1)}, u32[]{:S(2)}, u32[]{:S(2)}) collective-permute-start(bf16[192,2048]{1,0:T(8,128)(2,1)S(1)} %dynamic-slice_bitcast_fusion.3), channel_id=1, source_target_pairs={{0,1},{1,2},{2,3},{4,5},{5,6},{6,7},{8,9},{9,10},{10,11},{12,13},{... | collective-permute-start | bytes 2359304 | tf_op jit(solution)/shard_map/ppermute | solution.py:106
  827.3 31.3 %collective-permute-start.43 = (bf16[192,2048]{1,0:T(8,128)(2,1)S(1)}, bf16[192,2048]{1,0:T(8,128)(2,1)S(1)}, u32[]{:S(2)}, u32[]{:S(2)}) collective-permute-start(bf16[192,2048]{1,0:T(8,128)(2,1)S(1)} %get-tuple-element.115), channel_id=1, source_target_pairs={{0,1},{1,2},{2,3},{4,5},{5,6},{6,7},{8,9},{9,10},{10,11},{12,13},{... | collective-permute-start | bytes 2359304 | tf_op jit(solution)/shard_map/ppermute | solution.py:106
  832.4 26.2 %collective-permute-start.46 = (bf16[192,2048]{1,0:T(8,128)(2,1)S(1)}, bf16[192,2048]{1,0:T(8,128)(2,1)S(1)}, u32[]{:S(2)}, u32[]{:S(2)}) collective-permute-start(bf16[192,2048]{1,0:T(8,128)(2,1)S(1)} %get-tuple-element.116), channel_id=1, source_target_pairs={{1,0},{2,1},{3,2},{5,4},{6,5},{7,6},{9,8},{10,9},{11,10},{13,12},{... | collective-permute-start | bytes 2359304 | tf_op jit(solution)/shard_map/ppermute | solution.py:106
  834.8 32.5 %collective-permute-start.82 = (bf16[8,64,256]{2,1,0:T(8,128)(2,1)S(1)}, bf16[8,64,256]{2,1,0:T(8,128)(2,1)S(1)}, u32[]{:S(2)}, u32[]{:S(2)}) collective-permute-start(bf16[8,64,256]{2,1,0:T(8,128)(2,1)S(1)} %fusion.39), channel_id=1, source_target_pairs={{1,0},{2,1},{3,2},{5,4},{6,5},{7,6},{9,8},{10,9},{11,10},{13,12},{... | collective-permute-start | bytes 786440 | tf_op jit(solution)/shard_map/ppermute | solution.py:106
  842.0 33.4 %collective-permute-start.70 = (bf16[192,2048]{1,0:T(8,128)(2,1)S(1)}, bf16[192,2048]{1,0:T(8,128)(2,1)S(1)}, u32[]{:S(2)}, u32[]{:S(2)}) collective-permute-start(bf16[192,2048]{1,0:T(8,128)(2,1)S(1)} %fusion.22), channel_id=1, source_target_pairs={{0,1},{1,2},{2,3},{4,5},{5,6},{6,7},{8,9},{9,10},{10,11},{12,13},{... | collective-permute-start | bytes 2359304 | tf_op jit(solution)/shard_map/ppermute | solution.py:106
  859.1 33.2 %collective-permute-start.44 = (bf16[192,2048]{1,0:T(8,128)(2,1)S(1)}, bf16[192,2048]{1,0:T(8,128)(2,1)S(1)}, u32[]{:S(2)}, u32[]{:S(2)}) collective-permute-start(bf16[192,2048]{1,0:T(8,128)(2,1)S(1)} %get-tuple-element.113), channel_id=1, source_target_pairs={{0,1},{1,2},{2,3},{4,5},{5,6},{6,7},{8,9},{9,10},{10,11},{12,13},{... | collective-permute-start | bytes 2359304 | tf_op jit(solution)/shard_map/ppermute | solution.py:106
  863.5 30.1 %collective-permute-start.47 = (bf16[192,2048]{1,0:T(8,128)(2,1)S(1)}, bf16[192,2048]{1,0:T(8,128)(2,1)S(1)}, u32[]{:S(2)}, u32[]{:S(2)}) collective-permute-start(bf16[192,2048]{1,0:T(8,128)(2,1)S(1)} %get-tuple-element.114), channel_id=1, source_target_pairs={{1,0},{2,1},{3,2},{5,4},{6,5},{7,6},{9,8},{10,9},{11,10},{13,12},{... | collective-permute-start | bytes 2359304 | tf_op jit(solution)/shard_map/ppermute | solution.py:106
  867.3 69.7 %collective-permute-start.64 = (bf16[768,2048]{1,0:T(8,128)(2,1)}, bf16[768,2048]{1,0:T(8,128)(2,1)}, u32[]{:S(2)}, u32[]{:S(2)}) collective-permute-start(bf16[768,2048]{1,0:T(8,128)(2,1)} %slice.281), channel_id=1, source_target_pairs={{0,4},{4,0},{8,12},{12,8},{16,20},{20,16},{24,28},{28,24},{1,5},{5... | collective-permute-start | bytes 9437192 | tf_op jit(solution)/shard_map/ppermute | solution.py:48
  867.3 41.9 %collective-permute-start.80 = (bf16[8,64,256]{2,1,0:T(8,128)(2,1)}, bf16[8,64,256]{2,1,0:T(8,128)(2,1)}, u32[]{:S(2)}, u32[]{:S(2)}) collective-permute-start(bf16[8,64,256]{2,1,0:T(8,128)(2,1)} %get-tuple-element.70), channel_id=1, source_target_pairs={{0,1},{1,2},{2,3},{4,5},{5,6},{6,7},{8,9},{9,10},{10,11},{12,13},{... | collective-permute-start | bytes 786440 | tf_op jit(solution)/shard_map/ppermute | solution.py:106
  875.4 33.8 %collective-permute-start.83 = (bf16[8,64,256]{2,1,0:T(8,128)(2,1)}, bf16[8,64,256]{2,1,0:T(8,128)(2,1)}, u32[]{:S(2)}, u32[]{:S(2)}) collective-permute-start(bf16[8,64,256]{2,1,0:T(8,128)(2,1)} %add_convert_fusion.9), channel_id=1, source_target_pairs={{1,0},{2,1},{3,2},{5,4},{6,5},{7,6},{9,8},{10,9},{11,10},{13,12},{... | collective-permute-start | bytes 786440 | tf_op jit(solution)/shard_map/ppermute | solution.py:106
  892.3 20.1 %collective-permute-start.72 = (bf16[192,2048]{1,0:T(8,128)(2,1)}, bf16[192,2048]{1,0:T(8,128)(2,1)S(1)}, u32[]{:S(2)}, u32[]{:S(2)}) collective-permute-start(bf16[192,2048]{1,0:T(8,128)(2,1)} %get-tuple-element.73), channel_id=1, source_target_pairs={{1,0},{2,1},{3,2},{5,4},{6,5},{7,6},{9,8},{10,9},{11,10},{13,12},{... | collective-permute-start | bytes 2359304 | tf_op jit(solution)/shard_map/ppermute | solution.py:106
  895.4 95.5 %collective-permute-start.45 = (bf16[192,2048]{1,0:T(8,128)(2,1)}, bf16[192,2048]{1,0:T(8,128)(2,1)}, u32[]{:S(2)}, u32[]{:S(2)}) collective-permute-start(bf16[192,2048]{1,0:T(8,128)(2,1)} %get-tuple-element.111), channel_id=1, source_target_pairs={{0,1},{1,2},{2,3},{4,5},{5,6},{6,7},{8,9},{9,10},{10,11},{12,13},{... | collective-permute-start | bytes 2359304 | tf_op jit(solution)/shard_map/ppermute | solution.py:106
  913.8 20.5 %collective-permute-start.73 = (bf16[192,2048]{1,0:T(8,128)(2,1)S(1)}, bf16[192,2048]{1,0:T(8,128)(2,1)S(1)}, u32[]{:S(2)}, u32[]{:S(2)}) collective-permute-start(bf16[192,2048]{1,0:T(8,128)(2,1)S(1)} %fusion.23), channel_id=1, source_target_pairs={{1,0},{2,1},{3,2},{5,4},{6,5},{7,6},{9,8},{10,9},{11,10},{13,12},{... | collective-permute-start | bytes 2359304 | tf_op jit(solution)/shard_map/ppermute | solution.py:106
  926.6 21.3 %collective-permute-start.71 = (bf16[192,2048]{1,0:T(8,128)(2,1)}, bf16[192,2048]{1,0:T(8,128)(2,1)S(1)}, u32[]{:S(2)}, u32[]{:S(2)}) collective-permute-start(bf16[192,2048]{1,0:T(8,128)(2,1)} %get-tuple-element.72), channel_id=1, source_target_pairs={{0,1},{1,2},{2,3},{4,5},{5,6},{6,7},{8,9},{9,10},{10,11},{12,13},{... | collective-permute-start | bytes 2359304 | tf_op jit(solution)/shard_map/ppermute | solution.py:106
  962.2 28.7 %collective-permute-start.48 = (bf16[192,2048]{1,0:T(8,128)(2,1)}, bf16[192,2048]{1,0:T(8,128)(2,1)}, u32[]{:S(2)}, u32[]{:S(2)}) collective-permute-start(bf16[192,2048]{1,0:T(8,128)(2,1)} %get-tuple-element.112), channel_id=1, source_target_pairs={{1,0},{2,1},{3,2},{5,4},{6,5},{7,6},{9,8},{10,9},{11,10},{13,12},{... | collective-permute-start | bytes 2359304 | tf_op jit(solution)/shard_map/ppermute | solution.py:106
  (106 other events, 1692.3 us)
Sparse Core Ops, SparseCore 0:
  18.3 109.0 all-gather.8
  129.9 63.4 all-gather.10
  281.0 108.7 all-gather.4
  411.7 53.0 all-gather.6
  478.3 52.9 reduce-scatter.10
  534.1 52.5 reduce-scatter.8
  593.0 86.5 reduce-scatter.6
  740.9 83.4 reduce-scatter.4

commit v3 on v2

--- a/solution.py
+++ b/solution.py
@@ -44,6 +44,10 @@
     return lax.dot_general(a, b, (((ca,), (cb,)), ((), ())), preferred_element_type=f32)
 
 
+def after(value, *deps):
+    return lax.optimization_barrier((value,) + tuple(deps))[0]
+
+
 def flip(value, size, bit):
     return lax.ppermute(value, DP, [(i, i ^ (1 << bit)) for i in range(size)])
 
@@ -57,7 +61,7 @@
     return high, high[::-1]
 
 
-def gather_dp(value, size):
+def gather_dp(value, size, gate=()):
     width = value.shape[-1] // 2
     pieces = []
     for part, order in zip((value[:, :width], value[:, width:]), bit_lists(size)):
@@ -67,17 +71,16 @@
             out = jnp.stack([out, flip(out, size, bit)], axis=axis)
             have.append(bit)
         pieces.append(out.reshape(-1, width))
-    both = jnp.concatenate(pieces, axis=-1)
-    return jnp.concatenate([both, flip(both, size, 0)], axis=0)
-
-
-def scatter_dp(parts, size):
-    rows, width = parts.shape[0] // size, parts.shape[1]
-    half_rows = parts.shape[0] // 2
-    got = flip(parts[half_rows:], size, 0)
-    summed = (parts[:half_rows].astype(f32) + got.astype(f32)).astype(bf16)
+    sent = [after(piece, *gate) for piece in pieces] if gate else pieces
+    return pieces + [flip(piece, size, 0) for piece in sent]
+
+
+def scatter_dp(own, other, size):
+    rows, width = own.shape[0] * 2 // size, own.shape[1]
+    got = flip(other, size, 0)
+    summed = (own.astype(f32) + got.astype(f32)).astype(bf16)
     highs = size.bit_length() - 2
-    halves = []
+    halves, last = [], []
     for half, order in enumerate(bit_lists(size)):
         cur = summed[:, half * (width // 2) : (half + 1) * (width // 2)]
         cur = cur.reshape([2] * highs + [rows, width // 2])
@@ -87,10 +90,12 @@
             left.remove(bit)
             keep = lax.index_in_dim(cur, 0, axis, keepdims=False)
             send = lax.index_in_dim(cur, 1, axis, keepdims=False)
-            total = keep.astype(f32) + flip(send, size, bit).astype(f32)
+            brought = flip(send, size, bit)
+            total = keep.astype(f32) + brought.astype(f32)
             cur = total if k == len(order) - 1 else total.astype(bf16)
         halves.append(cur)
-    return jnp.concatenate(halves, axis=-1)
+        last.append(brought)
+    return jnp.concatenate(halves, axis=-1), summed, last
 
 
 def sum_dp(value, size):
@@ -106,45 +111,57 @@
     return lax.ppermute(value, "z", [(j, j + step) for j in range(zs) if 0 <= j + step < zs])
 
 
-def gather_z(value, zs, zi):
+def all_after(values, deps):
+    return list(lax.optimization_barrier(tuple(values) + tuple(deps))[: len(values)])
+
+
+def gather_z(value, zs, zi, gates={}):
     right, left = [value], [value]
-    for _ in range(zs - 1):
-        right.append(line(right[-1], zs, 1))
-        left.append(line(left[-1], zs, -1))
-    return [value] + [jnp.where(zi >= k, right[k], left[zs - k]) for k in range(1, zs)]
-
-
-def gather_z_true(value, zs, zi):
-    blocks = jnp.stack(gather_z(value, zs, zi)[::-1] * 2, axis=0)
+    for s in range(1, zs):
+        sent = all_after([right[-1], left[-1]], gates[s]) if s in gates else [right[-1], left[-1]]
+        right.append(line(sent[0], zs, 1))
+        left.append(line(sent[1], zs, -1))
+    blocks = [value] + [jnp.where(zi >= k, right[k], left[zs - k]) for k in range(1, zs)]
+    return blocks, list(zip(right, left))
+
+
+def true_order(blocks, zs, zi):
+    blocks = jnp.stack(blocks[::-1] * 2, axis=0)
     return lax.dynamic_slice_in_dim(blocks, zs - 1 - zi, zs, 0)
 
 
-def scatter_z(parts):
+def scatter_z(parts, gates={}):
     zs = len(parts)
     right, left = None, None
+    steps = []
     for s in range(1, zs):
         go_right = parts[s] if right is None else (parts[s].astype(f32) + right).astype(bf16)
         go_left = parts[zs - s] if left is None else (parts[zs - s].astype(f32) + left).astype(bf16)
-        right = line(go_right, zs, 1).astype(f32)
-        left = line(go_left, zs, -1).astype(f32)
-    return parts[0].astype(f32) + right + left
+        if s in gates:
+            go_right, go_left = all_after([go_right, go_left], gates[s](steps))
+        got_right, got_left = line(go_right, zs, 1), line(go_left, zs, -1)
+        steps.append((got_right, got_left))
+        right, left = got_right.astype(f32), got_left.astype(f32)
+    return parts[0].astype(f32) + right + left, steps
 
 
 def swap_core(value):
     return lax.ppermute(value, "c", [(0, 1), (1, 0)])
 
 
-def gather_cz(value, zs, zi):
-    got = jnp.concatenate(gather_z(value, zs, zi), axis=0)
+def both_cores(blocks):
+    got = jnp.concatenate(blocks, axis=0)
     return jnp.concatenate([got, swap_core(got)], axis=0)
 
 
-def scatter_cz(parts, zs):
+def mix_cores(parts):
     half = parts.shape[0] // 2
-    mixed = parts[:half].astype(f32) + swap_core(parts[half:].astype(bf16)).astype(f32)
-    mixed = mixed.astype(bf16)
-    block = half // zs
-    return scatter_z([mixed[k * block : (k + 1) * block] for k in range(zs)])
+    return (parts[:half].astype(f32) + swap_core(parts[half:]).astype(f32)).astype(bf16)
+
+
+def z_blocks(mixed, zs):
+    block = mixed.shape[0] // zs
+    return [mixed[k * block : (k + 1) * block] for k in range(zs)]
 
 
 BLOCK = 4 * LEN
@@ -165,12 +182,34 @@
     return cols[:, 0:1], cols[:, 1:2]
 
 
-def qkv_kernel(width, tok_ref, gain_ref, w_ref, hid_ref, raw_ref, sum_ref):
-    x = tok_ref[...].astype(f32)
-    inverse = lax.rsqrt(jnp.mean(x * x, axis=-1, keepdims=True) + NORM_EPS)
-    hidden = (x * inverse * gain_ref[...]).astype(bf16)
-    hid_ref[...] = hidden
-    raw = kdot(hidden, w_ref[...], 1, 1)
+def own_rows(half):
+    return pl.program_id(0) < half
+
+
+def picked_rows(half, own_ref, other_ref):
+    return jnp.where(own_rows(half), own_ref[...].astype(f32), other_ref[...].astype(f32))
+
+
+def store_rows(half, own_ref, other_ref, value):
+    @pl.when(own_rows(half))
+    def _():
+        own_ref[...] = value
+
+    @pl.when(jnp.logical_not(own_rows(half)))
+    def _():
+        other_ref[...] = value
+
+
+def qkv_kernel(
+    width, half, a_own, b_own, a_other, b_other, gain_ref, w_ref, hid_ref, raw_ref, sum_ref
+):
+    x_a = picked_rows(half, a_own, a_other)
+    x_b = picked_rows(half, b_own, b_other)
+    square = jnp.sum(x_a * x_a, axis=-1, keepdims=True) + jnp.sum(x_b * x_b, axis=-1, keepdims=True)
+    inverse = lax.rsqrt(square / D + NORM_EPS)
+    hid_ref[:, : D // 2] = (x_a * inverse * gain_ref[:, : D // 2]).astype(bf16)
+    hid_ref[:, D // 2 :] = (x_b * inverse * gain_ref[:, D // 2 :]).astype(bf16)
+    raw = kdot(hid_ref[...], w_ref[...], 1, 1)
     raw_ref[...] = raw
     q, k = raw[:, :width], raw[:, width : 2 * width]
     sum_ref[...] = to_rows(
@@ -203,7 +242,10 @@
     return lax.rsqrt(ss_q / D + NORM_EPS), lax.rsqrt(ss_k / D + NORM_EPS)
 
 
-def attend_kernel(width, raw_ref, sum_ref, gain_ref, cos_ref, sin_ref, mask_ref, w_ref, att_ref, part_ref):
+def attend_kernel(
+    width, half, raw_ref, sum_ref, gain_ref, cos_ref, sin_ref, mask_ref, w_ref,
+    att_ref, own_ref, other_ref,
+):
     inv_q, inv_k = inverses(sum_ref)
     raw = raw_ref[...]
     cos, sin = cos_ref[...], sin_ref[...]
@@ -215,21 +257,28 @@
             att_ref[at, head * HD : (head + 1) * HD] = kdot(
                 probs.astype(bf16), value[at], 1, 0
             ).astype(bf16)
-    part_ref[...] = kdot(att_ref[...], w_ref[...], 1, 1).astype(bf16)
+    store_rows(half, own_ref, other_ref, kdot(att_ref[...], w_ref[...], 1, 1).astype(bf16))
 
 
 def attend_back_kernel(
-    width, raw_ref, sum_ref, gain_ref, cos_ref, sin_ref, mask_ref, w_ref, grad_ref,
-    back_ref, dv_ref, dot_ref, gsum_ref,
+    width, half, raw_ref, sum_ref, gain_ref, cos_ref, sin_ref, mask_ref, w_ref, att_ref,
+    a_own, b_own, a_other, b_other, back_ref, dv_ref, dot_ref, gsum_ref, gout_ref,
 ):
     inv_q, inv_k = inverses(sum_ref)
     raw = raw_ref[...]
     cos, sin = cos_ref[...], sin_ref[...]
-    grad_heads = kdot(grad_ref[...], w_ref[...], 1, 0).astype(bf16)
+    grad_a = picked_rows(half, a_own, a_other).astype(bf16)
+    grad_b = picked_rows(half, b_own, b_other).astype(bf16)
+    grad_heads = kdot(grad_a, w_ref[: D // 2], 1, 0) + kdot(grad_b, w_ref[D // 2 :], 1, 0)
+    grad_heads = grad_heads.astype(bf16)
 
     @pl.when(pl.program_id(0) == 0)
     def _():
         gsum_ref[...] = jnp.zeros_like(gsum_ref)
+        gout_ref[...] = jnp.zeros_like(gout_ref)
+
+    gout_ref[: D // 2] += kdot(grad_a, att_ref[...], 0, 0)
+    gout_ref[D // 2 :] += kdot(grad_b, att_ref[...], 0, 0)
 
     dot_q = dot_k = 0.0
     for head in range(width // HD):
@@ -262,7 +311,7 @@
 
 
 def project_back_kernel(
-    width, raw_ref, sum_ref, back_ref, dv_ref, dot_ref, w_ref, proj_ref, part_ref
+    width, half, raw_ref, sum_ref, back_ref, dv_ref, dot_ref, w_ref, proj_ref, own_ref, other_ref
 ):
     inv_q, inv_k = inverses(sum_ref)
     mean_q, mean_k = to_cols(dot_ref[...] / D)
@@ -273,13 +322,19 @@
         inv_k * (back_ref[:, width:] - normed_k * mean_k)
     ).astype(bf16)
     proj_ref[:, 2 * width :] = dv_ref[...]
-    part_ref[...] = kdot(proj_ref[...], w_ref[...], 1, 0).astype(bf16)
+    store_rows(half, own_ref, other_ref, kdot(proj_ref[...], w_ref[...], 1, 0).astype(bf16))
 
 
 def by_rows(cols):
     return pl.BlockSpec((BLOCK, cols), lambda i: (i, 0))
 
 
+def pieces_spec(half, cols):
+    own = pl.BlockSpec((BLOCK, cols), lambda i: (jnp.minimum(i, half - 1), 0))
+    other = pl.BlockSpec((BLOCK, cols), lambda i: (jnp.maximum(i - half, 0), 0))
+    return own, other
+
+
 def across(rows):
     return pl.BlockSpec((rows, BLOCK), lambda i: (0, i))
 
@@ -288,17 +343,34 @@
     return pl.BlockSpec(shape, lambda i: (0,) * len(shape))
 
 
-def run_blocks(body, rows, in_specs, out_specs, out_shape, args, flops):
-    nbytes = sum(arg.size * arg.dtype.itemsize for arg in args)
-    nbytes += sum(out.size * out.dtype.itemsize for out in out_shape)
+def run_blocks(body, rows, in_specs, out_specs, out_shape, args):
     return pl.pallas_call(
         body,
         grid=(rows // BLOCK,),
         in_specs=in_specs,
         out_specs=out_specs,
         out_shape=out_shape,
-        cost_estimate=pl.CostEstimate(flops=flops, bytes_accessed=nbytes, transcendentals=0),
+        cost_estimate=pl.CostEstimate(flops=1, bytes_accessed=1, transcendentals=0),
     )(*args)
+
+
+def weight_grad_kernel(a_ref, b_ref, out_ref):
+    out_ref[...] = kdot(a_ref[...], b_ref[...], 0, 0).astype(bf16)
+
+
+def weight_grad(a, b):
+    tile_a, tile_b = 512, 1024
+    return pl.pallas_call(
+        weight_grad_kernel,
+        grid=(b.shape[1] // tile_b, a.shape[1] // tile_a),
+        in_specs=[
+            pl.BlockSpec((a.shape[0], tile_a), lambda n, m: (0, m)),
+            pl.BlockSpec((b.shape[0], tile_b), lambda n, m: (0, n)),
+        ],
+        out_specs=pl.BlockSpec((tile_a, tile_b), lambda n, m: (m, n)),
+        out_shape=jax.ShapeDtypeStruct((a.shape[1], b.shape[1]), bf16),
+        cost_estimate=pl.CostEstimate(flops=1, bytes_accessed=1, transcendentals=0),
+    )(a, b)
 
 
 def shape_of(rows, cols, dtype):
@@ -335,6 +407,8 @@
     moved = [
         lax.ppermute(w_qkv[t * sub : (t + 1) * sub], ALL, unit_perm(t, False)) for t in range(3)
     ]
+    slots, slot_steps = gather_z(jnp.concatenate(moved, axis=0), zs, zi)
+    tok_pieces = gather_dp(tokens, dps)
     inv3 = pow(3, -1, dps)
     slot_of = [[0, 0, 0] for _ in range(dps)]
     type_of = [[0, 0, 0] for _ in range(dps)]
@@ -355,6 +429,7 @@
             routes.astype(bf16).reshape(-1),
         ]
     )
+    mini = after(mini, *slot_steps[1])
     minis = lax.all_to_all(
         jnp.broadcast_to(mini[None], (world,) + mini.shape), ALL, 0, 0, tiled=True
     )
@@ -382,27 +457,68 @@
     cos_full = jnp.tile(jnp.concatenate([cos_table, cos_table], axis=1), (BLOCK // LEN, 1))
     sin_full = jnp.tile(jnp.concatenate([-sin_table, sin_table], axis=1), (BLOCK // LEN, 1))
 
-    tok_g = gather_dp(tokens, dps)
-    qkv_slots = gather_z_true(jnp.concatenate(moved, axis=0), zs, zi).reshape(3, width, D)
+    qkv_slots = true_order(slots, zs, zi).reshape(3, width, D)
     w_three = jnp.concatenate(
         [lax.dynamic_index_in_dim(qkv_slots, slot_of[k], 0, keepdims=False) for k in range(3)],
         axis=0,
     )
     out_cols = lax.all_to_all(
-        w_out.reshape(orow, dps, width).transpose(1, 0, 2), DP, 0, 0, tiled=True
-    )
-    w_out_c = gather_z_true(out_cols, zs, zi).transpose(1, 0, 2, 3).reshape(D, width)
+        after(w_out, *slot_steps[1]).reshape(orow, dps, width).transpose(1, 0, 2),
+        DP, 0, 0, tiled=True,
+    )
+    out_blocks, out_w_steps = gather_z(after(out_cols, *slot_steps[-1]), zs, zi)
+    w_out_c = true_order(out_blocks, zs, zi).transpose(1, 0, 2, 3).reshape(D, width)
+    dy_blocks, dy_steps = gather_z(after(cotangent, *out_w_steps[-1]), zs, zi)
+
+    def in_core_order(own, got):
+        first = ci == 0
+        return jnp.where(first, own, got), jnp.where(first, got, own)
 
     def core_half(weight):
-        swapped = lax.all_to_all(
-            weight.reshape((2, mine) + weight.shape[1:]), "c", 0, 0, tiled=True
-        )
-        return [swapped[:, e].reshape((2 * weight.shape[1], weight.shape[2])) for e in range(mine)]
-
-    gu_half = core_half(w_gate_up)
-    down_half = core_half(w_down)
+        split = weight.reshape((2, mine) + weight.shape[1:])
+        got = swap_core(lax.dynamic_index_in_dim(split, 1 - ci, 0, keepdims=False))
+        own = lax.dynamic_index_in_dim(split, ci, 0, keepdims=False)
+        both = in_core_order(own, got)
+        return [jnp.concatenate([half[e] for half in both], axis=0) for e in range(mine)]
+
+    gu_half = core_half(after(w_gate_up, *moved))
+    down_half = core_half(after(w_down, *moved))
+    blocks = all_rows // BLOCK
+    half = blocks // 2
+    own_spec, other_spec = pieces_spec(half, D // 2)
+    piece_specs = [own_spec, own_spec, other_spec, other_spec]
+    part_specs = list(pieces_spec(half, D))
+    part_shapes = [shape_of(all_rows // 2, D, bf16)] * 2
+    hidden_one, raw, sums = run_blocks(
+        functools.partial(qkv_kernel, width, half),
+        all_rows,
+        piece_specs + [whole((1, D)), whole((3 * width, D))],
+        [by_rows(D), by_rows(3 * width), across(8)],
+        [
+            shape_of(all_rows, D, bf16),
+            shape_of(all_rows, 3 * width, f32),
+            shape_of(8, all_rows, f32),
+        ],
+        tuple(tok_pieces) + (gains_f[:, 0][None], w_three),
+    )
+    sums = sum_dp(sums, dps)
+    mask_spec = pl.BlockSpec((BLOCK // LEN, LEN, LEN), lambda i: (i, 0, 0))
+    table_specs = [whole((8, width)), whole((BLOCK, HD)), whole((BLOCK, HD)), mask_spec]
+    tables = (gain_rows, cos_full, sin_full, mask)
+    attended, own, other = run_blocks(
+        functools.partial(attend_kernel, width, half),
+        all_rows,
+        [by_rows(3 * width), across(8)] + table_specs + [whole((D, width))],
+        [by_rows(width)] + part_specs,
+        [shape_of(all_rows, width, bf16)] + part_shapes,
+        (raw, sums) + tables + (w_out_c,),
+    )
+    attn_out, _, attn_last = scatter_dp(own, other, dps)
+
     expert_w = []
     for e in range(mine):
+        if e > 0:
+            gu_half[e], down_half[e] = all_after([gu_half[e], down_half[e]], attn_last)
         expert_w.append(
             (
                 lax.all_gather(gu_half[e], "q", axis=0, tiled=True),
@@ -410,35 +526,6 @@
             )
         )
 
-    hidden_one, raw, sums = run_blocks(
-        functools.partial(qkv_kernel, width),
-        all_rows,
-        [by_rows(D), whole((1, D)), whole((3 * width, D))],
-        [by_rows(D), by_rows(3 * width), across(8)],
-        [
-            shape_of(all_rows, D, bf16),
-            shape_of(all_rows, 3 * width, f32),
-            shape_of(8, all_rows, f32),
-        ],
-        (tok_g, gains_f[:, 0][None], w_three),
-        6 * all_rows * width * D,
-    )
-    dy_g = gather_cz(cotangent, zs, zi)
-    sums = sum_dp(sums, dps)
-    mask_spec = pl.BlockSpec((BLOCK // LEN, LEN, LEN), lambda i: (i, 0, 0))
-    table_specs = [whole((8, width)), whole((BLOCK, HD)), whole((BLOCK, HD)), mask_spec]
-    tables = (gain_rows, cos_full, sin_full, mask)
-    attended, part = run_blocks(
-        functools.partial(attend_kernel, width),
-        all_rows,
-        [by_rows(3 * width), across(8)] + table_specs + [whole((D, width))],
-        [by_rows(width), by_rows(D)],
-        [shape_of(all_rows, width, bf16), shape_of(all_rows, D, bf16)],
-        (raw, sums) + tables + (w_out_c,),
-        3 * all_rows * width * D,
-    )
-    part, dy_g = lax.optimization_barrier((part, dy_g))
-    attn_out = scatter_dp(part, dps)
     x_float = tokens.astype(f32)
     inverse_one = inverse_rms(x_float)
     normed_one = x_float * inverse_one
@@ -448,10 +535,16 @@
     hidden_two = (normed_two * gains_f[:, 3]).astype(bf16)
     router_probs = jax.nn.softmax(mm(hidden_two, router_low, 1, 0), axis=-1)
 
-    hidden_g = gather_cz(hidden_two, zs, zi)
+    dy_g = both_cores(dy_blocks)
+    hidden_blocks, _ = gather_z(after(hidden_two, *dy_steps[-1]), zs, zi, {2: [dy_g, router_probs]})
+    hidden_g = both_cores(hidden_blocks)
     router_g = jax.nn.softmax(mm(hidden_g, router_low, 1, 0), axis=-1)
     dy_f = dy_g.astype(f32)
     first_expert = zi * local_experts + ci * mine
+
+    early = [w for pair in expert_w for w in pair]
+    early = list(lax.optimization_barrier(tuple(early[:-1]))) + early[-1:]
+    expert_w = [tuple(early[2 * e : 2 * e + 2]) for e in range(mine)]
 
     passes = []
     for e in range(mine):
@@ -462,7 +555,8 @@
             jnp.where(jnp.arange(E)[None] == expert, router_g, 0.0), axis=1, keepdims=True
         )
         gate_val = jnp.where(picked, prob, 0.0)
-        gate_and_up = mm(hidden_g, gate_up, 1, 1)
+        hidden_e = after(hidden_g, passes[-1]["act"]) if passes else hidden_g
+        gate_and_up = mm(hidden_e, gate_up, 1, 1)
         g_part = gate_and_up[:, :FF]
         u_part = gate_and_up[:, FF:]
         sig = jax.nn.sigmoid(g_part)
@@ -477,23 +571,38 @@
         grad_both = jnp.concatenate([grad_g, grad_u], axis=-1).astype(bf16)
         rows_back = mm(grad_both, gate_up, 1, 0).astype(bf16).astype(f32)
         dn = mm(grad_eo, act, 0, 0).astype(bf16)
-        gu = mm(grad_both, hidden_g, 0, 0).astype(bf16)
         passes.append(
             dict(
                 out=gate_val * expert_out,
                 back=rows_back,
                 gate=grad_gate,
+                both=grad_both,
+                act=act,
                 dn=lax.psum_scatter(dn, "q", scatter_dimension=0, tiled=True),
-                gu=lax.psum_scatter(gu, "q", scatter_dimension=0, tiled=True),
             )
         )
 
     hid_part = sum([p["back"] for p in passes[1:]], passes[0]["back"])
     out_part = sum([p["out"] for p in passes[1:]], passes[0]["out"])
-    grad_hidden = scatter_cz(hid_part, zs)
     cols = jnp.stack([p["gate"] for p in passes], axis=0).reshape(mine, 2, zs, rows)
     cols = jnp.where(ci == 0, cols, cols[:, ::-1])
     cols = cols[:, :, (zi - jnp.arange(zs)) % zs]
+    hid_mixed = mix_cores(hid_part.astype(bf16))
+    out_mixed = mix_cores(out_part.astype(bf16))
+    gus = []
+
+    def fill(*deps):
+        p = passes[len(gus)]
+        gus.append(weight_grad(after(p["both"], *deps), hidden_g))
+        return gus[-1:]
+
+    hid_gates = {2: lambda steps: fill(hid_mixed), 3: lambda steps: [cols, out_mixed]}
+    if mine > 1:
+        hid_gates[3] = lambda steps: fill(*steps[0]) + [cols, out_mixed]
+    hid_sum, hid_steps = scatter_z(z_blocks(hid_mixed, zs), hid_gates)
+    while len(gus) < mine:
+        fill(*hid_steps[1])
+    grad_hidden = hid_sum
     got = lax.all_to_all(
         cols.transpose(1, 2, 0, 3).reshape(2 * zs, mine, rows), ("c", "z"), 0, 0, tiled=True
     )
@@ -509,67 +618,94 @@
         grad_hidden * gains_f[:, 3], normed_two, inverse_two
     )
 
-    grad_attn_g = gather_dp(grad_residual.astype(bf16), dps)
-    back, dv, dots, gain_sums = run_blocks(
-        functools.partial(attend_back_kernel, width),
+    def core_back(parts):
+        stacked = jnp.stack(parts, axis=0)
+        split = stacked.reshape((mine, 2, stacked.shape[1] // 2, stacked.shape[2]))
+        got = swap_core(lax.dynamic_index_in_dim(split, 1 - ci, 1, keepdims=False))
+        own = lax.dynamic_index_in_dim(split, ci, 1, keepdims=False)
+        return jnp.concatenate(in_core_order(own, got), axis=0).astype(f32)
+
+    grad_pieces = []
+
+    def out_gate(steps):
+        if len(steps) == 1:
+            grad_pieces.extend(
+                gather_dp(grad_residual.astype(bf16), dps, gate=gus[-1:] + list(steps[0]))
+            )
+        return []
+
+    out_total, out_steps = scatter_z(
+        z_blocks(after(out_mixed, *hid_steps[-1]), zs), {s: out_gate for s in range(2, zs)}
+    )
+    gus = [after(gu, *hid_steps[0]) for gu in gus[:-1]] + [after(gus[-1], *grad_pieces)]
+    gus = [lax.psum_scatter(gu, "q", scatter_dimension=0, tiled=True) for gu in gus]
+    back, dv, dots, gain_sums, grad_out_c = run_blocks(
+        functools.partial(attend_back_kernel, width, half),
         all_rows,
-        [by_rows(3 * width), across(8)] + table_specs + [whole((D, width)), by_rows(D)],
-        [by_rows(2 * width), by_rows(width), across(8), whole((8, width))],
+        [by_rows(3 * width), across(8)] + table_specs + [whole((D, width)), by_rows(width)]
+        + piece_specs,
+        [by_rows(2 * width), by_rows(width), across(8), whole((8, width)), whole((D, width))],
         [
             shape_of(all_rows, 2 * width, f32),
             shape_of(all_rows, width, bf16),
             shape_of(8, all_rows, f32),
             shape_of(8, width, f32),
+            shape_of(D, width, f32),
         ],
-        (raw, sums) + tables + (w_out_c, grad_attn_g),
-        5 * all_rows * width * D,
-    )
-    dots = sum_dp(dots, dps)
-    grad_projected, part = run_blocks(
-        functools.partial(project_back_kernel, width),
+        (raw, sums) + tables + (w_out_c, attended) + tuple(grad_pieces),
+    )
+
+    def z_parts(value):
+        return [
+            lax.dynamic_index_in_dim(value, (zi - k) % zs, 0, keepdims=False) for k in range(zs)
+        ]
+
+    dots = sum_dp(after(dots, *out_steps[1]), dps)
+    grad_projected, own, other = run_blocks(
+        functools.partial(project_back_kernel, width, half),
         all_rows,
         [
             by_rows(3 * width), across(8), by_rows(2 * width), by_rows(width), across(8),
             whole((3 * width, D)),
         ],
-        [by_rows(3 * width), by_rows(D)],
-        [shape_of(all_rows, 3 * width, bf16), shape_of(all_rows, D, bf16)],
+        [by_rows(3 * width)] + part_specs,
+        [shape_of(all_rows, 3 * width, bf16)] + part_shapes,
         (raw, sums, back, dv, dots, w_three),
-        6 * all_rows * width * D,
-    )
-    grad_h1 = scatter_dp(part, dps)
+    )
+    grad_h1, h1_summed, h1_last = scatter_dp(own, other, dps)
     gain_one = jnp.sum(grad_h1 * normed_one, axis=0)
     grad_tokens = grad_residual + norm_back(grad_h1 * gains_f[:, 0], normed_one, inverse_one)
-    result = residual + scatter_cz(out_part, zs)
-
-    def z_parts(value):
-        return [
-            lax.dynamic_index_in_dim(value, (zi - k) % zs, 0, keepdims=False) for k in range(zs)
-        ]
-
-    grad_out_c = mm(grad_attn_g, attended, 0, 0)
-    grad_cols = scatter_z(
-        z_parts(grad_out_c.astype(bf16).reshape(dps, zs, orow, width).transpose(1, 0, 2, 3))
-    ).astype(bf16)
-    grad_out = (
-        lax.all_to_all(grad_cols, DP, 0, 0, tiled=True)
-        .transpose(1, 0, 2)
-        .reshape(orow, D)
-        .astype(f32)
-    )
-    grad_three = mm(grad_projected, hidden_one, 0, 0).astype(bf16).reshape(3, width, D)
+    result = residual + out_total
+
+    hidden_late = after(hidden_one, *out_steps[-1])
+    grad_three = mm(grad_projected, hidden_late, 0, 0).astype(bf16).reshape(3, width, D)
     grad_slots = jnp.concatenate(
         [lax.dynamic_index_in_dim(grad_three, type_of[s], 0, keepdims=True) for s in range(3)],
         axis=0,
     )
-    own_slots = scatter_z(z_parts(grad_slots.reshape(zs, 3 * sub, D))).astype(bf16)
+    grad_cols = grad_out_c.astype(bf16).reshape(dps, zs, orow, width).transpose(1, 2, 0, 3)
+    parts = jnp.concatenate(
+        [grad_slots.reshape(zs, 3 * sub, D), grad_cols.reshape(zs, orow, D)], axis=1
+    )
+    dns = [p["dn"] for p in passes]
+    grad_down = core_back([after(dns[0], grad_projected)] + dns[1:])
+    own_sum, own_steps = scatter_z(z_parts(parts), {1: lambda steps: [h1_summed]})
+    grad_gate_up = core_back([after(gus[0], *own_steps[1])] + gus[1:])
+    own_sum = after(own_sum.astype(bf16), grad_gate_up, grad_down)
     grad_qkv = jnp.concatenate(
         [
-            lax.ppermute(own_slots[t * sub : (t + 1) * sub], ALL, unit_perm(t, True))
+            lax.ppermute(own_sum[t * sub : (t + 1) * sub], ALL, unit_perm(t, True))
             for t in range(3)
         ],
         axis=0,
     ).astype(f32)
+    own_cols = own_sum[3 * sub :].reshape(orow, dps, width).transpose(1, 0, 2)
+    grad_out = (
+        lax.all_to_all(own_cols, DP, 0, 0, tiled=True)
+        .transpose(1, 0, 2)
+        .reshape(orow, D)
+        .astype(f32)
+    )
 
     shard_cols = lax.dynamic_update_slice(jnp.zeros((D, 2), f32), gain_sums[:2].T, (di * width, 0))
     small_grads = jnp.concatenate(
@@ -581,12 +717,6 @@
         ),
         axis=0,
     ).reshape(D // world, E + 4)
-
-    def core_back(parts):
-        stacked = jnp.stack(parts, axis=0)
-        split = stacked.reshape((mine, 2, stacked.shape[1] // 2, stacked.shape[2]))
-        got = lax.all_to_all(split.transpose(1, 0, 2, 3), "c", 0, 0, tiled=True)
-        return got.reshape((local_experts,) + got.shape[2:]).astype(f32)
 
     return (
         result.astype(bf16),
@@ -595,8 +725,8 @@
         grad_out,
         small_own[:, :4],
         small_own[:, 4:],
-        core_back([p["gu"] for p in passes]),
-        core_back([p["dn"] for p in passes]),
+        grad_gate_up,
+        grad_down,
     )
 
 

time: 1040 us -> 957 us (0.920)
  waiting for transfers between devices: 272 us -> 225 us
  Pallas kernels: 66.1 us -> 110 us
  matrix products: 214 us -> 178 us
  starting transfers between devices: 224 us -> 188 us
    ppermute x26 -> x28, waiting for transfers between devices: 94.4 us -> 51.6 us  [flip(): return lax.ppermute(value, DP, [(i, i ^ 1 << bit) for i in range(size)])]
    dot_general x16 -> x13, matrix products: 213 us -> 174 us  [mm(): lax.dot_general(a, b, (((ca,), (cb,)), ((), ())), preferred_element_type=...]
    pallas_call x0 -> x2, Pallas kernels: none -> 38.4 us  [weight_grad(): pl.pallas_call(weight_grad_kernel, grid=(b.shape[1] // tile_b, a.shape[1]...]
    ppermute x48 -> x42, starting transfers between devices: 133 us -> 117 us  [line(): lax.ppermute(value, 'z', [(j, j + step) for j in range(zs) if 0 <= j + st...]
    all_to_all x5 -> x2, starting transfers between devices: 21.5 us -> 7.45 us  [the longest x1 4.04 us: per_device(): lax.all_to_all(after(w_out, *slot_steps[1]).reshape(orow, dps, width).tra...]
    concatenate x6 -> x8, other arithmetic: 33.4 us -> 19.4 us  [the longest x2 9.23 us: per_device(): grad_both = jnp.concatenate([grad_g, grad_u], axis=-1).astype(bf16)]
    all_to_all x5 -> x2, waiting for transfers between devices: 13.8 us -> 0.01 us  [the longest x1 0.01 us: per_device(): lax.all_to_all(after(w_out, *slot_steps[1]).reshape(orow, dps, width).tra...]
    slice x9 -> x5, local copies, waits for them, and re-layouts: 17.2 us -> 4.86 us  [the longest x2 2.56 us: mix_cores(): parts[half:]]
  transfers between devices with their start and end apart: 99 -> 96, of which waited for: 44 -> 35; matrix products, arithmetic and copies ran while one was open for 38% -> 38% of each run, Pallas kernels for 6% -> 12%
where the time goes in v3:
time: 957 us; the launch traced here: 947 us
  waiting for transfers between devices  225 us (24%)
  starting transfers between devices  188 us (20%)
  matrix products  178 us (19%)
  other arithmetic  119 us (12%)
  Pallas kernels  110 us (11%)
  local copies, waits for them, and re-layouts  86.8 us (9%)
  between operations  22.1 us (2%)
  blocking collectives  19.5 us (2%)
    dot_general x13, matrix products, mm(): lax.dot_general(a, b, (((ca,), (cb,)), ((), ())), preferred_element_type=...  174 us
    ppermute x42, waiting for transfers between devices, line(): lax.ppermute(value, 'z', [(j, j + step) for j in range(zs) if 0 <= j + st...  163 us
    ppermute x42, starting transfers between devices, line(): lax.ppermute(value, 'z', [(j, j + step) for j in range(zs) if 0 <= j + st...  117 us
    pallas_call x4, Pallas kernels, run_blocks(): pl.pallas_call(body, grid=(rows // BLOCK,), in_specs=in_specs, out_specs=...  71.2 us
    ppermute x28, waiting for transfers between devices, flip(): return lax.ppermute(value, DP, [(i, i ^ 1 << bit) for i in range(size)])  51.6 us
    pallas_call x2, Pallas kernels, weight_grad(): pl.pallas_call(weight_grad_kernel, grid=(b.shape[1] // tile_b, a.shape[1]...  38.4 us
    ppermute x28, starting transfers between devices, flip(): return lax.ppermute(value, DP, [(i, i ^ 1 << bit) for i in range(size)])  27.6 us
    unnamed x199, local copies, waits for them, and re-layouts  22.7 us
  transfers between devices with their start and end apart: 96, of which 35 were waited for; matrix products, arithmetic and copies ran while one was open for 38% of the time, Pallas kernels for 12%

profile of v3, /device:TPU:0, one launch (start us, length us, event | category | flops | bytes accessed | tf_op | source)
XLA Modules:
  0.0 946.6 jit_solution(6729203844991349888)
XLA Ops:
  15.4 11.2 %collective-permute-start.44 = (bf16[2,256,1024]{2,1,0:T(8,128)(2,1)}, bf16[2,256,1024]{2,1,0:T(8,128)(2,1)S(1)}, u32[]{:S(2)}, u32[]{:S(2)}) collective-permute-start(bf16[2,256,1024]{2,1,0:T(8,128)(2,1)} %dynamic-slice_bitcast_fusion.1), channel_id=1, source_target_pairs={{0,4},{4,0},{1,5},{5,1},{2,6},{6,2},{3,7},{7,3},{8,12},{12,8},{9,1... | collective-permute-start | bytes 3145736 | tf_op jit(solution)/shard_map/ppermute | solution.py:149
  55.6 5.4 collective-permute-start.9
  66.6 9.7 %collective-permute-done.10 = bf16[192,2048]{1,0:T(8,128)(2,1)} collective-permute-done((bf16[192,2048]{1,0:T(8,128)(2,1)S(1)}, bf16[192,2048]{1,0:T(8,128)(2,1)}, u32[]{:S(2)}, u32[]{:S(2)}) %collective-permute-start.10) | collective-permute-done | bytes 786464 | tf_op jit(solution)/shard_map/ppermute | solution.py:111
  80.8 5.4 all-to-all-start
  86.3 4.6 collective-permute-start.11
  94.4 7.4 collective-permute-done.3
  107.1 4.0 all-to-all-start.1
  125.0 9.4 collective-permute-done.12
  134.5 5.3 collective-permute-done.14
  139.8 4.6 collective-permute-start.18
  155.8 13.2 %shard_map.188 = (bf16[1536,2048]{1,0:T(8,128)(2,1)}, f32[1536,768]{1,0:T(8,128)}, f32[8,1536]{1,0:T(8,128)}) custom-call(bf16[768,1024]{1,0:T(8,128)(2,1)} %bitcast.4.a_own, bf16[768,1024]{1,0:T(8,128)(2,1)} %bitcast.307, bf16[768,1024]{1,0:T(8,128)(2,1)} %collective-permute-done.4.a_other, bf16[768,1024]{1,0:T(8,128)(2,1)} %collective-permute-done.5.b_other, ...), custom_call_target="tpu_custom_call" | custom-call | flops 1 | bytes 1 | tf_op jit(solution)/shard_map/pallas_call | solution.py:347
  172.1 4.6 collective-permute-start.19
  184.0 4.6 collective-permute-start.20
  193.1 6.8 collective-permute-done.23
  204.6 18.8 %shard_map.189 = (bf16[1536,256]{1,0:T(8,128)(2,1)}, bf16[768,2048]{1,0:T(8,128)(2,1)}, bf16[768,2048]{1,0:T(8,128)(2,1)}) custom-call(f32[1536,768]{1,0:T(8,128)} %get-tuple-element.60.raw_ref, f32[8,1536]{1,0:T(8,128)} %pad.11.sum_ref, f32[8,256]{1,0:T(8,128)} %pad.12.gain_ref, f32[384,128]{1,0:T(8,128)} %bitcast.324, f32[384,128]{1,0:T(8,128)} %bitcast.326, ...), custom_call_target="tpu_custom_call" | custom-call | flops 1 | bytes 1 | tf_op jit(solution)/shard_map/pallas_call | solution.py:347
  224.7 4.6 collective-permute-done.24
  236.5 4.2 collective-permute-start.29
  240.7 5.3 collective-permute-done.32
  247.3 5.1 collective-permute-done.25
  260.0 4.2 collective-permute-start.30
  271.7 7.6 collective-permute-done.30
  279.4 4.9 collective-permute-start.31
  291.1 7.9 collective-permute-done.31
  310.0 4.3 collective-permute-start.35
  320.7 11.1 %collective-permute-done.35 = bf16[192,2048]{1,0:T(8,128)(2,1)S(1)} collective-permute-done((bf16[192,2048]{1,0:T(8,128)(2,1)S(1)}, bf16[192,2048]{1,0:T(8,128)(2,1)S(1)}, u32[]{:S(2)}, u32[]{:S(2)}) %collective-permute-start.35) | collective-permute-done | bytes 786464 | tf_op jit(solution)/shard_map/ppermute | solution.py:111
  331.8 4.2 collective-permute-done.36
  337.2 4.6 collective-permute-start.40
  341.8 14.9 %collective-permute-done.38 = bf16[192,2048]{1,0:T(8,128)(2,1)S(1)} collective-permute-done((bf16[192,2048]{1,0:T(8,128)(2,1)S(1)}, bf16[192,2048]{1,0:T(8,128)(2,1)S(1)}, u32[]{:S(2)}, u32[]{:S(2)}) %collective-permute-start.38) | collective-permute-done | bytes 786464 | tf_op jit(solution)/shard_map/ppermute | solution.py:111
  359.0 4.6 collective-permute-start.41
  363.6 13.2 %collective-permute-done.39 = bf16[192,2048]{1,0:T(8,128)(2,1)S(1)} collective-permute-done((bf16[192,2048]{1,0:T(8,128)(2,1)S(1)}, bf16[192,2048]{1,0:T(8,128)(2,1)S(1)}, u32[]{:S(2)}, u32[]{:S(2)}) %collective-permute-start.39) | collective-permute-done | bytes 786464 | tf_op jit(solution)/shard_map/ppermute | solution.py:111
  392.1 5.2 fusion.83
  397.6 19.4 %fusion.84 = f32[1536,2048]{1,0:T(8,128)} fusion(bf16[1536,2048]{1,0:T(8,128)(2,1)} %constant_dynamic-update-slice_fusion.8.b_ref, bf16[2048,2048]{1,0:T(8,128)(2,1)} %all-gather.5.cloned.1.call-done), kind=kOutput, calls=%fused_computation.310 | convolution fusion | flops 12884901888 | bytes 27262976 | tf_op jit(solution)/shard_map/dot_general | solution.py:44
  417.0 16.1 %multiply_convert_fusion.3 = (bf16[1536,1024]{1,0:T(8,128)(2,1)}, bf16[1536,1024]{1,0:T(8,128)(2,1)}, bf16[1536,1024]{1,0:T(8,128)(2,1)S(1)}) fusion(f32[1536,2048]{1,0:T(8,128)} %fusion.84, bf16[2048,1024]{1,0:T(8,128)(2,1)S(1)} %copy-done.86, bf16[1536,2048]{1,0:T(8,128)(2,1)} %constant_dynamic-update-slice_fusion.3, f32[1536]{0:T(1024)S(1)} %broadcast_select_fusion.18), kind=kOutput, calls=%fused_computation.32 | convolution fusion | flops 6475481088 | bytes 32512000 | tf_op jit(solution)/shard_map/dot_general | solution.py:44
  433.1 12.8 %convolution_convert_fusion.5 = bf16[2048,1024]{1,0:T(8,128)(2,1)} fusion(bf16[1536,1024]{1,0:T(8,128)(2,1)S(1)} %get-tuple-element.173, bf16[1536,2048]{1,0:T(8,128)(2,1)} %constant_dynamic-update-slice_fusion.3, f32[1536]{0:T(1024)S(1)} %broadcast_select_fusion.18), kind=kOutput, calls=%fused_computation.51 | convolution fusion | flops 6453985280 | bytes 13637632 | tf_op jit(solution)/shard_map/dot_general | solution.py:44
  446.0 19.3 %fusion.85 = f32[1536,2048]{1,0:T(8,128)} fusion(bf16[1536,2048]{1,0:T(8,128)(2,1)} %constant_dynamic-update-slice_fusion.8.b_ref, bf16[2048,2048]{1,0:T(8,128)(2,1)} %all-gather.9.cloned.1.call-done), kind=kOutput, calls=%fused_computation.311 | convolution fusion | flops 12884901888 | bytes 27262976 | tf_op jit(solution)/shard_map/dot_general | solution.py:44
  465.3 18.6 %multiply_convert_fusion.1 = (bf16[1536,1024]{1,0:T(8,128)(2,1)S(1)}, bf16[1536,1024]{1,0:T(8,128)(2,1)}, bf16[1536,1024]{1,0:T(8,128)(2,1)S(1)}) fusion(f32[1536,2048]{1,0:T(8,128)} %fusion.85, bf16[2048,1024]{1,0:T(8,128)(2,1)} %all-gather.11.cloned.1.call-done, bf16[1536,2048]{1,0:T(8,128)(2,1)} %constant_dynamic-update-slice_fusion.3, ...), kind=kOutput, calls=%fused_computation.30 | convolution fusion | flops 6475481088 | bytes 32512000 | tf_op jit(solution)/shard_map/dot_general | solution.py:44
  485.6 12.2 %convolution_convert_fusion.4 = bf16[2048,1024]{1,0:T(8,128)(2,1)} fusion(bf16[1536,1024]{1,0:T(8,128)(2,1)S(1)} %get-tuple-element.174, bf16[1536,2048]{1,0:T(8,128)(2,1)} %constant_dynamic-update-slice_fusion.3, f32[1536]{0:T(1024)S(1)} %broadcast_select_fusion.17), kind=kOutput, calls=%fused_computation.50 | convolution fusion | flops 6453985280 | bytes 13637632 | tf_op jit(solution)/shard_map/dot_general | solution.py:44
  497.9 18.9 %convolution_convert_fusion = bf16[1536,2048]{1,0:T(8,128)(2,1)} fusion(bf16[2048,2048]{1,0:T(8,128)(2,1)} %all-gather.9.cloned.1.call-done, bf16[1536,1024]{1,0:T(8,128)(2,1)} %get-tuple-element.171, bf16[1536,1024]{1,0:T(8,128)(2,1)S(1)} %get-tuple-element.170), kind=kOutput, calls=%fused_computation.17 | convolution fusion | flops 12900630528 | bytes 20971520 | tf_op jit(solution)/shard_map/dot_general | solution.py:44
  516.8 18.0 %add_convert_fusion = bf16[1536,2048]{1,0:T(8,128)(2,1)S(1)} fusion(bf16[1536,2048]{1,0:T(8,128)(2,1)} %convolution_convert_fusion, bf16[2048,2048]{1,0:T(8,128)(2,1)} %all-gather.5.cloned.1.call-done, bf16[1536,1024]{1,0:T(8,128)(2,1)} %get-tuple-element.169, bf16[1536,1024]{1,0:T(8,128)(2,1)S(1)} %copy-done.37), kind=kOutput, calls=%fused_computation.16 | convolution fusion | flops 12913213440 | bytes 27262976 | tf_op jit(solution)/shard_map/dot_general | solution.py:44
  535.1 5.6 collective-permute-done.46
  543.4 5.2 collective-permute-start.47
  553.4 19.0 %shard_map.190 = bf16[2048,2048]{1,0:T(8,128)(2,1)} custom-call(bf16[1536,2048]{1,0:T(8,128)(2,1)} %pad_maximum_fusion.a_ref, bf16[1536,2048]{1,0:T(8,128)(2,1)} %constant_dynamic-update-slice_fusion.8.b_ref), custom_call_target="tpu_custom_call" | custom-call | flops 1 | bytes 1 | tf_op jit(solution)/shard_map/pallas_call | solution.py:363
  572.5 11.4 %convolution_convert_fusion.3 = bf16[1536,2048]{1,0:T(8,128)(2,1)} fusion(bf16[1536,1024]{1,0:T(8,128)(2,1)} %copy-done.89, bf16[2048,1024]{1,0:T(8,128)(2,1)} %all-gather.7.cloned.1.call-done), kind=kOutput, calls=%fused_computation.20 | convolution fusion | flops 6445596672 | bytes 13631488 | tf_op jit(solution)/shard_map/dot_general | solution.py:44
  583.9 13.4 %fusion.4 = (f32[1536]{0:T(1024)S(1)}, f32[1536]{0:T(1024)S(1)}, bf16[1536,2048]{1,0:T(8,128)(2,1)S(1)}) fusion(bf16[1536,2048]{1,0:T(8,128)(2,1)} %convolution_convert_fusion.3, bf16[1536,2048]{1,0:T(8,128)(2,1)} %constant_dynamic-update-slice_fusion.3, f32[1536]{0:T(1024)S(1)} %broadcast_select_fusion.17, f32[1536]{0:T(1024)S(1)} %copy-done.83, ...), kind=kOutput, calls=%fused_computation.14 | convolution fusion | flops 6480196608 | bytes 26238976 | tf_op jit(solution)/shard_map/dot_general | solution.py:44
  604.2 4.5 collective-permute-start.49
  610.2 5.7 pad_maximum_fusion.1.a_ref
  616.0 6.2 add_convert_fusion.3
  622.2 19.4 %shard_map.191 = bf16[2048,2048]{1,0:T(8,128)(2,1)} custom-call(bf16[1536,2048]{1,0:T(8,128)(2,1)} %pad_maximum_fusion.1.a_ref, bf16[1536,2048]{1,0:T(8,128)(2,1)} %constant_dynamic-update-slice_fusion.8.b_ref), custom_call_target="tpu_custom_call" | custom-call | flops 1 | bytes 1 | tf_op jit(solution)/shard_map/pallas_call | solution.py:363
  645.3 5.9 collective-permute-start.51
  653.6 19.5 %all_to_all.34 = f32[8,2,192]{2,1,0:T(2,128)S(1)} all-to-all(f32[8,2,192]{2,1,0:T(2,128)S(1)} %bitcast.346), channel_id=1, replica_groups=mesh['q'=4,'c'=2,'z'=4] {'c','z'}, dimensions={0} | all-to-all | bytes 24576 | tf_op jit(solution)/shard_map/all_to_all | solution.py:606
  678.6 10.1 %collective-permute-done.61 = bf16[192,1024]{1,0:T(8,128)(2,1)S(1)} collective-permute-done((bf16[192,1024]{1,0:T(8,128)(2,1)S(1)}, bf16[192,1024]{1,0:T(8,128)(2,1)S(1)}, u32[]{:S(2)}, u32[]{:S(2)}) %collective-permute-start.61) | collective-permute-done | bytes 393248 | tf_op jit(solution)/shard_map/ppermute | solution.py:52
  694.1 13.5 %collective-permute-done.62 = bf16[2,192,1024]{2,1,0:T(8,128)(2,1)S(1)} collective-permute-done((bf16[2,192,1024]{2,1,0:T(8,128)(2,1)S(1)}, bf16[2,192,1024]{2,1,0:T(8,128)(2,1)S(1)}, u32[]{:S(2)}, u32[]{:S(2)}) %collective-permute-start.62) | collective-permute-done | bytes 786464 | tf_op jit(solution)/shard_map/ppermute | solution.py:52
  725.4 26.4 %shard_map.192 = (f32[1536,512]{1,0:T(8,128)}, bf16[1536,256]{1,0:T(8,128)(2,1)}, f32[8,1536]{1,0:T(8,128)}, f32[8,256]{1,0:T(8,128)}, f32[2048,256]{1,0:T(8,128)}) custom-call(f32[1536,768]{1,0:T(8,128)} %get-tuple-element.60.raw_ref, f32[8,1536]{1,0:T(8,128)} %pad.11.sum_ref, f32[8,256]{1,0:T(8,128)} %pad.12.gain_ref, f32[384,128]{1,0:T(8,128)} %bitcast.325, ...), custom_call_target="tpu_custom_call" | custom-call | flops 1 | bytes 1 | tf_op jit(solution)/shard_map/pallas_call | solution.py:347
  762.8 5.3 collective-permute-start.57
  770.6 12.8 %shard_map.193 = (bf16[1536,768]{1,0:T(8,128)(2,1)}, bf16[768,2048]{1,0:T(8,128)(2,1)}, bf16[768,2048]{1,0:T(8,128)(2,1)}) custom-call(f32[1536,768]{1,0:T(8,128)} %get-tuple-element.60.raw_ref, f32[8,1536]{1,0:T(8,128)} %pad.11.sum_ref, f32[1536,512]{1,0:T(8,128)} %get-tuple-element.92.back_ref, bf16[1536,256]{1,0:T(8,128)(2,1)} %get-tuple-element.93.dv_ref, ...), custom_call_target="tpu_custom_call" | custom-call | flops 1 | bytes 1 | tf_op jit(solution)/shard_map/pallas_call | solution.py:347
  784.0 4.8 collective-permute-done.58
  790.7 8.4 convolution_convert_fusion.6
  818.5 15.5 %collective-permute-done.73 = bf16[256,2048]{1,0:T(8,128)(2,1)S(1)} collective-permute-done((bf16[256,2048]{1,0:T(8,128)(2,1)S(1)}, bf16[256,2048]{1,0:T(8,128)(2,1)S(1)}, u32[]{:S(2)}, u32[]{:S(2)}) %collective-permute-start.73) | collective-permute-done | bytes 1048608 | tf_op jit(solution)/shard_map/ppermute | solution.py:111
  834.0 4.2 collective-permute-done.76
  847.2 14.9 %collective-permute-done.74 = bf16[256,2048]{1,0:T(8,128)(2,1)S(1)} collective-permute-done((bf16[256,2048]{1,0:T(8,128)(2,1)S(1)}, bf16[256,2048]{1,0:T(8,128)(2,1)S(1)}, u32[]{:S(2)}, u32[]{:S(2)}) %collective-permute-start.74) | collective-permute-done | bytes 1048608 | tf_op jit(solution)/shard_map/ppermute | solution.py:111
  863.4 5.4 collective-permute-start.75
  884.1 4.9 all-to-all-start.4
  889.0 15.2 %collective-permute-done.78 = bf16[256,2048]{1,0:T(8,128)(2,1)} collective-permute-done((bf16[256,2048]{1,0:T(8,128)(2,1)}, bf16[256,2048]{1,0:T(8,128)(2,1)}, u32[]{:S(2)}, u32[]{:S(2)}) %collective-permute-start.78) | collective-permute-done | bytes 1048608 | tf_op jit(solution)/shard_map/ppermute | solution.py:111
  928.8 5.0 fusion.32
  (562 shorter events, 306.0 us)
Async XLA Ops:
  7.2 390.3 %all-gather.7.cloned.1.call-start = ((), (), s32[]{:S(2)}) async-start(), calls=%async_computation.10 | async-start | bytes 5242880 | tf_op jit(solution)/shard_map/all_gather | solution.py:525
  31.7 29.4 %collective-permute-start.2 = (bf16[192,1024]{1,0:T(8,128)(2,1)S(1)}, bf16[192,1024]{1,0:T(8,128)(2,1)S(1)}, u32[]{:S(2)}, u32[]{:S(2)}) collective-permute-start(bf16[192,1024]{1,0:T(8,128)(2,1)S(1)} %get-tuple-element.239), channel_id=1, source_target_pairs={{0,16},{4,20},{8,24},{12,28},{16,0},{20,4},{24,8},{28,12},{1,17},{... | collective-permute-start | bytes 1179656 | tf_op jit(solution)/shard_map/ppermute | solution.py:52
  33.3 29.7 %collective-permute-start = (bf16[192,1024]{1,0:T(8,128)(2,1)S(1)}, bf16[192,1024]{1,0:T(8,128)(2,1)}, u32[]{:S(2)}, u32[]{:S(2)}) collective-permute-start(bf16[192,1024]{1,0:T(8,128)(2,1)S(1)} %get-tuple-element.240), channel_id=1, source_target_pairs={{0,8},{4,12},{8,0},{12,4},{16,24},{20,28},{24,16},{28,20},{1,9},{5... | collective-permute-start | bytes 1179656 | tf_op jit(solution)/shard_map/ppermute | solution.py:52
  54.2 64.8 %collective-permute-start.43 = (bf16[2,256,2048]{2,1,0:T(8,128)(2,1)}, bf16[2,256,2048]{2,1,0:T(8,128)(2,1)}, u32[]{:S(2)}, u32[]{:S(2)}) collective-permute-start(bf16[2,256,2048]{2,1,0:T(8,128)(2,1)} %dynamic-slice_bitcast_fusion), channel_id=1, source_target_pairs={{0,4},{4,0},{1,5},{5,1},{2,6},{6,2},{3,7},{7,3},{8,12},{12,8},{9,1... | collective-permute-start | bytes 6291464 | tf_op jit(solution)/shard_map/ppermute | solution.py:149
  54.3 22.0 %collective-permute-start.10 = (bf16[192,2048]{1,0:T(8,128)(2,1)S(1)}, bf16[192,2048]{1,0:T(8,128)(2,1)}, u32[]{:S(2)}, u32[]{:S(2)}) collective-permute-start(bf16[192,2048]{1,0:T(8,128)(2,1)S(1)} %constant_dynamic-update-slice_fusion), channel_id=1, source_target_pairs={{1,0},{2,1},{3,2},{5,4},{6,5},{7,6},{9,8},{10,9},{11,10},{13,12},{... | collective-permute-start | bytes 2359304 | tf_op jit(solution)/shard_map/ppermute | solution.py:111
  55.6 21.7 %collective-permute-start.9 = (bf16[192,2048]{1,0:T(8,128)(2,1)S(1)}, bf16[192,2048]{1,0:T(8,128)(2,1)}, u32[]{:S(2)}, u32[]{:S(2)}) collective-permute-start(bf16[192,2048]{1,0:T(8,128)(2,1)S(1)} %constant_dynamic-update-slice_fusion), channel_id=1, source_target_pairs={{0,1},{1,2},{2,3},{4,5},{5,6},{6,7},{8,9},{9,10},{10,11},{12,13},{... | collective-permute-start | bytes 2359304 | tf_op jit(solution)/shard_map/ppermute | solution.py:111
  62.9 38.9 %collective-permute-start.3 = (bf16[2,192,1024]{2,1,0:T(8,128)(2,1)S(1)}, bf16[2,192,1024]{2,1,0:T(8,128)(2,1)}, u32[]{:S(2)}, u32[]{:S(2)}) collective-permute-start(bf16[2,192,1024]{2,1,0:T(8,128)(2,1)S(1)} %get-tuple-element.236), channel_id=1, source_target_pairs={{0,8},{4,12},{8,0},{12,4},{16,24},{20,28},{24,16},{28,20},{1,9},{5... | collective-permute-start | bytes 2359304 | tf_op jit(solution)/shard_map/ppermute | solution.py:52
  65.4 39.3 %collective-permute-start.1 = (bf16[2,192,1024]{2,1,0:T(8,128)(2,1)}, bf16[2,192,1024]{2,1,0:T(8,128)(2,1)}, u32[]{:S(2)}, u32[]{:S(2)}) collective-permute-start(bf16[2,192,1024]{2,1,0:T(8,128)(2,1)} %get-tuple-element.242), channel_id=1, source_target_pairs={{0,16},{4,20},{8,24},{12,28},{16,0},{20,4},{24,8},{28,12},{1,17},{... | collective-permute-start | bytes 2359304 | tf_op jit(solution)/shard_map/ppermute | solution.py:52
  80.8 26.2 %all-to-all-start = ((bf16[32,2,1504]{2,1,0:T(2,128)(2,1)}), bf16[32,2,1504]{2,1,0:T(2,128)(2,1)S(1)}, u32[]{:S(2)}, u32[]{:S(2)}) async-start(bf16[32,2,1504]{2,1,0:T(2,128)(2,1)} %reshape.523), calls=%async_computation | async-start | bytes 393216 | tf_op jit(solution)/shard_map/all_to_all | solution.py:433
  86.3 28.6 %collective-permute-start.11 = (bf16[192,2048]{1,0:T(8,128)(2,1)}, bf16[192,2048]{1,0:T(8,128)(2,1)}, u32[]{:S(2)}, u32[]{:S(2)}) collective-permute-start(bf16[192,2048]{1,0:T(8,128)(2,1)} %collective-permute-done.9), channel_id=1, source_target_pairs={{0,1},{1,2},{2,3},{4,5},{5,6},{6,7},{8,9},{9,10},{10,11},{12,13},{... | collective-permute-start | bytes 2359304 | tf_op jit(solution)/shard_map/ppermute | solution.py:111
  90.8 26.9 %collective-permute-start.13 = (bf16[192,2048]{1,0:T(8,128)(2,1)}, bf16[192,2048]{1,0:T(8,128)(2,1)}, u32[]{:S(2)}, u32[]{:S(2)}) collective-permute-start(bf16[192,2048]{1,0:T(8,128)(2,1)} %collective-permute-done.10), channel_id=1, source_target_pairs={{1,0},{2,1},{3,2},{5,4},{6,5},{7,6},{9,8},{10,9},{11,10},{13,12},{... | collective-permute-start | bytes 2359304 | tf_op jit(solution)/shard_map/ppermute | solution.py:111
  103.3 52.5 %collective-permute-start.5 = (bf16[768,1024]{1,0:T(8,128)(2,1)S(1)}, bf16[768,1024]{1,0:T(8,128)(2,1)}, u32[]{:S(2)}, u32[]{:S(2)}) collective-permute-start(bf16[768,1024]{1,0:T(8,128)(2,1)S(1)} %bitcast.306), channel_id=1, source_target_pairs={{0,4},{4,0},{8,12},{12,8},{16,20},{20,16},{24,28},{28,24},{1,5},{5... | collective-permute-start | bytes 4718600 | tf_op jit(solution)/shard_map/ppermute | solution.py:52
  107.1 48.7 %collective-permute-start.4 = (bf16[768,1024]{1,0:T(8,128)(2,1)}, bf16[768,1024]{1,0:T(8,128)(2,1)}, u32[]{:S(2)}, u32[]{:S(2)}) collective-permute-start(bf16[768,1024]{1,0:T(8,128)(2,1)} %bitcast.4.a_own), channel_id=1, source_target_pairs={{0,4},{4,0},{8,12},{12,8},{16,20},{20,16},{24,28},{28,24},{1,5},{5... | collective-permute-start | bytes 4718600 | tf_op jit(solution)/shard_map/ppermute | solution.py:52
  111.1 286.4 %all-gather.5.cloned.1.call-start = ((), (), s32[]{:S(2)}) async-start(), calls=%async_computation.9 | async-start | bytes 10485760 | tf_op jit(solution)/shard_map/all_gather | solution.py:524
  114.8 19.6 %collective-permute-start.12 = (bf16[192,2048]{1,0:T(8,128)(2,1)}, bf16[192,2048]{1,0:T(8,128)(2,1)}, u32[]{:S(2)}, u32[]{:S(2)}) collective-permute-start(bf16[192,2048]{1,0:T(8,128)(2,1)} %collective-permute-done.11), channel_id=1, source_target_pairs={{0,1},{1,2},{2,3},{4,5},{5,6},{6,7},{8,9},{9,10},{10,11},{12,13},{... | collective-permute-start | bytes 2359304 | tf_op jit(solution)/shard_map/ppermute | solution.py:111
  117.7 22.1 %collective-permute-start.14 = (bf16[192,2048]{1,0:T(8,128)(2,1)}, bf16[192,2048]{1,0:T(8,128)(2,1)}, u32[]{:S(2)}, u32[]{:S(2)}) collective-permute-start(bf16[192,2048]{1,0:T(8,128)(2,1)} %collective-permute-done.13), channel_id=1, source_target_pairs={{1,0},{2,1},{3,2},{5,4},{6,5},{7,6},{9,8},{10,9},{11,10},{13,12},{... | collective-permute-start | bytes 2359304 | tf_op jit(solution)/shard_map/ppermute | solution.py:111
  125.0 272.6 %all-gather.9.cloned.1.call-start = ((), (), s32[]{:S(2)}) async-start(), calls=%async_computation.11 | async-start | bytes 10485760 | tf_op jit(solution)/shard_map/all_gather | solution.py:524
  139.8 32.3 %collective-permute-start.18 = (bf16[8,64,256]{2,1,0:T(8,128)(2,1)}, bf16[8,64,256]{2,1,0:T(8,128)(2,1)}, u32[]{:S(2)}, u32[]{:S(2)}) collective-permute-start(bf16[8,64,256]{2,1,0:T(8,128)(2,1)} %all-to-all-done.1), channel_id=1, source_target_pairs={{0,1},{1,2},{2,3},{4,5},{5,6},{6,7},{8,9},{9,10},{10,11},{12,13},{... | collective-permute-start | bytes 786440 | tf_op jit(solution)/shard_map/ppermute | solution.py:111
  223.4 22.6 %collective-permute-start.32 = (bf16[192,2048]{1,0:T(8,128)(2,1)S(1)}, bf16[192,2048]{1,0:T(8,128)(2,1)}, u32[]{:S(2)}, u32[]{:S(2)}) collective-permute-start(bf16[192,2048]{1,0:T(8,128)(2,1)S(1)} %copy-done.12), channel_id=1, source_target_pairs={{1,0},{2,1},{3,2},{5,4},{6,5},{7,6},{9,8},{10,9},{11,10},{13,12},{... | collective-permute-start | bytes 2359304 | tf_op jit(solution)/shard_map/ppermute | solution.py:111
  232.7 19.6 %collective-permute-start.25 = (bf16[2,192,1024]{2,1,0:T(8,128)(2,1)S(1)}, bf16[2,192,1024]{2,1,0:T(8,128)(2,1)S(1)}, u32[]{:S(2)}, u32[]{:S(2)}) collective-permute-start(bf16[2,192,1024]{2,1,0:T(8,128)(2,1)S(1)} %slice_bitcast_fusion.6), channel_id=1, source_target_pairs={{0,8},{4,12},{8,0},{12,4},{16,24},{20,28},{24,16},{28,20},{1,9},{5... | collective-permute-start | bytes 2359304 | tf_op jit(solution)/shard_map/ppermute | solution.py:52
  234.5 21.0 %collective-permute-start.27 = (bf16[2,192,1024]{2,1,0:T(8,128)(2,1)S(1)}, bf16[2,192,1024]{2,1,0:T(8,128)(2,1)S(1)}, u32[]{:S(2)}, u32[]{:S(2)}) collective-permute-start(bf16[2,192,1024]{2,1,0:T(8,128)(2,1)S(1)} %bitcast.336), channel_id=1, source_target_pairs={{0,16},{4,20},{8,24},{12,28},{16,0},{20,4},{24,8},{28,12},{1,17},{... | collective-permute-start | bytes 2359304 | tf_op jit(solution)/shard_map/ppermute | solution.py:52
  236.5 23.5 %collective-permute-start.29 = (bf16[192,2048]{1,0:T(8,128)(2,1)S(1)}, bf16[192,2048]{1,0:T(8,128)(2,1)}, u32[]{:S(2)}, u32[]{:S(2)}) collective-permute-start(bf16[192,2048]{1,0:T(8,128)(2,1)S(1)} %copy-done.12), channel_id=1, source_target_pairs={{0,1},{1,2},{2,3},{4,5},{5,6},{6,7},{8,9},{9,10},{10,11},{12,13},{... | collective-permute-start | bytes 2359304 | tf_op jit(solution)/shard_map/ppermute | solution.py:111
  246.0 21.6 %collective-permute-start.33 = (bf16[192,2048]{1,0:T(8,128)(2,1)}, bf16[192,2048]{1,0:T(8,128)(2,1)}, u32[]{:S(2)}, u32[]{:S(2)}) collective-permute-start(bf16[192,2048]{1,0:T(8,128)(2,1)} %collective-permute-done.32), channel_id=1, source_target_pairs={{1,0},{2,1},{3,2},{5,4},{6,5},{7,6},{9,8},{10,9},{11,10},{13,12},{... | collective-permute-start | bytes 2359304 | tf_op jit(solution)/shard_map/ppermute | solution.py:111
  260.0 19.4 %collective-permute-start.30 = (bf16[192,2048]{1,0:T(8,128)(2,1)}, bf16[192,2048]{1,0:T(8,128)(2,1)}, u32[]{:S(2)}, u32[]{:S(2)}) collective-permute-start(bf16[192,2048]{1,0:T(8,128)(2,1)} %collective-permute-done.29), channel_id=1, source_target_pairs={{0,1},{1,2},{2,3},{4,5},{5,6},{6,7},{8,9},{9,10},{10,11},{12,13},{... | collective-permute-start | bytes 2359304 | tf_op jit(solution)/shard_map/ppermute | solution.py:111
  267.6 20.7 %collective-permute-start.34 = (bf16[192,2048]{1,0:T(8,128)(2,1)}, bf16[192,2048]{1,0:T(8,128)(2,1)}, u32[]{:S(2)}, u32[]{:S(2)}) collective-permute-start(bf16[192,2048]{1,0:T(8,128)(2,1)} %collective-permute-done.33), channel_id=1, source_target_pairs={{1,0},{2,1},{3,2},{5,4},{6,5},{7,6},{9,8},{10,9},{11,10},{13,12},{... | collective-permute-start | bytes 2359304 | tf_op jit(solution)/shard_map/ppermute | solution.py:111
  271.6 193.7 %all-gather.11.cloned.1.call-start = ((), (), s32[]{:S(2)}) async-start(), calls=%async_computation.12 | async-start | bytes 5242880 | tf_op jit(solution)/shard_map/all_gather | solution.py:525
  279.4 19.6 %collective-permute-start.31 = (bf16[192,2048]{1,0:T(8,128)(2,1)}, bf16[192,2048]{1,0:T(8,128)(2,1)S(1)}, u32[]{:S(2)}, u32[]{:S(2)}) collective-permute-start(bf16[192,2048]{1,0:T(8,128)(2,1)} %collective-permute-done.30), channel_id=1, source_target_pairs={{0,1},{1,2},{2,3},{4,5},{5,6},{6,7},{8,9},{9,10},{10,11},{12,13},{... | collective-permute-start | bytes 2359304 | tf_op jit(solution)/shard_map/ppermute | solution.py:111
  310.0 21.7 %collective-permute-start.35 = (bf16[192,2048]{1,0:T(8,128)(2,1)S(1)}, bf16[192,2048]{1,0:T(8,128)(2,1)S(1)}, u32[]{:S(2)}, u32[]{:S(2)}) collective-permute-start(bf16[192,2048]{1,0:T(8,128)(2,1)S(1)} %multiply_convert_fusion.6), channel_id=1, source_target_pairs={{0,1},{1,2},{2,3},{4,5},{5,6},{6,7},{8,9},{9,10},{10,11},{12,13},{... | collective-permute-start | bytes 2359304 | tf_op jit(solution)/shard_map/ppermute | solution.py:111
  314.4 21.6 %collective-permute-start.36 = (bf16[192,2048]{1,0:T(8,128)(2,1)S(1)}, bf16[192,2048]{1,0:T(8,128)(2,1)S(1)}, u32[]{:S(2)}, u32[]{:S(2)}) collective-permute-start(bf16[192,2048]{1,0:T(8,128)(2,1)S(1)} %multiply_convert_fusion.6), channel_id=1, source_target_pairs={{1,0},{2,1},{3,2},{5,4},{6,5},{7,6},{9,8},{10,9},{11,10},{13,12},{... | collective-permute-start | bytes 2359304 | tf_op jit(solution)/shard_map/ppermute | solution.py:111
  336.0 20.8 %collective-permute-start.38 = (bf16[192,2048]{1,0:T(8,128)(2,1)S(1)}, bf16[192,2048]{1,0:T(8,128)(2,1)S(1)}, u32[]{:S(2)}, u32[]{:S(2)}) collective-permute-start(bf16[192,2048]{1,0:T(8,128)(2,1)S(1)} %collective-permute-done.36), channel_id=1, source_target_pairs={{1,0},{2,1},{3,2},{5,4},{6,5},{7,6},{9,8},{10,9},{11,10},{13,12},{... | collective-permute-start | bytes 2359304 | tf_op jit(solution)/shard_map/ppermute | solution.py:111
  337.2 21.8 %collective-permute-start.40 = (bf16[192,2048]{1,0:T(8,128)(2,1)S(1)}, bf16[192,2048]{1,0:T(8,128)(2,1)S(1)}, u32[]{:S(2)}, u32[]{:S(2)}) collective-permute-start(bf16[192,2048]{1,0:T(8,128)(2,1)S(1)} %collective-permute-done.35), channel_id=1, source_target_pairs={{0,1},{1,2},{2,3},{4,5},{5,6},{6,7},{8,9},{9,10},{10,11},{12,13},{... | collective-permute-start | bytes 2359304 | tf_op jit(solution)/shard_map/ppermute | solution.py:111
  356.8 20.1 %collective-permute-start.39 = (bf16[192,2048]{1,0:T(8,128)(2,1)S(1)}, bf16[192,2048]{1,0:T(8,128)(2,1)S(1)}, u32[]{:S(2)}, u32[]{:S(2)}) collective-permute-start(bf16[192,2048]{1,0:T(8,128)(2,1)S(1)} %collective-permute-done.38), channel_id=1, source_target_pairs={{1,0},{2,1},{3,2},{5,4},{6,5},{7,6},{9,8},{10,9},{11,10},{13,12},{... | collective-permute-start | bytes 2359304 | tf_op jit(solution)/shard_map/ppermute | solution.py:111
  359.0 20.1 %collective-permute-start.41 = (bf16[192,2048]{1,0:T(8,128)(2,1)S(1)}, bf16[192,2048]{1,0:T(8,128)(2,1)S(1)}, u32[]{:S(2)}, u32[]{:S(2)}) collective-permute-start(bf16[192,2048]{1,0:T(8,128)(2,1)S(1)} %collective-permute-done.40), channel_id=1, source_target_pairs={{0,1},{1,2},{2,3},{4,5},{5,6},{6,7},{8,9},{9,10},{10,11},{12,13},{... | collective-permute-start | bytes 2359304 | tf_op jit(solution)/shard_map/ppermute | solution.py:111
  386.4 414.5 %reduce-scatter.9.cloned.1.call-start = ((), (), s32[]{:S(2)}) async-start(), calls=%async_computation.15 | async-start | bytes 5242880 | tf_op jit(solution)/shard_map/reduce_scatter | solution.py:581
  446.0 354.9 %reduce-scatter.11.cloned.1.call-start = ((), (), s32[]{:S(2)}) async-start(), calls=%async_computation.16 | async-start | bytes 5242880 | tf_op jit(solution)/shard_map/reduce_scatter | solution.py:581
  497.9 370.9 %reduce-scatter.5.cloned.1.call-start = ((), (), s32[]{:S(2)}) async-start(), calls=%async_computation.13 | async-start | bytes 10485760 | tf_op jit(solution)/shard_map/reduce_scatter | solution.py:641
  543.4 29.0 %collective-permute-start.47 = (bf16[192,2048]{1,0:T(8,128)(2,1)}, bf16[192,2048]{1,0:T(8,128)(2,1)}, u32[]{:S(2)}, u32[]{:S(2)}) collective-permute-start(bf16[192,2048]{1,0:T(8,128)(2,1)} %get-tuple-element.201), channel_id=1, source_target_pairs={{0,1},{1,2},{2,3},{4,5},{5,6},{6,7},{8,9},{9,10},{10,11},{12,13},{... | collective-permute-start | bytes 2359304 | tf_op jit(solution)/shard_map/ppermute | solution.py:111
  548.6 23.8 %collective-permute-start.48 = (bf16[192,2048]{1,0:T(8,128)(2,1)}, bf16[192,2048]{1,0:T(8,128)(2,1)}, u32[]{:S(2)}, u32[]{:S(2)}) collective-permute-start(bf16[192,2048]{1,0:T(8,128)(2,1)} %get-tuple-element.200), channel_id=1, source_target_pairs={{1,0},{2,1},{3,2},{5,4},{6,5},{7,6},{9,8},{10,9},{11,10},{13,12},{... | collective-permute-start | bytes 2359304 | tf_op jit(solution)/shard_map/ppermute | solution.py:111
  572.4 296.4 %reduce-scatter.7.cloned.1.call-start = ((), (), s32[]{:S(2)}) async-start(), calls=%async_computation.14 | async-start | bytes 10485760 | tf_op jit(solution)/shard_map/reduce_scatter | solution.py:641
  604.2 37.5 %collective-permute-start.49 = (bf16[192,2048]{1,0:T(8,128)(2,1)}, bf16[192,2048]{1,0:T(8,128)(2,1)S(1)}, u32[]{:S(2)}, u32[]{:S(2)}) collective-permute-start(bf16[192,2048]{1,0:T(8,128)(2,1)} %get-tuple-element.79), channel_id=1, source_target_pairs={{0,1},{1,2},{2,3},{4,5},{5,6},{6,7},{8,9},{9,10},{10,11},{12,13},{... | collective-permute-start | bytes 2359304 | tf_op jit(solution)/shard_map/ppermute | solution.py:111
  608.7 33.0 %collective-permute-start.50 = (bf16[192,2048]{1,0:T(8,128)(2,1)}, bf16[192,2048]{1,0:T(8,128)(2,1)}, u32[]{:S(2)}, u32[]{:S(2)}) collective-permute-start(bf16[192,2048]{1,0:T(8,128)(2,1)} %get-tuple-element.80), channel_id=1, source_target_pairs={{1,0},{2,1},{3,2},{5,4},{6,5},{7,6},{9,8},{10,9},{11,10},{13,12},{... | collective-permute-start | bytes 2359304 | tf_op jit(solution)/shard_map/ppermute | solution.py:111
  645.3 27.9 %collective-permute-start.51 = (bf16[192,2048]{1,0:T(8,128)(2,1)}, bf16[192,2048]{1,0:T(8,128)(2,1)}, u32[]{:S(2)}, u32[]{:S(2)}) collective-permute-start(bf16[192,2048]{1,0:T(8,128)(2,1)} %get-tuple-element.82), channel_id=1, source_target_pairs={{0,1},{1,2},{2,3},{4,5},{5,6},{6,7},{8,9},{9,10},{10,11},{12,13},{... | collective-permute-start | bytes 2359304 | tf_op jit(solution)/shard_map/ppermute | solution.py:111
  651.2 22.0 %collective-permute-start.52 = (bf16[192,2048]{1,0:T(8,128)(2,1)}, bf16[192,2048]{1,0:T(8,128)(2,1)}, u32[]{:S(2)}, u32[]{:S(2)}) collective-permute-start(bf16[192,2048]{1,0:T(8,128)(2,1)} %get-tuple-element.83), channel_id=1, source_target_pairs={{1,0},{2,1},{3,2},{5,4},{6,5},{7,6},{9,8},{10,9},{11,10},{13,12},{... | collective-permute-start | bytes 2359304 | tf_op jit(solution)/shard_map/ppermute | solution.py:111
  688.8 18.8 %collective-permute-start.62 = (bf16[2,192,1024]{2,1,0:T(8,128)(2,1)S(1)}, bf16[2,192,1024]{2,1,0:T(8,128)(2,1)S(1)}, u32[]{:S(2)}, u32[]{:S(2)}) collective-permute-start(bf16[2,192,1024]{2,1,0:T(8,128)(2,1)S(1)} %get-tuple-element.225), channel_id=1, source_target_pairs={{0,8},{4,12},{8,0},{12,4},{16,24},{20,28},{24,16},{28,20},{1,9},{5... | collective-permute-start | bytes 2359304 | tf_op jit(solution)/shard_map/ppermute | solution.py:52
  691.7 20.1 %collective-permute-start.54 = (bf16[192,2048]{1,0:T(8,128)(2,1)S(1)}, bf16[192,2048]{1,0:T(8,128)(2,1)S(1)}, u32[]{:S(2)}, u32[]{:S(2)}) collective-permute-start(bf16[192,2048]{1,0:T(8,128)(2,1)S(1)} %get-tuple-element.194), channel_id=1, source_target_pairs={{1,0},{2,1},{3,2},{5,4},{6,5},{7,6},{9,8},{10,9},{11,10},{13,12},{... | collective-permute-start | bytes 2359304 | tf_op jit(solution)/shard_map/ppermute | solution.py:111
  720.8 31.0 %collective-permute-start.55 = (bf16[192,2048]{1,0:T(8,128)(2,1)}, bf16[192,2048]{1,0:T(8,128)(2,1)}, u32[]{:S(2)}, u32[]{:S(2)}) collective-permute-start(bf16[192,2048]{1,0:T(8,128)(2,1)} %get-tuple-element.85), channel_id=1, source_target_pairs={{0,1},{1,2},{2,3},{4,5},{5,6},{6,7},{8,9},{9,10},{10,11},{12,13},{... | collective-permute-start | bytes 2359304 | tf_op jit(solution)/shard_map/ppermute | solution.py:111
  724.1 27.7 %collective-permute-start.56 = (bf16[192,2048]{1,0:T(8,128)(2,1)}, bf16[192,2048]{1,0:T(8,128)(2,1)}, u32[]{:S(2)}, u32[]{:S(2)}) collective-permute-start(bf16[192,2048]{1,0:T(8,128)(2,1)} %get-tuple-element.86), channel_id=1, source_target_pairs={{1,0},{2,1},{3,2},{5,4},{6,5},{7,6},{9,8},{10,9},{11,10},{13,12},{... | collective-permute-start | bytes 2359304 | tf_op jit(solution)/shard_map/ppermute | solution.py:111
  762.8 21.1 %collective-permute-start.57 = (bf16[192,2048]{1,0:T(8,128)(2,1)}, bf16[192,2048]{1,0:T(8,128)(2,1)}, u32[]{:S(2)}, u32[]{:S(2)}) collective-permute-start(bf16[192,2048]{1,0:T(8,128)(2,1)} %get-tuple-element.87), channel_id=1, source_target_pairs={{0,1},{1,2},{2,3},{4,5},{5,6},{6,7},{8,9},{9,10},{10,11},{12,13},{... | collective-permute-start | bytes 2359304 | tf_op jit(solution)/shard_map/ppermute | solution.py:111
  768.2 20.6 %collective-permute-start.58 = (bf16[192,2048]{1,0:T(8,128)(2,1)}, bf16[192,2048]{1,0:T(8,128)(2,1)}, u32[]{:S(2)}, u32[]{:S(2)}) collective-permute-start(bf16[192,2048]{1,0:T(8,128)(2,1)} %get-tuple-element.88), channel_id=1, source_target_pairs={{1,0},{2,1},{3,2},{5,4},{6,5},{7,6},{9,8},{10,9},{11,10},{13,12},{... | collective-permute-start | bytes 2359304 | tf_op jit(solution)/shard_map/ppermute | solution.py:111
  783.4 21.1 %collective-permute-start.68 = (bf16[768,2048]{1,0:T(8,128)(2,1)}, bf16[768,2048]{1,0:T(8,128)(2,1)}, u32[]{:S(2)}, u32[]{:S(2)}) collective-permute-start(bf16[768,2048]{1,0:T(8,128)(2,1)} %get-tuple-element.97), channel_id=1, source_target_pairs={{0,4},{4,0},{8,12},{12,8},{16,20},{20,16},{24,28},{28,24},{1,5},{5... | collective-permute-start | bytes 9437192 | tf_op jit(solution)/shard_map/ppermute | solution.py:52
  810.0 23.9 %collective-permute-start.73 = (bf16[256,2048]{1,0:T(8,128)(2,1)S(1)}, bf16[256,2048]{1,0:T(8,128)(2,1)S(1)}, u32[]{:S(2)}, u32[]{:S(2)}) collective-permute-start(bf16[256,2048]{1,0:T(8,128)(2,1)S(1)} %get-tuple-element.102), channel_id=1, source_target_pairs={{0,1},{1,2},{2,3},{4,5},{5,6},{6,7},{8,9},{9,10},{10,11},{12,13},{... | collective-permute-start | bytes 3145736 | tf_op jit(solution)/shard_map/ppermute | solution.py:111
  811.4 26.8 %collective-permute-start.76 = (bf16[256,2048]{1,0:T(8,128)(2,1)S(1)}, bf16[256,2048]{1,0:T(8,128)(2,1)S(1)}, u32[]{:S(2)}, u32[]{:S(2)}) collective-permute-start(bf16[256,2048]{1,0:T(8,128)(2,1)S(1)} %get-tuple-element.103), channel_id=1, source_target_pairs={{1,0},{2,1},{3,2},{5,4},{6,5},{7,6},{9,8},{10,9},{11,10},{13,12},{... | collective-permute-start | bytes 3145736 | tf_op jit(solution)/shard_map/ppermute | solution.py:111
  815.4 25.3 %collective-permute-start.69 = (bf16[2,192,1024]{2,1,0:T(8,128)(2,1)S(1)}, bf16[2,192,1024]{2,1,0:T(8,128)(2,1)S(1)}, u32[]{:S(2)}, u32[]{:S(2)}) collective-permute-start(bf16[2,192,1024]{2,1,0:T(8,128)(2,1)S(1)} %slice_bitcast_fusion.4), channel_id=1, source_target_pairs={{0,8},{4,12},{8,0},{12,4},{16,24},{20,28},{24,16},{28,20},{1,9},{5... | collective-permute-start | bytes 2359304 | tf_op jit(solution)/shard_map/ppermute | solution.py:52
  817.3 26.8 %collective-permute-start.71 = (bf16[2,192,1024]{2,1,0:T(8,128)(2,1)S(1)}, bf16[2,192,1024]{2,1,0:T(8,128)(2,1)S(1)}, u32[]{:S(2)}, u32[]{:S(2)}) collective-permute-start(bf16[2,192,1024]{2,1,0:T(8,128)(2,1)S(1)} %bitcast.334), channel_id=1, source_target_pairs={{0,16},{4,20},{8,24},{12,28},{16,0},{20,4},{24,8},{28,12},{1,17},{... | collective-permute-start | bytes 2359304 | tf_op jit(solution)/shard_map/ppermute | solution.py:52
  838.7 23.4 %collective-permute-start.74 = (bf16[256,2048]{1,0:T(8,128)(2,1)S(1)}, bf16[256,2048]{1,0:T(8,128)(2,1)S(1)}, u32[]{:S(2)}, u32[]{:S(2)}) collective-permute-start(bf16[256,2048]{1,0:T(8,128)(2,1)S(1)} %get-tuple-element.179), channel_id=1, source_target_pairs={{0,1},{1,2},{2,3},{4,5},{5,6},{6,7},{8,9},{9,10},{10,11},{12,13},{... | collective-permute-start | bytes 3145736 | tf_op jit(solution)/shard_map/ppermute | solution.py:111
  841.8 34.5 %collective-permute-start.70 = (bf16[192,1024]{1,0:T(8,128)(2,1)}, bf16[192,1024]{1,0:T(8,128)(2,1)}, u32[]{:S(2)}, u32[]{:S(2)}) collective-permute-start(bf16[192,1024]{1,0:T(8,128)(2,1)} %slice_bitcast_fusion.14), channel_id=1, source_target_pairs={{0,16},{4,20},{8,24},{12,28},{16,0},{20,4},{24,8},{28,12},{1,17},{... | collective-permute-start | bytes 1179656 | tf_op jit(solution)/shard_map/ppermute | solution.py:52
  842.9 26.0 %collective-permute-start.77 = (bf16[256,2048]{1,0:T(8,128)(2,1)S(1)}, bf16[256,2048]{1,0:T(8,128)(2,1)}, u32[]{:S(2)}, u32[]{:S(2)}) collective-permute-start(bf16[256,2048]{1,0:T(8,128)(2,1)S(1)} %get-tuple-element.180), channel_id=1, source_target_pairs={{1,0},{2,1},{3,2},{5,4},{6,5},{7,6},{9,8},{10,9},{11,10},{13,12},{... | collective-permute-start | bytes 3145736 | tf_op jit(solution)/shard_map/ppermute | solution.py:111
  845.3 32.1 %collective-permute-start.72 = (bf16[192,1024]{1,0:T(8,128)(2,1)}, bf16[192,1024]{1,0:T(8,128)(2,1)}, u32[]{:S(2)}, u32[]{:S(2)}) collective-permute-start(bf16[192,1024]{1,0:T(8,128)(2,1)} %slice_bitcast_fusion.12), channel_id=1, source_target_pairs={{0,8},{4,12},{8,0},{12,4},{16,24},{20,28},{24,16},{28,20},{1,9},{5... | collective-permute-start | bytes 1179656 | tf_op jit(solution)/shard_map/ppermute | solution.py:52
  863.4 25.5 %collective-permute-start.75 = (bf16[256,2048]{1,0:T(8,128)(2,1)}, bf16[256,2048]{1,0:T(8,128)(2,1)}, u32[]{:S(2)}, u32[]{:S(2)}) collective-permute-start(bf16[256,2048]{1,0:T(8,128)(2,1)} %add_convert_fusion.6), channel_id=1, source_target_pairs={{0,1},{1,2},{2,3},{4,5},{5,6},{6,7},{8,9},{9,10},{10,11},{12,13},{... | collective-permute-start | bytes 3145736 | tf_op jit(solution)/shard_map/ppermute | solution.py:111
  872.0 34.3 %collective-permute-start.79 = (bf16[2,256,2048]{2,1,0:T(8,128)(2,1)}, bf16[2,256,2048]{2,1,0:T(8,128)(2,1)}, u32[]{:S(2)}, u32[]{:S(2)}) collective-permute-start(bf16[2,256,2048]{2,1,0:T(8,128)(2,1)} %fusion.20), channel_id=1, source_target_pairs={{0,4},{4,0},{1,5},{5,1},{2,6},{6,2},{3,7},{7,3},{8,12},{12,8},{9,1... | collective-permute-start | bytes 6291464 | tf_op jit(solution)/shard_map/ppermute | solution.py:149
  874.8 29.4 %collective-permute-start.78 = (bf16[256,2048]{1,0:T(8,128)(2,1)}, bf16[256,2048]{1,0:T(8,128)(2,1)}, u32[]{:S(2)}, u32[]{:S(2)}) collective-permute-start(bf16[256,2048]{1,0:T(8,128)(2,1)} %add_convert_fusion.5), channel_id=1, source_target_pairs={{1,0},{2,1},{3,2},{5,4},{6,5},{7,6},{9,8},{10,9},{11,10},{13,12},{... | collective-permute-start | bytes 3145736 | tf_op jit(solution)/shard_map/ppermute | solution.py:111
  884.1 40.6 %all-to-all-start.4 = ((f32[32,1,1280]{2,1,0:T(1,128)}), f32[32,1,1280]{2,1,0:T(1,128)S(1)}, u32[]{:S(2)}, u32[]{:S(2)}) async-start(f32[32,1,1280]{2,1,0:T(1,128)} %all_to_all.28), calls=%async_computation.8 | async-start | bytes 327680 | tf_op jit(solution)/shard_map/all_to_all | solution.py:715
  912.9 24.2 %collective-permute-start.81 = (bf16[64,2048]{1,0:T(8,128)(2,1)}, bf16[64,2048]{1,0:T(8,128)(2,1)}, u32[]{:S(2)}, u32[]{:S(2)}) collective-permute-start(bf16[64,2048]{1,0:T(8,128)(2,1)} %get-tuple-element.218), channel_id=1, source_target_pairs={{0,0},{1,1},{6,2},{11,3},{12,4},{13,5},{18,6},{23,7},{24,8},{25,9}... | collective-permute-start | bytes 786440 | tf_op jit(solution)/shard_map/ppermute | solution.py:697
  916.7 20.5 %collective-permute-start.82 = (bf16[64,2048]{1,0:T(8,128)(2,1)}, bf16[64,2048]{1,0:T(8,128)(2,1)}, u32[]{:S(2)}, u32[]{:S(2)}) collective-permute-start(bf16[64,2048]{1,0:T(8,128)(2,1)} %get-tuple-element.217), channel_id=1, source_target_pairs={{0,0},{5,1},{6,2},{11,3},{12,4},{17,5},{18,6},{23,7},{24,8},{29,9}... | collective-permute-start | bytes 786440 | tf_op jit(solution)/shard_map/ppermute | solution.py:697
  (124 other events, 1753.3 us)
Sparse Core Ops, SparseCore 0:
  31.6 75.0 all-gather.6
  125.1 90.1 all-gather.4
  271.8 88.4 all-gather.8
  386.5 51.5 all-gather.10
  446.1 51.3 reduce-scatter.8
  500.3 52.5 reduce-scatter.10
  572.5 86.0 reduce-scatter.4
  717.8 84.6 reduce-scatter.6

commit v4 on v3

--- a/solution.py
+++ b/solution.py
@@ -126,8 +126,10 @@
 
 
 def true_order(blocks, zs, zi):
-    blocks = jnp.stack(blocks[::-1] * 2, axis=0)
-    return lax.dynamic_slice_in_dim(blocks, zs - 1 - zi, zs, 0)
+    out = jnp.zeros((zs,) + blocks[0].shape, blocks[0].dtype)
+    for k, block in enumerate(blocks):
+        out = lax.dynamic_update_index_in_dim(out, block, (zi - k) % zs, 0)
+    return out
 
 
 def scatter_z(parts, gates={}):
@@ -354,23 +356,31 @@
     )(*args)
 
 
-def weight_grad_kernel(a_ref, b_ref, out_ref):
-    out_ref[...] = kdot(a_ref[...], b_ref[...], 0, 0).astype(bf16)
-
-
-def weight_grad(a, b):
+def weight_grad_kernel(half, g_ref, u_ref, b_ref, out_ref):
+    @pl.when(pl.program_id(1) < half)
+    def _():
+        out_ref[...] = kdot(g_ref[...], b_ref[...], 0, 0).astype(bf16)
+
+    @pl.when(pl.program_id(1) >= half)
+    def _():
+        out_ref[...] = kdot(u_ref[...], b_ref[...], 0, 0).astype(bf16)
+
+
+def weight_grad(g, u, b):
     tile_a, tile_b = 512, 1024
+    half = g.shape[1] // tile_a
     return pl.pallas_call(
-        weight_grad_kernel,
-        grid=(b.shape[1] // tile_b, a.shape[1] // tile_a),
+        functools.partial(weight_grad_kernel, half),
+        grid=(b.shape[1] // tile_b, 2 * half),
         in_specs=[
-            pl.BlockSpec((a.shape[0], tile_a), lambda n, m: (0, m)),
+            pl.BlockSpec((g.shape[0], tile_a), lambda n, m: (0, jnp.minimum(m, half - 1))),
+            pl.BlockSpec((u.shape[0], tile_a), lambda n, m: (0, jnp.maximum(m - half, 0))),
             pl.BlockSpec((b.shape[0], tile_b), lambda n, m: (0, n)),
         ],
         out_specs=pl.BlockSpec((tile_a, tile_b), lambda n, m: (m, n)),
-        out_shape=jax.ShapeDtypeStruct((a.shape[1], b.shape[1]), bf16),
+        out_shape=jax.ShapeDtypeStruct((2 * g.shape[1], b.shape[1]), bf16),
         cost_estimate=pl.CostEstimate(flops=1, bytes_accessed=1, transcendentals=0),
-    )(a, b)
+    )(g, u, b)
 
 
 def shape_of(rows, cols, dtype):
@@ -462,13 +472,12 @@
         [lax.dynamic_index_in_dim(qkv_slots, slot_of[k], 0, keepdims=False) for k in range(3)],
         axis=0,
     )
-    out_cols = lax.all_to_all(
-        after(w_out, *slot_steps[1]).reshape(orow, dps, width).transpose(1, 0, 2),
-        DP, 0, 0, tiled=True,
-    )
-    out_blocks, out_w_steps = gather_z(after(out_cols, *slot_steps[-1]), zs, zi)
-    w_out_c = true_order(out_blocks, zs, zi).transpose(1, 0, 2, 3).reshape(D, width)
-    dy_blocks, dy_steps = gather_z(after(cotangent, *out_w_steps[-1]), zs, zi)
+    out_cols = after(w_out, *slot_steps[2]).reshape(orow, dps, width).transpose(1, 0, 2)
+    out_cols = jnp.broadcast_to(out_cols[:, None], (dps, zs, orow, width))
+    w_out_c = lax.all_to_all(
+        out_cols.reshape(world, orow, width), ALL, 0, 0, tiled=True
+    ).reshape(D, width)
+    dy_blocks, dy_steps = gather_z(after(cotangent, *slot_steps[-1]), zs, zi)
 
     def in_core_order(own, got):
         first = ci == 0
@@ -481,8 +490,8 @@
         both = in_core_order(own, got)
         return [jnp.concatenate([half[e] for half in both], axis=0) for e in range(mine)]
 
-    gu_half = core_half(after(w_gate_up, *moved))
-    down_half = core_half(after(w_down, *moved))
+    gu_half = core_half(after(w_gate_up, *slot_steps[1]))
+    down_half = core_half(after(w_down, *slot_steps[1]))
     blocks = all_rows // BLOCK
     half = blocks // 2
     own_spec, other_spec = pieces_spec(half, D // 2)
@@ -568,7 +577,8 @@
         grad_act = mm(grad_eo, down, 1, 0)
         grad_g = grad_act * u_part * sig * (1.0 + g_part * (1.0 - sig))
         grad_u = grad_act * silu
-        grad_both = jnp.concatenate([grad_g, grad_u], axis=-1).astype(bf16)
+        grad_g, grad_u = grad_g.astype(bf16), grad_u.astype(bf16)
+        grad_both = jnp.concatenate([grad_g, grad_u], axis=-1)
         rows_back = mm(grad_both, gate_up, 1, 0).astype(bf16).astype(f32)
         dn = mm(grad_eo, act, 0, 0).astype(bf16)
         passes.append(
@@ -576,7 +586,7 @@
                 out=gate_val * expert_out,
                 back=rows_back,
                 gate=grad_gate,
-                both=grad_both,
+                both=(grad_g, grad_u),
                 act=act,
                 dn=lax.psum_scatter(dn, "q", scatter_dimension=0, tiled=True),
             )
@@ -593,7 +603,7 @@
 
     def fill(*deps):
         p = passes[len(gus)]
-        gus.append(weight_grad(after(p["both"], *deps), hidden_g))
+        gus.append(weight_grad(*all_after(p["both"], deps), hidden_g))
         return gus[-1:]
 
     hid_gates = {2: lambda steps: fill(hid_mixed), 3: lambda steps: [cols, out_mixed]}
@@ -689,9 +699,9 @@
     )
     dns = [p["dn"] for p in passes]
     grad_down = core_back([after(dns[0], grad_projected)] + dns[1:])
-    own_sum, own_steps = scatter_z(z_parts(parts), {1: lambda steps: [h1_summed]})
+    own_sum, own_steps = scatter_z(z_parts(parts), {s: lambda steps: [] if steps else [h1_summed] for s in range(1, zs)})
     grad_gate_up = core_back([after(gus[0], *own_steps[1])] + gus[1:])
-    own_sum = after(own_sum.astype(bf16), grad_gate_up, grad_down)
+    own_sum = after(own_sum.astype(bf16), grad_down)
     grad_qkv = jnp.concatenate(
         [
             lax.ppermute(own_sum[t * sub : (t + 1) * sub], ALL, unit_perm(t, True))

time: 957 us -> 966 us (level)
  waiting for transfers between devices: 225 us -> 254 us
  local copies, waits for them, and re-layouts: 86.8 us -> 73 us
    ppermute x42 -> x36, waiting for transfers between devices: 163 us -> 183 us  [line(): lax.ppermute(value, 'z', [(j, j + step) for j in range(zs) if 0 <= j + st...]
    ppermute x8, starting transfers between devices: 11.4 us -> 0.61 us  [swap_core(): return lax.ppermute(value, 'c', [(0, 1), (1, 0)])]
    unnamed x19 -> x7, other arithmetic: 16.6 us -> 6.76 us
    ppermute x42 -> x36, starting transfers between devices: 117 us -> 122 us  [line(): lax.ppermute(value, 'z', [(j, j + step) for j in range(zs) if 0 <= j + st...]
    unnamed x199 -> x182, local copies, waits for them, and re-layouts: 22.7 us -> 19.3 us
  transfers between devices with their start and end apart: 96 -> 90, of which waited for: 35 -> 40; matrix products, arithmetic and copies ran while one was open for 38% -> 35% of each run, Pallas kernels for 12% -> 12%
where the time goes in v4:
time: 966 us; the launch traced here: 955 us
  waiting for transfers between devices  254 us (26%)
  starting transfers between devices  183 us (19%)
  matrix products  178 us (18%)
  Pallas kernels  114 us (12%)
  other arithmetic  110 us (11%)
  local copies, waits for them, and re-layouts  73 us (8%)
  between operations  22.3 us (2%)
  blocking collectives  21 us (2%)
    ppermute x36, waiting for transfers between devices, line(): lax.ppermute(value, 'z', [(j, j + step) for j in range(zs) if 0 <= j + st...  183 us
    dot_general x13, matrix products, mm(): lax.dot_general(a, b, (((ca,), (cb,)), ((), ())), preferred_element_type=...  175 us
    ppermute x36, starting transfers between devices, line(): lax.ppermute(value, 'z', [(j, j + step) for j in range(zs) if 0 <= j + st...  122 us
    pallas_call x4, Pallas kernels, run_blocks(): pl.pallas_call(body, grid=(rows // BLOCK,), in_specs=in_specs, out_specs=...  72.5 us
    ppermute x28, waiting for transfers between devices, flip(): return lax.ppermute(value, DP, [(i, i ^ 1 << bit) for i in range(size)])  56.5 us
    pallas_call x2, Pallas kernels, weight_grad(): pl.pallas_call(functools.partial(weight_grad_kernel, half), grid=(b.shape...  41.7 us
    ppermute x28, starting transfers between devices, flip(): return lax.ppermute(value, DP, [(i, i ^ 1 << bit) for i in range(size)])  27.3 us
    all_to_all x1, blocking collectives, per_device(): lax.all_to_all(cols.transpose(1, 2, 0, 3).reshape(2 * zs, mine, rows), ('...  21 us
  transfers between devices with their start and end apart: 90, of which 40 were waited for; matrix products, arithmetic and copies ran while one was open for 35% of the time, Pallas kernels for 12%

profile of v4, /device:TPU:0, one launch (start us, length us, event | category | flops | bytes accessed | tf_op | source)
XLA Modules:
  0.0 955.1 jit_solution(3453291342214825978)
XLA Ops:
  12.0 17.2 %collective-permute-start.9 = (bf16[192,2048]{1,0:T(8,128)(2,1)S(1)}, bf16[192,2048]{1,0:T(8,128)(2,1)}, u32[]{:S(2)}, u32[]{:S(2)}) collective-permute-start(bf16[192,2048]{1,0:T(8,128)(2,1)S(1)} %constant_dynamic-update-slice_fusion), channel_id=1, source_target_pairs={{0,1},{1,2},{2,3},{4,5},{5,6},{6,7},{8,9},{9,10},{10,11},{12,13},{... | collective-permute-start | bytes 2359304 | tf_op jit(solution)/shard_map/ppermute | solution.py:111
  29.2 15.2 %collective-permute-done.10 = bf16[192,2048]{1,0:T(8,128)(2,1)} collective-permute-done((bf16[192,2048]{1,0:T(8,128)(2,1)S(1)}, bf16[192,2048]{1,0:T(8,128)(2,1)}, u32[]{:S(2)}, u32[]{:S(2)}) %collective-permute-start.10) | collective-permute-done | bytes 786464 | tf_op jit(solution)/shard_map/ppermute | solution.py:111
  55.2 4.0 collective-permute-done.37
  72.8 10.0 %collective-permute-done.2 = bf16[192,1024]{1,0:T(8,128)(2,1)S(1)} collective-permute-done((bf16[192,1024]{1,0:T(8,128)(2,1)S(1)}, bf16[192,1024]{1,0:T(8,128)(2,1)S(1)}, u32[]{:S(2)}, u32[]{:S(2)}) %collective-permute-start.2) | collective-permute-done | bytes 393248 | tf_op jit(solution)/shard_map/ppermute | solution.py:52
  109.1 5.7 all-to-all-start
  114.8 4.6 collective-permute-start.13
  137.0 7.0 all-to-all-start.1
  144.1 3.9 collective-permute-start.14
  152.8 25.8 %collective-permute-done.14 = bf16[192,2048]{1,0:T(8,128)(2,1)S(1)} collective-permute-done((bf16[192,2048]{1,0:T(8,128)(2,1)}, bf16[192,2048]{1,0:T(8,128)(2,1)S(1)}, u32[]{:S(2)}, u32[]{:S(2)}) %collective-permute-start.14) | collective-permute-done | bytes 786464 | tf_op jit(solution)/shard_map/ppermute | solution.py:111
  185.1 14.3 %shard_map.188 = (bf16[1536,2048]{1,0:T(8,128)(2,1)}, f32[1536,768]{1,0:T(8,128)}, f32[8,1536]{1,0:T(8,128)}) custom-call(bf16[768,1024]{1,0:T(8,128)(2,1)} %bitcast.4.a_own, bf16[768,1024]{1,0:T(8,128)(2,1)} %bitcast.9.b_own, bf16[768,1024]{1,0:T(8,128)(2,1)} %collective-permute-done.4.a_other, bf16[768,1024]{1,0:T(8,128)(2,1)} %collective-permute-done.5.b_other, ...), custom_call_target="tpu_custom_call" | custom-call | flops 1 | bytes 1 | tf_op jit(solution)/shard_map/pallas_call | solution.py:349
  212.5 18.8 %shard_map.189 = (bf16[1536,256]{1,0:T(8,128)(2,1)}, bf16[768,2048]{1,0:T(8,128)(2,1)}, bf16[768,2048]{1,0:T(8,128)(2,1)}) custom-call(f32[1536,768]{1,0:T(8,128)} %get-tuple-element.65.raw_ref, f32[8,1536]{1,0:T(8,128)} %pad.11.sum_ref, f32[8,256]{1,0:T(8,128)} %pad.12.gain_ref, f32[384,128]{1,0:T(8,128)} %bitcast.294, f32[384,128]{1,0:T(8,128)} %bitcast.296, ...), custom_call_target="tpu_custom_call" | custom-call | flops 1 | bytes 1 | tf_op jit(solution)/shard_map/pallas_call | solution.py:349
  232.5 10.2 %collective-permute-start.23 = (bf16[192,2048]{1,0:T(8,128)(2,1)S(1)}, bf16[192,2048]{1,0:T(8,128)(2,1)}, u32[]{:S(2)}, u32[]{:S(2)}) collective-permute-start(bf16[192,2048]{1,0:T(8,128)(2,1)S(1)} %copy-done.13), channel_id=1, source_target_pairs={{0,1},{1,2},{2,3},{4,5},{5,6},{6,7},{8,9},{9,10},{10,11},{12,13},{... | collective-permute-start | bytes 2359304 | tf_op jit(solution)/shard_map/ppermute | solution.py:111
  242.7 15.4 %collective-permute-done.26 = bf16[192,2048]{1,0:T(8,128)(2,1)S(1)} collective-permute-done((bf16[192,2048]{1,0:T(8,128)(2,1)S(1)}, bf16[192,2048]{1,0:T(8,128)(2,1)S(1)}, u32[]{:S(2)}, u32[]{:S(2)}) %collective-permute-start.26) | collective-permute-done | bytes 786464 | tf_op jit(solution)/shard_map/ppermute | solution.py:111
  266.1 5.5 collective-permute-start.24
  271.6 8.2 collective-permute-done.27
  297.1 5.3 collective-permute-start.25
  305.3 11.9 %collective-permute-done.25 = bf16[192,2048]{1,0:T(8,128)(2,1)S(1)} collective-permute-done((bf16[192,2048]{1,0:T(8,128)(2,1)}, bf16[192,2048]{1,0:T(8,128)(2,1)S(1)}, u32[]{:S(2)}, u32[]{:S(2)}) %collective-permute-start.25) | collective-permute-done | bytes 786464 | tf_op jit(solution)/shard_map/ppermute | solution.py:111
  326.4 4.5 collective-permute-start.29
  335.9 12.4 %collective-permute-done.29 = bf16[192,2048]{1,0:T(8,128)(2,1)S(1)} collective-permute-done((bf16[192,2048]{1,0:T(8,128)(2,1)S(1)}, bf16[192,2048]{1,0:T(8,128)(2,1)S(1)}, u32[]{:S(2)}, u32[]{:S(2)}) %collective-permute-start.29) | collective-permute-done | bytes 786464 | tf_op jit(solution)/shard_map/ppermute | solution.py:111
  348.3 4.2 collective-permute-done.30
  353.8 4.6 collective-permute-start.34
  358.4 14.9 %collective-permute-done.32 = bf16[192,2048]{1,0:T(8,128)(2,1)S(1)} collective-permute-done((bf16[192,2048]{1,0:T(8,128)(2,1)S(1)}, bf16[192,2048]{1,0:T(8,128)(2,1)S(1)}, u32[]{:S(2)}, u32[]{:S(2)}) %collective-permute-start.32) | collective-permute-done | bytes 786464 | tf_op jit(solution)/shard_map/ppermute | solution.py:111
  375.5 4.6 collective-permute-start.35
  380.1 13.3 %collective-permute-done.33 = bf16[192,2048]{1,0:T(8,128)(2,1)S(1)} collective-permute-done((bf16[192,2048]{1,0:T(8,128)(2,1)S(1)}, bf16[192,2048]{1,0:T(8,128)(2,1)S(1)}, u32[]{:S(2)}, u32[]{:S(2)}) %collective-permute-start.33) | collective-permute-done | bytes 786464 | tf_op jit(solution)/shard_map/ppermute | solution.py:111
  404.7 4.0 constant_dynamic-update-slice_fusion.8.b_ref
  408.7 4.8 fusion.93
  413.8 19.3 %fusion.94 = f32[1536,2048]{1,0:T(8,128)} fusion(bf16[1536,2048]{1,0:T(8,128)(2,1)} %constant_dynamic-update-slice_fusion.8.b_ref, bf16[2048,2048]{1,0:T(8,128)(2,1)} %all-gather.5.cloned.1.call-done), kind=kOutput, calls=%fused_computation.295 | convolution fusion | flops 12884901888 | bytes 27262976 | tf_op jit(solution)/shard_map/dot_general | solution.py:44
  433.2 16.2 %multiply_convert_fusion.3 = (bf16[1536,1024]{1,0:T(8,128)(2,1)}, bf16[1536,1024]{1,0:T(8,128)(2,1)}, bf16[1536,1024]{1,0:T(8,128)(2,1)S(1)}) fusion(f32[1536,2048]{1,0:T(8,128)} %fusion.94, bf16[2048,1024]{1,0:T(8,128)(2,1)S(1)} %copy-done.79, bf16[1536,2048]{1,0:T(8,128)(2,1)} %copy-done.62, f32[1536]{0:T(1024)S(1)} %broadcast_select_fusion.12), kind=kOutput, calls=%fused_computation.36 | convolution fusion | flops 6475481088 | bytes 32512000 | tf_op jit(solution)/shard_map/dot_general | solution.py:44
  449.3 12.8 %convolution_convert_fusion.5 = bf16[2048,1024]{1,0:T(8,128)(2,1)} fusion(bf16[1536,1024]{1,0:T(8,128)(2,1)S(1)} %get-tuple-element.183, bf16[1536,2048]{1,0:T(8,128)(2,1)} %copy-done.62, f32[1536]{0:T(1024)S(1)} %broadcast_select_fusion.12), kind=kOutput, calls=%fused_computation.55 | convolution fusion | flops 6453985280 | bytes 13637632 | tf_op jit(solution)/shard_map/dot_general | solution.py:44
  462.2 19.2 %fusion.95 = f32[1536,2048]{1,0:T(8,128)} fusion(bf16[1536,2048]{1,0:T(8,128)(2,1)} %constant_dynamic-update-slice_fusion.8.b_ref, bf16[2048,2048]{1,0:T(8,128)(2,1)} %all-gather.9.cloned.1.call-done), kind=kOutput, calls=%fused_computation.296 | convolution fusion | flops 12884901888 | bytes 27262976 | tf_op jit(solution)/shard_map/dot_general | solution.py:44
  481.5 18.8 %multiply_convert_fusion.1 = (bf16[1536,1024]{1,0:T(8,128)(2,1)S(1)}, bf16[1536,1024]{1,0:T(8,128)(2,1)}, bf16[1536,1024]{1,0:T(8,128)(2,1)S(1)}) fusion(f32[1536,2048]{1,0:T(8,128)} %fusion.95, bf16[2048,1024]{1,0:T(8,128)(2,1)} %all-gather.11.cloned.1.call-done, bf16[1536,2048]{1,0:T(8,128)(2,1)} %copy-done.62, f32[1536]{0:T(1024)S(1)} %broadcast_select_fusion.11), kind=kOutput, calls=%fused_computation.34 | convolution fusion | flops 6475481088 | bytes 32512000 | tf_op jit(solution)/shard_map/dot_general | solution.py:44
  502.0 13.0 %convolution_convert_fusion.4 = bf16[2048,1024]{1,0:T(8,128)(2,1)} fusion(bf16[1536,1024]{1,0:T(8,128)(2,1)S(1)} %get-tuple-element.184, bf16[1536,2048]{1,0:T(8,128)(2,1)} %copy-done.62, f32[1536]{0:T(1024)S(1)} %broadcast_select_fusion.11), kind=kOutput, calls=%fused_computation.54 | convolution fusion | flops 6453985280 | bytes 13637632 | tf_op jit(solution)/shard_map/dot_general | solution.py:44
  515.1 19.0 %convolution_convert_fusion = bf16[1536,2048]{1,0:T(8,128)(2,1)} fusion(bf16[2048,2048]{1,0:T(8,128)(2,1)} %all-gather.9.cloned.1.call-done, bf16[1536,1024]{1,0:T(8,128)(2,1)} %get-tuple-element.87.u_ref, bf16[1536,1024]{1,0:T(8,128)(2,1)S(1)} %get-tuple-element.86.g_ref), kind=kOutput, calls=%fused_computation.17 | convolution fusion | flops 12900630528 | bytes 20971520 | tf_op jit(solution)/shard_map/dot_general | solution.py:44
  534.1 18.1 %add_convert_fusion = bf16[1536,2048]{1,0:T(8,128)(2,1)S(1)} fusion(bf16[1536,2048]{1,0:T(8,128)(2,1)} %convolution_convert_fusion, bf16[2048,2048]{1,0:T(8,128)(2,1)} %all-gather.5.cloned.1.call-done, bf16[1536,1024]{1,0:T(8,128)(2,1)} %get-tuple-element.83.u_ref, bf16[1536,1024]{1,0:T(8,128)(2,1)S(1)} %copy-done.34), kind=kOutput, calls=%fused_computation.16 | convolution fusion | flops 12913213440 | bytes 27262976 | tf_op jit(solution)/shard_map/dot_general | solution.py:44
  552.5 5.6 collective-permute-done.40
  561.1 4.8 collective-permute-start.41
  567.2 20.6 %shard_map.190 = bf16[2048,2048]{1,0:T(8,128)(2,1)} custom-call(bf16[1536,1024]{1,0:T(8,128)(2,1)} %get-tuple-element.82.g_ref, bf16[1536,1024]{1,0:T(8,128)(2,1)} %get-tuple-element.83.u_ref, bf16[1536,2048]{1,0:T(8,128)(2,1)} %constant_dynamic-update-slice_fusion.8.b_ref), custom_call_target="tpu_custom_call" | custom-call | flops 1 | bytes 1 | tf_op jit(solution)/shard_map/pallas_call | solution.py:372
  588.0 11.4 %convolution_convert_fusion.3 = bf16[1536,2048]{1,0:T(8,128)(2,1)} fusion(bf16[1536,1024]{1,0:T(8,128)(2,1)} %copy-done.81, bf16[2048,1024]{1,0:T(8,128)(2,1)} %all-gather.7.cloned.1.call-done), kind=kOutput, calls=%fused_computation.20 | convolution fusion | flops 6445596672 | bytes 13631488 | tf_op jit(solution)/shard_map/dot_general | solution.py:44
  599.4 13.3 %fusion.4 = (f32[1536]{0:T(1024)S(1)}, f32[1536]{0:T(1024)S(1)}, bf16[1536,2048]{1,0:T(8,128)(2,1)S(1)}) fusion(bf16[1536,2048]{1,0:T(8,128)(2,1)} %convolution_convert_fusion.3, bf16[1536,2048]{1,0:T(8,128)(2,1)} %copy-done.62, f32[1536]{0:T(1024)S(1)} %broadcast_select_fusion.11, f32[1536]{0:T(1024)S(1)} %copy-done.74, ...), kind=kOutput, calls=%fused_computation.14 | convolution fusion | flops 6480196608 | bytes 26238976 | tf_op jit(solution)/shard_map/dot_general | solution.py:44
  619.4 4.6 collective-permute-start.43
  625.8 6.3 add_convert_fusion.3
  632.1 21.1 %shard_map.191 = bf16[2048,2048]{1,0:T(8,128)(2,1)} custom-call(bf16[1536,1024]{1,0:T(8,128)(2,1)} %copy-done.33, bf16[1536,1024]{1,0:T(8,128)(2,1)} %get-tuple-element.87.u_ref, bf16[1536,2048]{1,0:T(8,128)(2,1)} %constant_dynamic-update-slice_fusion.8.b_ref), custom_call_target="tpu_custom_call" | custom-call | flops 1 | bytes 1 | tf_op jit(solution)/shard_map/pallas_call | solution.py:372
  653.3 3.6 add_convert_fusion.10
  656.9 5.2 collective-permute-start.45
  664.5 21.0 %all_to_all.34 = f32[8,2,192]{2,1,0:T(2,128)S(1)} all-to-all(f32[8,2,192]{2,1,0:T(2,128)S(1)} %bitcast.317), channel_id=1, replica_groups=mesh['q'=4,'c'=2,'z'=4] {'c','z'}, dimensions={0} | all-to-all | bytes 24576 | tf_op jit(solution)/shard_map/all_to_all | solution.py:616
  692.1 9.0 collective-permute-done.55
  707.5 12.4 %collective-permute-done.56 = bf16[2,192,1024]{2,1,0:T(8,128)(2,1)S(1)} collective-permute-done((bf16[2,192,1024]{2,1,0:T(8,128)(2,1)S(1)}, bf16[2,192,1024]{2,1,0:T(8,128)(2,1)S(1)}, u32[]{:S(2)}, u32[]{:S(2)}) %collective-permute-start.56) | collective-permute-done | bytes 786464 | tf_op jit(solution)/shard_map/ppermute | solution.py:52
  721.3 4.2 collective-permute-done.48
  738.9 26.7 %shard_map.192 = (f32[1536,512]{1,0:T(8,128)}, bf16[1536,256]{1,0:T(8,128)(2,1)}, f32[8,1536]{1,0:T(8,128)}, f32[8,256]{1,0:T(8,128)}, f32[2048,256]{1,0:T(8,128)}) custom-call(f32[1536,768]{1,0:T(8,128)} %get-tuple-element.65.raw_ref, f32[8,1536]{1,0:T(8,128)} %pad.11.sum_ref, f32[8,256]{1,0:T(8,128)} %pad.12.gain_ref, f32[384,128]{1,0:T(8,128)} %bitcast.295, ...), custom_call_target="tpu_custom_call" | custom-call | flops 1 | bytes 1 | tf_op jit(solution)/shard_map/pallas_call | solution.py:349
  768.2 3.9 collective-permute-done.60
  775.8 5.7 collective-permute-start.51
  783.8 12.7 %shard_map.193 = (bf16[1536,768]{1,0:T(8,128)(2,1)}, bf16[768,2048]{1,0:T(8,128)(2,1)}, bf16[768,2048]{1,0:T(8,128)(2,1)}) custom-call(f32[1536,768]{1,0:T(8,128)} %get-tuple-element.65.raw_ref, f32[8,1536]{1,0:T(8,128)} %pad.11.sum_ref, f32[1536,512]{1,0:T(8,128)} %get-tuple-element.98.back_ref, bf16[1536,256]{1,0:T(8,128)(2,1)} %get-tuple-element.99.dv_ref, ...), custom_call_target="tpu_custom_call" | custom-call | flops 1 | bytes 1 | tf_op jit(solution)/shard_map/pallas_call | solution.py:349
  797.0 5.0 collective-permute-done.52
  804.0 8.1 convolution_convert_fusion.6
  830.5 16.2 %collective-permute-done.67 = bf16[256,2048]{1,0:T(8,128)(2,1)S(1)} collective-permute-done((bf16[256,2048]{1,0:T(8,128)(2,1)S(1)}, bf16[256,2048]{1,0:T(8,128)(2,1)S(1)}, u32[]{:S(2)}, u32[]{:S(2)}) %collective-permute-start.67) | collective-permute-done | bytes 1048608 | tf_op jit(solution)/shard_map/ppermute | solution.py:111
  846.7 4.2 collective-permute-done.68
  854.7 4.6 collective-permute-start.69
  863.2 14.1 %collective-permute-done.70 = bf16[256,2048]{1,0:T(8,128)(2,1)S(1)} collective-permute-done((bf16[256,2048]{1,0:T(8,128)(2,1)S(1)}, bf16[256,2048]{1,0:T(8,128)(2,1)S(1)}, u32[]{:S(2)}, u32[]{:S(2)}) %collective-permute-start.70) | collective-permute-done | bytes 1048608 | tf_op jit(solution)/shard_map/ppermute | solution.py:111
  881.3 5.4 collective-permute-start.71
  900.6 6.6 collective-permute-done.71
  907.2 5.4 collective-permute-done.72
  915.6 3.7 collective-permute-start.74
  931.4 5.0 fusion.40
  944.1 3.9 maximum_convert_fusion
  (521 shorter events, 271.9 us)
Async XLA Ops:
  7.2 406.6 %all-gather.7.cloned.1.call-start = ((), (), s32[]{:S(2)}) async-start(), calls=%async_computation.10 | async-start | bytes 5242880 | tf_op jit(solution)/shard_map/all_gather | solution.py:534
  10.7 33.7 %collective-permute-start.10 = (bf16[192,2048]{1,0:T(8,128)(2,1)S(1)}, bf16[192,2048]{1,0:T(8,128)(2,1)}, u32[]{:S(2)}, u32[]{:S(2)}) collective-permute-start(bf16[192,2048]{1,0:T(8,128)(2,1)S(1)} %constant_dynamic-update-slice_fusion), channel_id=1, source_target_pairs={{1,0},{2,1},{3,2},{5,4},{6,5},{7,6},{9,8},{10,9},{11,10},{13,12},{... | collective-permute-start | bytes 2359304 | tf_op jit(solution)/shard_map/ppermute | solution.py:111
  12.0 33.4 %collective-permute-start.9 = (bf16[192,2048]{1,0:T(8,128)(2,1)S(1)}, bf16[192,2048]{1,0:T(8,128)(2,1)}, u32[]{:S(2)}, u32[]{:S(2)}) collective-permute-start(bf16[192,2048]{1,0:T(8,128)(2,1)S(1)} %constant_dynamic-update-slice_fusion), channel_id=1, source_target_pairs={{0,1},{1,2},{2,3},{4,5},{5,6},{6,7},{8,9},{9,10},{10,11},{12,13},{... | collective-permute-start | bytes 2359304 | tf_op jit(solution)/shard_map/ppermute | solution.py:111
  53.1 360.7 %all-gather.5.cloned.1.call-start = ((), (), s32[]{:S(2)}) async-start(), calls=%async_computation.9 | async-start | bytes 10485760 | tf_op jit(solution)/shard_map/all_gather | solution.py:533
  63.2 19.6 %collective-permute-start.2 = (bf16[192,1024]{1,0:T(8,128)(2,1)S(1)}, bf16[192,1024]{1,0:T(8,128)(2,1)S(1)}, u32[]{:S(2)}, u32[]{:S(2)}) collective-permute-start(bf16[192,1024]{1,0:T(8,128)(2,1)S(1)} %get-tuple-element.249), channel_id=1, source_target_pairs={{0,16},{4,20},{8,24},{12,28},{16,0},{20,4},{24,8},{28,12},{1,17},{... | collective-permute-start | bytes 1179656 | tf_op jit(solution)/shard_map/ppermute | solution.py:52
  64.8 23.3 %collective-permute-start = (bf16[192,1024]{1,0:T(8,128)(2,1)S(1)}, bf16[192,1024]{1,0:T(8,128)(2,1)}, u32[]{:S(2)}, u32[]{:S(2)}) collective-permute-start(bf16[192,1024]{1,0:T(8,128)(2,1)S(1)} %get-tuple-element.250), channel_id=1, source_target_pairs={{0,8},{4,12},{8,0},{12,4},{16,24},{20,28},{24,16},{28,20},{1,9},{5... | collective-permute-start | bytes 1179656 | tf_op jit(solution)/shard_map/ppermute | solution.py:52
  69.3 50.1 %collective-permute-start.11 = (bf16[192,2048]{1,0:T(8,128)(2,1)}, bf16[192,2048]{1,0:T(8,128)(2,1)}, u32[]{:S(2)}, u32[]{:S(2)}) collective-permute-start(bf16[192,2048]{1,0:T(8,128)(2,1)} %collective-permute-done.10), channel_id=1, source_target_pairs={{1,0},{2,1},{3,2},{5,4},{6,5},{7,6},{9,8},{10,9},{11,10},{13,12},{... | collective-permute-start | bytes 2359304 | tf_op jit(solution)/shard_map/ppermute | solution.py:111
  85.5 35.6 %collective-permute-start.3 = (bf16[2,192,1024]{2,1,0:T(8,128)(2,1)}, bf16[2,192,1024]{2,1,0:T(8,128)(2,1)}, u32[]{:S(2)}, u32[]{:S(2)}) collective-permute-start(bf16[2,192,1024]{2,1,0:T(8,128)(2,1)} %get-tuple-element.246), channel_id=1, source_target_pairs={{0,8},{4,12},{8,0},{12,4},{16,24},{20,28},{24,16},{28,20},{1,9},{5... | collective-permute-start | bytes 2359304 | tf_op jit(solution)/shard_map/ppermute | solution.py:52
  90.1 37.7 %collective-permute-start.1 = (bf16[2,192,1024]{2,1,0:T(8,128)(2,1)}, bf16[2,192,1024]{2,1,0:T(8,128)(2,1)}, u32[]{:S(2)}, u32[]{:S(2)}) collective-permute-start(bf16[2,192,1024]{2,1,0:T(8,128)(2,1)} %get-tuple-element.252), channel_id=1, source_target_pairs={{0,16},{4,20},{8,24},{12,28},{16,0},{20,4},{24,8},{28,12},{1,17},{... | collective-permute-start | bytes 2359304 | tf_op jit(solution)/shard_map/ppermute | solution.py:52
  109.1 21.1 %all-to-all-start = ((bf16[32,2,1504]{2,1,0:T(2,128)(2,1)}), bf16[32,2,1504]{2,1,0:T(2,128)(2,1)S(1)}, u32[]{:S(2)}, u32[]{:S(2)}) async-start(bf16[32,2,1504]{2,1,0:T(2,128)(2,1)} %reshape.528), calls=%async_computation | async-start | bytes 393216 | tf_op jit(solution)/shard_map/all_to_all | solution.py:443
  114.8 21.1 %collective-permute-start.13 = (bf16[192,2048]{1,0:T(8,128)(2,1)}, bf16[192,2048]{1,0:T(8,128)(2,1)}, u32[]{:S(2)}, u32[]{:S(2)}) collective-permute-start(bf16[192,2048]{1,0:T(8,128)(2,1)} %collective-permute-done.9), channel_id=1, source_target_pairs={{0,1},{1,2},{2,3},{4,5},{5,6},{6,7},{8,9},{9,10},{10,11},{12,13},{... | collective-permute-start | bytes 2359304 | tf_op jit(solution)/shard_map/ppermute | solution.py:111
  119.3 28.7 %collective-permute-start.12 = (bf16[192,2048]{1,0:T(8,128)(2,1)}, bf16[192,2048]{1,0:T(8,128)(2,1)}, u32[]{:S(2)}, u32[]{:S(2)}) collective-permute-start(bf16[192,2048]{1,0:T(8,128)(2,1)} %collective-permute-done.11), channel_id=1, source_target_pairs={{1,0},{2,1},{3,2},{5,4},{6,5},{7,6},{9,8},{10,9},{11,10},{13,12},{... | collective-permute-start | bytes 2359304 | tf_op jit(solution)/shard_map/ppermute | solution.py:111
  124.3 60.8 %collective-permute-start.5 = (bf16[768,1024]{1,0:T(8,128)(2,1)}, bf16[768,1024]{1,0:T(8,128)(2,1)}, u32[]{:S(2)}, u32[]{:S(2)}) collective-permute-start(bf16[768,1024]{1,0:T(8,128)(2,1)} %bitcast.9.b_own), channel_id=1, source_target_pairs={{0,4},{4,0},{8,12},{12,8},{16,20},{20,16},{24,28},{28,24},{1,5},{5... | collective-permute-start | bytes 4718600 | tf_op jit(solution)/shard_map/ppermute | solution.py:52
  130.2 54.9 %collective-permute-start.4 = (bf16[768,1024]{1,0:T(8,128)(2,1)}, bf16[768,1024]{1,0:T(8,128)(2,1)}, u32[]{:S(2)}, u32[]{:S(2)}) collective-permute-start(bf16[768,1024]{1,0:T(8,128)(2,1)} %bitcast.4.a_own), channel_id=1, source_target_pairs={{0,4},{4,0},{8,12},{12,8},{16,20},{20,16},{24,28},{28,24},{1,5},{5... | collective-permute-start | bytes 4718600 | tf_op jit(solution)/shard_map/ppermute | solution.py:52
  137.0 74.0 %all-to-all-start.1 = ((bf16[32,64,256]{2,1,0:T(8,128)(2,1)}), bf16[32,64,256]{2,1,0:T(8,128)(2,1)S(1)}, u32[]{:S(2)}, u32[]{:S(2)}) async-start(bf16[32,64,256]{2,1,0:T(8,128)(2,1)} %bitcast.284), calls=%async_computation.1 | async-start | bytes 2097152 | tf_op jit(solution)/shard_map/all_to_all | solution.py:477
  144.0 269.8 %all-gather.9.cloned.1.call-start = ((), (), s32[]{:S(2)}) async-start(), calls=%async_computation.11 | async-start | bytes 10485760 | tf_op jit(solution)/shard_map/all_gather | solution.py:533
  144.1 34.5 %collective-permute-start.14 = (bf16[192,2048]{1,0:T(8,128)(2,1)}, bf16[192,2048]{1,0:T(8,128)(2,1)S(1)}, u32[]{:S(2)}, u32[]{:S(2)}) collective-permute-start(bf16[192,2048]{1,0:T(8,128)(2,1)} %collective-permute-done.13), channel_id=1, source_target_pairs={{0,1},{1,2},{2,3},{4,5},{5,6},{6,7},{8,9},{9,10},{10,11},{12,13},{... | collective-permute-start | bytes 2359304 | tf_op jit(solution)/shard_map/ppermute | solution.py:111
  231.2 28.1 %collective-permute-start.18 = (bf16[768,2048]{1,0:T(8,128)(2,1)}, bf16[768,2048]{1,0:T(8,128)(2,1)S(1)}, u32[]{:S(2)}, u32[]{:S(2)}) collective-permute-start(bf16[768,2048]{1,0:T(8,128)(2,1)} %get-tuple-element.69), channel_id=1, source_target_pairs={{0,4},{4,0},{8,12},{12,8},{16,20},{20,16},{24,28},{28,24},{1,5},{5... | collective-permute-start | bytes 9437192 | tf_op jit(solution)/shard_map/ppermute | solution.py:52
  231.2 26.8 %collective-permute-start.26 = (bf16[192,2048]{1,0:T(8,128)(2,1)S(1)}, bf16[192,2048]{1,0:T(8,128)(2,1)S(1)}, u32[]{:S(2)}, u32[]{:S(2)}) collective-permute-start(bf16[192,2048]{1,0:T(8,128)(2,1)S(1)} %copy-done.13), channel_id=1, source_target_pairs={{1,0},{2,1},{3,2},{5,4},{6,5},{7,6},{9,8},{10,9},{11,10},{13,12},{... | collective-permute-start | bytes 2359304 | tf_op jit(solution)/shard_map/ppermute | solution.py:111
  232.5 33.6 %collective-permute-start.23 = (bf16[192,2048]{1,0:T(8,128)(2,1)S(1)}, bf16[192,2048]{1,0:T(8,128)(2,1)}, u32[]{:S(2)}, u32[]{:S(2)}) collective-permute-start(bf16[192,2048]{1,0:T(8,128)(2,1)S(1)} %copy-done.13), channel_id=1, source_target_pairs={{0,1},{1,2},{2,3},{4,5},{5,6},{6,7},{8,9},{9,10},{10,11},{12,13},{... | collective-permute-start | bytes 2359304 | tf_op jit(solution)/shard_map/ppermute | solution.py:111
  258.1 21.6 %collective-permute-start.27 = (bf16[192,2048]{1,0:T(8,128)(2,1)S(1)}, bf16[192,2048]{1,0:T(8,128)(2,1)}, u32[]{:S(2)}, u32[]{:S(2)}) collective-permute-start(bf16[192,2048]{1,0:T(8,128)(2,1)S(1)} %collective-permute-done.26), channel_id=1, source_target_pairs={{1,0},{2,1},{3,2},{5,4},{6,5},{7,6},{9,8},{10,9},{11,10},{13,12},{... | collective-permute-start | bytes 2359304 | tf_op jit(solution)/shard_map/ppermute | solution.py:111
  262.9 19.4 %collective-permute-start.19 = (bf16[2,192,1024]{2,1,0:T(8,128)(2,1)S(1)}, bf16[2,192,1024]{2,1,0:T(8,128)(2,1)S(1)}, u32[]{:S(2)}, u32[]{:S(2)}) collective-permute-start(bf16[2,192,1024]{2,1,0:T(8,128)(2,1)S(1)} %slice_bitcast_fusion.6), channel_id=1, source_target_pairs={{0,8},{4,12},{8,0},{12,4},{16,24},{20,28},{24,16},{28,20},{1,9},{5... | collective-permute-start | bytes 2359304 | tf_op jit(solution)/shard_map/ppermute | solution.py:52
  264.6 20.3 %collective-permute-start.21 = (bf16[2,192,1024]{2,1,0:T(8,128)(2,1)S(1)}, bf16[2,192,1024]{2,1,0:T(8,128)(2,1)S(1)}, u32[]{:S(2)}, u32[]{:S(2)}) collective-permute-start(bf16[2,192,1024]{2,1,0:T(8,128)(2,1)S(1)} %bitcast.306), channel_id=1, source_target_pairs={{0,16},{4,20},{8,24},{12,28},{16,0},{20,4},{24,8},{28,12},{1,17},{... | collective-permute-start | bytes 2359304 | tf_op jit(solution)/shard_map/ppermute | solution.py:52
  266.1 31.0 %collective-permute-start.24 = (bf16[192,2048]{1,0:T(8,128)(2,1)}, bf16[192,2048]{1,0:T(8,128)(2,1)}, u32[]{:S(2)}, u32[]{:S(2)}) collective-permute-start(bf16[192,2048]{1,0:T(8,128)(2,1)} %collective-permute-done.23), channel_id=1, source_target_pairs={{0,1},{1,2},{2,3},{4,5},{5,6},{6,7},{8,9},{9,10},{10,11},{12,13},{... | collective-permute-start | bytes 2359304 | tf_op jit(solution)/shard_map/ppermute | solution.py:111
  279.7 22.7 %collective-permute-start.28 = (bf16[192,2048]{1,0:T(8,128)(2,1)}, bf16[192,2048]{1,0:T(8,128)(2,1)}, u32[]{:S(2)}, u32[]{:S(2)}) collective-permute-start(bf16[192,2048]{1,0:T(8,128)(2,1)} %collective-permute-done.27), channel_id=1, source_target_pairs={{1,0},{2,1},{3,2},{5,4},{6,5},{7,6},{9,8},{10,9},{11,10},{13,12},{... | collective-permute-start | bytes 2359304 | tf_op jit(solution)/shard_map/ppermute | solution.py:111
  297.0 184.5 %all-gather.11.cloned.1.call-start = ((), (), s32[]{:S(2)}) async-start(), calls=%async_computation.12 | async-start | bytes 5242880 | tf_op jit(solution)/shard_map/all_gather | solution.py:534
  297.1 20.1 %collective-permute-start.25 = (bf16[192,2048]{1,0:T(8,128)(2,1)}, bf16[192,2048]{1,0:T(8,128)(2,1)S(1)}, u32[]{:S(2)}, u32[]{:S(2)}) collective-permute-start(bf16[192,2048]{1,0:T(8,128)(2,1)} %collective-permute-done.24), channel_id=1, source_target_pairs={{0,1},{1,2},{2,3},{4,5},{5,6},{6,7},{8,9},{9,10},{10,11},{12,13},{... | collective-permute-start | bytes 2359304 | tf_op jit(solution)/shard_map/ppermute | solution.py:111
  326.4 21.9 %collective-permute-start.29 = (bf16[192,2048]{1,0:T(8,128)(2,1)S(1)}, bf16[192,2048]{1,0:T(8,128)(2,1)S(1)}, u32[]{:S(2)}, u32[]{:S(2)}) collective-permute-start(bf16[192,2048]{1,0:T(8,128)(2,1)S(1)} %multiply_convert_fusion.6), channel_id=1, source_target_pairs={{0,1},{1,2},{2,3},{4,5},{5,6},{6,7},{8,9},{9,10},{10,11},{12,13},{... | collective-permute-start | bytes 2359304 | tf_op jit(solution)/shard_map/ppermute | solution.py:111
  330.9 21.6 %collective-permute-start.30 = (bf16[192,2048]{1,0:T(8,128)(2,1)S(1)}, bf16[192,2048]{1,0:T(8,128)(2,1)S(1)}, u32[]{:S(2)}, u32[]{:S(2)}) collective-permute-start(bf16[192,2048]{1,0:T(8,128)(2,1)S(1)} %multiply_convert_fusion.6), channel_id=1, source_target_pairs={{1,0},{2,1},{3,2},{5,4},{6,5},{7,6},{9,8},{10,9},{11,10},{13,12},{... | collective-permute-start | bytes 2359304 | tf_op jit(solution)/shard_map/ppermute | solution.py:111
  352.5 20.8 %collective-permute-start.32 = (bf16[192,2048]{1,0:T(8,128)(2,1)S(1)}, bf16[192,2048]{1,0:T(8,128)(2,1)S(1)}, u32[]{:S(2)}, u32[]{:S(2)}) collective-permute-start(bf16[192,2048]{1,0:T(8,128)(2,1)S(1)} %collective-permute-done.30), channel_id=1, source_target_pairs={{1,0},{2,1},{3,2},{5,4},{6,5},{7,6},{9,8},{10,9},{11,10},{13,12},{... | collective-permute-start | bytes 2359304 | tf_op jit(solution)/shard_map/ppermute | solution.py:111
  353.8 21.8 %collective-permute-start.34 = (bf16[192,2048]{1,0:T(8,128)(2,1)S(1)}, bf16[192,2048]{1,0:T(8,128)(2,1)S(1)}, u32[]{:S(2)}, u32[]{:S(2)}) collective-permute-start(bf16[192,2048]{1,0:T(8,128)(2,1)S(1)} %collective-permute-done.29), channel_id=1, source_target_pairs={{0,1},{1,2},{2,3},{4,5},{5,6},{6,7},{8,9},{9,10},{10,11},{12,13},{... | collective-permute-start | bytes 2359304 | tf_op jit(solution)/shard_map/ppermute | solution.py:111
  373.3 20.1 %collective-permute-start.33 = (bf16[192,2048]{1,0:T(8,128)(2,1)S(1)}, bf16[192,2048]{1,0:T(8,128)(2,1)S(1)}, u32[]{:S(2)}, u32[]{:S(2)}) collective-permute-start(bf16[192,2048]{1,0:T(8,128)(2,1)S(1)} %collective-permute-done.32), channel_id=1, source_target_pairs={{1,0},{2,1},{3,2},{5,4},{6,5},{7,6},{9,8},{10,9},{11,10},{13,12},{... | collective-permute-start | bytes 2359304 | tf_op jit(solution)/shard_map/ppermute | solution.py:111
  375.5 20.1 %collective-permute-start.35 = (bf16[192,2048]{1,0:T(8,128)(2,1)S(1)}, bf16[192,2048]{1,0:T(8,128)(2,1)S(1)}, u32[]{:S(2)}, u32[]{:S(2)}) collective-permute-start(bf16[192,2048]{1,0:T(8,128)(2,1)S(1)} %collective-permute-done.34), channel_id=1, source_target_pairs={{0,1},{1,2},{2,3},{4,5},{5,6},{6,7},{8,9},{9,10},{10,11},{12,13},{... | collective-permute-start | bytes 2359304 | tf_op jit(solution)/shard_map/ppermute | solution.py:111
  403.0 410.9 %reduce-scatter.5.cloned.1.call-start = ((), (), s32[]{:S(2)}) async-start(), calls=%async_computation.13 | async-start | bytes 5242880 | tf_op jit(solution)/shard_map/reduce_scatter | solution.py:591
  462.2 351.7 %reduce-scatter.7.cloned.1.call-start = ((), (), s32[]{:S(2)}) async-start(), calls=%async_computation.14 | async-start | bytes 5242880 | tf_op jit(solution)/shard_map/reduce_scatter | solution.py:591
  515.0 382.1 %reduce-scatter.9.cloned.1.call-start = ((), (), s32[]{:S(2)}) async-start(), calls=%async_computation.15 | async-start | bytes 10485760 | tf_op jit(solution)/shard_map/reduce_scatter | solution.py:651
  561.1 26.8 %collective-permute-start.41 = (bf16[192,2048]{1,0:T(8,128)(2,1)}, bf16[192,2048]{1,0:T(8,128)(2,1)}, u32[]{:S(2)}, u32[]{:S(2)}) collective-permute-start(bf16[192,2048]{1,0:T(8,128)(2,1)} %get-tuple-element.211), channel_id=1, source_target_pairs={{0,1},{1,2},{2,3},{4,5},{5,6},{6,7},{8,9},{9,10},{10,11},{12,13},{... | collective-permute-start | bytes 2359304 | tf_op jit(solution)/shard_map/ppermute | solution.py:111
  566.0 21.9 %collective-permute-start.42 = (bf16[192,2048]{1,0:T(8,128)(2,1)}, bf16[192,2048]{1,0:T(8,128)(2,1)}, u32[]{:S(2)}, u32[]{:S(2)}) collective-permute-start(bf16[192,2048]{1,0:T(8,128)(2,1)} %get-tuple-element.210), channel_id=1, source_target_pairs={{1,0},{2,1},{3,2},{5,4},{6,5},{7,6},{9,8},{10,9},{11,10},{13,12},{... | collective-permute-start | bytes 2359304 | tf_op jit(solution)/shard_map/ppermute | solution.py:111
  587.9 309.2 %reduce-scatter.11.cloned.1.call-start = ((), (), s32[]{:S(2)}) async-start(), calls=%async_computation.16 | async-start | bytes 10485760 | tf_op jit(solution)/shard_map/reduce_scatter | solution.py:651
  619.4 33.9 %collective-permute-start.43 = (bf16[192,2048]{1,0:T(8,128)(2,1)}, bf16[192,2048]{1,0:T(8,128)(2,1)S(1)}, u32[]{:S(2)}, u32[]{:S(2)}) collective-permute-start(bf16[192,2048]{1,0:T(8,128)(2,1)} %get-tuple-element.84), channel_id=1, source_target_pairs={{0,1},{1,2},{2,3},{4,5},{5,6},{6,7},{8,9},{9,10},{10,11},{12,13},{... | collective-permute-start | bytes 2359304 | tf_op jit(solution)/shard_map/ppermute | solution.py:111
  624.0 29.3 %collective-permute-start.44 = (bf16[192,2048]{1,0:T(8,128)(2,1)}, bf16[192,2048]{1,0:T(8,128)(2,1)}, u32[]{:S(2)}, u32[]{:S(2)}) collective-permute-start(bf16[192,2048]{1,0:T(8,128)(2,1)} %get-tuple-element.85), channel_id=1, source_target_pairs={{1,0},{2,1},{3,2},{5,4},{6,5},{7,6},{9,8},{10,9},{11,10},{13,12},{... | collective-permute-start | bytes 2359304 | tf_op jit(solution)/shard_map/ppermute | solution.py:111
  656.9 28.7 %collective-permute-start.45 = (bf16[192,2048]{1,0:T(8,128)(2,1)}, bf16[192,2048]{1,0:T(8,128)(2,1)}, u32[]{:S(2)}, u32[]{:S(2)}) collective-permute-start(bf16[192,2048]{1,0:T(8,128)(2,1)} %get-tuple-element.88), channel_id=1, source_target_pairs={{0,1},{1,2},{2,3},{4,5},{5,6},{6,7},{8,9},{9,10},{10,11},{12,13},{... | collective-permute-start | bytes 2359304 | tf_op jit(solution)/shard_map/ppermute | solution.py:111
  662.1 23.5 %collective-permute-start.46 = (bf16[192,2048]{1,0:T(8,128)(2,1)}, bf16[192,2048]{1,0:T(8,128)(2,1)}, u32[]{:S(2)}, u32[]{:S(2)}) collective-permute-start(bf16[192,2048]{1,0:T(8,128)(2,1)} %get-tuple-element.89), channel_id=1, source_target_pairs={{1,0},{2,1},{3,2},{5,4},{6,5},{7,6},{9,8},{10,9},{11,10},{13,12},{... | collective-permute-start | bytes 2359304 | tf_op jit(solution)/shard_map/ppermute | solution.py:111
  701.2 18.8 %collective-permute-start.56 = (bf16[2,192,1024]{2,1,0:T(8,128)(2,1)S(1)}, bf16[2,192,1024]{2,1,0:T(8,128)(2,1)S(1)}, u32[]{:S(2)}, u32[]{:S(2)}) collective-permute-start(bf16[2,192,1024]{2,1,0:T(8,128)(2,1)S(1)} %get-tuple-element.235), channel_id=1, source_target_pairs={{0,8},{4,12},{8,0},{12,4},{16,24},{20,28},{24,16},{28,20},{1,9},{5... | collective-permute-start | bytes 2359304 | tf_op jit(solution)/shard_map/ppermute | solution.py:52
  705.4 20.0 %collective-permute-start.48 = (bf16[192,2048]{1,0:T(8,128)(2,1)S(1)}, bf16[192,2048]{1,0:T(8,128)(2,1)S(1)}, u32[]{:S(2)}, u32[]{:S(2)}) collective-permute-start(bf16[192,2048]{1,0:T(8,128)(2,1)S(1)} %get-tuple-element.204), channel_id=1, source_target_pairs={{1,0},{2,1},{3,2},{5,4},{6,5},{7,6},{9,8},{10,9},{11,10},{13,12},{... | collective-permute-start | bytes 2359304 | tf_op jit(solution)/shard_map/ppermute | solution.py:111
  706.8 18.6 %collective-permute-start.54 = (bf16[2,192,1024]{2,1,0:T(8,128)(2,1)S(1)}, bf16[2,192,1024]{2,1,0:T(8,128)(2,1)S(1)}, u32[]{:S(2)}, u32[]{:S(2)}) collective-permute-start(bf16[2,192,1024]{2,1,0:T(8,128)(2,1)S(1)} %get-tuple-element.241), channel_id=1, source_target_pairs={{0,16},{4,20},{8,24},{12,28},{16,0},{20,4},{24,8},{28,12},{1,17},{... | collective-permute-start | bytes 2359304 | tf_op jit(solution)/shard_map/ppermute | solution.py:52
  734.3 31.3 %collective-permute-start.49 = (bf16[192,2048]{1,0:T(8,128)(2,1)}, bf16[192,2048]{1,0:T(8,128)(2,1)}, u32[]{:S(2)}, u32[]{:S(2)}) collective-permute-start(bf16[192,2048]{1,0:T(8,128)(2,1)} %get-tuple-element.91), channel_id=1, source_target_pairs={{0,1},{1,2},{2,3},{4,5},{5,6},{6,7},{8,9},{9,10},{10,11},{12,13},{... | collective-permute-start | bytes 2359304 | tf_op jit(solution)/shard_map/ppermute | solution.py:111
  737.6 28.0 %collective-permute-start.50 = (bf16[192,2048]{1,0:T(8,128)(2,1)}, bf16[192,2048]{1,0:T(8,128)(2,1)}, u32[]{:S(2)}, u32[]{:S(2)}) collective-permute-start(bf16[192,2048]{1,0:T(8,128)(2,1)} %get-tuple-element.92), channel_id=1, source_target_pairs={{1,0},{2,1},{3,2},{5,4},{6,5},{7,6},{9,8},{10,9},{11,10},{13,12},{... | collective-permute-start | bytes 2359304 | tf_op jit(solution)/shard_map/ppermute | solution.py:111
  775.8 21.2 %collective-permute-start.51 = (bf16[192,2048]{1,0:T(8,128)(2,1)}, bf16[192,2048]{1,0:T(8,128)(2,1)}, u32[]{:S(2)}, u32[]{:S(2)}) collective-permute-start(bf16[192,2048]{1,0:T(8,128)(2,1)} %get-tuple-element.93), channel_id=1, source_target_pairs={{0,1},{1,2},{2,3},{4,5},{5,6},{6,7},{8,9},{9,10},{10,11},{12,13},{... | collective-permute-start | bytes 2359304 | tf_op jit(solution)/shard_map/ppermute | solution.py:111
  781.5 20.5 %collective-permute-start.52 = (bf16[192,2048]{1,0:T(8,128)(2,1)}, bf16[192,2048]{1,0:T(8,128)(2,1)}, u32[]{:S(2)}, u32[]{:S(2)}) collective-permute-start(bf16[192,2048]{1,0:T(8,128)(2,1)} %get-tuple-element.94), channel_id=1, source_target_pairs={{1,0},{2,1},{3,2},{5,4},{6,5},{7,6},{9,8},{10,9},{11,10},{13,12},{... | collective-permute-start | bytes 2359304 | tf_op jit(solution)/shard_map/ppermute | solution.py:111
  796.4 21.1 %collective-permute-start.62 = (bf16[768,2048]{1,0:T(8,128)(2,1)}, bf16[768,2048]{1,0:T(8,128)(2,1)}, u32[]{:S(2)}, u32[]{:S(2)}) collective-permute-start(bf16[768,2048]{1,0:T(8,128)(2,1)} %get-tuple-element.103), channel_id=1, source_target_pairs={{0,4},{4,0},{8,12},{12,8},{16,20},{20,16},{24,28},{28,24},{1,5},{5... | collective-permute-start | bytes 9437192 | tf_op jit(solution)/shard_map/ppermute | solution.py:52
  822.7 24.1 %collective-permute-start.67 = (bf16[256,2048]{1,0:T(8,128)(2,1)S(1)}, bf16[256,2048]{1,0:T(8,128)(2,1)S(1)}, u32[]{:S(2)}, u32[]{:S(2)}) collective-permute-start(bf16[256,2048]{1,0:T(8,128)(2,1)S(1)} %get-tuple-element.108), channel_id=1, source_target_pairs={{0,1},{1,2},{2,3},{4,5},{5,6},{6,7},{8,9},{9,10},{10,11},{12,13},{... | collective-permute-start | bytes 3145736 | tf_op jit(solution)/shard_map/ppermute | solution.py:111
  824.4 26.5 %collective-permute-start.68 = (bf16[256,2048]{1,0:T(8,128)(2,1)S(1)}, bf16[256,2048]{1,0:T(8,128)(2,1)S(1)}, u32[]{:S(2)}, u32[]{:S(2)}) collective-permute-start(bf16[256,2048]{1,0:T(8,128)(2,1)S(1)} %get-tuple-element.109), channel_id=1, source_target_pairs={{1,0},{2,1},{3,2},{5,4},{6,5},{7,6},{9,8},{10,9},{11,10},{13,12},{... | collective-permute-start | bytes 3145736 | tf_op jit(solution)/shard_map/ppermute | solution.py:111
  828.3 24.5 %collective-permute-start.63 = (bf16[2,192,1024]{2,1,0:T(8,128)(2,1)S(1)}, bf16[2,192,1024]{2,1,0:T(8,128)(2,1)S(1)}, u32[]{:S(2)}, u32[]{:S(2)}) collective-permute-start(bf16[2,192,1024]{2,1,0:T(8,128)(2,1)S(1)} %slice_bitcast_fusion.4), channel_id=1, source_target_pairs={{0,8},{4,12},{8,0},{12,4},{16,24},{20,28},{24,16},{28,20},{1,9},{5... | collective-permute-start | bytes 2359304 | tf_op jit(solution)/shard_map/ppermute | solution.py:52
  829.3 29.9 %collective-permute-start.65 = (bf16[2,192,1024]{2,1,0:T(8,128)(2,1)S(1)}, bf16[2,192,1024]{2,1,0:T(8,128)(2,1)S(1)}, u32[]{:S(2)}, u32[]{:S(2)}) collective-permute-start(bf16[2,192,1024]{2,1,0:T(8,128)(2,1)S(1)} %bitcast.305), channel_id=1, source_target_pairs={{0,16},{4,20},{8,24},{12,28},{16,0},{20,4},{24,8},{28,12},{1,17},{... | collective-permute-start | bytes 2359304 | tf_op jit(solution)/shard_map/ppermute | solution.py:52
  851.5 25.7 %collective-permute-start.70 = (bf16[256,2048]{1,0:T(8,128)(2,1)S(1)}, bf16[256,2048]{1,0:T(8,128)(2,1)S(1)}, u32[]{:S(2)}, u32[]{:S(2)}) collective-permute-start(bf16[256,2048]{1,0:T(8,128)(2,1)S(1)} %get-tuple-element.111), channel_id=1, source_target_pairs={{1,0},{2,1},{3,2},{5,4},{6,5},{7,6},{9,8},{10,9},{11,10},{13,12},{... | collective-permute-start | bytes 3145736 | tf_op jit(solution)/shard_map/ppermute | solution.py:111
  854.7 25.3 %collective-permute-start.69 = (bf16[256,2048]{1,0:T(8,128)(2,1)S(1)}, bf16[256,2048]{1,0:T(8,128)(2,1)S(1)}, u32[]{:S(2)}, u32[]{:S(2)}) collective-permute-start(bf16[256,2048]{1,0:T(8,128)(2,1)S(1)} %get-tuple-element.110), channel_id=1, source_target_pairs={{0,1},{1,2},{2,3},{4,5},{5,6},{6,7},{8,9},{9,10},{10,11},{12,13},{... | collective-permute-start | bytes 3145736 | tf_op jit(solution)/shard_map/ppermute | solution.py:111
  859.6 28.6 %collective-permute-start.66 = (bf16[192,1024]{1,0:T(8,128)(2,1)S(1)}, bf16[192,1024]{1,0:T(8,128)(2,1)S(1)}, u32[]{:S(2)}, u32[]{:S(2)}) collective-permute-start(bf16[192,1024]{1,0:T(8,128)(2,1)S(1)} %slice_bitcast_fusion.12), channel_id=1, source_target_pairs={{0,8},{4,12},{8,0},{12,4},{16,24},{20,28},{24,16},{28,20},{1,9},{5... | collective-permute-start | bytes 1179656 | tf_op jit(solution)/shard_map/ppermute | solution.py:52
  881.3 25.9 %collective-permute-start.71 = (bf16[256,2048]{1,0:T(8,128)(2,1)}, bf16[256,2048]{1,0:T(8,128)(2,1)}, u32[]{:S(2)}, u32[]{:S(2)}) collective-permute-start(bf16[256,2048]{1,0:T(8,128)(2,1)} %add_convert_fusion.6), channel_id=1, source_target_pairs={{0,1},{1,2},{2,3},{4,5},{5,6},{6,7},{8,9},{9,10},{10,11},{12,13},{... | collective-permute-start | bytes 3145736 | tf_op jit(solution)/shard_map/ppermute | solution.py:111
  886.7 25.9 %collective-permute-start.72 = (bf16[256,2048]{1,0:T(8,128)(2,1)}, bf16[256,2048]{1,0:T(8,128)(2,1)}, u32[]{:S(2)}, u32[]{:S(2)}) collective-permute-start(bf16[256,2048]{1,0:T(8,128)(2,1)} %add_convert_fusion.5), channel_id=1, source_target_pairs={{1,0},{2,1},{3,2},{5,4},{6,5},{7,6},{9,8},{10,9},{11,10},{13,12},{... | collective-permute-start | bytes 3145736 | tf_op jit(solution)/shard_map/ppermute | solution.py:111
  893.6 33.7 %all-to-all-start.4 = ((f32[32,1,1280]{2,1,0:T(1,128)}), f32[32,1,1280]{2,1,0:T(1,128)S(1)}, u32[]{:S(2)}, u32[]{:S(2)}) async-start(f32[32,1,1280]{2,1,0:T(1,128)} %all_to_all.28), calls=%async_computation.6 | async-start | bytes 327680 | tf_op jit(solution)/shard_map/all_to_all | solution.py:725
  900.3 42.1 %collective-permute-start.77 = (bf16[2,256,2048]{2,1,0:T(8,128)(2,1)}, bf16[2,256,2048]{2,1,0:T(8,128)(2,1)}, u32[]{:S(2)}, u32[]{:S(2)}) collective-permute-start(bf16[2,256,2048]{2,1,0:T(8,128)(2,1)} %fusion.28), channel_id=1, source_target_pairs={{0,4},{4,0},{1,5},{5,1},{2,6},{6,2},{3,7},{7,3},{8,12},{12,8},{9,1... | collective-permute-start | bytes 6291464 | tf_op jit(solution)/shard_map/ppermute | solution.py:151
  915.6 24.3 %collective-permute-start.74 = (bf16[64,2048]{1,0:T(8,128)(2,1)}, bf16[64,2048]{1,0:T(8,128)(2,1)}, u32[]{:S(2)}, u32[]{:S(2)}) collective-permute-start(bf16[64,2048]{1,0:T(8,128)(2,1)} %get-tuple-element.228), channel_id=1, source_target_pairs={{0,0},{1,1},{6,2},{11,3},{12,4},{13,5},{18,6},{23,7},{24,8},{25,9}... | collective-permute-start | bytes 786440 | tf_op jit(solution)/shard_map/ppermute | solution.py:707
  919.3 20.6 %collective-permute-start.75 = (bf16[64,2048]{1,0:T(8,128)(2,1)}, bf16[64,2048]{1,0:T(8,128)(2,1)}, u32[]{:S(2)}, u32[]{:S(2)}) collective-permute-start(bf16[64,2048]{1,0:T(8,128)(2,1)} %get-tuple-element.227), channel_id=1, source_target_pairs={{0,0},{5,1},{6,2},{11,3},{12,4},{17,5},{18,6},{23,7},{24,8},{29,9}... | collective-permute-start | bytes 786440 | tf_op jit(solution)/shard_map/ppermute | solution.py:707
  (110 other events, 1894.8 us)
Sparse Core Ops, SparseCore 0:
  53.2 80.5 all-gather.6
  135.7 98.0 all-gather.4
  297.1 89.4 all-gather.8
  403.1 53.7 all-gather.10
  462.3 53.8 reduce-scatter.4
  519.1 52.5 reduce-scatter.6
  588.0 87.4 reduce-scatter.8
  731.4 83.3 reduce-scatter.10

commit v5 on v4

--- a/solution.py
+++ b/solution.py
@@ -417,8 +417,11 @@
     moved = [
         lax.ppermute(w_qkv[t * sub : (t + 1) * sub], ALL, unit_perm(t, False)) for t in range(3)
     ]
-    slots, slot_steps = gather_z(jnp.concatenate(moved, axis=0), zs, zi)
     tok_pieces = gather_dp(tokens, dps)
+    slots, slot_steps = gather_z(
+        jnp.concatenate(moved, axis=0), zs, zi,
+        {s: [] if s < zs - 1 else tok_pieces[:2] for s in range(2, zs)},
+    )
     inv3 = pow(3, -1, dps)
     slot_of = [[0, 0, 0] for _ in range(dps)]
     type_of = [[0, 0, 0] for _ in range(dps)]
@@ -472,12 +475,15 @@
         [lax.dynamic_index_in_dim(qkv_slots, slot_of[k], 0, keepdims=False) for k in range(3)],
         axis=0,
     )
-    out_cols = after(w_out, *slot_steps[2]).reshape(orow, dps, width).transpose(1, 0, 2)
+    out_cols = after(w_out, *slot_steps[-1]).reshape(orow, dps, width).transpose(1, 0, 2)
     out_cols = jnp.broadcast_to(out_cols[:, None], (dps, zs, orow, width))
     w_out_c = lax.all_to_all(
         out_cols.reshape(world, orow, width), ALL, 0, 0, tiled=True
     ).reshape(D, width)
-    dy_blocks, dy_steps = gather_z(after(cotangent, *slot_steps[-1]), zs, zi)
+    dy_all = lax.all_gather(after(cotangent, *slot_steps[2]), "z", axis=0)
+    dy_blocks = [
+        lax.dynamic_index_in_dim(dy_all, (zi - k) % zs, 0, keepdims=False) for k in range(zs)
+    ]
 
     def in_core_order(own, got):
         first = ci == 0
@@ -490,8 +496,8 @@
         both = in_core_order(own, got)
         return [jnp.concatenate([half[e] for half in both], axis=0) for e in range(mine)]
 
-    gu_half = core_half(after(w_gate_up, *slot_steps[1]))
-    down_half = core_half(after(w_down, *slot_steps[1]))
+    gu_half = core_half(after(w_gate_up, *slot_steps[-1]))
+    down_half = core_half(after(w_down, *moved))
     blocks = all_rows // BLOCK
     half = blocks // 2
     own_spec, other_spec = pieces_spec(half, D // 2)
@@ -545,15 +551,11 @@
     router_probs = jax.nn.softmax(mm(hidden_two, router_low, 1, 0), axis=-1)
 
     dy_g = both_cores(dy_blocks)
-    hidden_blocks, _ = gather_z(after(hidden_two, *dy_steps[-1]), zs, zi, {2: [dy_g, router_probs]})
+    hidden_blocks, _ = gather_z(hidden_two, zs, zi, {2: [dy_g, router_probs]})
     hidden_g = both_cores(hidden_blocks)
     router_g = jax.nn.softmax(mm(hidden_g, router_low, 1, 0), axis=-1)
     dy_f = dy_g.astype(f32)
     first_expert = zi * local_experts + ci * mine
-
-    early = [w for pair in expert_w for w in pair]
-    early = list(lax.optimization_barrier(tuple(early[:-1]))) + early[-1:]
-    expert_w = [tuple(early[2 * e : 2 * e + 2]) for e in range(mine)]
 
     passes = []
     for e in range(mine):
@@ -564,7 +566,7 @@
             jnp.where(jnp.arange(E)[None] == expert, router_g, 0.0), axis=1, keepdims=True
         )
         gate_val = jnp.where(picked, prob, 0.0)
-        hidden_e = after(hidden_g, passes[-1]["act"]) if passes else hidden_g
+        hidden_e = after(hidden_g, passes[-1]["rows"]) if passes else hidden_g
         gate_and_up = mm(hidden_e, gate_up, 1, 1)
         g_part = gate_and_up[:, :FF]
         u_part = gate_and_up[:, FF:]
@@ -579,15 +581,15 @@
         grad_u = grad_act * silu
         grad_g, grad_u = grad_g.astype(bf16), grad_u.astype(bf16)
         grad_both = jnp.concatenate([grad_g, grad_u], axis=-1)
-        rows_back = mm(grad_both, gate_up, 1, 0).astype(bf16).astype(f32)
+        rows_back = mm(grad_both, gate_up, 1, 0).astype(bf16)
         dn = mm(grad_eo, act, 0, 0).astype(bf16)
         passes.append(
             dict(
                 out=gate_val * expert_out,
-                back=rows_back,
+                back=rows_back.astype(f32),
+                rows=rows_back,
                 gate=grad_gate,
                 both=(grad_g, grad_u),
-                act=act,
                 dn=lax.psum_scatter(dn, "q", scatter_dimension=0, tiled=True),
             )
         )

time: 966 us -> 960 us (level)
  waiting for transfers between devices: 254 us -> 276 us
  starting transfers between devices: 183 us -> 164 us
  other arithmetic: 110 us -> 96.3 us
  local copies, waits for them, and re-layouts: 73 us -> 84.5 us
    ppermute x28, waiting for transfers between devices: 56.5 us -> 95.3 us  [flip(): return lax.ppermute(value, DP, [(i, i ^ 1 << bit) for i in range(size)])]
    ppermute x36 -> x30, starting transfers between devices: 122 us -> 97.1 us  [line(): lax.ppermute(value, 'z', [(j, j + step) for j in range(zs) if 0 <= j + st...]
    ppermute x36 -> x30, waiting for transfers between devices: 183 us -> 166 us  [line(): lax.ppermute(value, 'z', [(j, j + step) for j in range(zs) if 0 <= j + st...]
    unnamed x182 -> x206, local copies, waits for them, and re-layouts: 19.3 us -> 24 us
  transfers between devices with their start and end apart: 90 -> 85, of which waited for: 40 -> 40; matrix products, arithmetic and copies ran while one was open for 35% -> 35% of each run, Pallas kernels for 12% -> 12%
where the time goes in v5:
time: 960 us; the launch traced here: 950 us
  waiting for transfers between devices  276 us (29%)
  matrix products  175 us (18%)
  starting transfers between devices  164 us (17%)
  Pallas kernels  112 us (12%)
  other arithmetic  96.3 us (10%)
  local copies, waits for them, and re-layouts  84.5 us (9%)
  between operations  22.3 us (2%)
  blocking collectives  20.3 us (2%)
    dot_general x13, matrix products, mm(): lax.dot_general(a, b, (((ca,), (cb,)), ((), ())), preferred_element_type=...  171 us
    ppermute x30, waiting for transfers between devices, line(): lax.ppermute(value, 'z', [(j, j + step) for j in range(zs) if 0 <= j + st...  166 us
    ppermute x30, starting transfers between devices, line(): lax.ppermute(value, 'z', [(j, j + step) for j in range(zs) if 0 <= j + st...  97.1 us
    ppermute x28, waiting for transfers between devices, flip(): return lax.ppermute(value, DP, [(i, i ^ 1 << bit) for i in range(size)])  95.3 us
    pallas_call x4, Pallas kernels, run_blocks(): pl.pallas_call(body, grid=(rows // BLOCK,), in_specs=in_specs, out_specs=...  71 us
    pallas_call x2, Pallas kernels, weight_grad(): pl.pallas_call(functools.partial(weight_grad_kernel, half), grid=(b.shape...  41.2 us
    ppermute x28, starting transfers between devices, flip(): return lax.ppermute(value, DP, [(i, i ^ 1 << bit) for i in range(size)])  28.5 us
    unnamed x206, local copies, waits for them, and re-layouts  24 us
  transfers between devices with their start and end apart: 85, of which 40 were waited for; matrix products, arithmetic and copies ran while one was open for 35% of the time, Pallas kernels for 12%

profile of v5, /device:TPU:0, one launch (start us, length us, event | category | flops | bytes accessed | tf_op | source)
XLA Modules:
  0.0 950.0 jit_solution(11822859096880751850)
XLA Ops:
  11.9 16.3 %collective-permute-start.9 = (bf16[192,2048]{1,0:T(8,128)(2,1)S(1)}, bf16[192,2048]{1,0:T(8,128)(2,1)S(1)}, u32[]{:S(2)}, u32[]{:S(2)}) collective-permute-start(bf16[192,2048]{1,0:T(8,128)(2,1)S(1)} %constant_dynamic-update-slice_fusion), channel_id=1, source_target_pairs={{0,1},{1,2},{2,3},{4,5},{5,6},{6,7},{8,9},{9,10},{10,11},{12,13},{... | collective-permute-start | bytes 2359304 | tf_op jit(solution)/shard_map/ppermute | solution.py:111
  33.3 6.2 collective-permute-done.2
  45.4 5.3 collective-permute-start.11
  54.5 3.7 collective-permute-done.3
  58.3 7.7 collective-permute-done.11
  66.1 5.1 collective-permute-done.12
  76.8 4.9 collective-permute-start.14
  81.7 45.5 %collective-permute-done.13 = bf16[192,2048]{1,0:T(8,128)(2,1)S(1)} collective-permute-done((bf16[192,2048]{1,0:T(8,128)(2,1)}, bf16[192,2048]{1,0:T(8,128)(2,1)S(1)}, u32[]{:S(2)}, u32[]{:S(2)}) %collective-permute-start.13) | collective-permute-done | bytes 786464 | tf_op jit(solution)/shard_map/ppermute | solution.py:111
  131.5 4.4 collective-permute-done.31
  155.1 14.0 %all-to-all-start = ((bf16[32,2,1504]{2,1,0:T(2,128)(2,1)}), bf16[32,2,1504]{2,1,0:T(2,128)(2,1)S(1)}, u32[]{:S(2)}, u32[]{:S(2)}) async-start(bf16[32,2,1504]{2,1,0:T(2,128)(2,1)} %reshape.529), calls=%async_computation | async-start | bytes 393216 | tf_op jit(solution)/shard_map/all_to_all | solution.py:446
  196.4 12.9 %shard_map.188 = (bf16[1536,2048]{1,0:T(8,128)(2,1)}, f32[1536,768]{1,0:T(8,128)}, f32[8,1536]{1,0:T(8,128)}) custom-call(bf16[768,1024]{1,0:T(8,128)(2,1)} %bitcast.4.a_own, bf16[768,1024]{1,0:T(8,128)(2,1)} %bitcast.9.b_own, bf16[768,1024]{1,0:T(8,128)(2,1)} %collective-permute-done.4.a_other, bf16[768,1024]{1,0:T(8,128)(2,1)} %collective-permute-done.5.b_other, ...), custom_call_target="tpu_custom_call" | custom-call | flops 1 | bytes 1 | tf_op jit(solution)/shard_map/pallas_call | solution.py:349
  228.0 18.8 %shard_map.189 = (bf16[1536,256]{1,0:T(8,128)(2,1)}, bf16[768,2048]{1,0:T(8,128)(2,1)}, bf16[768,2048]{1,0:T(8,128)(2,1)}) custom-call(f32[1536,768]{1,0:T(8,128)} %get-tuple-element.69.raw_ref, f32[8,1536]{1,0:T(8,128)} %pad.11.sum_ref, f32[8,256]{1,0:T(8,128)} %pad.12.gain_ref, f32[384,128]{1,0:T(8,128)} %bitcast.310, f32[384,128]{1,0:T(8,128)} %bitcast.312, ...), custom_call_target="tpu_custom_call" | custom-call | flops 1 | bytes 1 | tf_op jit(solution)/shard_map/pallas_call | solution.py:349
  247.9 4.9 collective-permute-done.18
  252.7 4.2 add_convert_fusion.4
  260.5 27.2 %collective-permute-done.19 = bf16[2,192,1024]{2,1,0:T(8,128)(2,1)S(1)} collective-permute-done((bf16[2,192,1024]{2,1,0:T(8,128)(2,1)S(1)}, bf16[2,192,1024]{2,1,0:T(8,128)(2,1)S(1)}, u32[]{:S(2)}, u32[]{:S(2)}) %collective-permute-start.19) | collective-permute-done | bytes 786464 | tf_op jit(solution)/shard_map/ppermute | solution.py:52
  296.2 13.9 %collective-permute-done.20 = bf16[192,1024]{1,0:T(8,128)(2,1)} collective-permute-done((bf16[192,1024]{1,0:T(8,128)(2,1)}, bf16[192,1024]{1,0:T(8,128)(2,1)}, u32[]{:S(2)}, u32[]{:S(2)}) %collective-permute-start.20) | collective-permute-done | bytes 393248 | tf_op jit(solution)/shard_map/ppermute | solution.py:52
  335.4 11.4 %collective-permute-done.23 = bf16[192,2048]{1,0:T(8,128)(2,1)S(1)} collective-permute-done((bf16[192,2048]{1,0:T(8,128)(2,1)S(1)}, bf16[192,2048]{1,0:T(8,128)(2,1)S(1)}, u32[]{:S(2)}, u32[]{:S(2)}) %collective-permute-start.23) | collective-permute-done | bytes 786464 | tf_op jit(solution)/shard_map/ppermute | solution.py:111
  346.8 4.2 collective-permute-done.24
  352.2 4.6 collective-permute-start.28
  356.8 14.9 %collective-permute-done.26 = bf16[192,2048]{1,0:T(8,128)(2,1)S(1)} collective-permute-done((bf16[192,2048]{1,0:T(8,128)(2,1)S(1)}, bf16[192,2048]{1,0:T(8,128)(2,1)S(1)}, u32[]{:S(2)}, u32[]{:S(2)}) %collective-permute-start.26) | collective-permute-done | bytes 786464 | tf_op jit(solution)/shard_map/ppermute | solution.py:111
  373.1 4.6 collective-permute-start.29
  377.7 14.1 %collective-permute-done.27 = bf16[192,2048]{1,0:T(8,128)(2,1)S(1)} collective-permute-done((bf16[192,2048]{1,0:T(8,128)(2,1)S(1)}, bf16[192,2048]{1,0:T(8,128)(2,1)S(1)}, u32[]{:S(2)}, u32[]{:S(2)}) %collective-permute-start.27) | collective-permute-done | bytes 786464 | tf_op jit(solution)/shard_map/ppermute | solution.py:111
  402.9 3.9 constant_dynamic-update-slice_fusion.8.b_ref
  406.9 4.5 fusion.93
  412.2 19.1 %fusion.94 = f32[1536,2048]{1,0:T(8,128)} fusion(bf16[1536,2048]{1,0:T(8,128)(2,1)} %constant_dynamic-update-slice_fusion.8.b_ref, bf16[2048,2048]{1,0:T(8,128)(2,1)} %all-gather.7.cloned.1.call-done), kind=kOutput, calls=%fused_computation.296 | convolution fusion | flops 12884901888 | bytes 27262976 | tf_op jit(solution)/shard_map/dot_general | solution.py:44
  431.3 15.4 %multiply_convert_fusion.4 = (bf16[1536,1024]{1,0:T(8,128)(2,1)S(1)}, bf16[1536,1024]{1,0:T(8,128)(2,1)S(1)}, bf16[1536,1024]{1,0:T(8,128)(2,1)S(1)}) fusion(f32[1536,2048]{1,0:T(8,128)} %fusion.94, bf16[2048,1024]{1,0:T(8,128)(2,1)} %all-gather.9.cloned.1.call-done, bf16[1536,2048]{1,0:T(8,128)(2,1)} %copy-done.69, f32[1536]{0:T(1024)S(1)} %broadcast_select_fusion.9), kind=kOutput, calls=%fused_computation.40 | convolution fusion | flops 6475481088 | bytes 32512000 | tf_op jit(solution)/shard_map/dot_general | solution.py:44
  446.7 21.4 %convolution_convert_fusion.2 = bf16[1536,2048]{1,0:T(8,128)(2,1)} fusion(bf16[2048,2048]{1,0:T(8,128)(2,1)} %all-gather.7.cloned.1.call-done, bf16[1536,1024]{1,0:T(8,128)(2,1)S(1)} %get-tuple-element.83.u_ref, bf16[1536,1024]{1,0:T(8,128)(2,1)S(1)} %get-tuple-element.82.g_ref), kind=kOutput, calls=%fused_computation.19 | convolution fusion | flops 12900630528 | bytes 20971520 | tf_op jit(solution)/shard_map/dot_general | solution.py:44
  468.2 8.9 convolution_convert_fusion.5
  477.2 19.3 %fusion.95 = f32[1536,2048]{1,0:T(8,128)} fusion(bf16[1536,2048]{1,0:T(8,128)(2,1)} %constant_dynamic-update-slice_fusion.8.b_ref, bf16[2048,2048]{1,0:T(8,128)(2,1)} %all-gather.11.cloned.1.call-done), kind=kOutput, calls=%fused_computation.297 | convolution fusion | flops 12884901888 | bytes 27262976 | tf_op jit(solution)/shard_map/dot_general | solution.py:44
  496.5 18.6 %multiply_convert_fusion.1 = (bf16[1536,1024]{1,0:T(8,128)(2,1)S(1)}, bf16[1536,1024]{1,0:T(8,128)(2,1)}, bf16[1536,1024]{1,0:T(8,128)(2,1)S(1)}) fusion(f32[1536,2048]{1,0:T(8,128)} %fusion.95, bf16[2048,1024]{1,0:T(8,128)(2,1)} %all-gather.13.cloned.1.call-done, bf16[1536,2048]{1,0:T(8,128)(2,1)} %copy-done.69, f32[1536]{0:T(1024)S(1)} %copy-done.81), kind=kOutput, calls=%fused_computation.34 | convolution fusion | flops 6475481088 | bytes 32512000 | tf_op jit(solution)/shard_map/dot_general | solution.py:44
  516.7 12.4 %convolution_convert_fusion.4 = bf16[2048,1024]{1,0:T(8,128)(2,1)} fusion(bf16[1536,1024]{1,0:T(8,128)(2,1)S(1)} %get-tuple-element.187, bf16[1536,2048]{1,0:T(8,128)(2,1)} %copy-done.69, f32[1536]{0:T(1024)S(1)} %copy-done.81), kind=kOutput, calls=%fused_computation.54 | convolution fusion | flops 6453985280 | bytes 13637632 | tf_op jit(solution)/shard_map/dot_general | solution.py:44
  529.2 17.8 %add_convert_fusion = bf16[1536,2048]{1,0:T(8,128)(2,1)S(1)} fusion(bf16[1536,2048]{1,0:T(8,128)(2,1)} %convolution_convert_fusion.2, bf16[2048,2048]{1,0:T(8,128)(2,1)} %all-gather.11.cloned.1.call-done, bf16[1536,1024]{1,0:T(8,128)(2,1)} %get-tuple-element.87.u_ref, bf16[1536,1024]{1,0:T(8,128)(2,1)S(1)} %get-tuple-element.86.g_ref), kind=kOutput, calls=%fused_computation.16 | convolution fusion | flops 12913213440 | bytes 27262976 | tf_op jit(solution)/shard_map/dot_general | solution.py:44
  547.6 5.4 collective-permute-done.34
  555.9 5.2 collective-permute-start.35
  562.4 20.6 %shard_map.190 = bf16[2048,2048]{1,0:T(8,128)(2,1)} custom-call(bf16[1536,1024]{1,0:T(8,128)(2,1)} %copy-done.35, bf16[1536,1024]{1,0:T(8,128)(2,1)} %copy-done.36, bf16[1536,2048]{1,0:T(8,128)(2,1)} %constant_dynamic-update-slice_fusion.8.b_ref), custom_call_target="tpu_custom_call" | custom-call | flops 1 | bytes 1 | tf_op jit(solution)/shard_map/pallas_call | solution.py:372
  583.1 12.0 %convolution_convert_fusion.3 = bf16[1536,2048]{1,0:T(8,128)(2,1)} fusion(bf16[1536,1024]{1,0:T(8,128)(2,1)} %copy-done.88, bf16[2048,1024]{1,0:T(8,128)(2,1)} %all-gather.9.cloned.1.call-done), kind=kOutput, calls=%fused_computation.20 | convolution fusion | flops 6445596672 | bytes 13631488 | tf_op jit(solution)/shard_map/dot_general | solution.py:44
  595.1 13.7 %fusion.4 = (f32[1536]{0:T(1024)S(1)}, f32[1536]{0:T(1024)S(1)}, bf16[1536,2048]{1,0:T(8,128)(2,1)S(1)}) fusion(bf16[1536,2048]{1,0:T(8,128)(2,1)} %convolution_convert_fusion.3, bf16[1536,2048]{1,0:T(8,128)(2,1)} %copy-done.69, f32[1536]{0:T(1024)S(1)} %copy-done.81, f32[1536]{0:T(1024)S(1)} %broadcast_select_fusion.9, ...), kind=kOutput, calls=%fused_computation.14 | convolution fusion | flops 6480196608 | bytes 26238976 | tf_op jit(solution)/shard_map/dot_general | solution.py:44
  615.5 4.2 collective-permute-start.37
  621.1 6.4 add_convert_fusion.3
  627.5 20.6 %shard_map.191 = bf16[2048,2048]{1,0:T(8,128)(2,1)} custom-call(bf16[1536,1024]{1,0:T(8,128)(2,1)} %copy-done.34, bf16[1536,1024]{1,0:T(8,128)(2,1)} %get-tuple-element.87.u_ref, bf16[1536,2048]{1,0:T(8,128)(2,1)} %constant_dynamic-update-slice_fusion.8.b_ref), custom_call_target="tpu_custom_call" | custom-call | flops 1 | bytes 1 | tf_op jit(solution)/shard_map/pallas_call | solution.py:372
  648.2 4.0 add_convert_fusion.10
  652.2 5.4 collective-permute-start.39
  660.1 20.3 %all_to_all.34 = f32[8,2,192]{2,1,0:T(2,128)S(1)} all-to-all(f32[8,2,192]{2,1,0:T(2,128)S(1)} %bitcast.339), channel_id=1, replica_groups=mesh['q'=4,'c'=2,'z'=4] {'c','z'}, dimensions={0} | all-to-all | bytes 24576 | tf_op jit(solution)/shard_map/all_to_all | solution.py:618
  687.5 8.4 collective-permute-done.49
  703.0 11.8 %collective-permute-done.50 = bf16[2,192,1024]{2,1,0:T(8,128)(2,1)S(1)} collective-permute-done((bf16[2,192,1024]{2,1,0:T(8,128)(2,1)S(1)}, bf16[2,192,1024]{2,1,0:T(8,128)(2,1)S(1)}, u32[]{:S(2)}, u32[]{:S(2)}) %collective-permute-start.50) | collective-permute-done | bytes 786464 | tf_op jit(solution)/shard_map/ppermute | solution.py:52
  716.0 4.2 collective-permute-done.42
  733.7 26.5 %shard_map.192 = (f32[1536,512]{1,0:T(8,128)}, bf16[1536,256]{1,0:T(8,128)(2,1)}, f32[8,1536]{1,0:T(8,128)}, f32[8,256]{1,0:T(8,128)}, f32[2048,256]{1,0:T(8,128)}) custom-call(f32[1536,768]{1,0:T(8,128)} %get-tuple-element.69.raw_ref, f32[8,1536]{1,0:T(8,128)} %pad.11.sum_ref, f32[8,256]{1,0:T(8,128)} %pad.12.gain_ref, f32[384,128]{1,0:T(8,128)} %bitcast.311, ...), custom_call_target="tpu_custom_call" | custom-call | flops 1 | bytes 1 | tf_op jit(solution)/shard_map/pallas_call | solution.py:349
  763.0 3.7 collective-permute-done.54
  771.3 5.7 collective-permute-start.45
  779.1 12.7 %shard_map.193 = (bf16[1536,768]{1,0:T(8,128)(2,1)}, bf16[768,2048]{1,0:T(8,128)(2,1)}, bf16[768,2048]{1,0:T(8,128)(2,1)}) custom-call(f32[1536,768]{1,0:T(8,128)} %get-tuple-element.69.raw_ref, f32[8,1536]{1,0:T(8,128)} %pad.11.sum_ref, f32[1536,512]{1,0:T(8,128)} %get-tuple-element.98.back_ref, bf16[1536,256]{1,0:T(8,128)(2,1)} %get-tuple-element.99.dv_ref, ...), custom_call_target="tpu_custom_call" | custom-call | flops 1 | bytes 1 | tf_op jit(solution)/shard_map/pallas_call | solution.py:349
  792.5 5.0 collective-permute-done.46
  799.4 8.0 convolution_convert_fusion.6
  824.8 17.0 %collective-permute-done.61 = bf16[256,2048]{1,0:T(8,128)(2,1)S(1)} collective-permute-done((bf16[256,2048]{1,0:T(8,128)(2,1)S(1)}, bf16[256,2048]{1,0:T(8,128)(2,1)S(1)}, u32[]{:S(2)}, u32[]{:S(2)}) %collective-permute-start.61) | collective-permute-done | bytes 1048608 | tf_op jit(solution)/shard_map/ppermute | solution.py:111
  841.9 4.2 collective-permute-done.62
  849.1 4.6 collective-permute-start.63
  858.3 14.1 %collective-permute-done.64 = bf16[256,2048]{1,0:T(8,128)(2,1)S(1)} collective-permute-done((bf16[256,2048]{1,0:T(8,128)(2,1)S(1)}, bf16[256,2048]{1,0:T(8,128)(2,1)S(1)}, u32[]{:S(2)}, u32[]{:S(2)}) %collective-permute-start.64) | collective-permute-done | bytes 1048608 | tf_op jit(solution)/shard_map/ppermute | solution.py:111
  875.9 5.4 collective-permute-start.65
  888.2 3.9 all-to-all-start.4
  895.6 6.4 collective-permute-done.65
  902.0 5.6 collective-permute-done.66
  910.6 3.7 collective-permute-start.68
  917.9 3.6 collective-permute-start.70
  926.4 5.0 fusion.40
  939.1 3.9 maximum_convert_fusion
  (535 shorter events, 256.4 us)
Async XLA Ops:
  7.2 306.3 %all-gather.15.cloned.1.call-start = ((), (), s32[]{:S(2)}) async-start(), calls=%async_computation.17 | async-start | bytes 3932160 | tf_op jit(solution)/shard_map/all_gather | solution.py:483
  10.7 33.6 %collective-permute-start.10 = (bf16[192,2048]{1,0:T(8,128)(2,1)S(1)}, bf16[192,2048]{1,0:T(8,128)(2,1)S(1)}, u32[]{:S(2)}, u32[]{:S(2)}) collective-permute-start(bf16[192,2048]{1,0:T(8,128)(2,1)S(1)} %constant_dynamic-update-slice_fusion), channel_id=1, source_target_pairs={{1,0},{2,1},{3,2},{5,4},{6,5},{7,6},{9,8},{10,9},{11,10},{13,12},{... | collective-permute-start | bytes 2359304 | tf_op jit(solution)/shard_map/ppermute | solution.py:111
  11.9 33.4 %collective-permute-start.9 = (bf16[192,2048]{1,0:T(8,128)(2,1)S(1)}, bf16[192,2048]{1,0:T(8,128)(2,1)S(1)}, u32[]{:S(2)}, u32[]{:S(2)}) collective-permute-start(bf16[192,2048]{1,0:T(8,128)(2,1)S(1)} %constant_dynamic-update-slice_fusion), channel_id=1, source_target_pairs={{0,1},{1,2},{2,3},{4,5},{5,6},{6,7},{8,9},{9,10},{10,11},{12,13},{... | collective-permute-start | bytes 2359304 | tf_op jit(solution)/shard_map/ppermute | solution.py:111
  29.8 22.1 %collective-permute-start = (bf16[192,1024]{1,0:T(8,128)(2,1)S(1)}, bf16[192,1024]{1,0:T(8,128)(2,1)S(1)}, u32[]{:S(2)}, u32[]{:S(2)}) collective-permute-start(bf16[192,1024]{1,0:T(8,128)(2,1)S(1)} %get-tuple-element.254), channel_id=1, source_target_pairs={{0,8},{4,12},{8,0},{12,4},{16,24},{20,28},{24,16},{28,20},{1,9},{5... | collective-permute-start | bytes 1179656 | tf_op jit(solution)/shard_map/ppermute | solution.py:52
  39.6 18.6 %collective-permute-start.3 = (bf16[2,192,1024]{2,1,0:T(8,128)(2,1)S(1)}, bf16[2,192,1024]{2,1,0:T(8,128)(2,1)S(1)}, u32[]{:S(2)}, u32[]{:S(2)}) collective-permute-start(bf16[2,192,1024]{2,1,0:T(8,128)(2,1)S(1)} %get-tuple-element.250), channel_id=1, source_target_pairs={{0,8},{4,12},{8,0},{12,4},{16,24},{20,28},{24,16},{28,20},{1,9},{5... | collective-permute-start | bytes 2359304 | tf_op jit(solution)/shard_map/ppermute | solution.py:52
  45.4 20.7 %collective-permute-start.11 = (bf16[192,2048]{1,0:T(8,128)(2,1)S(1)}, bf16[192,2048]{1,0:T(8,128)(2,1)}, u32[]{:S(2)}, u32[]{:S(2)}) collective-permute-start(bf16[192,2048]{1,0:T(8,128)(2,1)S(1)} %collective-permute-done.9), channel_id=1, source_target_pairs={{0,1},{1,2},{2,3},{4,5},{5,6},{6,7},{8,9},{9,10},{10,11},{12,13},{... | collective-permute-start | bytes 2359304 | tf_op jit(solution)/shard_map/ppermute | solution.py:111
  50.7 20.5 %collective-permute-start.12 = (bf16[192,2048]{1,0:T(8,128)(2,1)S(1)}, bf16[192,2048]{1,0:T(8,128)(2,1)}, u32[]{:S(2)}, u32[]{:S(2)}) collective-permute-start(bf16[192,2048]{1,0:T(8,128)(2,1)S(1)} %collective-permute-done.10), channel_id=1, source_target_pairs={{1,0},{2,1},{3,2},{5,4},{6,5},{7,6},{9,8},{10,9},{11,10},{13,12},{... | collective-permute-start | bytes 2359304 | tf_op jit(solution)/shard_map/ppermute | solution.py:111
  52.9 18.9 %collective-permute-start.1 = (bf16[2,192,1024]{2,1,0:T(8,128)(2,1)}, bf16[2,192,1024]{2,1,0:T(8,128)(2,1)}, u32[]{:S(2)}, u32[]{:S(2)}) collective-permute-start(bf16[2,192,1024]{2,1,0:T(8,128)(2,1)} %get-tuple-element.256), channel_id=1, source_target_pairs={{0,16},{4,20},{8,24},{12,28},{16,0},{20,4},{24,8},{28,12},{1,17},{... | collective-permute-start | bytes 2359304 | tf_op jit(solution)/shard_map/ppermute | solution.py:52
  71.2 341.0 %all-gather.7.cloned.1.call-start = ((), (), s32[]{:S(2)}) async-start(), calls=%async_computation.9 | async-start | bytes 10485760 | tf_op jit(solution)/shard_map/all_gather | solution.py:539
  75.5 51.7 %collective-permute-start.13 = (bf16[192,2048]{1,0:T(8,128)(2,1)}, bf16[192,2048]{1,0:T(8,128)(2,1)S(1)}, u32[]{:S(2)}, u32[]{:S(2)}) collective-permute-start(bf16[192,2048]{1,0:T(8,128)(2,1)} %collective-permute-done.12), channel_id=1, source_target_pairs={{1,0},{2,1},{3,2},{5,4},{6,5},{7,6},{9,8},{10,9},{11,10},{13,12},{... | collective-permute-start | bytes 2359304 | tf_op jit(solution)/shard_map/ppermute | solution.py:111
  76.8 50.4 %collective-permute-start.14 = (bf16[192,2048]{1,0:T(8,128)(2,1)}, bf16[192,2048]{1,0:T(8,128)(2,1)S(1)}, u32[]{:S(2)}, u32[]{:S(2)}) collective-permute-start(bf16[192,2048]{1,0:T(8,128)(2,1)} %collective-permute-done.11), channel_id=1, source_target_pairs={{0,1},{1,2},{2,3},{4,5},{5,6},{6,7},{8,9},{9,10},{10,11},{12,13},{... | collective-permute-start | bytes 2359304 | tf_op jit(solution)/shard_map/ppermute | solution.py:111
  150.5 22.1 %collective-permute-start.32 = (bf16[2,256,1024]{2,1,0:T(8,128)(2,1)}, bf16[2,256,1024]{2,1,0:T(8,128)(2,1)}, u32[]{:S(2)}, u32[]{:S(2)}) collective-permute-start(bf16[2,256,1024]{2,1,0:T(8,128)(2,1)} %dynamic-slice_bitcast_fusion.1), channel_id=1, source_target_pairs={{0,4},{4,0},{1,5},{5,1},{2,6},{6,2},{3,7},{7,3},{8,12},{12,8},{9,1... | collective-permute-start | bytes 3145736 | tf_op jit(solution)/shard_map/ppermute | solution.py:151
  155.1 23.3 %all-to-all-start = ((bf16[32,2,1504]{2,1,0:T(2,128)(2,1)}), bf16[32,2,1504]{2,1,0:T(2,128)(2,1)S(1)}, u32[]{:S(2)}, u32[]{:S(2)}) async-start(bf16[32,2,1504]{2,1,0:T(2,128)(2,1)} %reshape.529), calls=%async_computation | async-start | bytes 393216 | tf_op jit(solution)/shard_map/all_to_all | solution.py:446
  172.1 24.3 %collective-permute-start.5 = (bf16[768,1024]{1,0:T(8,128)(2,1)}, bf16[768,1024]{1,0:T(8,128)(2,1)}, u32[]{:S(2)}, u32[]{:S(2)}) collective-permute-start(bf16[768,1024]{1,0:T(8,128)(2,1)} %bitcast.9.b_own), channel_id=1, source_target_pairs={{0,4},{4,0},{8,12},{12,8},{16,20},{20,16},{24,28},{28,24},{1,5},{5... | collective-permute-start | bytes 4718600 | tf_op jit(solution)/shard_map/ppermute | solution.py:52
  172.3 24.0 %collective-permute-start.4 = (bf16[768,1024]{1,0:T(8,128)(2,1)}, bf16[768,1024]{1,0:T(8,128)(2,1)}, u32[]{:S(2)}, u32[]{:S(2)}) collective-permute-start(bf16[768,1024]{1,0:T(8,128)(2,1)} %bitcast.4.a_own), channel_id=1, source_target_pairs={{0,4},{4,0},{8,12},{12,8},{16,20},{20,16},{24,28},{28,24},{1,5},{5... | collective-permute-start | bytes 4718600 | tf_op jit(solution)/shard_map/ppermute | solution.py:52
  183.2 41.7 %all-to-all-start.1 = ((bf16[32,64,256]{2,1,0:T(8,128)(2,1)}), bf16[32,64,256]{2,1,0:T(8,128)(2,1)S(1)}, u32[]{:S(2)}, u32[]{:S(2)}) async-start(bf16[32,64,256]{2,1,0:T(8,128)(2,1)} %bitcast.296), calls=%async_computation.1 | async-start | bytes 2097152 | tf_op jit(solution)/shard_map/all_to_all | solution.py:480
  186.0 245.3 %all-gather.9.cloned.1.call-start = ((), (), s32[]{:S(2)}) async-start(), calls=%async_computation.10 | async-start | bytes 5242880 | tf_op jit(solution)/shard_map/all_gather | solution.py:540
  247.8 229.3 %all-gather.11.cloned.1.call-start = ((), (), s32[]{:S(2)}) async-start(), calls=%async_computation.11 | async-start | bytes 10485760 | tf_op jit(solution)/shard_map/all_gather | solution.py:539
  257.2 30.5 %collective-permute-start.19 = (bf16[2,192,1024]{2,1,0:T(8,128)(2,1)S(1)}, bf16[2,192,1024]{2,1,0:T(8,128)(2,1)S(1)}, u32[]{:S(2)}, u32[]{:S(2)}) collective-permute-start(bf16[2,192,1024]{2,1,0:T(8,128)(2,1)S(1)} %slice_bitcast_fusion.6), channel_id=1, source_target_pairs={{0,8},{4,12},{8,0},{12,4},{16,24},{20,28},{24,16},{28,20},{1,9},{5... | collective-permute-start | bytes 2359304 | tf_op jit(solution)/shard_map/ppermute | solution.py:52
  259.0 32.2 %collective-permute-start.21 = (bf16[2,192,1024]{2,1,0:T(8,128)(2,1)S(1)}, bf16[2,192,1024]{2,1,0:T(8,128)(2,1)S(1)}, u32[]{:S(2)}, u32[]{:S(2)}) collective-permute-start(bf16[2,192,1024]{2,1,0:T(8,128)(2,1)S(1)} %bitcast.325), channel_id=1, source_target_pairs={{0,16},{4,20},{8,24},{12,28},{16,0},{20,4},{24,8},{28,12},{1,17},{... | collective-permute-start | bytes 2359304 | tf_op jit(solution)/shard_map/ppermute | solution.py:52
  289.7 20.4 %collective-permute-start.20 = (bf16[192,1024]{1,0:T(8,128)(2,1)}, bf16[192,1024]{1,0:T(8,128)(2,1)}, u32[]{:S(2)}, u32[]{:S(2)}) collective-permute-start(bf16[192,1024]{1,0:T(8,128)(2,1)} %slice_bitcast_fusion.18), channel_id=1, source_target_pairs={{0,16},{4,20},{8,24},{12,28},{16,0},{20,4},{24,8},{28,12},{1,17},{... | collective-permute-start | bytes 1179656 | tf_op jit(solution)/shard_map/ppermute | solution.py:52
  293.1 20.3 %collective-permute-start.22 = (bf16[192,1024]{1,0:T(8,128)(2,1)}, bf16[192,1024]{1,0:T(8,128)(2,1)}, u32[]{:S(2)}, u32[]{:S(2)}) collective-permute-start(bf16[192,1024]{1,0:T(8,128)(2,1)} %slice_bitcast_fusion.16), channel_id=1, source_target_pairs={{0,8},{4,12},{8,0},{12,4},{16,24},{20,28},{24,16},{28,20},{1,9},{5... | collective-permute-start | bytes 1179656 | tf_op jit(solution)/shard_map/ppermute | solution.py:52
  313.4 183.0 %all-gather.13.cloned.1.call-start = ((), (), s32[]{:S(2)}) async-start(), calls=%async_computation.12 | async-start | bytes 5242880 | tf_op jit(solution)/shard_map/all_gather | solution.py:540
  320.5 12.0 %collective-permute-start.25 = (bf16[768,2048]{1,0:T(8,128)(2,1)}, bf16[768,2048]{1,0:T(8,128)(2,1)}, u32[]{:S(2)}, u32[]{:S(2)}) collective-permute-start(bf16[768,2048]{1,0:T(8,128)(2,1)} %pad_maximum_fusion.1), channel_id=1, source_target_pairs={{0,4},{4,0},{1,5},{5,1},{2,6},{6,2},{3,7},{7,3},{8,12},{12,8},{9,1... | collective-permute-start | bytes 9437192 | tf_op jit(solution)/shard_map/ppermute | solution.py:151
  325.9 20.9 %collective-permute-start.23 = (bf16[192,2048]{1,0:T(8,128)(2,1)S(1)}, bf16[192,2048]{1,0:T(8,128)(2,1)S(1)}, u32[]{:S(2)}, u32[]{:S(2)}) collective-permute-start(bf16[192,2048]{1,0:T(8,128)(2,1)S(1)} %get-tuple-element.179), channel_id=1, source_target_pairs={{0,1},{1,2},{2,3},{4,5},{5,6},{6,7},{8,9},{9,10},{10,11},{12,13},{... | collective-permute-start | bytes 2359304 | tf_op jit(solution)/shard_map/ppermute | solution.py:111
  329.4 21.6 %collective-permute-start.24 = (bf16[192,2048]{1,0:T(8,128)(2,1)S(1)}, bf16[192,2048]{1,0:T(8,128)(2,1)S(1)}, u32[]{:S(2)}, u32[]{:S(2)}) collective-permute-start(bf16[192,2048]{1,0:T(8,128)(2,1)S(1)} %get-tuple-element.179), channel_id=1, source_target_pairs={{1,0},{2,1},{3,2},{5,4},{6,5},{7,6},{9,8},{10,9},{11,10},{13,12},{... | collective-permute-start | bytes 2359304 | tf_op jit(solution)/shard_map/ppermute | solution.py:111
  351.0 20.8 %collective-permute-start.26 = (bf16[192,2048]{1,0:T(8,128)(2,1)S(1)}, bf16[192,2048]{1,0:T(8,128)(2,1)S(1)}, u32[]{:S(2)}, u32[]{:S(2)}) collective-permute-start(bf16[192,2048]{1,0:T(8,128)(2,1)S(1)} %collective-permute-done.24), channel_id=1, source_target_pairs={{1,0},{2,1},{3,2},{5,4},{6,5},{7,6},{9,8},{10,9},{11,10},{13,12},{... | collective-permute-start | bytes 2359304 | tf_op jit(solution)/shard_map/ppermute | solution.py:111
  352.2 20.8 %collective-permute-start.28 = (bf16[192,2048]{1,0:T(8,128)(2,1)S(1)}, bf16[192,2048]{1,0:T(8,128)(2,1)S(1)}, u32[]{:S(2)}, u32[]{:S(2)}) collective-permute-start(bf16[192,2048]{1,0:T(8,128)(2,1)S(1)} %collective-permute-done.23), channel_id=1, source_target_pairs={{0,1},{1,2},{2,3},{4,5},{5,6},{6,7},{8,9},{9,10},{10,11},{12,13},{... | collective-permute-start | bytes 2359304 | tf_op jit(solution)/shard_map/ppermute | solution.py:111
  371.8 20.1 %collective-permute-start.27 = (bf16[192,2048]{1,0:T(8,128)(2,1)S(1)}, bf16[192,2048]{1,0:T(8,128)(2,1)S(1)}, u32[]{:S(2)}, u32[]{:S(2)}) collective-permute-start(bf16[192,2048]{1,0:T(8,128)(2,1)S(1)} %collective-permute-done.26), channel_id=1, source_target_pairs={{1,0},{2,1},{3,2},{5,4},{6,5},{7,6},{9,8},{10,9},{11,10},{13,12},{... | collective-permute-start | bytes 2359304 | tf_op jit(solution)/shard_map/ppermute | solution.py:111
  373.1 19.9 %collective-permute-start.29 = (bf16[192,2048]{1,0:T(8,128)(2,1)S(1)}, bf16[192,2048]{1,0:T(8,128)(2,1)S(1)}, u32[]{:S(2)}, u32[]{:S(2)}) collective-permute-start(bf16[192,2048]{1,0:T(8,128)(2,1)S(1)} %collective-permute-done.28), channel_id=1, source_target_pairs={{0,1},{1,2},{2,3},{4,5},{5,6},{6,7},{8,9},{9,10},{10,11},{12,13},{... | collective-permute-start | bytes 2359304 | tf_op jit(solution)/shard_map/ppermute | solution.py:111
  401.2 398.2 %reduce-scatter.5.cloned.1.call-start = ((), (), s32[]{:S(2)}) async-start(), calls=%async_computation.13 | async-start | bytes 5242880 | tf_op jit(solution)/shard_map/reduce_scatter | solution.py:593
  477.1 332.1 %reduce-scatter.7.cloned.1.call-start = ((), (), s32[]{:S(2)}) async-start(), calls=%async_computation.14 | async-start | bytes 5242880 | tf_op jit(solution)/shard_map/reduce_scatter | solution.py:593
  529.1 363.0 %reduce-scatter.9.cloned.1.call-start = ((), (), s32[]{:S(2)}) async-start(), calls=%async_computation.15 | async-start | bytes 10485760 | tf_op jit(solution)/shard_map/reduce_scatter | solution.py:653
  555.9 27.1 %collective-permute-start.35 = (bf16[192,2048]{1,0:T(8,128)(2,1)}, bf16[192,2048]{1,0:T(8,128)(2,1)}, u32[]{:S(2)}, u32[]{:S(2)}) collective-permute-start(bf16[192,2048]{1,0:T(8,128)(2,1)} %get-tuple-element.215), channel_id=1, source_target_pairs={{0,1},{1,2},{2,3},{4,5},{5,6},{6,7},{8,9},{9,10},{10,11},{12,13},{... | collective-permute-start | bytes 2359304 | tf_op jit(solution)/shard_map/ppermute | solution.py:111
  561.1 21.9 %collective-permute-start.36 = (bf16[192,2048]{1,0:T(8,128)(2,1)}, bf16[192,2048]{1,0:T(8,128)(2,1)}, u32[]{:S(2)}, u32[]{:S(2)}) collective-permute-start(bf16[192,2048]{1,0:T(8,128)(2,1)} %get-tuple-element.214), channel_id=1, source_target_pairs={{1,0},{2,1},{3,2},{5,4},{6,5},{7,6},{9,8},{10,9},{11,10},{13,12},{... | collective-permute-start | bytes 2359304 | tf_op jit(solution)/shard_map/ppermute | solution.py:111
  583.0 309.2 %reduce-scatter.11.cloned.1.call-start = ((), (), s32[]{:S(2)}) async-start(), calls=%async_computation.16 | async-start | bytes 10485760 | tf_op jit(solution)/shard_map/reduce_scatter | solution.py:653
  615.5 32.7 %collective-permute-start.37 = (bf16[192,2048]{1,0:T(8,128)(2,1)}, bf16[192,2048]{1,0:T(8,128)(2,1)S(1)}, u32[]{:S(2)}, u32[]{:S(2)}) collective-permute-start(bf16[192,2048]{1,0:T(8,128)(2,1)} %get-tuple-element.84), channel_id=1, source_target_pairs={{0,1},{1,2},{2,3},{4,5},{5,6},{6,7},{8,9},{9,10},{10,11},{12,13},{... | collective-permute-start | bytes 2359304 | tf_op jit(solution)/shard_map/ppermute | solution.py:111
  619.7 28.5 %collective-permute-start.38 = (bf16[192,2048]{1,0:T(8,128)(2,1)}, bf16[192,2048]{1,0:T(8,128)(2,1)}, u32[]{:S(2)}, u32[]{:S(2)}) collective-permute-start(bf16[192,2048]{1,0:T(8,128)(2,1)} %get-tuple-element.85), channel_id=1, source_target_pairs={{1,0},{2,1},{3,2},{5,4},{6,5},{7,6},{9,8},{10,9},{11,10},{13,12},{... | collective-permute-start | bytes 2359304 | tf_op jit(solution)/shard_map/ppermute | solution.py:111
  652.2 28.3 %collective-permute-start.39 = (bf16[192,2048]{1,0:T(8,128)(2,1)}, bf16[192,2048]{1,0:T(8,128)(2,1)}, u32[]{:S(2)}, u32[]{:S(2)}) collective-permute-start(bf16[192,2048]{1,0:T(8,128)(2,1)} %get-tuple-element.88), channel_id=1, source_target_pairs={{0,1},{1,2},{2,3},{4,5},{5,6},{6,7},{8,9},{9,10},{10,11},{12,13},{... | collective-permute-start | bytes 2359304 | tf_op jit(solution)/shard_map/ppermute | solution.py:111
  657.6 22.9 %collective-permute-start.40 = (bf16[192,2048]{1,0:T(8,128)(2,1)}, bf16[192,2048]{1,0:T(8,128)(2,1)}, u32[]{:S(2)}, u32[]{:S(2)}) collective-permute-start(bf16[192,2048]{1,0:T(8,128)(2,1)} %get-tuple-element.89), channel_id=1, source_target_pairs={{1,0},{2,1},{3,2},{5,4},{6,5},{7,6},{9,8},{10,9},{11,10},{13,12},{... | collective-permute-start | bytes 2359304 | tf_op jit(solution)/shard_map/ppermute | solution.py:111
  686.2 15.3 %collective-permute-start.47 = (bf16[192,1024]{1,0:T(8,128)(2,1)S(1)}, bf16[192,1024]{1,0:T(8,128)(2,1)S(1)}, u32[]{:S(2)}, u32[]{:S(2)}) collective-permute-start(bf16[192,1024]{1,0:T(8,128)(2,1)S(1)} %get-tuple-element.243), channel_id=1, source_target_pairs={{0,8},{4,12},{8,0},{12,4},{16,24},{20,28},{24,16},{28,20},{1,9},{5... | collective-permute-start | bytes 1179656 | tf_op jit(solution)/shard_map/ppermute | solution.py:52
  696.1 18.8 %collective-permute-start.50 = (bf16[2,192,1024]{2,1,0:T(8,128)(2,1)S(1)}, bf16[2,192,1024]{2,1,0:T(8,128)(2,1)S(1)}, u32[]{:S(2)}, u32[]{:S(2)}) collective-permute-start(bf16[2,192,1024]{2,1,0:T(8,128)(2,1)S(1)} %get-tuple-element.239), channel_id=1, source_target_pairs={{0,8},{4,12},{8,0},{12,4},{16,24},{20,28},{24,16},{28,20},{1,9},{5... | collective-permute-start | bytes 2359304 | tf_op jit(solution)/shard_map/ppermute | solution.py:52
  697.7 18.4 %collective-permute-start.41 = (bf16[192,2048]{1,0:T(8,128)(2,1)S(1)}, bf16[192,2048]{1,0:T(8,128)(2,1)S(1)}, u32[]{:S(2)}, u32[]{:S(2)}) collective-permute-start(bf16[192,2048]{1,0:T(8,128)(2,1)S(1)} %get-tuple-element.209), channel_id=1, source_target_pairs={{0,1},{1,2},{2,3},{4,5},{5,6},{6,7},{8,9},{9,10},{10,11},{12,13},{... | collective-permute-start | bytes 2359304 | tf_op jit(solution)/shard_map/ppermute | solution.py:111
  700.2 20.0 %collective-permute-start.42 = (bf16[192,2048]{1,0:T(8,128)(2,1)S(1)}, bf16[192,2048]{1,0:T(8,128)(2,1)S(1)}, u32[]{:S(2)}, u32[]{:S(2)}) collective-permute-start(bf16[192,2048]{1,0:T(8,128)(2,1)S(1)} %get-tuple-element.208), channel_id=1, source_target_pairs={{1,0},{2,1},{3,2},{5,4},{6,5},{7,6},{9,8},{10,9},{11,10},{13,12},{... | collective-permute-start | bytes 2359304 | tf_op jit(solution)/shard_map/ppermute | solution.py:111
  701.6 18.6 %collective-permute-start.48 = (bf16[2,192,1024]{2,1,0:T(8,128)(2,1)S(1)}, bf16[2,192,1024]{2,1,0:T(8,128)(2,1)S(1)}, u32[]{:S(2)}, u32[]{:S(2)}) collective-permute-start(bf16[2,192,1024]{2,1,0:T(8,128)(2,1)S(1)} %get-tuple-element.245), channel_id=1, source_target_pairs={{0,16},{4,20},{8,24},{12,28},{16,0},{20,4},{24,8},{28,12},{1,17},{... | collective-permute-start | bytes 2359304 | tf_op jit(solution)/shard_map/ppermute | solution.py:52
  729.0 31.2 %collective-permute-start.43 = (bf16[192,2048]{1,0:T(8,128)(2,1)}, bf16[192,2048]{1,0:T(8,128)(2,1)}, u32[]{:S(2)}, u32[]{:S(2)}) collective-permute-start(bf16[192,2048]{1,0:T(8,128)(2,1)} %get-tuple-element.91), channel_id=1, source_target_pairs={{0,1},{1,2},{2,3},{4,5},{5,6},{6,7},{8,9},{9,10},{10,11},{12,13},{... | collective-permute-start | bytes 2359304 | tf_op jit(solution)/shard_map/ppermute | solution.py:111
  732.4 27.8 %collective-permute-start.44 = (bf16[192,2048]{1,0:T(8,128)(2,1)}, bf16[192,2048]{1,0:T(8,128)(2,1)}, u32[]{:S(2)}, u32[]{:S(2)}) collective-permute-start(bf16[192,2048]{1,0:T(8,128)(2,1)} %get-tuple-element.92), channel_id=1, source_target_pairs={{1,0},{2,1},{3,2},{5,4},{6,5},{7,6},{9,8},{10,9},{11,10},{13,12},{... | collective-permute-start | bytes 2359304 | tf_op jit(solution)/shard_map/ppermute | solution.py:111
  771.3 21.2 %collective-permute-start.45 = (bf16[192,2048]{1,0:T(8,128)(2,1)}, bf16[192,2048]{1,0:T(8,128)(2,1)}, u32[]{:S(2)}, u32[]{:S(2)}) collective-permute-start(bf16[192,2048]{1,0:T(8,128)(2,1)} %get-tuple-element.93), channel_id=1, source_target_pairs={{0,1},{1,2},{2,3},{4,5},{5,6},{6,7},{8,9},{9,10},{10,11},{12,13},{... | collective-permute-start | bytes 2359304 | tf_op jit(solution)/shard_map/ppermute | solution.py:111
  777.0 20.5 %collective-permute-start.46 = (bf16[192,2048]{1,0:T(8,128)(2,1)}, bf16[192,2048]{1,0:T(8,128)(2,1)}, u32[]{:S(2)}, u32[]{:S(2)}) collective-permute-start(bf16[192,2048]{1,0:T(8,128)(2,1)} %get-tuple-element.94), channel_id=1, source_target_pairs={{1,0},{2,1},{3,2},{5,4},{6,5},{7,6},{9,8},{10,9},{11,10},{13,12},{... | collective-permute-start | bytes 2359304 | tf_op jit(solution)/shard_map/ppermute | solution.py:111
  791.8 20.9 %collective-permute-start.56 = (bf16[768,2048]{1,0:T(8,128)(2,1)}, bf16[768,2048]{1,0:T(8,128)(2,1)}, u32[]{:S(2)}, u32[]{:S(2)}) collective-permute-start(bf16[768,2048]{1,0:T(8,128)(2,1)} %get-tuple-element.103), channel_id=1, source_target_pairs={{0,4},{4,0},{8,12},{12,8},{16,20},{20,16},{24,28},{28,24},{1,5},{5... | collective-permute-start | bytes 9437192 | tf_op jit(solution)/shard_map/ppermute | solution.py:52
  817.8 24.1 %collective-permute-start.61 = (bf16[256,2048]{1,0:T(8,128)(2,1)S(1)}, bf16[256,2048]{1,0:T(8,128)(2,1)S(1)}, u32[]{:S(2)}, u32[]{:S(2)}) collective-permute-start(bf16[256,2048]{1,0:T(8,128)(2,1)S(1)} %get-tuple-element.108), channel_id=1, source_target_pairs={{0,1},{1,2},{2,3},{4,5},{5,6},{6,7},{8,9},{9,10},{10,11},{12,13},{... | collective-permute-start | bytes 3145736 | tf_op jit(solution)/shard_map/ppermute | solution.py:111
  819.5 26.5 %collective-permute-start.62 = (bf16[256,2048]{1,0:T(8,128)(2,1)S(1)}, bf16[256,2048]{1,0:T(8,128)(2,1)S(1)}, u32[]{:S(2)}, u32[]{:S(2)}) collective-permute-start(bf16[256,2048]{1,0:T(8,128)(2,1)S(1)} %get-tuple-element.109), channel_id=1, source_target_pairs={{1,0},{2,1},{3,2},{5,4},{6,5},{7,6},{9,8},{10,9},{11,10},{13,12},{... | collective-permute-start | bytes 3145736 | tf_op jit(solution)/shard_map/ppermute | solution.py:111
  823.5 24.5 %collective-permute-start.57 = (bf16[2,192,1024]{2,1,0:T(8,128)(2,1)S(1)}, bf16[2,192,1024]{2,1,0:T(8,128)(2,1)S(1)}, u32[]{:S(2)}, u32[]{:S(2)}) collective-permute-start(bf16[2,192,1024]{2,1,0:T(8,128)(2,1)S(1)} %slice_bitcast_fusion.4), channel_id=1, source_target_pairs={{0,8},{4,12},{8,0},{12,4},{16,24},{20,28},{24,16},{28,20},{1,9},{5... | collective-permute-start | bytes 2359304 | tf_op jit(solution)/shard_map/ppermute | solution.py:52
  824.1 29.6 %collective-permute-start.59 = (bf16[2,192,1024]{2,1,0:T(8,128)(2,1)S(1)}, bf16[2,192,1024]{2,1,0:T(8,128)(2,1)S(1)}, u32[]{:S(2)}, u32[]{:S(2)}) collective-permute-start(bf16[2,192,1024]{2,1,0:T(8,128)(2,1)S(1)} %bitcast.321), channel_id=1, source_target_pairs={{0,16},{4,20},{8,24},{12,28},{16,0},{20,4},{24,8},{28,12},{1,17},{... | collective-permute-start | bytes 2359304 | tf_op jit(solution)/shard_map/ppermute | solution.py:52
  846.7 25.7 %collective-permute-start.64 = (bf16[256,2048]{1,0:T(8,128)(2,1)S(1)}, bf16[256,2048]{1,0:T(8,128)(2,1)S(1)}, u32[]{:S(2)}, u32[]{:S(2)}) collective-permute-start(bf16[256,2048]{1,0:T(8,128)(2,1)S(1)} %get-tuple-element.111), channel_id=1, source_target_pairs={{1,0},{2,1},{3,2},{5,4},{6,5},{7,6},{9,8},{10,9},{11,10},{13,12},{... | collective-permute-start | bytes 3145736 | tf_op jit(solution)/shard_map/ppermute | solution.py:111
  849.1 25.5 %collective-permute-start.63 = (bf16[256,2048]{1,0:T(8,128)(2,1)S(1)}, bf16[256,2048]{1,0:T(8,128)(2,1)S(1)}, u32[]{:S(2)}, u32[]{:S(2)}) collective-permute-start(bf16[256,2048]{1,0:T(8,128)(2,1)S(1)} %get-tuple-element.110), channel_id=1, source_target_pairs={{0,1},{1,2},{2,3},{4,5},{5,6},{6,7},{8,9},{9,10},{10,11},{12,13},{... | collective-permute-start | bytes 3145736 | tf_op jit(solution)/shard_map/ppermute | solution.py:111
  854.0 28.8 %collective-permute-start.60 = (bf16[192,1024]{1,0:T(8,128)(2,1)S(1)}, bf16[192,1024]{1,0:T(8,128)(2,1)S(1)}, u32[]{:S(2)}, u32[]{:S(2)}) collective-permute-start(bf16[192,1024]{1,0:T(8,128)(2,1)S(1)} %slice_bitcast_fusion.12), channel_id=1, source_target_pairs={{0,8},{4,12},{8,0},{12,4},{16,24},{20,28},{24,16},{28,20},{1,9},{5... | collective-permute-start | bytes 1179656 | tf_op jit(solution)/shard_map/ppermute | solution.py:52
  875.9 26.1 %collective-permute-start.65 = (bf16[256,2048]{1,0:T(8,128)(2,1)}, bf16[256,2048]{1,0:T(8,128)(2,1)}, u32[]{:S(2)}, u32[]{:S(2)}) collective-permute-start(bf16[256,2048]{1,0:T(8,128)(2,1)} %add_convert_fusion.6), channel_id=1, source_target_pairs={{0,1},{1,2},{2,3},{4,5},{5,6},{6,7},{8,9},{9,10},{10,11},{12,13},{... | collective-permute-start | bytes 3145736 | tf_op jit(solution)/shard_map/ppermute | solution.py:111
  881.3 26.3 %collective-permute-start.66 = (bf16[256,2048]{1,0:T(8,128)(2,1)}, bf16[256,2048]{1,0:T(8,128)(2,1)}, u32[]{:S(2)}, u32[]{:S(2)}) collective-permute-start(bf16[256,2048]{1,0:T(8,128)(2,1)} %add_convert_fusion.5), channel_id=1, source_target_pairs={{1,0},{2,1},{3,2},{5,4},{6,5},{7,6},{9,8},{10,9},{11,10},{13,12},{... | collective-permute-start | bytes 3145736 | tf_op jit(solution)/shard_map/ppermute | solution.py:111
  888.2 34.0 %all-to-all-start.4 = ((f32[32,1,1280]{2,1,0:T(1,128)}), f32[32,1,1280]{2,1,0:T(1,128)S(1)}, u32[]{:S(2)}, u32[]{:S(2)}) async-start(f32[32,1,1280]{2,1,0:T(1,128)} %all_to_all.28), calls=%async_computation.6 | async-start | bytes 327680 | tf_op jit(solution)/shard_map/all_to_all | solution.py:727
  895.4 42.0 %collective-permute-start.71 = (bf16[2,256,2048]{2,1,0:T(8,128)(2,1)}, bf16[2,256,2048]{2,1,0:T(8,128)(2,1)}, u32[]{:S(2)}, u32[]{:S(2)}) collective-permute-start(bf16[2,256,2048]{2,1,0:T(8,128)(2,1)} %fusion.28), channel_id=1, source_target_pairs={{0,4},{4,0},{1,5},{5,1},{2,6},{6,2},{3,7},{7,3},{8,12},{12,8},{9,1... | collective-permute-start | bytes 6291464 | tf_op jit(solution)/shard_map/ppermute | solution.py:151
  910.6 24.3 %collective-permute-start.68 = (bf16[64,2048]{1,0:T(8,128)(2,1)}, bf16[64,2048]{1,0:T(8,128)(2,1)}, u32[]{:S(2)}, u32[]{:S(2)}) collective-permute-start(bf16[64,2048]{1,0:T(8,128)(2,1)} %get-tuple-element.232), channel_id=1, source_target_pairs={{0,0},{1,1},{6,2},{11,3},{12,4},{13,5},{18,6},{23,7},{24,8},{25,9}... | collective-permute-start | bytes 786440 | tf_op jit(solution)/shard_map/ppermute | solution.py:709
  914.3 20.6 %collective-permute-start.69 = (bf16[64,2048]{1,0:T(8,128)(2,1)}, bf16[64,2048]{1,0:T(8,128)(2,1)}, u32[]{:S(2)}, u32[]{:S(2)}) collective-permute-start(bf16[64,2048]{1,0:T(8,128)(2,1)} %get-tuple-element.231), channel_id=1, source_target_pairs={{0,0},{5,1},{6,2},{11,3},{12,4},{17,5},{18,6},{23,7},{24,8},{29,9}... | collective-permute-start | bytes 786440 | tf_op jit(solution)/shard_map/ppermute | solution.py:709
  917.9 17.0 %collective-permute-start.70 = (bf16[64,2048]{1,0:T(8,128)(2,1)}, bf16[64,2048]{1,0:T(8,128)(2,1)}, u32[]{:S(2)}, u32[]{:S(2)}) collective-permute-start(bf16[64,2048]{1,0:T(8,128)(2,1)} %get-tuple-element.230), channel_id=1, source_target_pairs={{0,0},{5,1},{10,2},{11,3},{12,4},{17,5},{22,6},{23,7},{24,8},{29,9... | collective-permute-start | bytes 786440 | tf_op jit(solution)/shard_map/ppermute | solution.py:709
  (116 other events, 1588.8 us)
Sparse Core Ops, SparseCore 0:
  71.3 76.5 all-gather.14
  149.7 96.9 all-gather.6
  249.1 71.8 all-gather.8
  322.7 87.4 all-gather.10
  411.9 52.5 all-gather.12
  477.2 52.6 reduce-scatter.4
  532.9 52.5 reduce-scatter.6
  589.2 86.3 reduce-scatter.8
  726.1 83.8 reduce-scatter.10

commit v6 on v5

--- a/solution.py
+++ b/solution.py
@@ -417,9 +417,34 @@
     moved = [
         lax.ppermute(w_qkv[t * sub : (t + 1) * sub], ALL, unit_perm(t, False)) for t in range(3)
     ]
+    def in_core_order(own, got):
+        first = ci == 0
+        return jnp.where(first, own, got), jnp.where(first, got, own)
+
+    def core_half(weight):
+        split = weight.reshape((2, mine) + weight.shape[1:])
+        got = swap_core(lax.dynamic_index_in_dim(split, 1 - ci, 0, keepdims=False))
+        own = lax.dynamic_index_in_dim(split, ci, 0, keepdims=False)
+        both = in_core_order(own, got)
+        return [jnp.concatenate([half[e] for half in both], axis=0) for e in range(mine)]
+
+    down_half = core_half(w_down)
+
+    mini = jnp.concatenate(
+        [
+            norm_gains.reshape(-1),
+            w_router.reshape(-1),
+            segments.astype(bf16).reshape(-1),
+            routes.astype(bf16).reshape(-1),
+        ]
+    )
+    minis = lax.all_to_all(
+        jnp.broadcast_to(mini[None], (world,) + mini.shape), ALL, 0, 0, tiled=True
+    )
+
     tok_pieces = gather_dp(tokens, dps)
     slots, slot_steps = gather_z(
-        jnp.concatenate(moved, axis=0), zs, zi,
+        after(jnp.concatenate(moved, axis=0), minis, *down_half), zs, zi,
         {s: [] if s < zs - 1 else tok_pieces[:2] for s in range(2, zs)},
     )
     inv3 = pow(3, -1, dps)
@@ -434,18 +459,6 @@
     slot_of = jnp.asarray(slot_of, jnp.int32)[di]
     type_of = jnp.asarray(type_of, jnp.int32)[di]
 
-    mini = jnp.concatenate(
-        [
-            norm_gains.reshape(-1),
-            w_router.reshape(-1),
-            segments.astype(bf16).reshape(-1),
-            routes.astype(bf16).reshape(-1),
-        ]
-    )
-    mini = after(mini, *slot_steps[1])
-    minis = lax.all_to_all(
-        jnp.broadcast_to(mini[None], (world,) + mini.shape), ALL, 0, 0, tiled=True
-    )
     at = 0
     split = []
     for part in (norm_gains, w_router, segments, routes):
@@ -480,24 +493,12 @@
     w_out_c = lax.all_to_all(
         out_cols.reshape(world, orow, width), ALL, 0, 0, tiled=True
     ).reshape(D, width)
-    dy_all = lax.all_gather(after(cotangent, *slot_steps[2]), "z", axis=0)
+    first_down = lax.all_gather(down_half[0], "q", axis=0, tiled=True)
+    dy_all = lax.all_gather(after(cotangent, first_down, *slot_steps[-1]), "z", axis=0)
     dy_blocks = [
         lax.dynamic_index_in_dim(dy_all, (zi - k) % zs, 0, keepdims=False) for k in range(zs)
     ]
 
-    def in_core_order(own, got):
-        first = ci == 0
-        return jnp.where(first, own, got), jnp.where(first, got, own)
-
-    def core_half(weight):
-        split = weight.reshape((2, mine) + weight.shape[1:])
-        got = swap_core(lax.dynamic_index_in_dim(split, 1 - ci, 0, keepdims=False))
-        own = lax.dynamic_index_in_dim(split, ci, 0, keepdims=False)
-        both = in_core_order(own, got)
-        return [jnp.concatenate([half[e] for half in both], axis=0) for e in range(mine)]
-
-    gu_half = core_half(after(w_gate_up, *slot_steps[-1]))
-    down_half = core_half(after(w_down, *moved))
     blocks = all_rows // BLOCK
     half = blocks // 2
     own_spec, other_spec = pieces_spec(half, D // 2)
@@ -516,6 +517,7 @@
         ],
         tuple(tok_pieces) + (gains_f[:, 0][None], w_three),
     )
+    gu_half = core_half(after(w_gate_up, hidden_one))
     sums = sum_dp(sums, dps)
     mask_spec = pl.BlockSpec((BLOCK // LEN, LEN, LEN), lambda i: (i, 0, 0))
     table_specs = [whole((8, width)), whole((BLOCK, HD)), whole((BLOCK, HD)), mask_spec]
@@ -537,7 +539,7 @@
         expert_w.append(
             (
                 lax.all_gather(gu_half[e], "q", axis=0, tiled=True),
-                lax.all_gather(down_half[e], "q", axis=0, tiled=True),
+                lax.all_gather(down_half[e], "q", axis=0, tiled=True) if e else first_down,
             )
         )
 

time: 960 us -> 947 us (0.986)
  starting transfers between devices: 164 us -> 152 us
    ppermute x30, waiting for transfers between devices: 166 us -> 115 us  [line(): lax.ppermute(value, 'z', [(j, j + step) for j in range(zs) if 0 <= j + st...]
    all_to_all x1, waiting for transfers between devices: 0.01 us -> 37.6 us  [per_device(): lax.all_to_all(out_cols.reshape(world, orow, width), ALL, 0, 0, tiled=True)]
    ppermute x30, starting transfers between devices: 97.1 us -> 83.7 us  [line(): lax.ppermute(value, 'z', [(j, j + step) for j in range(zs) if 0 <= j + st...]
    ppermute x28, waiting for transfers between devices: 95.3 us -> 108 us  [flip(): return lax.ppermute(value, DP, [(i, i ^ 1 << bit) for i in range(size)])]
    unnamed x206 -> x180, local copies, waits for them, and re-layouts: 24 us -> 23.9 us
  transfers between devices with their start and end apart: 85 -> 85, of which waited for: 40 -> 37; matrix products, arithmetic and copies ran while one was open for 35% -> 34% of each run, Pallas kernels for 12% -> 12%
where the time goes in v6:
time: 947 us; the launch traced here: 937 us
  waiting for transfers between devices  280 us (30%)
  matrix products  176 us (19%)
  starting transfers between devices  152 us (16%)
  Pallas kernels  113 us (12%)
  other arithmetic  96.4 us (10%)
  local copies, waits for them, and re-layouts  76.4 us (8%)
  between operations  22.3 us (2%)
  blocking collectives  20.7 us (2%)
    dot_general x13, matrix products, mm(): lax.dot_general(a, b, (((ca,), (cb,)), ((), ())), preferred_element_type=...  173 us
    ppermute x30, waiting for transfers between devices, line(): lax.ppermute(value, 'z', [(j, j + step) for j in range(zs) if 0 <= j + st...  115 us
    ppermute x28, waiting for transfers between devices, flip(): return lax.ppermute(value, DP, [(i, i ^ 1 << bit) for i in range(size)])  108 us
    ppermute x30, starting transfers between devices, line(): lax.ppermute(value, 'z', [(j, j + step) for j in range(zs) if 0 <= j + st...  83.7 us
    pallas_call x4, Pallas kernels, run_blocks(): pl.pallas_call(body, grid=(rows // BLOCK,), in_specs=in_specs, out_specs=...  71.4 us
    pallas_call x2, Pallas kernels, weight_grad(): pl.pallas_call(functools.partial(weight_grad_kernel, half), grid=(b.shape...  41.6 us
    all_to_all x1, waiting for transfers between devices, per_device(): lax.all_to_all(out_cols.reshape(world, orow, width), ALL, 0, 0, tiled=True)  37.6 us
    ppermute x28, starting transfers between devices, flip(): return lax.ppermute(value, DP, [(i, i ^ 1 << bit) for i in range(size)])  25.5 us
  transfers between devices with their start and end apart: 85, of which 37 were waited for; matrix products, arithmetic and copies ran while one was open for 34% of the time, Pallas kernels for 12%

profile of v6, /device:TPU:0, one launch (start us, length us, event | category | flops | bytes accessed | tf_op | source)
XLA Modules:
  0.0 937.3 jit_solution(12367436468507196822)
XLA Ops:
  30.1 7.1 all-to-all-start
  41.2 5.3 all-to-all-done
  59.6 16.6 %collective-permute-done = bf16[192,1024]{1,0:T(8,128)(2,1)S(1)} collective-permute-done((bf16[192,1024]{1,0:T(8,128)(2,1)}, bf16[192,1024]{1,0:T(8,128)(2,1)S(1)}, u32[]{:S(2)}, u32[]{:S(2)}) %collective-permute-start) | collective-permute-done | bytes 393248 | tf_op jit(solution)/shard_map/ppermute | solution.py:52
  78.7 5.4 collective-permute-start.12
  92.6 7.8 collective-permute-done.3
  113.1 4.6 collective-permute-start.15
  117.7 8.9 collective-permute-done.14
  131.2 3.7 collective-permute-done.15
  141.6 13.0 %shard_map.188 = (bf16[1536,2048]{1,0:T(8,128)(2,1)}, f32[1536,768]{1,0:T(8,128)}, f32[8,1536]{1,0:T(8,128)}) custom-call(bf16[768,1024]{1,0:T(8,128)(2,1)} %bitcast.4.a_own, bf16[768,1024]{1,0:T(8,128)(2,1)} %bitcast.290, bf16[768,1024]{1,0:T(8,128)(2,1)} %collective-permute-done.4.a_other, bf16[768,1024]{1,0:T(8,128)(2,1)} %collective-permute-done.5.b_other, ...), custom_call_target="tpu_custom_call" | custom-call | flops 1 | bytes 1 | tf_op jit(solution)/shard_map/pallas_call | solution.py:349
  156.6 4.1 collective-permute-done.32
  166.2 5.3 all-to-all-start.1
  182.6 37.6 %all-to-all-done.1 = bf16[32,64,256]{2,1,0:T(8,128)(2,1)S(1)} async-done(((bf16[32,64,256]{2,1,0:T(8,128)(2,1)}), bf16[32,64,256]{2,1,0:T(8,128)(2,1)S(1)}, u32[]{:S(2)}, u32[]{:S(2)}) %all-to-all-start.1) | async-done | bytes 1048608 | tf_op jit(solution)/shard_map/all_to_all | solution.py:493
  221.6 18.7 %shard_map.189 = (bf16[1536,256]{1,0:T(8,128)(2,1)}, bf16[768,2048]{1,0:T(8,128)(2,1)}, bf16[768,2048]{1,0:T(8,128)(2,1)}) custom-call(f32[1536,768]{1,0:T(8,128)} %get-tuple-element.68.raw_ref, f32[8,1536]{1,0:T(8,128)} %pad.11.sum_ref, f32[8,256]{1,0:T(8,128)} %pad.12.gain_ref, f32[384,128]{1,0:T(8,128)} %bitcast.312, f32[384,128]{1,0:T(8,128)} %bitcast.314, ...), custom_call_target="tpu_custom_call" | custom-call | flops 1 | bytes 1 | tf_op jit(solution)/shard_map/pallas_call | solution.py:349
  241.6 5.5 collective-permute-done.19
  253.0 24.4 %collective-permute-done.20 = bf16[2,192,1024]{2,1,0:T(8,128)(2,1)S(1)} collective-permute-done((bf16[2,192,1024]{2,1,0:T(8,128)(2,1)S(1)}, bf16[2,192,1024]{2,1,0:T(8,128)(2,1)S(1)}, u32[]{:S(2)}, u32[]{:S(2)}) %collective-permute-start.20) | collective-permute-done | bytes 786464 | tf_op jit(solution)/shard_map/ppermute | solution.py:52
  281.9 16.0 %collective-permute-done.21 = bf16[192,1024]{1,0:T(8,128)(2,1)} collective-permute-done((bf16[192,1024]{1,0:T(8,128)(2,1)S(1)}, bf16[192,1024]{1,0:T(8,128)(2,1)}, u32[]{:S(2)}, u32[]{:S(2)}) %collective-permute-start.21) | collective-permute-done | bytes 393248 | tf_op jit(solution)/shard_map/ppermute | solution.py:52
  312.1 3.7 collective-permute-start.24
  321.0 12.0 %collective-permute-done.24 = bf16[192,2048]{1,0:T(8,128)(2,1)S(1)} collective-permute-done((bf16[192,2048]{1,0:T(8,128)(2,1)S(1)}, bf16[192,2048]{1,0:T(8,128)(2,1)S(1)}, u32[]{:S(2)}, u32[]{:S(2)}) %collective-permute-start.24) | collective-permute-done | bytes 786464 | tf_op jit(solution)/shard_map/ppermute | solution.py:111
  333.0 4.4 collective-permute-done.25
  338.7 4.6 collective-permute-start.29
  343.3 14.8 %collective-permute-done.27 = bf16[192,2048]{1,0:T(8,128)(2,1)S(1)} collective-permute-done((bf16[192,2048]{1,0:T(8,128)(2,1)S(1)}, bf16[192,2048]{1,0:T(8,128)(2,1)S(1)}, u32[]{:S(2)}, u32[]{:S(2)}) %collective-permute-start.27) | collective-permute-done | bytes 786464 | tf_op jit(solution)/shard_map/ppermute | solution.py:111
  359.4 4.6 collective-permute-start.30
  364.0 14.0 %collective-permute-done.28 = bf16[192,2048]{1,0:T(8,128)(2,1)S(1)} collective-permute-done((bf16[192,2048]{1,0:T(8,128)(2,1)S(1)}, bf16[192,2048]{1,0:T(8,128)(2,1)S(1)}, u32[]{:S(2)}, u32[]{:S(2)}) %collective-permute-start.28) | collective-permute-done | bytes 786464 | tf_op jit(solution)/shard_map/ppermute | solution.py:111
  389.1 4.0 constant_dynamic-update-slice_fusion.5.b_ref
  393.1 4.5 fusion.93
  397.9 19.1 %fusion.94 = f32[1536,2048]{1,0:T(8,128)} fusion(bf16[1536,2048]{1,0:T(8,128)(2,1)} %constant_dynamic-update-slice_fusion.5.b_ref, bf16[2048,2048]{1,0:T(8,128)(2,1)} %all-gather.9.cloned.1.call-done), kind=kOutput, calls=%fused_computation.294 | convolution fusion | flops 12884901888 | bytes 27262976 | tf_op jit(solution)/shard_map/dot_general | solution.py:44
  416.9 18.3 %multiply_convert_fusion.4 = (bf16[1536,1024]{1,0:T(8,128)(2,1)S(1)}, bf16[1536,1024]{1,0:T(8,128)(2,1)S(1)}, bf16[1536,1024]{1,0:T(8,128)(2,1)}) fusion(f32[1536,2048]{1,0:T(8,128)} %fusion.94, bf16[2048,1024]{1,0:T(8,128)(2,1)} %all-gather.7.cloned.1.call-done, bf16[1536,2048]{1,0:T(8,128)(2,1)} %copy-done.58, f32[1536]{0:T(1024)S(1)} %broadcast_select_fusion.9), kind=kOutput, calls=%fused_computation.40 | convolution fusion | flops 6475481088 | bytes 32512000 | tf_op jit(solution)/shard_map/dot_general | solution.py:44
  435.3 20.4 %convolution_convert_fusion.2 = bf16[1536,2048]{1,0:T(8,128)(2,1)} fusion(bf16[2048,2048]{1,0:T(8,128)(2,1)} %all-gather.9.cloned.1.call-done, bf16[1536,1024]{1,0:T(8,128)(2,1)S(1)} %get-tuple-element.82.u_ref, bf16[1536,1024]{1,0:T(8,128)(2,1)S(1)} %get-tuple-element.81.g_ref), kind=kOutput, calls=%fused_computation.19 | convolution fusion | flops 12900630528 | bytes 20971520 | tf_op jit(solution)/shard_map/dot_general | solution.py:44
  455.7 8.9 convolution_convert_fusion.5
  464.7 19.2 %fusion.95 = f32[1536,2048]{1,0:T(8,128)} fusion(bf16[1536,2048]{1,0:T(8,128)(2,1)} %constant_dynamic-update-slice_fusion.5.b_ref, bf16[2048,2048]{1,0:T(8,128)(2,1)} %all-gather.11.cloned.1.call-done), kind=kOutput, calls=%fused_computation.295 | convolution fusion | flops 12884901888 | bytes 27262976 | tf_op jit(solution)/shard_map/dot_general | solution.py:44
  483.9 18.4 %multiply_convert_fusion.1 = (bf16[1536,1024]{1,0:T(8,128)(2,1)S(1)}, bf16[1536,1024]{1,0:T(8,128)(2,1)}, bf16[1536,1024]{1,0:T(8,128)(2,1)S(1)}) fusion(f32[1536,2048]{1,0:T(8,128)} %fusion.95, bf16[2048,1024]{1,0:T(8,128)(2,1)} %all-gather.13.cloned.1.call-done, bf16[1536,2048]{1,0:T(8,128)(2,1)} %copy-done.58, f32[1536]{0:T(1024)S(1)} %broadcast_select_fusion.8), kind=kOutput, calls=%fused_computation.34 | convolution fusion | flops 6475481088 | bytes 32512000 | tf_op jit(solution)/shard_map/dot_general | solution.py:44
  504.1 12.4 %convolution_convert_fusion.4 = bf16[2048,1024]{1,0:T(8,128)(2,1)} fusion(bf16[1536,1024]{1,0:T(8,128)(2,1)S(1)} %get-tuple-element.185, bf16[1536,2048]{1,0:T(8,128)(2,1)} %copy-done.58, f32[1536]{0:T(1024)S(1)} %broadcast_select_fusion.8), kind=kOutput, calls=%fused_computation.54 | convolution fusion | flops 6453985280 | bytes 13637632 | tf_op jit(solution)/shard_map/dot_general | solution.py:44
  516.6 17.8 %add_convert_fusion = bf16[1536,2048]{1,0:T(8,128)(2,1)S(1)} fusion(bf16[1536,2048]{1,0:T(8,128)(2,1)} %convolution_convert_fusion.2, bf16[2048,2048]{1,0:T(8,128)(2,1)} %all-gather.11.cloned.1.call-done, bf16[1536,1024]{1,0:T(8,128)(2,1)} %get-tuple-element.86.u_ref, bf16[1536,1024]{1,0:T(8,128)(2,1)S(1)} %get-tuple-element.85.g_ref), kind=kOutput, calls=%fused_computation.16 | convolution fusion | flops 12913213440 | bytes 27262976 | tf_op jit(solution)/shard_map/dot_general | solution.py:44
  534.9 5.5 collective-permute-done.34
  543.3 5.4 collective-permute-start.35
  549.9 20.8 %shard_map.190 = bf16[2048,2048]{1,0:T(8,128)(2,1)} custom-call(bf16[1536,1024]{1,0:T(8,128)(2,1)} %copy-done.37, bf16[1536,1024]{1,0:T(8,128)(2,1)} %copy-done.38, bf16[1536,2048]{1,0:T(8,128)(2,1)} %constant_dynamic-update-slice_fusion.5.b_ref), custom_call_target="tpu_custom_call" | custom-call | flops 1 | bytes 1 | tf_op jit(solution)/shard_map/pallas_call | solution.py:372
  570.8 11.9 %convolution_convert_fusion.3 = bf16[1536,2048]{1,0:T(8,128)(2,1)} fusion(bf16[1536,1024]{1,0:T(8,128)(2,1)} %get-tuple-element.186, bf16[2048,1024]{1,0:T(8,128)(2,1)} %all-gather.7.cloned.1.call-done), kind=kOutput, calls=%fused_computation.20 | convolution fusion | flops 6445596672 | bytes 13631488 | tf_op jit(solution)/shard_map/dot_general | solution.py:44
  582.7 13.2 %fusion.4 = (f32[1536]{0:T(1024)S(1)}, f32[1536]{0:T(1024)S(1)}, bf16[1536,2048]{1,0:T(8,128)(2,1)S(1)}) fusion(bf16[1536,2048]{1,0:T(8,128)(2,1)} %convolution_convert_fusion.3, bf16[1536,2048]{1,0:T(8,128)(2,1)} %copy-done.58, f32[1536]{0:T(1024)S(1)} %broadcast_select_fusion.8, f32[1536]{0:T(1024)S(1)} %broadcast_select_fusion.9, ...), kind=kOutput, calls=%fused_computation.14 | convolution fusion | flops 6480196608 | bytes 26238976 | tf_op jit(solution)/shard_map/dot_general | solution.py:44
  602.6 4.7 collective-permute-start.37
  608.7 6.3 add_convert_fusion.3
  615.0 20.8 %shard_map.191 = bf16[2048,2048]{1,0:T(8,128)(2,1)} custom-call(bf16[1536,1024]{1,0:T(8,128)(2,1)} %copy-done.36, bf16[1536,1024]{1,0:T(8,128)(2,1)} %get-tuple-element.86.u_ref, bf16[1536,2048]{1,0:T(8,128)(2,1)} %constant_dynamic-update-slice_fusion.5.b_ref), custom_call_target="tpu_custom_call" | custom-call | flops 1 | bytes 1 | tf_op jit(solution)/shard_map/pallas_call | solution.py:372
  639.5 5.5 collective-permute-start.39
  647.4 20.7 %all_to_all.34 = f32[8,2,192]{2,1,0:T(2,128)S(1)} all-to-all(f32[8,2,192]{2,1,0:T(2,128)S(1)} %bitcast.339), channel_id=1, replica_groups=mesh['q'=4,'c'=2,'z'=4] {'c','z'}, dimensions={0} | all-to-all | bytes 24576 | tf_op jit(solution)/shard_map/all_to_all | solution.py:620
  673.9 9.7 %collective-permute-done.49 = bf16[192,1024]{1,0:T(8,128)(2,1)S(1)} collective-permute-done((bf16[192,1024]{1,0:T(8,128)(2,1)S(1)}, bf16[192,1024]{1,0:T(8,128)(2,1)S(1)}, u32[]{:S(2)}, u32[]{:S(2)}) %collective-permute-start.49) | collective-permute-done | bytes 393248 | tf_op jit(solution)/shard_map/ppermute | solution.py:52
  689.4 13.0 %collective-permute-done.50 = bf16[2,192,1024]{2,1,0:T(8,128)(2,1)S(1)} collective-permute-done((bf16[2,192,1024]{2,1,0:T(8,128)(2,1)S(1)}, bf16[2,192,1024]{2,1,0:T(8,128)(2,1)S(1)}, u32[]{:S(2)}, u32[]{:S(2)}) %collective-permute-start.50) | collective-permute-done | bytes 786464 | tf_op jit(solution)/shard_map/ppermute | solution.py:52
  703.1 4.2 collective-permute-done.42
  716.1 3.8 collective-permute-start.43
  721.3 26.5 %shard_map.192 = (f32[1536,512]{1,0:T(8,128)}, bf16[1536,256]{1,0:T(8,128)(2,1)}, f32[8,1536]{1,0:T(8,128)}, f32[8,256]{1,0:T(8,128)}, f32[2048,256]{1,0:T(8,128)}) custom-call(f32[1536,768]{1,0:T(8,128)} %get-tuple-element.68.raw_ref, f32[8,1536]{1,0:T(8,128)} %pad.11.sum_ref, f32[8,256]{1,0:T(8,128)} %pad.12.gain_ref, f32[384,128]{1,0:T(8,128)} %bitcast.313, ...), custom_call_target="tpu_custom_call" | custom-call | flops 1 | bytes 1 | tf_op jit(solution)/shard_map/pallas_call | solution.py:349
  758.1 5.4 collective-permute-start.45
  765.6 13.2 %shard_map.193 = (bf16[1536,768]{1,0:T(8,128)(2,1)}, bf16[768,2048]{1,0:T(8,128)(2,1)}, bf16[768,2048]{1,0:T(8,128)(2,1)}) custom-call(f32[1536,768]{1,0:T(8,128)} %get-tuple-element.68.raw_ref, f32[8,1536]{1,0:T(8,128)} %pad.11.sum_ref, f32[1536,512]{1,0:T(8,128)} %get-tuple-element.97.back_ref, bf16[1536,256]{1,0:T(8,128)(2,1)} %get-tuple-element.98.dv_ref, ...), custom_call_target="tpu_custom_call" | custom-call | flops 1 | bytes 1 | tf_op jit(solution)/shard_map/pallas_call | solution.py:349
  779.2 4.8 collective-permute-done.46
  785.9 8.2 convolution_convert_fusion.6
  812.7 15.8 %collective-permute-done.61 = bf16[256,2048]{1,0:T(8,128)(2,1)S(1)} collective-permute-done((bf16[256,2048]{1,0:T(8,128)(2,1)S(1)}, bf16[256,2048]{1,0:T(8,128)(2,1)S(1)}, u32[]{:S(2)}, u32[]{:S(2)}) %collective-permute-start.61) | collective-permute-done | bytes 1048608 | tf_op jit(solution)/shard_map/ppermute | solution.py:111
  828.5 4.2 collective-permute-done.62
  836.7 4.6 collective-permute-start.63
  845.0 14.1 %collective-permute-done.64 = bf16[256,2048]{1,0:T(8,128)(2,1)S(1)} collective-permute-done((bf16[256,2048]{1,0:T(8,128)(2,1)S(1)}, bf16[256,2048]{1,0:T(8,128)(2,1)S(1)}, u32[]{:S(2)}, u32[]{:S(2)}) %collective-permute-start.64) | collective-permute-done | bytes 1048608 | tf_op jit(solution)/shard_map/ppermute | solution.py:111
  863.4 5.4 collective-permute-start.65
  875.7 3.7 all-to-all-start.4
  882.8 6.4 collective-permute-done.65
  889.3 5.6 collective-permute-done.66
  897.8 3.7 collective-permute-start.68
  901.5 3.6 collective-permute-start.69
  913.7 5.0 fusion.40
  926.4 3.9 maximum_convert_fusion
  (510 shorter events, 250.3 us)
Async XLA Ops:
  7.2 130.0 %all-gather.7.cloned.1.call-start = ((), (), s32[]{:S(2)}) async-start(), calls=%async_computation.9 | async-start | bytes 5242880 | tf_op jit(solution)/shard_map/all_gather | solution.py:496
  15.0 25.1 %collective-permute-start.6 = (bf16[64,2048]{1,0:T(8,128)(2,1)}, bf16[64,2048]{1,0:T(8,128)(2,1)}, u32[]{:S(2)}, u32[]{:S(2)}) collective-permute-start(bf16[64,2048]{1,0:T(8,128)(2,1)} %get-tuple-element.244), channel_id=1, source_target_pairs={{0,0},{1,1},{2,6},{3,11},{4,12},{5,13},{6,18},{7,23},{8,24},{9,25}... | collective-permute-start | bytes 786440 | tf_op jit(solution)/shard_map/ppermute | solution.py:418
  18.6 21.5 %collective-permute-start.7 = (bf16[64,2048]{1,0:T(8,128)(2,1)}, bf16[64,2048]{1,0:T(8,128)(2,1)}, u32[]{:S(2)}, u32[]{:S(2)}) collective-permute-start(bf16[64,2048]{1,0:T(8,128)(2,1)} %get-tuple-element.246), channel_id=1, source_target_pairs={{0,0},{1,5},{2,6},{3,11},{4,12},{5,17},{6,18},{7,23},{8,24},{9,29}... | collective-permute-start | bytes 786440 | tf_op jit(solution)/shard_map/ppermute | solution.py:418
  22.2 17.9 %collective-permute-start.8 = (bf16[64,2048]{1,0:T(8,128)(2,1)}, bf16[64,2048]{1,0:T(8,128)(2,1)}, u32[]{:S(2)}, u32[]{:S(2)}) collective-permute-start(bf16[64,2048]{1,0:T(8,128)(2,1)} %get-tuple-element.245), channel_id=1, source_target_pairs={{0,0},{1,5},{2,10},{3,11},{4,12},{5,17},{6,22},{7,23},{8,24},{9,29... | collective-permute-start | bytes 786440 | tf_op jit(solution)/shard_map/ppermute | solution.py:418
  37.2 262.6 %all-gather.15.cloned.1.call-start = ((), (), s32[]{:S(2)}) async-start(), calls=%async_computation.17 | async-start | bytes 3932160 | tf_op jit(solution)/shard_map/all_gather | solution.py:497
  38.3 18.5 %collective-permute-start.2 = (bf16[192,1024]{1,0:T(8,128)(2,1)}, bf16[192,1024]{1,0:T(8,128)(2,1)}, u32[]{:S(2)}, u32[]{:S(2)}) collective-permute-start(bf16[192,1024]{1,0:T(8,128)(2,1)} %get-tuple-element.251), channel_id=1, source_target_pairs={{0,16},{4,20},{8,24},{12,28},{16,0},{20,4},{24,8},{28,12},{1,17},{... | collective-permute-start | bytes 1179656 | tf_op jit(solution)/shard_map/ppermute | solution.py:52
  51.7 27.0 %collective-permute-start.10 = (bf16[192,2048]{1,0:T(8,128)(2,1)S(1)}, bf16[192,2048]{1,0:T(8,128)(2,1)}, u32[]{:S(2)}, u32[]{:S(2)}) collective-permute-start(bf16[192,2048]{1,0:T(8,128)(2,1)S(1)} %pad_maximum_fusion.15), channel_id=1, source_target_pairs={{0,1},{1,2},{2,3},{4,5},{5,6},{6,7},{8,9},{9,10},{10,11},{12,13},{... | collective-permute-start | bytes 2359304 | tf_op jit(solution)/shard_map/ppermute | solution.py:111
  54.2 24.5 %collective-permute-start.11 = (bf16[192,2048]{1,0:T(8,128)(2,1)S(1)}, bf16[192,2048]{1,0:T(8,128)(2,1)}, u32[]{:S(2)}, u32[]{:S(2)}) collective-permute-start(bf16[192,2048]{1,0:T(8,128)(2,1)S(1)} %pad_maximum_fusion.15), channel_id=1, source_target_pairs={{1,0},{2,1},{3,2},{5,4},{6,5},{7,6},{9,8},{10,9},{11,10},{13,12},{... | collective-permute-start | bytes 2359304 | tf_op jit(solution)/shard_map/ppermute | solution.py:111
  55.5 20.7 %collective-permute-start = (bf16[192,1024]{1,0:T(8,128)(2,1)}, bf16[192,1024]{1,0:T(8,128)(2,1)S(1)}, u32[]{:S(2)}, u32[]{:S(2)}) collective-permute-start(bf16[192,1024]{1,0:T(8,128)(2,1)} %get-tuple-element.252), channel_id=1, source_target_pairs={{0,8},{4,12},{8,0},{12,4},{16,24},{20,28},{24,16},{28,20},{1,9},{5... | collective-permute-start | bytes 1179656 | tf_op jit(solution)/shard_map/ppermute | solution.py:52
  58.8 41.7 %collective-permute-start.3 = (bf16[2,192,1024]{2,1,0:T(8,128)(2,1)}, bf16[2,192,1024]{2,1,0:T(8,128)(2,1)}, u32[]{:S(2)}, u32[]{:S(2)}) collective-permute-start(bf16[2,192,1024]{2,1,0:T(8,128)(2,1)} %get-tuple-element.248), channel_id=1, source_target_pairs={{0,8},{4,12},{8,0},{12,4},{16,24},{20,28},{24,16},{28,20},{1,9},{5... | collective-permute-start | bytes 2359304 | tf_op jit(solution)/shard_map/ppermute | solution.py:52
  77.4 24.5 %collective-permute-start.1 = (bf16[2,192,1024]{2,1,0:T(8,128)(2,1)}, bf16[2,192,1024]{2,1,0:T(8,128)(2,1)}, u32[]{:S(2)}, u32[]{:S(2)}) collective-permute-start(bf16[2,192,1024]{2,1,0:T(8,128)(2,1)} %get-tuple-element.254), channel_id=1, source_target_pairs={{0,16},{4,20},{8,24},{12,28},{16,0},{20,4},{24,8},{28,12},{1,17},{... | collective-permute-start | bytes 2359304 | tf_op jit(solution)/shard_map/ppermute | solution.py:52
  78.7 26.3 %collective-permute-start.12 = (bf16[192,2048]{1,0:T(8,128)(2,1)}, bf16[192,2048]{1,0:T(8,128)(2,1)}, u32[]{:S(2)}, u32[]{:S(2)}) collective-permute-start(bf16[192,2048]{1,0:T(8,128)(2,1)} %collective-permute-done.10), channel_id=1, source_target_pairs={{0,1},{1,2},{2,3},{4,5},{5,6},{6,7},{8,9},{9,10},{10,11},{12,13},{... | collective-permute-start | bytes 2359304 | tf_op jit(solution)/shard_map/ppermute | solution.py:111
  84.1 20.9 %collective-permute-start.13 = (bf16[192,2048]{1,0:T(8,128)(2,1)}, bf16[192,2048]{1,0:T(8,128)(2,1)}, u32[]{:S(2)}, u32[]{:S(2)}) collective-permute-start(bf16[192,2048]{1,0:T(8,128)(2,1)} %collective-permute-done.11), channel_id=1, source_target_pairs={{1,0},{2,1},{3,2},{5,4},{6,5},{7,6},{9,8},{10,9},{11,10},{13,12},{... | collective-permute-start | bytes 2359304 | tf_op jit(solution)/shard_map/ppermute | solution.py:111
  105.0 21.6 %collective-permute-start.14 = (bf16[192,2048]{1,0:T(8,128)(2,1)}, bf16[192,2048]{1,0:T(8,128)(2,1)}, u32[]{:S(2)}, u32[]{:S(2)}) collective-permute-start(bf16[192,2048]{1,0:T(8,128)(2,1)} %collective-permute-done.13), channel_id=1, source_target_pairs={{1,0},{2,1},{3,2},{5,4},{6,5},{7,6},{9,8},{10,9},{11,10},{13,12},{... | collective-permute-start | bytes 2359304 | tf_op jit(solution)/shard_map/ppermute | solution.py:111
  112.6 29.0 %collective-permute-start.5 = (bf16[768,1024]{1,0:T(8,128)(2,1)S(1)}, bf16[768,1024]{1,0:T(8,128)(2,1)}, u32[]{:S(2)}, u32[]{:S(2)}) collective-permute-start(bf16[768,1024]{1,0:T(8,128)(2,1)S(1)} %bitcast.289), channel_id=1, source_target_pairs={{0,4},{4,0},{8,12},{12,8},{16,20},{20,16},{24,28},{28,24},{1,5},{5... | collective-permute-start | bytes 4718600 | tf_op jit(solution)/shard_map/ppermute | solution.py:52
  112.6 29.0 %collective-permute-start.4 = (bf16[768,1024]{1,0:T(8,128)(2,1)}, bf16[768,1024]{1,0:T(8,128)(2,1)}, u32[]{:S(2)}, u32[]{:S(2)}) collective-permute-start(bf16[768,1024]{1,0:T(8,128)(2,1)} %bitcast.4.a_own), channel_id=1, source_target_pairs={{0,4},{4,0},{8,12},{12,8},{16,20},{20,16},{24,28},{28,24},{1,5},{5... | collective-permute-start | bytes 4718600 | tf_op jit(solution)/shard_map/ppermute | solution.py:52
  113.1 21.8 %collective-permute-start.15 = (bf16[192,2048]{1,0:T(8,128)(2,1)}, bf16[192,2048]{1,0:T(8,128)(2,1)S(1)}, u32[]{:S(2)}, u32[]{:S(2)}) collective-permute-start(bf16[192,2048]{1,0:T(8,128)(2,1)} %collective-permute-done.12), channel_id=1, source_target_pairs={{0,1},{1,2},{2,3},{4,5},{5,6},{6,7},{8,9},{9,10},{10,11},{12,13},{... | collective-permute-start | bytes 2359304 | tf_op jit(solution)/shard_map/ppermute | solution.py:111
  137.2 260.6 %all-gather.9.cloned.1.call-start = ((), (), s32[]{:S(2)}) async-start(), calls=%async_computation.10 | async-start | bytes 10485760 | tf_op jit(solution)/shard_map/all_gather | solution.py:541
  166.2 54.1 %all-to-all-start.1 = ((bf16[32,64,256]{2,1,0:T(8,128)(2,1)}), bf16[32,64,256]{2,1,0:T(8,128)(2,1)S(1)}, u32[]{:S(2)}, u32[]{:S(2)}) async-start(bf16[32,64,256]{2,1,0:T(8,128)(2,1)} %bitcast.298), calls=%async_computation.1 | async-start | bytes 2097152 | tf_op jit(solution)/shard_map/all_to_all | solution.py:493
  171.5 293.2 %all-gather.11.cloned.1.call-start = ((), (), s32[]{:S(2)}) async-start(), calls=%async_computation.11 | async-start | bytes 10485760 | tf_op jit(solution)/shard_map/all_gather | solution.py:541
  250.6 26.7 %collective-permute-start.20 = (bf16[2,192,1024]{2,1,0:T(8,128)(2,1)S(1)}, bf16[2,192,1024]{2,1,0:T(8,128)(2,1)S(1)}, u32[]{:S(2)}, u32[]{:S(2)}) collective-permute-start(bf16[2,192,1024]{2,1,0:T(8,128)(2,1)S(1)} %slice_bitcast_fusion.6), channel_id=1, source_target_pairs={{0,8},{4,12},{8,0},{12,4},{16,24},{20,28},{24,16},{28,20},{1,9},{5... | collective-permute-start | bytes 2359304 | tf_op jit(solution)/shard_map/ppermute | solution.py:52
  252.2 27.0 %collective-permute-start.22 = (bf16[2,192,1024]{2,1,0:T(8,128)(2,1)S(1)}, bf16[2,192,1024]{2,1,0:T(8,128)(2,1)S(1)}, u32[]{:S(2)}, u32[]{:S(2)}) collective-permute-start(bf16[2,192,1024]{2,1,0:T(8,128)(2,1)S(1)} %bitcast.326), channel_id=1, source_target_pairs={{0,16},{4,20},{8,24},{12,28},{16,0},{20,4},{24,8},{28,12},{1,17},{... | collective-permute-start | bytes 2359304 | tf_op jit(solution)/shard_map/ppermute | solution.py:52
  277.7 20.2 %collective-permute-start.21 = (bf16[192,1024]{1,0:T(8,128)(2,1)S(1)}, bf16[192,1024]{1,0:T(8,128)(2,1)}, u32[]{:S(2)}, u32[]{:S(2)}) collective-permute-start(bf16[192,1024]{1,0:T(8,128)(2,1)S(1)} %slice_bitcast_fusion.18), channel_id=1, source_target_pairs={{0,16},{4,20},{8,24},{12,28},{16,0},{20,4},{24,8},{28,12},{1,17},{... | collective-permute-start | bytes 1179656 | tf_op jit(solution)/shard_map/ppermute | solution.py:52
  279.5 20.1 %collective-permute-start.23 = (bf16[192,1024]{1,0:T(8,128)(2,1)S(1)}, bf16[192,1024]{1,0:T(8,128)(2,1)}, u32[]{:S(2)}, u32[]{:S(2)}) collective-permute-start(bf16[192,1024]{1,0:T(8,128)(2,1)S(1)} %slice_bitcast_fusion.16), channel_id=1, source_target_pairs={{0,8},{4,12},{8,0},{12,4},{16,24},{20,28},{24,16},{28,20},{1,9},{5... | collective-permute-start | bytes 1179656 | tf_op jit(solution)/shard_map/ppermute | solution.py:52
  299.7 184.2 %all-gather.13.cloned.1.call-start = ((), (), s32[]{:S(2)}) async-start(), calls=%async_computation.12 | async-start | bytes 5242880 | tf_op jit(solution)/shard_map/all_gather | solution.py:542
  312.1 20.9 %collective-permute-start.24 = (bf16[192,2048]{1,0:T(8,128)(2,1)S(1)}, bf16[192,2048]{1,0:T(8,128)(2,1)S(1)}, u32[]{:S(2)}, u32[]{:S(2)}) collective-permute-start(bf16[192,2048]{1,0:T(8,128)(2,1)S(1)} %get-tuple-element.177), channel_id=1, source_target_pairs={{0,1},{1,2},{2,3},{4,5},{5,6},{6,7},{8,9},{9,10},{10,11},{12,13},{... | collective-permute-start | bytes 2359304 | tf_op jit(solution)/shard_map/ppermute | solution.py:111
  315.8 21.6 %collective-permute-start.25 = (bf16[192,2048]{1,0:T(8,128)(2,1)S(1)}, bf16[192,2048]{1,0:T(8,128)(2,1)S(1)}, u32[]{:S(2)}, u32[]{:S(2)}) collective-permute-start(bf16[192,2048]{1,0:T(8,128)(2,1)S(1)} %get-tuple-element.177), channel_id=1, source_target_pairs={{1,0},{2,1},{3,2},{5,4},{6,5},{7,6},{9,8},{10,9},{11,10},{13,12},{... | collective-permute-start | bytes 2359304 | tf_op jit(solution)/shard_map/ppermute | solution.py:111
  337.4 20.7 %collective-permute-start.27 = (bf16[192,2048]{1,0:T(8,128)(2,1)S(1)}, bf16[192,2048]{1,0:T(8,128)(2,1)S(1)}, u32[]{:S(2)}, u32[]{:S(2)}) collective-permute-start(bf16[192,2048]{1,0:T(8,128)(2,1)S(1)} %collective-permute-done.25), channel_id=1, source_target_pairs={{1,0},{2,1},{3,2},{5,4},{6,5},{7,6},{9,8},{10,9},{11,10},{13,12},{... | collective-permute-start | bytes 2359304 | tf_op jit(solution)/shard_map/ppermute | solution.py:111
  338.7 20.7 %collective-permute-start.29 = (bf16[192,2048]{1,0:T(8,128)(2,1)S(1)}, bf16[192,2048]{1,0:T(8,128)(2,1)S(1)}, u32[]{:S(2)}, u32[]{:S(2)}) collective-permute-start(bf16[192,2048]{1,0:T(8,128)(2,1)S(1)} %collective-permute-done.24), channel_id=1, source_target_pairs={{0,1},{1,2},{2,3},{4,5},{5,6},{6,7},{8,9},{9,10},{10,11},{12,13},{... | collective-permute-start | bytes 2359304 | tf_op jit(solution)/shard_map/ppermute | solution.py:111
  358.1 19.9 %collective-permute-start.28 = (bf16[192,2048]{1,0:T(8,128)(2,1)S(1)}, bf16[192,2048]{1,0:T(8,128)(2,1)S(1)}, u32[]{:S(2)}, u32[]{:S(2)}) collective-permute-start(bf16[192,2048]{1,0:T(8,128)(2,1)S(1)} %collective-permute-done.27), channel_id=1, source_target_pairs={{1,0},{2,1},{3,2},{5,4},{6,5},{7,6},{9,8},{10,9},{11,10},{13,12},{... | collective-permute-start | bytes 2359304 | tf_op jit(solution)/shard_map/ppermute | solution.py:111
  359.4 19.8 %collective-permute-start.30 = (bf16[192,2048]{1,0:T(8,128)(2,1)S(1)}, bf16[192,2048]{1,0:T(8,128)(2,1)S(1)}, u32[]{:S(2)}, u32[]{:S(2)}) collective-permute-start(bf16[192,2048]{1,0:T(8,128)(2,1)S(1)} %collective-permute-done.29), channel_id=1, source_target_pairs={{0,1},{1,2},{2,3},{4,5},{5,6},{6,7},{8,9},{9,10},{10,11},{12,13},{... | collective-permute-start | bytes 2359304 | tf_op jit(solution)/shard_map/ppermute | solution.py:111
  387.4 398.6 %reduce-scatter.5.cloned.1.call-start = ((), (), s32[]{:S(2)}) async-start(), calls=%async_computation.13 | async-start | bytes 5242880 | tf_op jit(solution)/shard_map/reduce_scatter | solution.py:595
  464.6 331.3 %reduce-scatter.7.cloned.1.call-start = ((), (), s32[]{:S(2)}) async-start(), calls=%async_computation.14 | async-start | bytes 5242880 | tf_op jit(solution)/shard_map/reduce_scatter | solution.py:595
  516.5 362.9 %reduce-scatter.9.cloned.1.call-start = ((), (), s32[]{:S(2)}) async-start(), calls=%async_computation.15 | async-start | bytes 10485760 | tf_op jit(solution)/shard_map/reduce_scatter | solution.py:655
  543.3 27.4 %collective-permute-start.35 = (bf16[192,2048]{1,0:T(8,128)(2,1)}, bf16[192,2048]{1,0:T(8,128)(2,1)}, u32[]{:S(2)}, u32[]{:S(2)}) collective-permute-start(bf16[192,2048]{1,0:T(8,128)(2,1)} %get-tuple-element.213), channel_id=1, source_target_pairs={{0,1},{1,2},{2,3},{4,5},{5,6},{6,7},{8,9},{9,10},{10,11},{12,13},{... | collective-permute-start | bytes 2359304 | tf_op jit(solution)/shard_map/ppermute | solution.py:111
  548.6 22.1 %collective-permute-start.36 = (bf16[192,2048]{1,0:T(8,128)(2,1)}, bf16[192,2048]{1,0:T(8,128)(2,1)}, u32[]{:S(2)}, u32[]{:S(2)}) collective-permute-start(bf16[192,2048]{1,0:T(8,128)(2,1)} %get-tuple-element.212), channel_id=1, source_target_pairs={{1,0},{2,1},{3,2},{5,4},{6,5},{7,6},{9,8},{10,9},{11,10},{13,12},{... | collective-permute-start | bytes 2359304 | tf_op jit(solution)/shard_map/ppermute | solution.py:111
  570.7 308.7 %reduce-scatter.11.cloned.1.call-start = ((), (), s32[]{:S(2)}) async-start(), calls=%async_computation.16 | async-start | bytes 10485760 | tf_op jit(solution)/shard_map/reduce_scatter | solution.py:655
  602.6 33.4 %collective-permute-start.37 = (bf16[192,2048]{1,0:T(8,128)(2,1)}, bf16[192,2048]{1,0:T(8,128)(2,1)S(1)}, u32[]{:S(2)}, u32[]{:S(2)}) collective-permute-start(bf16[192,2048]{1,0:T(8,128)(2,1)} %get-tuple-element.83), channel_id=1, source_target_pairs={{0,1},{1,2},{2,3},{4,5},{5,6},{6,7},{8,9},{9,10},{10,11},{12,13},{... | collective-permute-start | bytes 2359304 | tf_op jit(solution)/shard_map/ppermute | solution.py:111
  607.3 28.6 %collective-permute-start.38 = (bf16[192,2048]{1,0:T(8,128)(2,1)}, bf16[192,2048]{1,0:T(8,128)(2,1)}, u32[]{:S(2)}, u32[]{:S(2)}) collective-permute-start(bf16[192,2048]{1,0:T(8,128)(2,1)} %get-tuple-element.84), channel_id=1, source_target_pairs={{1,0},{2,1},{3,2},{5,4},{6,5},{7,6},{9,8},{10,9},{11,10},{13,12},{... | collective-permute-start | bytes 2359304 | tf_op jit(solution)/shard_map/ppermute | solution.py:111
  639.5 28.7 %collective-permute-start.39 = (bf16[192,2048]{1,0:T(8,128)(2,1)}, bf16[192,2048]{1,0:T(8,128)(2,1)}, u32[]{:S(2)}, u32[]{:S(2)}) collective-permute-start(bf16[192,2048]{1,0:T(8,128)(2,1)} %get-tuple-element.87), channel_id=1, source_target_pairs={{0,1},{1,2},{2,3},{4,5},{5,6},{6,7},{8,9},{9,10},{10,11},{12,13},{... | collective-permute-start | bytes 2359304 | tf_op jit(solution)/shard_map/ppermute | solution.py:111
  645.0 23.2 %collective-permute-start.40 = (bf16[192,2048]{1,0:T(8,128)(2,1)}, bf16[192,2048]{1,0:T(8,128)(2,1)}, u32[]{:S(2)}, u32[]{:S(2)}) collective-permute-start(bf16[192,2048]{1,0:T(8,128)(2,1)} %get-tuple-element.88), channel_id=1, source_target_pairs={{1,0},{2,1},{3,2},{5,4},{6,5},{7,6},{9,8},{10,9},{11,10},{13,12},{... | collective-permute-start | bytes 2359304 | tf_op jit(solution)/shard_map/ppermute | solution.py:111
  683.7 18.7 %collective-permute-start.50 = (bf16[2,192,1024]{2,1,0:T(8,128)(2,1)S(1)}, bf16[2,192,1024]{2,1,0:T(8,128)(2,1)S(1)}, u32[]{:S(2)}, u32[]{:S(2)}) collective-permute-start(bf16[2,192,1024]{2,1,0:T(8,128)(2,1)S(1)} %get-tuple-element.237), channel_id=1, source_target_pairs={{0,8},{4,12},{8,0},{12,4},{16,24},{20,28},{24,16},{28,20},{1,9},{5... | collective-permute-start | bytes 2359304 | tf_op jit(solution)/shard_map/ppermute | solution.py:52
  684.8 18.3 %collective-permute-start.41 = (bf16[192,2048]{1,0:T(8,128)(2,1)S(1)}, bf16[192,2048]{1,0:T(8,128)(2,1)S(1)}, u32[]{:S(2)}, u32[]{:S(2)}) collective-permute-start(bf16[192,2048]{1,0:T(8,128)(2,1)S(1)} %get-tuple-element.207), channel_id=1, source_target_pairs={{0,1},{1,2},{2,3},{4,5},{5,6},{6,7},{8,9},{9,10},{10,11},{12,13},{... | collective-permute-start | bytes 2359304 | tf_op jit(solution)/shard_map/ppermute | solution.py:111
  687.2 20.0 %collective-permute-start.42 = (bf16[192,2048]{1,0:T(8,128)(2,1)S(1)}, bf16[192,2048]{1,0:T(8,128)(2,1)S(1)}, u32[]{:S(2)}, u32[]{:S(2)}) collective-permute-start(bf16[192,2048]{1,0:T(8,128)(2,1)S(1)} %get-tuple-element.206), channel_id=1, source_target_pairs={{1,0},{2,1},{3,2},{5,4},{6,5},{7,6},{9,8},{10,9},{11,10},{13,12},{... | collective-permute-start | bytes 2359304 | tf_op jit(solution)/shard_map/ppermute | solution.py:111
  688.7 18.6 %collective-permute-start.48 = (bf16[2,192,1024]{2,1,0:T(8,128)(2,1)S(1)}, bf16[2,192,1024]{2,1,0:T(8,128)(2,1)S(1)}, u32[]{:S(2)}, u32[]{:S(2)}) collective-permute-start(bf16[2,192,1024]{2,1,0:T(8,128)(2,1)S(1)} %get-tuple-element.243), channel_id=1, source_target_pairs={{0,16},{4,20},{8,24},{12,28},{16,0},{20,4},{24,8},{28,12},{1,17},{... | collective-permute-start | bytes 2359304 | tf_op jit(solution)/shard_map/ppermute | solution.py:52
  716.1 31.6 %collective-permute-start.43 = (bf16[192,2048]{1,0:T(8,128)(2,1)}, bf16[192,2048]{1,0:T(8,128)(2,1)}, u32[]{:S(2)}, u32[]{:S(2)}) collective-permute-start(bf16[192,2048]{1,0:T(8,128)(2,1)} %get-tuple-element.90), channel_id=1, source_target_pairs={{0,1},{1,2},{2,3},{4,5},{5,6},{6,7},{8,9},{9,10},{10,11},{12,13},{... | collective-permute-start | bytes 2359304 | tf_op jit(solution)/shard_map/ppermute | solution.py:111
  720.0 27.8 %collective-permute-start.44 = (bf16[192,2048]{1,0:T(8,128)(2,1)}, bf16[192,2048]{1,0:T(8,128)(2,1)}, u32[]{:S(2)}, u32[]{:S(2)}) collective-permute-start(bf16[192,2048]{1,0:T(8,128)(2,1)} %get-tuple-element.91), channel_id=1, source_target_pairs={{1,0},{2,1},{3,2},{5,4},{6,5},{7,6},{9,8},{10,9},{11,10},{13,12},{... | collective-permute-start | bytes 2359304 | tf_op jit(solution)/shard_map/ppermute | solution.py:111
  758.1 21.1 %collective-permute-start.45 = (bf16[192,2048]{1,0:T(8,128)(2,1)}, bf16[192,2048]{1,0:T(8,128)(2,1)}, u32[]{:S(2)}, u32[]{:S(2)}) collective-permute-start(bf16[192,2048]{1,0:T(8,128)(2,1)} %get-tuple-element.92), channel_id=1, source_target_pairs={{0,1},{1,2},{2,3},{4,5},{5,6},{6,7},{8,9},{9,10},{10,11},{12,13},{... | collective-permute-start | bytes 2359304 | tf_op jit(solution)/shard_map/ppermute | solution.py:111
  763.5 20.5 %collective-permute-start.46 = (bf16[192,2048]{1,0:T(8,128)(2,1)}, bf16[192,2048]{1,0:T(8,128)(2,1)}, u32[]{:S(2)}, u32[]{:S(2)}) collective-permute-start(bf16[192,2048]{1,0:T(8,128)(2,1)} %get-tuple-element.93), channel_id=1, source_target_pairs={{1,0},{2,1},{3,2},{5,4},{6,5},{7,6},{9,8},{10,9},{11,10},{13,12},{... | collective-permute-start | bytes 2359304 | tf_op jit(solution)/shard_map/ppermute | solution.py:111
  778.7 20.7 %collective-permute-start.56 = (bf16[768,2048]{1,0:T(8,128)(2,1)}, bf16[768,2048]{1,0:T(8,128)(2,1)}, u32[]{:S(2)}, u32[]{:S(2)}) collective-permute-start(bf16[768,2048]{1,0:T(8,128)(2,1)} %get-tuple-element.102), channel_id=1, source_target_pairs={{0,4},{4,0},{8,12},{12,8},{16,20},{20,16},{24,28},{28,24},{1,5},{5... | collective-permute-start | bytes 9437192 | tf_op jit(solution)/shard_map/ppermute | solution.py:52
  804.5 24.0 %collective-permute-start.61 = (bf16[256,2048]{1,0:T(8,128)(2,1)S(1)}, bf16[256,2048]{1,0:T(8,128)(2,1)S(1)}, u32[]{:S(2)}, u32[]{:S(2)}) collective-permute-start(bf16[256,2048]{1,0:T(8,128)(2,1)S(1)} %get-tuple-element.106), channel_id=1, source_target_pairs={{0,1},{1,2},{2,3},{4,5},{5,6},{6,7},{8,9},{9,10},{10,11},{12,13},{... | collective-permute-start | bytes 3145736 | tf_op jit(solution)/shard_map/ppermute | solution.py:111
  806.1 26.6 %collective-permute-start.62 = (bf16[256,2048]{1,0:T(8,128)(2,1)S(1)}, bf16[256,2048]{1,0:T(8,128)(2,1)S(1)}, u32[]{:S(2)}, u32[]{:S(2)}) collective-permute-start(bf16[256,2048]{1,0:T(8,128)(2,1)S(1)} %get-tuple-element.107), channel_id=1, source_target_pairs={{1,0},{2,1},{3,2},{5,4},{6,5},{7,6},{9,8},{10,9},{11,10},{13,12},{... | collective-permute-start | bytes 3145736 | tf_op jit(solution)/shard_map/ppermute | solution.py:111
  810.0 24.6 %collective-permute-start.57 = (bf16[2,192,1024]{2,1,0:T(8,128)(2,1)S(1)}, bf16[2,192,1024]{2,1,0:T(8,128)(2,1)S(1)}, u32[]{:S(2)}, u32[]{:S(2)}) collective-permute-start(bf16[2,192,1024]{2,1,0:T(8,128)(2,1)S(1)} %slice_bitcast_fusion.4), channel_id=1, source_target_pairs={{0,8},{4,12},{8,0},{12,4},{16,24},{20,28},{24,16},{28,20},{1,9},{5... | collective-permute-start | bytes 2359304 | tf_op jit(solution)/shard_map/ppermute | solution.py:52
  811.3 30.0 %collective-permute-start.59 = (bf16[2,192,1024]{2,1,0:T(8,128)(2,1)S(1)}, bf16[2,192,1024]{2,1,0:T(8,128)(2,1)S(1)}, u32[]{:S(2)}, u32[]{:S(2)}) collective-permute-start(bf16[2,192,1024]{2,1,0:T(8,128)(2,1)S(1)} %bitcast.323), channel_id=1, source_target_pairs={{0,16},{4,20},{8,24},{12,28},{16,0},{20,4},{24,8},{28,12},{1,17},{... | collective-permute-start | bytes 2359304 | tf_op jit(solution)/shard_map/ppermute | solution.py:52
  833.3 25.8 %collective-permute-start.64 = (bf16[256,2048]{1,0:T(8,128)(2,1)S(1)}, bf16[256,2048]{1,0:T(8,128)(2,1)S(1)}, u32[]{:S(2)}, u32[]{:S(2)}) collective-permute-start(bf16[256,2048]{1,0:T(8,128)(2,1)S(1)} %get-tuple-element.109), channel_id=1, source_target_pairs={{1,0},{2,1},{3,2},{5,4},{6,5},{7,6},{9,8},{10,9},{11,10},{13,12},{... | collective-permute-start | bytes 3145736 | tf_op jit(solution)/shard_map/ppermute | solution.py:111
  836.7 25.3 %collective-permute-start.63 = (bf16[256,2048]{1,0:T(8,128)(2,1)S(1)}, bf16[256,2048]{1,0:T(8,128)(2,1)S(1)}, u32[]{:S(2)}, u32[]{:S(2)}) collective-permute-start(bf16[256,2048]{1,0:T(8,128)(2,1)S(1)} %get-tuple-element.108), channel_id=1, source_target_pairs={{0,1},{1,2},{2,3},{4,5},{5,6},{6,7},{8,9},{9,10},{10,11},{12,13},{... | collective-permute-start | bytes 3145736 | tf_op jit(solution)/shard_map/ppermute | solution.py:111
  841.7 28.6 %collective-permute-start.60 = (bf16[192,1024]{1,0:T(8,128)(2,1)S(1)}, bf16[192,1024]{1,0:T(8,128)(2,1)S(1)}, u32[]{:S(2)}, u32[]{:S(2)}) collective-permute-start(bf16[192,1024]{1,0:T(8,128)(2,1)S(1)} %slice_bitcast_fusion.12), channel_id=1, source_target_pairs={{0,8},{4,12},{8,0},{12,4},{16,24},{20,28},{24,16},{28,20},{1,9},{5... | collective-permute-start | bytes 1179656 | tf_op jit(solution)/shard_map/ppermute | solution.py:52
  863.4 25.9 %collective-permute-start.65 = (bf16[256,2048]{1,0:T(8,128)(2,1)}, bf16[256,2048]{1,0:T(8,128)(2,1)}, u32[]{:S(2)}, u32[]{:S(2)}) collective-permute-start(bf16[256,2048]{1,0:T(8,128)(2,1)} %add_convert_fusion.6), channel_id=1, source_target_pairs={{0,1},{1,2},{2,3},{4,5},{5,6},{6,7},{8,9},{9,10},{10,11},{12,13},{... | collective-permute-start | bytes 3145736 | tf_op jit(solution)/shard_map/ppermute | solution.py:111
  868.8 26.0 %collective-permute-start.66 = (bf16[256,2048]{1,0:T(8,128)(2,1)}, bf16[256,2048]{1,0:T(8,128)(2,1)}, u32[]{:S(2)}, u32[]{:S(2)}) collective-permute-start(bf16[256,2048]{1,0:T(8,128)(2,1)} %add_convert_fusion.5), channel_id=1, source_target_pairs={{1,0},{2,1},{3,2},{5,4},{6,5},{7,6},{9,8},{10,9},{11,10},{13,12},{... | collective-permute-start | bytes 3145736 | tf_op jit(solution)/shard_map/ppermute | solution.py:111
  875.7 33.9 %all-to-all-start.4 = ((f32[32,1,1280]{2,1,0:T(1,128)}), f32[32,1,1280]{2,1,0:T(1,128)S(1)}, u32[]{:S(2)}, u32[]{:S(2)}) async-start(f32[32,1,1280]{2,1,0:T(1,128)} %all_to_all.28), calls=%async_computation.6 | async-start | bytes 327680 | tf_op jit(solution)/shard_map/all_to_all | solution.py:729
  882.6 42.1 %collective-permute-start.71 = (bf16[2,256,2048]{2,1,0:T(8,128)(2,1)}, bf16[2,256,2048]{2,1,0:T(8,128)(2,1)}, u32[]{:S(2)}, u32[]{:S(2)}) collective-permute-start(bf16[2,256,2048]{2,1,0:T(8,128)(2,1)} %fusion.28), channel_id=1, source_target_pairs={{0,4},{4,0},{1,5},{5,1},{2,6},{6,2},{3,7},{7,3},{8,12},{12,8},{9,1... | collective-permute-start | bytes 6291464 | tf_op jit(solution)/shard_map/ppermute | solution.py:151
  897.8 24.4 %collective-permute-start.68 = (bf16[64,2048]{1,0:T(8,128)(2,1)}, bf16[64,2048]{1,0:T(8,128)(2,1)}, u32[]{:S(2)}, u32[]{:S(2)}) collective-permute-start(bf16[64,2048]{1,0:T(8,128)(2,1)} %get-tuple-element.230), channel_id=1, source_target_pairs={{0,0},{1,1},{6,2},{11,3},{12,4},{13,5},{18,6},{23,7},{24,8},{25,9}... | collective-permute-start | bytes 786440 | tf_op jit(solution)/shard_map/ppermute | solution.py:711
  901.5 20.7 %collective-permute-start.69 = (bf16[64,2048]{1,0:T(8,128)(2,1)}, bf16[64,2048]{1,0:T(8,128)(2,1)}, u32[]{:S(2)}, u32[]{:S(2)}) collective-permute-start(bf16[64,2048]{1,0:T(8,128)(2,1)} %get-tuple-element.229), channel_id=1, source_target_pairs={{0,0},{5,1},{6,2},{11,3},{12,4},{17,5},{18,6},{23,7},{24,8},{29,9}... | collective-permute-start | bytes 786440 | tf_op jit(solution)/shard_map/ppermute | solution.py:711
  905.1 17.1 %collective-permute-start.70 = (bf16[64,2048]{1,0:T(8,128)(2,1)}, bf16[64,2048]{1,0:T(8,128)(2,1)}, u32[]{:S(2)}, u32[]{:S(2)}) collective-permute-start(bf16[64,2048]{1,0:T(8,128)(2,1)} %get-tuple-element.228), channel_id=1, source_target_pairs={{0,0},{5,1},{10,2},{11,3},{12,4},{17,5},{22,6},{23,7},{24,8},{29,9... | collective-permute-start | bytes 786440 | tf_op jit(solution)/shard_map/ppermute | solution.py:711
  (104 other events, 1594.9 us)
Sparse Core Ops, SparseCore 0:
  14.2 77.5 all-gather.6
  137.3 86.3 all-gather.14
  225.6 103.7 all-gather.8
  331.0 87.4 all-gather.10
  420.2 52.5 all-gather.12
  476.2 52.5 reduce-scatter.4
  531.8 52.5 reduce-scatter.6
  588.1 86.3 reduce-scatter.8
  713.2 84.4 reduce-scatter.10

commit v7 on v6

--- a/solution.py
+++ b/solution.py
@@ -493,8 +493,8 @@
     w_out_c = lax.all_to_all(
         out_cols.reshape(world, orow, width), ALL, 0, 0, tiled=True
     ).reshape(D, width)
-    first_down = lax.all_gather(down_half[0], "q", axis=0, tiled=True)
-    dy_all = lax.all_gather(after(cotangent, first_down, *slot_steps[-1]), "z", axis=0)
+    first_down = lax.all_gather(after(down_half[0], *slot_steps[1]), "q", axis=0, tiled=True)
+    dy_all = lax.all_gather(cotangent, "z", axis=0)
     dy_blocks = [
         lax.dynamic_index_in_dim(dy_all, (zi - k) % zs, 0, keepdims=False) for k in range(zs)
     ]
@@ -515,7 +515,7 @@
             shape_of(all_rows, 3 * width, f32),
             shape_of(8, all_rows, f32),
         ],
-        tuple(tok_pieces) + (gains_f[:, 0][None], w_three),
+        tuple(tok_pieces) + (after(gains_f[:, 0][None], dy_all), w_three),
     )
     gu_half = core_half(after(w_gate_up, hidden_one))
     sums = sum_dp(sums, dps)

time: 947 us -> 975 us (1.030)
  waiting for transfers between devices: 280 us -> 315 us
    ppermute x30, waiting for transfers between devices: 115 us -> 154 us  [line(): lax.ppermute(value, 'z', [(j, j + step) for j in range(zs) if 0 <= j + st...]
    all_to_all x1, waiting for transfers between devices: 37.6 us -> 8.99 us  [per_device(): lax.all_to_all(out_cols.reshape(world, orow, width), ALL, 0, 0, tiled=True)]
    all_gather x1, waiting for transfers between devices: 0.01 us -> 19.2 us  [per_device(): lax.all_gather(down_half[e], 'q', axis=0, tiled=True)]
    unnamed x180 -> x178, local copies, waits for them, and re-layouts: 23.9 us -> 20.4 us
  transfers between devices with their start and end apart: 85 -> 85, of which waited for: 37 -> 42; matrix products, arithmetic and copies ran while one was open for 34% -> 32% of each run, Pallas kernels for 12% -> 10%
where the time goes in v7:
time: 975 us; the launch traced here: 964 us
  waiting for transfers between devices  315 us (32%)
  matrix products  175 us (18%)
  starting transfers between devices  156 us (16%)
  Pallas kernels  113 us (12%)
  other arithmetic  96 us (10%)
  local copies, waits for them, and re-layouts  70.6 us (7%)
  between operations  22.3 us (2%)
  blocking collectives  15.1 us (2%)
    dot_general x13, matrix products, mm(): lax.dot_general(a, b, (((ca,), (cb,)), ((), ())), preferred_element_type=...  172 us
    ppermute x30, waiting for transfers between devices, line(): lax.ppermute(value, 'z', [(j, j + step) for j in range(zs) if 0 <= j + st...  154 us
    ppermute x28, waiting for transfers between devices, flip(): return lax.ppermute(value, DP, [(i, i ^ 1 << bit) for i in range(size)])  117 us
    ppermute x30, starting transfers between devices, line(): lax.ppermute(value, 'z', [(j, j + step) for j in range(zs) if 0 <= j + st...  87.5 us
    pallas_call x4, Pallas kernels, run_blocks(): pl.pallas_call(body, grid=(rows // BLOCK,), in_specs=in_specs, out_specs=...  71.1 us
    pallas_call x2, Pallas kernels, weight_grad(): pl.pallas_call(functools.partial(weight_grad_kernel, half), grid=(b.shape...  41.7 us
    ppermute x28, starting transfers between devices, flip(): return lax.ppermute(value, DP, [(i, i ^ 1 << bit) for i in range(size)])  27.7 us
    unnamed x178, local copies, waits for them, and re-layouts  20.4 us
  transfers between devices with their start and end apart: 85, of which 42 were waited for; matrix products, arithmetic and copies ran while one was open for 32% of the time, Pallas kernels for 10%

profile of v7, /device:TPU:0, one launch (start us, length us, event | category | flops | bytes accessed | tf_op | source)
XLA Modules:
  0.0 963.8 jit_solution(14555130312359364857)
XLA Ops:
  22.9 8.6 all-to-all-start
  35.7 5.2 all-to-all-done
  53.8 8.2 collective-permute-done
  64.5 17.8 %collective-permute-done.10 = bf16[192,2048]{1,0:T(8,128)(2,1)} collective-permute-done((bf16[192,2048]{1,0:T(8,128)(2,1)S(1)}, bf16[192,2048]{1,0:T(8,128)(2,1)}, u32[]{:S(2)}, u32[]{:S(2)}) %collective-permute-start.10) | collective-permute-done | bytes 786464 | tf_op jit(solution)/shard_map/ppermute | solution.py:111
  82.3 22.2 %collective-permute-done.11 = bf16[192,2048]{1,0:T(8,128)(2,1)} collective-permute-done((bf16[192,2048]{1,0:T(8,128)(2,1)S(1)}, bf16[192,2048]{1,0:T(8,128)(2,1)}, u32[]{:S(2)}, u32[]{:S(2)}) %collective-permute-start.11) | collective-permute-done | bytes 786464 | tf_op jit(solution)/shard_map/ppermute | solution.py:111
  119.7 8.6 collective-permute-done.12
  135.9 4.6 collective-permute-start.15
  140.6 11.5 %collective-permute-done.14 = bf16[192,2048]{1,0:T(8,128)(2,1)} collective-permute-done((bf16[192,2048]{1,0:T(8,128)(2,1)}, bf16[192,2048]{1,0:T(8,128)(2,1)}, u32[]{:S(2)}, u32[]{:S(2)}) %collective-permute-start.14) | collective-permute-done | bytes 786464 | tf_op jit(solution)/shard_map/ppermute | solution.py:111
  161.6 12.9 %shard_map.188 = (bf16[1536,2048]{1,0:T(8,128)(2,1)}, f32[1536,768]{1,0:T(8,128)}, f32[8,1536]{1,0:T(8,128)}) custom-call(bf16[768,1024]{1,0:T(8,128)(2,1)} %bitcast.4.a_own, bf16[768,1024]{1,0:T(8,128)(2,1)} %bitcast.291, bf16[768,1024]{1,0:T(8,128)(2,1)} %collective-permute-done.4.a_other, bf16[768,1024]{1,0:T(8,128)(2,1)} %collective-permute-done.5.b_other, ...), custom_call_target="tpu_custom_call" | custom-call | flops 1 | bytes 1 | tf_op jit(solution)/shard_map/pallas_call | solution.py:349
  176.5 4.1 collective-permute-done.32
  186.1 6.3 all-to-all-start.1
  197.5 5.8 collective-permute-done.17
  208.4 9.0 all-to-all-done.1
  218.7 18.7 %shard_map.189 = (bf16[1536,256]{1,0:T(8,128)(2,1)}, bf16[768,2048]{1,0:T(8,128)(2,1)}, bf16[768,2048]{1,0:T(8,128)(2,1)}) custom-call(f32[1536,768]{1,0:T(8,128)} %get-tuple-element.70.raw_ref, f32[8,1536]{1,0:T(8,128)} %pad.11.sum_ref, f32[8,256]{1,0:T(8,128)} %pad.12.gain_ref, f32[384,128]{1,0:T(8,128)} %bitcast.313, f32[384,128]{1,0:T(8,128)} %bitcast.315, ...), custom_call_target="tpu_custom_call" | custom-call | flops 1 | bytes 1 | tf_op jit(solution)/shard_map/pallas_call | solution.py:349
  239.3 5.6 collective-permute-done.19
  244.8 4.2 add_convert_fusion.4
  251.6 34.8 %collective-permute-done.22 = bf16[2,192,1024]{2,1,0:T(8,128)(2,1)S(1)} collective-permute-done((bf16[2,192,1024]{2,1,0:T(8,128)(2,1)S(1)}, bf16[2,192,1024]{2,1,0:T(8,128)(2,1)S(1)}, u32[]{:S(2)}, u32[]{:S(2)}) %collective-permute-start.22) | collective-permute-done | bytes 786464 | tf_op jit(solution)/shard_map/ppermute | solution.py:52
  290.8 16.1 %collective-permute-done.23 = bf16[192,1024]{1,0:T(8,128)(2,1)} collective-permute-done((bf16[192,1024]{1,0:T(8,128)(2,1)S(1)}, bf16[192,1024]{1,0:T(8,128)(2,1)}, u32[]{:S(2)}, u32[]{:S(2)}) %collective-permute-start.23) | collective-permute-done | bytes 393248 | tf_op jit(solution)/shard_map/ppermute | solution.py:52
  328.1 10.9 %collective-permute-done.24 = bf16[192,2048]{1,0:T(8,128)(2,1)S(1)} collective-permute-done((bf16[192,2048]{1,0:T(8,128)(2,1)S(1)}, bf16[192,2048]{1,0:T(8,128)(2,1)S(1)}, u32[]{:S(2)}, u32[]{:S(2)}) %collective-permute-start.24) | collective-permute-done | bytes 786464 | tf_op jit(solution)/shard_map/ppermute | solution.py:111
  339.0 4.2 collective-permute-done.25
  344.5 4.6 collective-permute-start.29
  349.1 13.4 %collective-permute-done.27 = bf16[192,2048]{1,0:T(8,128)(2,1)S(1)} collective-permute-done((bf16[192,2048]{1,0:T(8,128)(2,1)S(1)}, bf16[192,2048]{1,0:T(8,128)(2,1)S(1)}, u32[]{:S(2)}, u32[]{:S(2)}) %collective-permute-start.27) | collective-permute-done | bytes 786464 | tf_op jit(solution)/shard_map/ppermute | solution.py:111
  363.8 4.8 collective-permute-start.30
  368.6 12.4 %collective-permute-done.28 = bf16[192,2048]{1,0:T(8,128)(2,1)S(1)} collective-permute-done((bf16[192,2048]{1,0:T(8,128)(2,1)S(1)}, bf16[192,2048]{1,0:T(8,128)(2,1)S(1)}, u32[]{:S(2)}, u32[]{:S(2)}) %collective-permute-start.28) | collective-permute-done | bytes 786464 | tf_op jit(solution)/shard_map/ppermute | solution.py:111
  392.2 4.0 constant_dynamic-update-slice_fusion.5.b_ref
  396.2 4.5 fusion.93
  401.5 19.8 %fusion.94 = f32[1536,2048]{1,0:T(8,128)} fusion(bf16[1536,2048]{1,0:T(8,128)(2,1)} %constant_dynamic-update-slice_fusion.5.b_ref, bf16[2048,2048]{1,0:T(8,128)(2,1)} %all-gather.7.cloned.1.call-done), kind=kOutput, calls=%fused_computation.294 | convolution fusion | flops 12884901888 | bytes 27262976 | tf_op jit(solution)/shard_map/dot_general | solution.py:44
  421.3 15.4 %multiply_convert_fusion.4 = (bf16[1536,1024]{1,0:T(8,128)(2,1)S(1)}, bf16[1536,1024]{1,0:T(8,128)(2,1)S(1)}, bf16[1536,1024]{1,0:T(8,128)(2,1)S(1)}) fusion(f32[1536,2048]{1,0:T(8,128)} %fusion.94, bf16[2048,1024]{1,0:T(8,128)(2,1)} %all-gather.9.cloned.1.call-done, bf16[1536,2048]{1,0:T(8,128)(2,1)} %copy-done.58, f32[1536]{0:T(1024)S(1)} %broadcast_select_fusion.9), kind=kOutput, calls=%fused_computation.40 | convolution fusion | flops 6475481088 | bytes 32512000 | tf_op jit(solution)/shard_map/dot_general | solution.py:44
  436.7 21.4 %convolution_convert_fusion.2 = bf16[1536,2048]{1,0:T(8,128)(2,1)} fusion(bf16[2048,2048]{1,0:T(8,128)(2,1)} %all-gather.7.cloned.1.call-done, bf16[1536,1024]{1,0:T(8,128)(2,1)S(1)} %get-tuple-element.84.u_ref, bf16[1536,1024]{1,0:T(8,128)(2,1)S(1)} %get-tuple-element.83.g_ref), kind=kOutput, calls=%fused_computation.19 | convolution fusion | flops 12900630528 | bytes 20971520 | tf_op jit(solution)/shard_map/dot_general | solution.py:44
  458.1 8.9 convolution_convert_fusion.5
  467.1 19.2 %fusion.95 = f32[1536,2048]{1,0:T(8,128)} fusion(bf16[1536,2048]{1,0:T(8,128)(2,1)} %constant_dynamic-update-slice_fusion.5.b_ref, bf16[2048,2048]{1,0:T(8,128)(2,1)} %all-gather.11.cloned.1.call-done), kind=kOutput, calls=%fused_computation.295 | convolution fusion | flops 12884901888 | bytes 27262976 | tf_op jit(solution)/shard_map/dot_general | solution.py:44
  486.3 19.2 %all-gather.13.cloned.1.call-done = bf16[2048,1024]{1,0:T(8,128)(2,1)} async-done(((bf16[512,1024]{1,0:T(8,128)(2,1)}), bf16[2048,1024]{1,0:T(8,128)(2,1)}) %all-gather.13.cloned.1.call-update) | async-done | bytes 4194320 | tf_op jit(solution)/shard_map/all_gather | solution.py:542
  505.5 18.2 %multiply_convert_fusion.1 = (bf16[1536,1024]{1,0:T(8,128)(2,1)S(1)}, bf16[1536,1024]{1,0:T(8,128)(2,1)}, bf16[1536,1024]{1,0:T(8,128)(2,1)S(1)}) fusion(f32[1536,2048]{1,0:T(8,128)} %fusion.95, bf16[2048,1024]{1,0:T(8,128)(2,1)} %all-gather.13.cloned.1.call-done, bf16[1536,2048]{1,0:T(8,128)(2,1)} %copy-done.58, f32[1536]{0:T(1024)S(1)} %copy-done.70), kind=kOutput, calls=%fused_computation.34 | convolution fusion | flops 6475481088 | bytes 32512000 | tf_op jit(solution)/shard_map/dot_general | solution.py:44
  525.4 12.8 %convolution_convert_fusion.4 = bf16[2048,1024]{1,0:T(8,128)(2,1)} fusion(bf16[1536,1024]{1,0:T(8,128)(2,1)S(1)} %get-tuple-element.187, bf16[1536,2048]{1,0:T(8,128)(2,1)} %copy-done.58, f32[1536]{0:T(1024)S(1)} %copy-done.70), kind=kOutput, calls=%fused_computation.54 | convolution fusion | flops 6453985280 | bytes 13637632 | tf_op jit(solution)/shard_map/dot_general | solution.py:44
  538.3 17.9 %add_convert_fusion = bf16[1536,2048]{1,0:T(8,128)(2,1)S(1)} fusion(bf16[1536,2048]{1,0:T(8,128)(2,1)} %convolution_convert_fusion.2, bf16[2048,2048]{1,0:T(8,128)(2,1)} %all-gather.11.cloned.1.call-done, bf16[1536,1024]{1,0:T(8,128)(2,1)} %get-tuple-element.88.u_ref, bf16[1536,1024]{1,0:T(8,128)(2,1)S(1)} %get-tuple-element.87.g_ref), kind=kOutput, calls=%fused_computation.16 | convolution fusion | flops 12913213440 | bytes 27262976 | tf_op jit(solution)/shard_map/dot_general | solution.py:44
  556.5 5.6 collective-permute-done.34
  566.4 5.4 collective-permute-start.35
  571.8 20.7 %shard_map.190 = bf16[2048,2048]{1,0:T(8,128)(2,1)} custom-call(bf16[1536,1024]{1,0:T(8,128)(2,1)} %copy-done.37, bf16[1536,1024]{1,0:T(8,128)(2,1)} %copy-done.38, bf16[1536,2048]{1,0:T(8,128)(2,1)} %constant_dynamic-update-slice_fusion.5.b_ref), custom_call_target="tpu_custom_call" | custom-call | flops 1 | bytes 1 | tf_op jit(solution)/shard_map/pallas_call | solution.py:372
  592.5 12.0 %convolution_convert_fusion.1 = bf16[1536,2048]{1,0:T(8,128)(2,1)} fusion(bf16[1536,1024]{1,0:T(8,128)(2,1)} %copy-done.77, bf16[2048,1024]{1,0:T(8,128)(2,1)} %all-gather.13.cloned.1.call-done), kind=kOutput, calls=%fused_computation.18 | convolution fusion | flops 6445596672 | bytes 13631488 | tf_op jit(solution)/shard_map/dot_general | solution.py:44
  604.6 13.2 %fusion.4 = (f32[1536]{0:T(1024)S(1)}, f32[1536]{0:T(1024)S(1)}, bf16[1536,2048]{1,0:T(8,128)(2,1)S(1)}) fusion(bf16[1536,2048]{1,0:T(8,128)(2,1)} %copy-done.58, bf16[1536,2048]{1,0:T(8,128)(2,1)} %convolution_convert_fusion.1, f32[1536]{0:T(1024)S(1)} %copy-done.70, f32[1536]{0:T(1024)S(1)} %broadcast_select_fusion.9, ...), kind=kOutput, calls=%fused_computation.14 | convolution fusion | flops 6480196608 | bytes 26238976 | tf_op jit(solution)/shard_map/dot_general | solution.py:44
  625.7 5.5 collective-permute-start.37
  631.2 6.1 add_convert_fusion.3
  637.3 21.0 %shard_map.191 = bf16[2048,2048]{1,0:T(8,128)(2,1)} custom-call(bf16[1536,1024]{1,0:T(8,128)(2,1)} %copy-done.36, bf16[1536,1024]{1,0:T(8,128)(2,1)} %get-tuple-element.88.u_ref, bf16[1536,2048]{1,0:T(8,128)(2,1)} %constant_dynamic-update-slice_fusion.5.b_ref), custom_call_target="tpu_custom_call" | custom-call | flops 1 | bytes 1 | tf_op jit(solution)/shard_map/pallas_call | solution.py:372
  663.5 5.5 collective-permute-start.39
  670.1 15.1 %all_to_all.34 = f32[8,2,192]{2,1,0:T(2,128)S(1)} all-to-all(f32[8,2,192]{2,1,0:T(2,128)S(1)} %bitcast.338), channel_id=1, replica_groups=mesh['q'=4,'c'=2,'z'=4] {'c','z'}, dimensions={0} | all-to-all | bytes 24576 | tf_op jit(solution)/shard_map/all_to_all | solution.py:620
  692.0 17.6 %collective-permute-done.47 = bf16[192,1024]{1,0:T(8,128)(2,1)S(1)} collective-permute-done((bf16[192,1024]{1,0:T(8,128)(2,1)S(1)}, bf16[192,1024]{1,0:T(8,128)(2,1)S(1)}, u32[]{:S(2)}, u32[]{:S(2)}) %collective-permute-start.47) | collective-permute-done | bytes 393248 | tf_op jit(solution)/shard_map/ppermute | solution.py:52
  712.7 4.7 collective-permute-start.41
  718.6 12.3 %collective-permute-done.50 = bf16[2,192,1024]{2,1,0:T(8,128)(2,1)S(1)} collective-permute-done((bf16[2,192,1024]{2,1,0:T(8,128)(2,1)S(1)}, bf16[2,192,1024]{2,1,0:T(8,128)(2,1)S(1)}, u32[]{:S(2)}, u32[]{:S(2)}) %collective-permute-start.50) | collective-permute-done | bytes 786464 | tf_op jit(solution)/shard_map/ppermute | solution.py:52
  733.1 4.2 collective-permute-done.42
  746.1 4.0 collective-permute-start.43
  751.4 26.4 %shard_map.192 = (f32[1536,512]{1,0:T(8,128)}, bf16[1536,256]{1,0:T(8,128)(2,1)}, f32[8,1536]{1,0:T(8,128)}, f32[8,256]{1,0:T(8,128)}, f32[2048,256]{1,0:T(8,128)}) custom-call(f32[1536,768]{1,0:T(8,128)} %get-tuple-element.70.raw_ref, f32[8,1536]{1,0:T(8,128)} %pad.11.sum_ref, f32[8,256]{1,0:T(8,128)} %pad.12.gain_ref, f32[384,128]{1,0:T(8,128)} %bitcast.314, ...), custom_call_target="tpu_custom_call" | custom-call | flops 1 | bytes 1 | tf_op jit(solution)/shard_map/pallas_call | solution.py:349
  790.2 5.9 collective-permute-start.45
  796.9 13.0 %shard_map.193 = (bf16[1536,768]{1,0:T(8,128)(2,1)}, bf16[768,2048]{1,0:T(8,128)(2,1)}, bf16[768,2048]{1,0:T(8,128)(2,1)}) custom-call(f32[1536,768]{1,0:T(8,128)} %get-tuple-element.70.raw_ref, f32[8,1536]{1,0:T(8,128)} %pad.11.sum_ref, f32[1536,512]{1,0:T(8,128)} %get-tuple-element.99.back_ref, bf16[1536,256]{1,0:T(8,128)(2,1)} %get-tuple-element.100.dv_ref, ...), custom_call_target="tpu_custom_call" | custom-call | flops 1 | bytes 1 | tf_op jit(solution)/shard_map/pallas_call | solution.py:349
  813.6 8.2 convolution_convert_fusion.6
  833.5 5.0 collective-permute-start.61
  843.4 16.2 %collective-permute-done.62 = bf16[256,2048]{1,0:T(8,128)(2,1)S(1)} collective-permute-done((bf16[256,2048]{1,0:T(8,128)(2,1)S(1)}, bf16[256,2048]{1,0:T(8,128)(2,1)S(1)}, u32[]{:S(2)}, u32[]{:S(2)}) %collective-permute-start.62) | collective-permute-done | bytes 1048608 | tf_op jit(solution)/shard_map/ppermute | solution.py:111
  861.4 4.5 collective-permute-start.63
  870.0 6.0 collective-permute-done.60
  876.2 11.2 %collective-permute-done.63 = bf16[256,2048]{1,0:T(8,128)(2,1)S(1)} collective-permute-done((bf16[256,2048]{1,0:T(8,128)(2,1)S(1)}, bf16[256,2048]{1,0:T(8,128)(2,1)S(1)}, u32[]{:S(2)}, u32[]{:S(2)}) %collective-permute-start.63) | collective-permute-done | bytes 1048608 | tf_op jit(solution)/shard_map/ppermute | solution.py:111
  895.2 5.8 collective-permute-start.65
  906.4 4.0 all-to-all-start.4
  913.9 6.2 collective-permute-done.66
  940.1 5.0 fusion.40
  952.9 3.9 maximum_convert_fusion
  (507 shorter events, 251.5 us)
Async XLA Ops:
  9.6 32.3 %collective-permute-start.9 = (bf16[2,256,1024]{2,1,0:T(8,128)(2,1)}, bf16[2,256,1024]{2,1,0:T(8,128)(2,1)}, u32[]{:S(2)}, u32[]{:S(2)}) collective-permute-start(bf16[2,256,1024]{2,1,0:T(8,128)(2,1)} %dynamic-slice_bitcast_fusion.4), channel_id=1, source_target_pairs={{0,4},{4,0},{1,5},{5,1},{2,6},{6,2},{3,7},{7,3},{8,12},{12,8},{9,1... | collective-permute-start | bytes 3145736 | tf_op jit(solution)/shard_map/ppermute | solution.py:151
  12.0 22.5 %collective-permute-start.8 = (bf16[64,2048]{1,0:T(8,128)(2,1)}, bf16[64,2048]{1,0:T(8,128)(2,1)S(1)}, u32[]{:S(2)}, u32[]{:S(2)}) collective-permute-start(bf16[64,2048]{1,0:T(8,128)(2,1)} %get-tuple-element.247), channel_id=1, source_target_pairs={{0,0},{1,5},{2,10},{3,11},{4,12},{5,17},{6,22},{7,23},{8,24},{9,29... | collective-permute-start | bytes 786440 | tf_op jit(solution)/shard_map/ppermute | solution.py:418
  13.6 21.0 %collective-permute-start.7 = (bf16[64,2048]{1,0:T(8,128)(2,1)}, bf16[64,2048]{1,0:T(8,128)(2,1)}, u32[]{:S(2)}, u32[]{:S(2)}) collective-permute-start(bf16[64,2048]{1,0:T(8,128)(2,1)} %get-tuple-element.248), channel_id=1, source_target_pairs={{0,0},{1,5},{2,6},{3,11},{4,12},{5,17},{6,18},{7,23},{8,24},{9,29}... | collective-permute-start | bytes 786440 | tf_op jit(solution)/shard_map/ppermute | solution.py:418
  22.9 18.0 %all-to-all-start = ((bf16[32,2,1504]{2,1,0:T(2,128)(2,1)}), bf16[32,2,1504]{2,1,0:T(2,128)(2,1)S(1)}, u32[]{:S(2)}, u32[]{:S(2)}) async-start(bf16[32,2,1504]{2,1,0:T(2,128)(2,1)} %reshape.529), calls=%async_computation | async-start | bytes 393216 | tf_op jit(solution)/shard_map/all_to_all | solution.py:441
  31.6 130.0 %all-gather.15.cloned.1.call-start = ((), (), s32[]{:S(2)}) async-start(), calls=%async_computation.17 | async-start | bytes 3932160 | tf_op jit(solution)/shard_map/all_gather | solution.py:497
  32.7 18.3 %collective-permute-start.2 = (bf16[192,1024]{1,0:T(8,128)(2,1)}, bf16[192,1024]{1,0:T(8,128)(2,1)}, u32[]{:S(2)}, u32[]{:S(2)}) collective-permute-start(bf16[192,1024]{1,0:T(8,128)(2,1)} %get-tuple-element.253), channel_id=1, source_target_pairs={{0,16},{4,20},{8,24},{12,28},{16,0},{20,4},{24,8},{28,12},{1,17},{... | collective-permute-start | bytes 1179656 | tf_op jit(solution)/shard_map/ppermute | solution.py:52
  34.5 367.0 %all-gather.7.cloned.1.call-start = ((), (), s32[]{:S(2)}) async-start(), calls=%async_computation.9 | async-start | bytes 10485760 | tf_op jit(solution)/shard_map/all_gather | solution.py:541
  46.1 36.2 %collective-permute-start.10 = (bf16[192,2048]{1,0:T(8,128)(2,1)S(1)}, bf16[192,2048]{1,0:T(8,128)(2,1)}, u32[]{:S(2)}, u32[]{:S(2)}) collective-permute-start(bf16[192,2048]{1,0:T(8,128)(2,1)S(1)} %pad_maximum_fusion.15), channel_id=1, source_target_pairs={{0,1},{1,2},{2,3},{4,5},{5,6},{6,7},{8,9},{9,10},{10,11},{12,13},{... | collective-permute-start | bytes 2359304 | tf_op jit(solution)/shard_map/ppermute | solution.py:111
  48.5 56.0 %collective-permute-start.11 = (bf16[192,2048]{1,0:T(8,128)(2,1)S(1)}, bf16[192,2048]{1,0:T(8,128)(2,1)}, u32[]{:S(2)}, u32[]{:S(2)}) collective-permute-start(bf16[192,2048]{1,0:T(8,128)(2,1)S(1)} %pad_maximum_fusion.15), channel_id=1, source_target_pairs={{1,0},{2,1},{3,2},{5,4},{6,5},{7,6},{9,8},{10,9},{11,10},{13,12},{... | collective-permute-start | bytes 2359304 | tf_op jit(solution)/shard_map/ppermute | solution.py:111
  53.0 62.2 %collective-permute-start.3 = (bf16[2,192,1024]{2,1,0:T(8,128)(2,1)}, bf16[2,192,1024]{2,1,0:T(8,128)(2,1)}, u32[]{:S(2)}, u32[]{:S(2)}) collective-permute-start(bf16[2,192,1024]{2,1,0:T(8,128)(2,1)} %get-tuple-element.250), channel_id=1, source_target_pairs={{0,8},{4,12},{8,0},{12,4},{16,24},{20,28},{24,16},{28,20},{1,9},{5... | collective-permute-start | bytes 2359304 | tf_op jit(solution)/shard_map/ppermute | solution.py:52
  63.3 53.5 %collective-permute-start.1 = (bf16[2,192,1024]{2,1,0:T(8,128)(2,1)}, bf16[2,192,1024]{2,1,0:T(8,128)(2,1)}, u32[]{:S(2)}, u32[]{:S(2)}) collective-permute-start(bf16[2,192,1024]{2,1,0:T(8,128)(2,1)} %get-tuple-element.256), channel_id=1, source_target_pairs={{0,16},{4,20},{8,24},{12,28},{16,0},{20,4},{24,8},{28,12},{1,17},{... | collective-permute-start | bytes 2359304 | tf_op jit(solution)/shard_map/ppermute | solution.py:52
  104.4 23.9 %collective-permute-start.12 = (bf16[192,2048]{1,0:T(8,128)(2,1)}, bf16[192,2048]{1,0:T(8,128)(2,1)}, u32[]{:S(2)}, u32[]{:S(2)}) collective-permute-start(bf16[192,2048]{1,0:T(8,128)(2,1)} %collective-permute-done.10), channel_id=1, source_target_pairs={{0,1},{1,2},{2,3},{4,5},{5,6},{6,7},{8,9},{9,10},{10,11},{12,13},{... | collective-permute-start | bytes 2359304 | tf_op jit(solution)/shard_map/ppermute | solution.py:111
  106.7 23.6 %collective-permute-start.13 = (bf16[192,2048]{1,0:T(8,128)(2,1)}, bf16[192,2048]{1,0:T(8,128)(2,1)}, u32[]{:S(2)}, u32[]{:S(2)}) collective-permute-start(bf16[192,2048]{1,0:T(8,128)(2,1)} %collective-permute-done.11), channel_id=1, source_target_pairs={{1,0},{2,1},{3,2},{5,4},{6,5},{7,6},{9,8},{10,9},{11,10},{13,12},{... | collective-permute-start | bytes 2359304 | tf_op jit(solution)/shard_map/ppermute | solution.py:111
  130.3 21.8 %collective-permute-start.14 = (bf16[192,2048]{1,0:T(8,128)(2,1)}, bf16[192,2048]{1,0:T(8,128)(2,1)}, u32[]{:S(2)}, u32[]{:S(2)}) collective-permute-start(bf16[192,2048]{1,0:T(8,128)(2,1)} %collective-permute-done.13), channel_id=1, source_target_pairs={{1,0},{2,1},{3,2},{5,4},{6,5},{7,6},{9,8},{10,9},{11,10},{13,12},{... | collective-permute-start | bytes 2359304 | tf_op jit(solution)/shard_map/ppermute | solution.py:111
  135.4 26.2 %collective-permute-start.4 = (bf16[768,1024]{1,0:T(8,128)(2,1)}, bf16[768,1024]{1,0:T(8,128)(2,1)}, u32[]{:S(2)}, u32[]{:S(2)}) collective-permute-start(bf16[768,1024]{1,0:T(8,128)(2,1)} %bitcast.4.a_own), channel_id=1, source_target_pairs={{0,4},{4,0},{8,12},{12,8},{16,20},{20,16},{24,28},{28,24},{1,5},{5... | collective-permute-start | bytes 4718600 | tf_op jit(solution)/shard_map/ppermute | solution.py:52
  135.4 26.1 %collective-permute-start.5 = (bf16[768,1024]{1,0:T(8,128)(2,1)S(1)}, bf16[768,1024]{1,0:T(8,128)(2,1)}, u32[]{:S(2)}, u32[]{:S(2)}) collective-permute-start(bf16[768,1024]{1,0:T(8,128)(2,1)S(1)} %bitcast.290), channel_id=1, source_target_pairs={{0,4},{4,0},{8,12},{12,8},{16,20},{20,16},{24,28},{28,24},{1,5},{5... | collective-permute-start | bytes 4718600 | tf_op jit(solution)/shard_map/ppermute | solution.py:52
  135.9 21.9 %collective-permute-start.15 = (bf16[192,2048]{1,0:T(8,128)(2,1)}, bf16[192,2048]{1,0:T(8,128)(2,1)S(1)}, u32[]{:S(2)}, u32[]{:S(2)}) collective-permute-start(bf16[192,2048]{1,0:T(8,128)(2,1)} %collective-permute-done.12), channel_id=1, source_target_pairs={{0,1},{1,2},{2,3},{4,5},{5,6},{6,7},{8,9},{9,10},{10,11},{12,13},{... | collective-permute-start | bytes 2359304 | tf_op jit(solution)/shard_map/ppermute | solution.py:111
  186.1 31.3 %all-to-all-start.1 = ((bf16[32,64,256]{2,1,0:T(8,128)(2,1)}), bf16[32,64,256]{2,1,0:T(8,128)(2,1)S(1)}, u32[]{:S(2)}, u32[]{:S(2)}) async-start(bf16[32,64,256]{2,1,0:T(8,128)(2,1)} %bitcast.299), calls=%async_computation.1 | async-start | bytes 2097152 | tf_op jit(solution)/shard_map/all_to_all | solution.py:493
  192.4 228.8 %all-gather.9.cloned.1.call-start = ((), (), s32[]{:S(2)}) async-start(), calls=%async_computation.10 | async-start | bytes 5242880 | tf_op jit(solution)/shard_map/all_gather | solution.py:496
  239.2 227.9 %all-gather.11.cloned.1.call-start = ((), (), s32[]{:S(2)}) async-start(), calls=%async_computation.11 | async-start | bytes 10485760 | tf_op jit(solution)/shard_map/all_gather | solution.py:541
  249.2 37.2 %collective-permute-start.22 = (bf16[2,192,1024]{2,1,0:T(8,128)(2,1)S(1)}, bf16[2,192,1024]{2,1,0:T(8,128)(2,1)S(1)}, u32[]{:S(2)}, u32[]{:S(2)}) collective-permute-start(bf16[2,192,1024]{2,1,0:T(8,128)(2,1)S(1)} %bitcast.327), channel_id=1, source_target_pairs={{0,16},{4,20},{8,24},{12,28},{16,0},{20,4},{24,8},{28,12},{1,17},{... | collective-permute-start | bytes 2359304 | tf_op jit(solution)/shard_map/ppermute | solution.py:52
  251.0 37.3 %collective-permute-start.20 = (bf16[2,192,1024]{2,1,0:T(8,128)(2,1)S(1)}, bf16[2,192,1024]{2,1,0:T(8,128)(2,1)S(1)}, u32[]{:S(2)}, u32[]{:S(2)}) collective-permute-start(bf16[2,192,1024]{2,1,0:T(8,128)(2,1)S(1)} %slice_bitcast_fusion.6), channel_id=1, source_target_pairs={{0,8},{4,12},{8,0},{12,4},{16,24},{20,28},{24,16},{28,20},{1,9},{5... | collective-permute-start | bytes 2359304 | tf_op jit(solution)/shard_map/ppermute | solution.py:52
  286.7 20.2 %collective-permute-start.23 = (bf16[192,1024]{1,0:T(8,128)(2,1)S(1)}, bf16[192,1024]{1,0:T(8,128)(2,1)}, u32[]{:S(2)}, u32[]{:S(2)}) collective-permute-start(bf16[192,1024]{1,0:T(8,128)(2,1)S(1)} %slice_bitcast_fusion.16), channel_id=1, source_target_pairs={{0,8},{4,12},{8,0},{12,4},{16,24},{20,28},{24,16},{28,20},{1,9},{5... | collective-permute-start | bytes 1179656 | tf_op jit(solution)/shard_map/ppermute | solution.py:52
  288.6 18.7 %collective-permute-start.21 = (bf16[192,1024]{1,0:T(8,128)(2,1)S(1)}, bf16[192,1024]{1,0:T(8,128)(2,1)}, u32[]{:S(2)}, u32[]{:S(2)}) collective-permute-start(bf16[192,1024]{1,0:T(8,128)(2,1)S(1)} %slice_bitcast_fusion.18), channel_id=1, source_target_pairs={{0,16},{4,20},{8,24},{12,28},{16,0},{20,4},{24,8},{28,12},{1,17},{... | collective-permute-start | bytes 1179656 | tf_op jit(solution)/shard_map/ppermute | solution.py:52
  307.4 198.2 %all-gather.13.cloned.1.call-start = ((), (), s32[]{:S(2)}) async-start(), calls=%async_computation.12 | async-start | bytes 5242880 | tf_op jit(solution)/shard_map/all_gather | solution.py:542
  319.6 19.4 %collective-permute-start.24 = (bf16[192,2048]{1,0:T(8,128)(2,1)S(1)}, bf16[192,2048]{1,0:T(8,128)(2,1)S(1)}, u32[]{:S(2)}, u32[]{:S(2)}) collective-permute-start(bf16[192,2048]{1,0:T(8,128)(2,1)S(1)} %get-tuple-element.179), channel_id=1, source_target_pairs={{0,1},{1,2},{2,3},{4,5},{5,6},{6,7},{8,9},{9,10},{10,11},{12,13},{... | collective-permute-start | bytes 2359304 | tf_op jit(solution)/shard_map/ppermute | solution.py:111
  323.1 20.1 %collective-permute-start.25 = (bf16[192,2048]{1,0:T(8,128)(2,1)S(1)}, bf16[192,2048]{1,0:T(8,128)(2,1)S(1)}, u32[]{:S(2)}, u32[]{:S(2)}) collective-permute-start(bf16[192,2048]{1,0:T(8,128)(2,1)S(1)} %get-tuple-element.179), channel_id=1, source_target_pairs={{1,0},{2,1},{3,2},{5,4},{6,5},{7,6},{9,8},{10,9},{11,10},{13,12},{... | collective-permute-start | bytes 2359304 | tf_op jit(solution)/shard_map/ppermute | solution.py:111
  343.2 19.3 %collective-permute-start.27 = (bf16[192,2048]{1,0:T(8,128)(2,1)S(1)}, bf16[192,2048]{1,0:T(8,128)(2,1)S(1)}, u32[]{:S(2)}, u32[]{:S(2)}) collective-permute-start(bf16[192,2048]{1,0:T(8,128)(2,1)S(1)} %collective-permute-done.25), channel_id=1, source_target_pairs={{1,0},{2,1},{3,2},{5,4},{6,5},{7,6},{9,8},{10,9},{11,10},{13,12},{... | collective-permute-start | bytes 2359304 | tf_op jit(solution)/shard_map/ppermute | solution.py:111
  344.5 19.3 %collective-permute-start.29 = (bf16[192,2048]{1,0:T(8,128)(2,1)S(1)}, bf16[192,2048]{1,0:T(8,128)(2,1)S(1)}, u32[]{:S(2)}, u32[]{:S(2)}) collective-permute-start(bf16[192,2048]{1,0:T(8,128)(2,1)S(1)} %collective-permute-done.24), channel_id=1, source_target_pairs={{0,1},{1,2},{2,3},{4,5},{5,6},{6,7},{8,9},{9,10},{10,11},{12,13},{... | collective-permute-start | bytes 2359304 | tf_op jit(solution)/shard_map/ppermute | solution.py:111
  362.5 18.6 %collective-permute-start.28 = (bf16[192,2048]{1,0:T(8,128)(2,1)S(1)}, bf16[192,2048]{1,0:T(8,128)(2,1)S(1)}, u32[]{:S(2)}, u32[]{:S(2)}) collective-permute-start(bf16[192,2048]{1,0:T(8,128)(2,1)S(1)} %collective-permute-done.27), channel_id=1, source_target_pairs={{1,0},{2,1},{3,2},{5,4},{6,5},{7,6},{9,8},{10,9},{11,10},{13,12},{... | collective-permute-start | bytes 2359304 | tf_op jit(solution)/shard_map/ppermute | solution.py:111
  363.8 18.5 %collective-permute-start.30 = (bf16[192,2048]{1,0:T(8,128)(2,1)S(1)}, bf16[192,2048]{1,0:T(8,128)(2,1)S(1)}, u32[]{:S(2)}, u32[]{:S(2)}) collective-permute-start(bf16[192,2048]{1,0:T(8,128)(2,1)S(1)} %collective-permute-done.29), channel_id=1, source_target_pairs={{0,1},{1,2},{2,3},{4,5},{5,6},{6,7},{8,9},{9,10},{10,11},{12,13},{... | collective-permute-start | bytes 2359304 | tf_op jit(solution)/shard_map/ppermute | solution.py:111
  390.4 423.1 %reduce-scatter.5.cloned.1.call-start = ((), (), s32[]{:S(2)}) async-start(), calls=%async_computation.13 | async-start | bytes 5242880 | tf_op jit(solution)/shard_map/reduce_scatter | solution.py:595
  467.1 356.5 %reduce-scatter.7.cloned.1.call-start = ((), (), s32[]{:S(2)}) async-start(), calls=%async_computation.14 | async-start | bytes 5242880 | tf_op jit(solution)/shard_map/reduce_scatter | solution.py:595
  538.2 372.3 %reduce-scatter.9.cloned.1.call-start = ((), (), s32[]{:S(2)}) async-start(), calls=%async_computation.15 | async-start | bytes 10485760 | tf_op jit(solution)/shard_map/reduce_scatter | solution.py:655
  565.1 27.4 %collective-permute-start.36 = (bf16[192,2048]{1,0:T(8,128)(2,1)}, bf16[192,2048]{1,0:T(8,128)(2,1)}, u32[]{:S(2)}, u32[]{:S(2)}) collective-permute-start(bf16[192,2048]{1,0:T(8,128)(2,1)} %get-tuple-element.214), channel_id=1, source_target_pairs={{1,0},{2,1},{3,2},{5,4},{6,5},{7,6},{9,8},{10,9},{11,10},{13,12},{... | collective-permute-start | bytes 2359304 | tf_op jit(solution)/shard_map/ppermute | solution.py:111
  566.4 26.1 %collective-permute-start.35 = (bf16[192,2048]{1,0:T(8,128)(2,1)}, bf16[192,2048]{1,0:T(8,128)(2,1)}, u32[]{:S(2)}, u32[]{:S(2)}) collective-permute-start(bf16[192,2048]{1,0:T(8,128)(2,1)} %get-tuple-element.215), channel_id=1, source_target_pairs={{0,1},{1,2},{2,3},{4,5},{5,6},{6,7},{8,9},{9,10},{10,11},{12,13},{... | collective-permute-start | bytes 2359304 | tf_op jit(solution)/shard_map/ppermute | solution.py:111
  592.5 318.0 %reduce-scatter.11.cloned.1.call-start = ((), (), s32[]{:S(2)}) async-start(), calls=%async_computation.16 | async-start | bytes 10485760 | tf_op jit(solution)/shard_map/reduce_scatter | solution.py:655
  624.4 34.0 %collective-permute-start.38 = (bf16[192,2048]{1,0:T(8,128)(2,1)}, bf16[192,2048]{1,0:T(8,128)(2,1)S(1)}, u32[]{:S(2)}, u32[]{:S(2)}) collective-permute-start(bf16[192,2048]{1,0:T(8,128)(2,1)} %get-tuple-element.86), channel_id=1, source_target_pairs={{1,0},{2,1},{3,2},{5,4},{6,5},{7,6},{9,8},{10,9},{11,10},{13,12},{... | collective-permute-start | bytes 2359304 | tf_op jit(solution)/shard_map/ppermute | solution.py:111
  625.7 32.7 %collective-permute-start.37 = (bf16[192,2048]{1,0:T(8,128)(2,1)}, bf16[192,2048]{1,0:T(8,128)(2,1)}, u32[]{:S(2)}, u32[]{:S(2)}) collective-permute-start(bf16[192,2048]{1,0:T(8,128)(2,1)} %get-tuple-element.85), channel_id=1, source_target_pairs={{0,1},{1,2},{2,3},{4,5},{5,6},{6,7},{8,9},{9,10},{10,11},{12,13},{... | collective-permute-start | bytes 2359304 | tf_op jit(solution)/shard_map/ppermute | solution.py:111
  662.2 23.1 %collective-permute-start.40 = (bf16[192,2048]{1,0:T(8,128)(2,1)}, bf16[192,2048]{1,0:T(8,128)(2,1)}, u32[]{:S(2)}, u32[]{:S(2)}) collective-permute-start(bf16[192,2048]{1,0:T(8,128)(2,1)} %get-tuple-element.90), channel_id=1, source_target_pairs={{1,0},{2,1},{3,2},{5,4},{6,5},{7,6},{9,8},{10,9},{11,10},{13,12},{... | collective-permute-start | bytes 2359304 | tf_op jit(solution)/shard_map/ppermute | solution.py:111
  663.5 21.8 %collective-permute-start.39 = (bf16[192,2048]{1,0:T(8,128)(2,1)}, bf16[192,2048]{1,0:T(8,128)(2,1)}, u32[]{:S(2)}, u32[]{:S(2)}) collective-permute-start(bf16[192,2048]{1,0:T(8,128)(2,1)} %get-tuple-element.89), channel_id=1, source_target_pairs={{0,1},{1,2},{2,3},{4,5},{5,6},{6,7},{8,9},{9,10},{10,11},{12,13},{... | collective-permute-start | bytes 2359304 | tf_op jit(solution)/shard_map/ppermute | solution.py:111
  689.6 20.0 %collective-permute-start.47 = (bf16[192,1024]{1,0:T(8,128)(2,1)S(1)}, bf16[192,1024]{1,0:T(8,128)(2,1)S(1)}, u32[]{:S(2)}, u32[]{:S(2)}) collective-permute-start(bf16[192,1024]{1,0:T(8,128)(2,1)S(1)} %get-tuple-element.243), channel_id=1, source_target_pairs={{0,8},{4,12},{8,0},{12,4},{16,24},{20,28},{24,16},{28,20},{1,9},{5... | collective-permute-start | bytes 1179656 | tf_op jit(solution)/shard_map/ppermute | solution.py:52
  691.1 20.2 %collective-permute-start.49 = (bf16[192,1024]{1,0:T(8,128)(2,1)S(1)}, bf16[192,1024]{1,0:T(8,128)(2,1)S(1)}, u32[]{:S(2)}, u32[]{:S(2)}) collective-permute-start(bf16[192,1024]{1,0:T(8,128)(2,1)S(1)} %get-tuple-element.242), channel_id=1, source_target_pairs={{0,16},{4,20},{8,24},{12,28},{16,0},{20,4},{24,8},{28,12},{1,17},{... | collective-permute-start | bytes 1179656 | tf_op jit(solution)/shard_map/ppermute | solution.py:52
  709.7 21.4 %collective-permute-start.48 = (bf16[2,192,1024]{2,1,0:T(8,128)(2,1)S(1)}, bf16[2,192,1024]{2,1,0:T(8,128)(2,1)S(1)}, u32[]{:S(2)}, u32[]{:S(2)}) collective-permute-start(bf16[2,192,1024]{2,1,0:T(8,128)(2,1)S(1)} %get-tuple-element.245), channel_id=1, source_target_pairs={{0,16},{4,20},{8,24},{12,28},{16,0},{20,4},{24,8},{28,12},{1,17},{... | collective-permute-start | bytes 2359304 | tf_op jit(solution)/shard_map/ppermute | solution.py:52
  711.4 19.5 %collective-permute-start.50 = (bf16[2,192,1024]{2,1,0:T(8,128)(2,1)S(1)}, bf16[2,192,1024]{2,1,0:T(8,128)(2,1)S(1)}, u32[]{:S(2)}, u32[]{:S(2)}) collective-permute-start(bf16[2,192,1024]{2,1,0:T(8,128)(2,1)S(1)} %get-tuple-element.239), channel_id=1, source_target_pairs={{0,8},{4,12},{8,0},{12,4},{16,24},{20,28},{24,16},{28,20},{1,9},{5... | collective-permute-start | bytes 2359304 | tf_op jit(solution)/shard_map/ppermute | solution.py:52
  712.7 20.4 %collective-permute-start.41 = (bf16[192,2048]{1,0:T(8,128)(2,1)S(1)}, bf16[192,2048]{1,0:T(8,128)(2,1)S(1)}, u32[]{:S(2)}, u32[]{:S(2)}) collective-permute-start(bf16[192,2048]{1,0:T(8,128)(2,1)S(1)} %get-tuple-element.209), channel_id=1, source_target_pairs={{0,1},{1,2},{2,3},{4,5},{5,6},{6,7},{8,9},{9,10},{10,11},{12,13},{... | collective-permute-start | bytes 2359304 | tf_op jit(solution)/shard_map/ppermute | solution.py:111
  717.3 19.9 %collective-permute-start.42 = (bf16[192,2048]{1,0:T(8,128)(2,1)S(1)}, bf16[192,2048]{1,0:T(8,128)(2,1)S(1)}, u32[]{:S(2)}, u32[]{:S(2)}) collective-permute-start(bf16[192,2048]{1,0:T(8,128)(2,1)S(1)} %get-tuple-element.208), channel_id=1, source_target_pairs={{1,0},{2,1},{3,2},{5,4},{6,5},{7,6},{9,8},{10,9},{11,10},{13,12},{... | collective-permute-start | bytes 2359304 | tf_op jit(solution)/shard_map/ppermute | solution.py:111
  746.1 31.7 %collective-permute-start.43 = (bf16[192,2048]{1,0:T(8,128)(2,1)}, bf16[192,2048]{1,0:T(8,128)(2,1)}, u32[]{:S(2)}, u32[]{:S(2)}) collective-permute-start(bf16[192,2048]{1,0:T(8,128)(2,1)} %get-tuple-element.92), channel_id=1, source_target_pairs={{0,1},{1,2},{2,3},{4,5},{5,6},{6,7},{8,9},{9,10},{10,11},{12,13},{... | collective-permute-start | bytes 2359304 | tf_op jit(solution)/shard_map/ppermute | solution.py:111
  750.1 27.7 %collective-permute-start.44 = (bf16[192,2048]{1,0:T(8,128)(2,1)}, bf16[192,2048]{1,0:T(8,128)(2,1)}, u32[]{:S(2)}, u32[]{:S(2)}) collective-permute-start(bf16[192,2048]{1,0:T(8,128)(2,1)} %get-tuple-element.93), channel_id=1, source_target_pairs={{1,0},{2,1},{3,2},{5,4},{6,5},{7,6},{9,8},{10,9},{11,10},{13,12},{... | collective-permute-start | bytes 2359304 | tf_op jit(solution)/shard_map/ppermute | solution.py:111
  788.9 21.6 %collective-permute-start.46 = (bf16[192,2048]{1,0:T(8,128)(2,1)}, bf16[192,2048]{1,0:T(8,128)(2,1)}, u32[]{:S(2)}, u32[]{:S(2)}) collective-permute-start(bf16[192,2048]{1,0:T(8,128)(2,1)} %get-tuple-element.95), channel_id=1, source_target_pairs={{1,0},{2,1},{3,2},{5,4},{6,5},{7,6},{9,8},{10,9},{11,10},{13,12},{... | collective-permute-start | bytes 2359304 | tf_op jit(solution)/shard_map/ppermute | solution.py:111
  790.2 21.4 %collective-permute-start.45 = (bf16[192,2048]{1,0:T(8,128)(2,1)}, bf16[192,2048]{1,0:T(8,128)(2,1)}, u32[]{:S(2)}, u32[]{:S(2)}) collective-permute-start(bf16[192,2048]{1,0:T(8,128)(2,1)} %get-tuple-element.94), channel_id=1, source_target_pairs={{0,1},{1,2},{2,3},{4,5},{5,6},{6,7},{8,9},{9,10},{10,11},{12,13},{... | collective-permute-start | bytes 2359304 | tf_op jit(solution)/shard_map/ppermute | solution.py:111
  832.2 27.4 %collective-permute-start.62 = (bf16[256,2048]{1,0:T(8,128)(2,1)S(1)}, bf16[256,2048]{1,0:T(8,128)(2,1)S(1)}, u32[]{:S(2)}, u32[]{:S(2)}) collective-permute-start(bf16[256,2048]{1,0:T(8,128)(2,1)S(1)} %get-tuple-element.109), channel_id=1, source_target_pairs={{1,0},{2,1},{3,2},{5,4},{6,5},{7,6},{9,8},{10,9},{11,10},{13,12},{... | collective-permute-start | bytes 3145736 | tf_op jit(solution)/shard_map/ppermute | solution.py:111
  833.5 27.3 %collective-permute-start.61 = (bf16[256,2048]{1,0:T(8,128)(2,1)S(1)}, bf16[256,2048]{1,0:T(8,128)(2,1)S(1)}, u32[]{:S(2)}, u32[]{:S(2)}) collective-permute-start(bf16[256,2048]{1,0:T(8,128)(2,1)S(1)} %get-tuple-element.108), channel_id=1, source_target_pairs={{0,1},{1,2},{2,3},{4,5},{5,6},{6,7},{8,9},{9,10},{10,11},{12,13},{... | collective-permute-start | bytes 3145736 | tf_op jit(solution)/shard_map/ppermute | solution.py:111
  841.2 24.7 %collective-permute-start.59 = (bf16[2,192,1024]{2,1,0:T(8,128)(2,1)S(1)}, bf16[2,192,1024]{2,1,0:T(8,128)(2,1)S(1)}, u32[]{:S(2)}, u32[]{:S(2)}) collective-permute-start(bf16[2,192,1024]{2,1,0:T(8,128)(2,1)S(1)} %bitcast.325), channel_id=1, source_target_pairs={{0,16},{4,20},{8,24},{12,28},{16,0},{20,4},{24,8},{28,12},{1,17},{... | collective-permute-start | bytes 2359304 | tf_op jit(solution)/shard_map/ppermute | solution.py:52
  842.4 26.0 %collective-permute-start.57 = (bf16[2,192,1024]{2,1,0:T(8,128)(2,1)S(1)}, bf16[2,192,1024]{2,1,0:T(8,128)(2,1)S(1)}, u32[]{:S(2)}, u32[]{:S(2)}) collective-permute-start(bf16[2,192,1024]{2,1,0:T(8,128)(2,1)S(1)} %slice_bitcast_fusion.4), channel_id=1, source_target_pairs={{0,8},{4,12},{8,0},{12,4},{16,24},{20,28},{24,16},{28,20},{1,9},{5... | collective-permute-start | bytes 2359304 | tf_op jit(solution)/shard_map/ppermute | solution.py:52
  861.4 25.9 %collective-permute-start.63 = (bf16[256,2048]{1,0:T(8,128)(2,1)S(1)}, bf16[256,2048]{1,0:T(8,128)(2,1)S(1)}, u32[]{:S(2)}, u32[]{:S(2)}) collective-permute-start(bf16[256,2048]{1,0:T(8,128)(2,1)S(1)} %get-tuple-element.110), channel_id=1, source_target_pairs={{0,1},{1,2},{2,3},{4,5},{5,6},{6,7},{8,9},{9,10},{10,11},{12,13},{... | collective-permute-start | bytes 3145736 | tf_op jit(solution)/shard_map/ppermute | solution.py:111
  867.2 25.4 %collective-permute-start.64 = (bf16[256,2048]{1,0:T(8,128)(2,1)S(1)}, bf16[256,2048]{1,0:T(8,128)(2,1)S(1)}, u32[]{:S(2)}, u32[]{:S(2)}) collective-permute-start(bf16[256,2048]{1,0:T(8,128)(2,1)S(1)} %get-tuple-element.111), channel_id=1, source_target_pairs={{1,0},{2,1},{3,2},{5,4},{6,5},{7,6},{9,8},{10,9},{11,10},{13,12},{... | collective-permute-start | bytes 3145736 | tf_op jit(solution)/shard_map/ppermute | solution.py:111
  868.8 32.2 %collective-permute-start.58 = (bf16[192,1024]{1,0:T(8,128)(2,1)S(1)}, bf16[192,1024]{1,0:T(8,128)(2,1)S(1)}, u32[]{:S(2)}, u32[]{:S(2)}) collective-permute-start(bf16[192,1024]{1,0:T(8,128)(2,1)S(1)} %slice_bitcast_fusion.14), channel_id=1, source_target_pairs={{0,16},{4,20},{8,24},{12,28},{16,0},{20,4},{24,8},{28,12},{1,17},{... | collective-permute-start | bytes 1179656 | tf_op jit(solution)/shard_map/ppermute | solution.py:52
  893.9 26.2 %collective-permute-start.66 = (bf16[256,2048]{1,0:T(8,128)(2,1)}, bf16[256,2048]{1,0:T(8,128)(2,1)}, u32[]{:S(2)}, u32[]{:S(2)}) collective-permute-start(bf16[256,2048]{1,0:T(8,128)(2,1)} %add_convert_fusion.5), channel_id=1, source_target_pairs={{1,0},{2,1},{3,2},{5,4},{6,5},{7,6},{9,8},{10,9},{11,10},{13,12},{... | collective-permute-start | bytes 3145736 | tf_op jit(solution)/shard_map/ppermute | solution.py:111
  895.2 26.1 %collective-permute-start.65 = (bf16[256,2048]{1,0:T(8,128)(2,1)}, bf16[256,2048]{1,0:T(8,128)(2,1)}, u32[]{:S(2)}, u32[]{:S(2)}) collective-permute-start(bf16[256,2048]{1,0:T(8,128)(2,1)} %add_convert_fusion.6), channel_id=1, source_target_pairs={{0,1},{1,2},{2,3},{4,5},{5,6},{6,7},{8,9},{9,10},{10,11},{12,13},{... | collective-permute-start | bytes 3145736 | tf_op jit(solution)/shard_map/ppermute | solution.py:111
  906.4 29.6 %all-to-all-start.4 = ((f32[32,1,1280]{2,1,0:T(1,128)}), f32[32,1,1280]{2,1,0:T(1,128)S(1)}, u32[]{:S(2)}, u32[]{:S(2)}) async-start(f32[32,1,1280]{2,1,0:T(1,128)} %all_to_all.28), calls=%async_computation.6 | async-start | bytes 327680 | tf_op jit(solution)/shard_map/all_to_all | solution.py:729
  913.7 37.4 %collective-permute-start.71 = (bf16[2,256,2048]{2,1,0:T(8,128)(2,1)}, bf16[2,256,2048]{2,1,0:T(8,128)(2,1)}, u32[]{:S(2)}, u32[]{:S(2)}) collective-permute-start(bf16[2,256,2048]{2,1,0:T(8,128)(2,1)} %fusion.28), channel_id=1, source_target_pairs={{0,4},{4,0},{1,5},{5,1},{2,6},{6,2},{3,7},{7,3},{8,12},{12,8},{9,1... | collective-permute-start | bytes 6291464 | tf_op jit(solution)/shard_map/ppermute | solution.py:151
  924.4 24.3 %collective-permute-start.70 = (bf16[64,2048]{1,0:T(8,128)(2,1)}, bf16[64,2048]{1,0:T(8,128)(2,1)}, u32[]{:S(2)}, u32[]{:S(2)}) collective-permute-start(bf16[64,2048]{1,0:T(8,128)(2,1)} %get-tuple-element.230), channel_id=1, source_target_pairs={{0,0},{5,1},{10,2},{11,3},{12,4},{17,5},{22,6},{23,7},{24,8},{29,9... | collective-permute-start | bytes 786440 | tf_op jit(solution)/shard_map/ppermute | solution.py:711
  928.1 20.6 %collective-permute-start.69 = (bf16[64,2048]{1,0:T(8,128)(2,1)}, bf16[64,2048]{1,0:T(8,128)(2,1)}, u32[]{:S(2)}, u32[]{:S(2)}) collective-permute-start(bf16[64,2048]{1,0:T(8,128)(2,1)} %get-tuple-element.231), channel_id=1, source_target_pairs={{0,0},{5,1},{6,2},{11,3},{12,4},{17,5},{18,6},{23,7},{24,8},{29,9}... | collective-permute-start | bytes 786440 | tf_op jit(solution)/shard_map/ppermute | solution.py:711
  (103 other events, 1674.0 us)
Sparse Core Ops, SparseCore 0:
  34.6 83.0 all-gather.14
  185.0 122.5 all-gather.6
  309.4 52.5 all-gather.8
  363.7 87.4 all-gather.10
  452.9 52.5 all-gather.12
  508.9 52.5 reduce-scatter.4
  564.5 52.5 reduce-scatter.6
  620.8 96.8 reduce-scatter.8
  743.2 85.4 reduce-scatter.10

commit v8 on v6

--- a/solution.py
+++ b/solution.py
@@ -488,7 +488,7 @@
         [lax.dynamic_index_in_dim(qkv_slots, slot_of[k], 0, keepdims=False) for k in range(3)],
         axis=0,
     )
-    out_cols = after(w_out, *slot_steps[-1]).reshape(orow, dps, width).transpose(1, 0, 2)
+    out_cols = after(w_out, *slot_steps[2]).reshape(orow, dps, width).transpose(1, 0, 2)
     out_cols = jnp.broadcast_to(out_cols[:, None], (dps, zs, orow, width))
     w_out_c = lax.all_to_all(
         out_cols.reshape(world, orow, width), ALL, 0, 0, tiled=True
@@ -515,7 +515,7 @@
             shape_of(all_rows, 3 * width, f32),
             shape_of(8, all_rows, f32),
         ],
-        tuple(tok_pieces) + (gains_f[:, 0][None], w_three),
+        tuple(tok_pieces) + (after(gains_f[:, 0][None], w_out_c), w_three),
     )
     gu_half = core_half(after(w_gate_up, hidden_one))
     sums = sum_dp(sums, dps)

time: 947 us -> 942 us (level)
  waiting for transfers between devices: 280 us -> 265 us
    all_to_all x1, waiting for transfers between devices: 37.6 us -> 11.8 us  [per_device(): lax.all_to_all(out_cols.reshape(world, orow, width), ALL, 0, 0, tiled=True)]
    ppermute x30, starting transfers between devices: 83.7 us -> 103 us  [line(): lax.ppermute(value, 'z', [(j, j + step) for j in range(zs) if 0 <= j + st...]
    ppermute x28, waiting for transfers between devices: 108 us -> 121 us  [flip(): return lax.ppermute(value, DP, [(i, i ^ 1 << bit) for i in range(size)])]
    unnamed x180 -> x178, local copies, waits for them, and re-layouts: 23.9 us -> 24.6 us
  transfers between devices with their start and end apart: 85 -> 85, of which waited for: 37 -> 38; matrix products, arithmetic and copies ran while one was open for 34% -> 35% of each run, Pallas kernels for 12% -> 12%
where the time goes in v8:
time: 942 us; the launch traced here: 933 us
  waiting for transfers between devices  265 us (28%)
  matrix products  177 us (19%)
  starting transfers between devices  160 us (17%)
  Pallas kernels  113 us (12%)
  other arithmetic  96.5 us (10%)
  local copies, waits for them, and re-layouts  78 us (8%)
  between operations  22.3 us (2%)
  blocking collectives  20.8 us (2%)
    dot_general x13, matrix products, mm(): lax.dot_general(a, b, (((ca,), (cb,)), ((), ())), preferred_element_type=...  173 us
    ppermute x28, waiting for transfers between devices, flip(): return lax.ppermute(value, DP, [(i, i ^ 1 << bit) for i in range(size)])  121 us
    ppermute x30, waiting for transfers between devices, line(): lax.ppermute(value, 'z', [(j, j + step) for j in range(zs) if 0 <= j + st...  113 us
    ppermute x30, starting transfers between devices, line(): lax.ppermute(value, 'z', [(j, j + step) for j in range(zs) if 0 <= j + st...  103 us
    pallas_call x4, Pallas kernels, run_blocks(): pl.pallas_call(body, grid=(rows // BLOCK,), in_specs=in_specs, out_specs=...  71.5 us
    pallas_call x2, Pallas kernels, weight_grad(): pl.pallas_call(functools.partial(weight_grad_kernel, half), grid=(b.shape...  41.8 us
    unnamed x178, local copies, waits for them, and re-layouts  24.6 us
    all_to_all x1, blocking collectives, per_device(): lax.all_to_all(cols.transpose(1, 2, 0, 3).reshape(2 * zs, mine, rows), ('...  20.8 us
  transfers between devices with their start and end apart: 85, of which 38 were waited for; matrix products, arithmetic and copies ran while one was open for 35% of the time, Pallas kernels for 12%

profile of v8, /device:TPU:0, one launch (start us, length us, event | category | flops | bytes accessed | tf_op | source)
XLA Modules:
  0.0 932.7 jit_solution(5567500919712106327)
XLA Ops:
  16.6 3.6 collective-permute-start.7
  25.9 9.1 all-to-all-start
  39.0 5.4 all-to-all-done
  56.5 15.7 %collective-permute-done = bf16[192,1024]{1,0:T(8,128)(2,1)S(1)} collective-permute-done((bf16[192,1024]{1,0:T(8,128)(2,1)}, bf16[192,1024]{1,0:T(8,128)(2,1)S(1)}, u32[]{:S(2)}, u32[]{:S(2)}) %collective-permute-start) | collective-permute-done | bytes 393248 | tf_op jit(solution)/shard_map/ppermute | solution.py:52
  75.4 5.7 collective-permute-start.12
  89.6 12.7 %collective-permute-done.3 = bf16[2,192,1024]{2,1,0:T(8,128)(2,1)} collective-permute-done((bf16[2,192,1024]{2,1,0:T(8,128)(2,1)}, bf16[2,192,1024]{2,1,0:T(8,128)(2,1)}, u32[]{:S(2)}, u32[]{:S(2)}) %collective-permute-start.3) | collective-permute-done | bytes 786464 | tf_op jit(solution)/shard_map/ppermute | solution.py:52
  115.4 5.4 collective-permute-start.15
  125.4 3.9 collective-permute-done.14
  133.9 4.2 collective-permute-done.15
  144.8 11.8 %all-to-all-done.1 = bf16[32,64,256]{2,1,0:T(8,128)(2,1)S(1)} async-done(((bf16[32,64,256]{2,1,0:T(8,128)(2,1)}), bf16[32,64,256]{2,1,0:T(8,128)(2,1)S(1)}, u32[]{:S(2)}, u32[]{:S(2)}) %all-to-all-start.1) | async-done | bytes 1048608 | tf_op jit(solution)/shard_map/all_to_all | solution.py:493
  156.6 13.3 %shard_map.188 = (bf16[1536,2048]{1,0:T(8,128)(2,1)}, f32[1536,768]{1,0:T(8,128)}, f32[8,1536]{1,0:T(8,128)}) custom-call(bf16[768,1024]{1,0:T(8,128)(2,1)} %bitcast.4.a_own, bf16[768,1024]{1,0:T(8,128)(2,1)} %bitcast.9.b_own, bf16[768,1024]{1,0:T(8,128)(2,1)} %collective-permute-done.4.a_other, bf16[768,1024]{1,0:T(8,128)(2,1)} %collective-permute-done.5.b_other, ...), custom_call_target="tpu_custom_call" | custom-call | flops 1 | bytes 1 | tf_op jit(solution)/shard_map/pallas_call | solution.py:349
  172.0 4.1 collective-permute-done.32
  191.8 18.7 %shard_map.189 = (bf16[1536,256]{1,0:T(8,128)(2,1)}, bf16[768,2048]{1,0:T(8,128)(2,1)}, bf16[768,2048]{1,0:T(8,128)(2,1)}) custom-call(f32[1536,768]{1,0:T(8,128)} %get-tuple-element.71.raw_ref, f32[8,1536]{1,0:T(8,128)} %pad.11.sum_ref, f32[8,256]{1,0:T(8,128)} %pad.12.gain_ref, f32[384,128]{1,0:T(8,128)} %bitcast.310, f32[384,128]{1,0:T(8,128)} %bitcast.312, ...), custom_call_target="tpu_custom_call" | custom-call | flops 1 | bytes 1 | tf_op jit(solution)/shard_map/pallas_call | solution.py:349
  210.5 5.9 collective-permute-done.19
  221.0 33.4 %collective-permute-done.20 = bf16[2,192,1024]{2,1,0:T(8,128)(2,1)S(1)} collective-permute-done((bf16[2,192,1024]{2,1,0:T(8,128)(2,1)S(1)}, bf16[2,192,1024]{2,1,0:T(8,128)(2,1)S(1)}, u32[]{:S(2)}, u32[]{:S(2)}) %collective-permute-start.20) | collective-permute-done | bytes 786464 | tf_op jit(solution)/shard_map/ppermute | solution.py:52
  260.1 10.6 %collective-permute-done.21 = bf16[192,1024]{1,0:T(8,128)(2,1)} collective-permute-done((bf16[192,1024]{1,0:T(8,128)(2,1)S(1)}, bf16[192,1024]{1,0:T(8,128)(2,1)}, u32[]{:S(2)}, u32[]{:S(2)}) %collective-permute-start.21) | collective-permute-done | bytes 393248 | tf_op jit(solution)/shard_map/ppermute | solution.py:52
  283.5 19.8 %collective-permute-start.24 = (bf16[192,2048]{1,0:T(8,128)(2,1)S(1)}, bf16[192,2048]{1,0:T(8,128)(2,1)S(1)}, u32[]{:S(2)}, u32[]{:S(2)}) collective-permute-start(bf16[192,2048]{1,0:T(8,128)(2,1)S(1)} %get-tuple-element.179), channel_id=1, source_target_pairs={{0,1},{1,2},{2,3},{4,5},{5,6},{6,7},{8,9},{9,10},{10,11},{12,13},{... | collective-permute-start | bytes 2359304 | tf_op jit(solution)/shard_map/ppermute | solution.py:111
  308.8 12.0 %collective-permute-done.24 = bf16[192,2048]{1,0:T(8,128)(2,1)S(1)} collective-permute-done((bf16[192,2048]{1,0:T(8,128)(2,1)S(1)}, bf16[192,2048]{1,0:T(8,128)(2,1)S(1)}, u32[]{:S(2)}, u32[]{:S(2)}) %collective-permute-start.24) | collective-permute-done | bytes 786464 | tf_op jit(solution)/shard_map/ppermute | solution.py:111
  320.7 4.2 collective-permute-done.25
  326.2 4.6 collective-permute-start.29
  330.8 14.8 %collective-permute-done.27 = bf16[192,2048]{1,0:T(8,128)(2,1)S(1)} collective-permute-done((bf16[192,2048]{1,0:T(8,128)(2,1)S(1)}, bf16[192,2048]{1,0:T(8,128)(2,1)S(1)}, u32[]{:S(2)}, u32[]{:S(2)}) %collective-permute-start.27) | collective-permute-done | bytes 786464 | tf_op jit(solution)/shard_map/ppermute | solution.py:111
  346.9 4.6 collective-permute-start.30
  351.5 14.3 %collective-permute-done.28 = bf16[192,2048]{1,0:T(8,128)(2,1)S(1)} collective-permute-done((bf16[192,2048]{1,0:T(8,128)(2,1)S(1)}, bf16[192,2048]{1,0:T(8,128)(2,1)S(1)}, u32[]{:S(2)}, u32[]{:S(2)}) %collective-permute-start.28) | collective-permute-done | bytes 786464 | tf_op jit(solution)/shard_map/ppermute | solution.py:111
  376.9 4.0 constant_dynamic-update-slice_fusion.5.b_ref
  380.9 4.5 fusion.93
  385.7 19.1 %fusion.94 = f32[1536,2048]{1,0:T(8,128)} fusion(bf16[1536,2048]{1,0:T(8,128)(2,1)} %constant_dynamic-update-slice_fusion.5.b_ref, bf16[2048,2048]{1,0:T(8,128)(2,1)} %all-gather.9.cloned.1.call-done), kind=kOutput, calls=%fused_computation.294 | convolution fusion | flops 12884901888 | bytes 27262976 | tf_op jit(solution)/shard_map/dot_general | solution.py:44
  404.7 18.3 %multiply_convert_fusion.4 = (bf16[1536,1024]{1,0:T(8,128)(2,1)S(1)}, bf16[1536,1024]{1,0:T(8,128)(2,1)S(1)}, bf16[1536,1024]{1,0:T(8,128)(2,1)}) fusion(f32[1536,2048]{1,0:T(8,128)} %fusion.94, bf16[2048,1024]{1,0:T(8,128)(2,1)} %all-gather.7.cloned.1.call-done, bf16[1536,2048]{1,0:T(8,128)(2,1)} %copy-done.57, f32[1536]{0:T(1024)S(1)} %broadcast_select_fusion.9), kind=kOutput, calls=%fused_computation.40 | convolution fusion | flops 6475481088 | bytes 32512000 | tf_op jit(solution)/shard_map/dot_general | solution.py:44
  423.1 20.4 %convolution_convert_fusion.2 = bf16[1536,2048]{1,0:T(8,128)(2,1)} fusion(bf16[2048,2048]{1,0:T(8,128)(2,1)} %all-gather.9.cloned.1.call-done, bf16[1536,1024]{1,0:T(8,128)(2,1)S(1)} %get-tuple-element.84.u_ref, bf16[1536,1024]{1,0:T(8,128)(2,1)S(1)} %get-tuple-element.83.g_ref), kind=kOutput, calls=%fused_computation.19 | convolution fusion | flops 12900630528 | bytes 20971520 | tf_op jit(solution)/shard_map/dot_general | solution.py:44
  443.6 8.9 convolution_convert_fusion.5
  452.6 19.2 %fusion.95 = f32[1536,2048]{1,0:T(8,128)} fusion(bf16[1536,2048]{1,0:T(8,128)(2,1)} %constant_dynamic-update-slice_fusion.5.b_ref, bf16[2048,2048]{1,0:T(8,128)(2,1)} %all-gather.11.cloned.1.call-done), kind=kOutput, calls=%fused_computation.295 | convolution fusion | flops 12884901888 | bytes 27262976 | tf_op jit(solution)/shard_map/dot_general | solution.py:44
  471.8 18.9 %multiply_convert_fusion.1 = (bf16[1536,1024]{1,0:T(8,128)(2,1)S(1)}, bf16[1536,1024]{1,0:T(8,128)(2,1)}, bf16[1536,1024]{1,0:T(8,128)(2,1)S(1)}) fusion(f32[1536,2048]{1,0:T(8,128)} %fusion.95, bf16[2048,1024]{1,0:T(8,128)(2,1)} %all-gather.13.cloned.1.call-done, bf16[1536,2048]{1,0:T(8,128)(2,1)} %copy-done.57, f32[1536]{0:T(1024)S(1)} %broadcast_select_fusion.8), kind=kOutput, calls=%fused_computation.34 | convolution fusion | flops 6475481088 | bytes 32512000 | tf_op jit(solution)/shard_map/dot_general | solution.py:44
  492.4 12.4 %convolution_convert_fusion.4 = bf16[2048,1024]{1,0:T(8,128)(2,1)} fusion(bf16[1536,1024]{1,0:T(8,128)(2,1)S(1)} %get-tuple-element.187, bf16[1536,2048]{1,0:T(8,128)(2,1)} %copy-done.57, f32[1536]{0:T(1024)S(1)} %broadcast_select_fusion.8), kind=kOutput, calls=%fused_computation.54 | convolution fusion | flops 6453985280 | bytes 13637632 | tf_op jit(solution)/shard_map/dot_general | solution.py:44
  504.9 17.8 %add_convert_fusion = bf16[1536,2048]{1,0:T(8,128)(2,1)S(1)} fusion(bf16[1536,2048]{1,0:T(8,128)(2,1)} %convolution_convert_fusion.2, bf16[2048,2048]{1,0:T(8,128)(2,1)} %all-gather.11.cloned.1.call-done, bf16[1536,1024]{1,0:T(8,128)(2,1)} %get-tuple-element.88.u_ref, bf16[1536,1024]{1,0:T(8,128)(2,1)S(1)} %get-tuple-element.87.g_ref), kind=kOutput, calls=%fused_computation.16 | convolution fusion | flops 12913213440 | bytes 27262976 | tf_op jit(solution)/shard_map/dot_general | solution.py:44
  523.3 5.3 collective-permute-done.34
  531.6 6.2 collective-permute-start.35
  539.1 21.0 %shard_map.190 = bf16[2048,2048]{1,0:T(8,128)(2,1)} custom-call(bf16[1536,1024]{1,0:T(8,128)(2,1)} %copy-done.35, bf16[1536,1024]{1,0:T(8,128)(2,1)} %copy-done.36, bf16[1536,2048]{1,0:T(8,128)(2,1)} %constant_dynamic-update-slice_fusion.5.b_ref), custom_call_target="tpu_custom_call" | custom-call | flops 1 | bytes 1 | tf_op jit(solution)/shard_map/pallas_call | solution.py:372
  560.1 11.9 %convolution_convert_fusion.3 = bf16[1536,2048]{1,0:T(8,128)(2,1)} fusion(bf16[1536,1024]{1,0:T(8,128)(2,1)} %get-tuple-element.188, bf16[2048,1024]{1,0:T(8,128)(2,1)} %all-gather.7.cloned.1.call-done), kind=kOutput, calls=%fused_computation.20 | convolution fusion | flops 6445596672 | bytes 13631488 | tf_op jit(solution)/shard_map/dot_general | solution.py:44
  572.0 13.2 %fusion.4 = (f32[1536]{0:T(1024)S(1)}, f32[1536]{0:T(1024)S(1)}, bf16[1536,2048]{1,0:T(8,128)(2,1)S(1)}) fusion(bf16[1536,2048]{1,0:T(8,128)(2,1)} %convolution_convert_fusion.3, bf16[1536,2048]{1,0:T(8,128)(2,1)} %copy-done.57, f32[1536]{0:T(1024)S(1)} %broadcast_select_fusion.8, f32[1536]{0:T(1024)S(1)} %broadcast_select_fusion.9, ...), kind=kOutput, calls=%fused_computation.14 | convolution fusion | flops 6480196608 | bytes 26238976 | tf_op jit(solution)/shard_map/dot_general | solution.py:44
  592.3 4.2 collective-permute-start.37
  598.0 6.3 add_convert_fusion.3
  604.3 20.9 %shard_map.191 = bf16[2048,2048]{1,0:T(8,128)(2,1)} custom-call(bf16[1536,1024]{1,0:T(8,128)(2,1)} %copy-done.34, bf16[1536,1024]{1,0:T(8,128)(2,1)} %get-tuple-element.88.u_ref, bf16[1536,2048]{1,0:T(8,128)(2,1)} %constant_dynamic-update-slice_fusion.5.b_ref), custom_call_target="tpu_custom_call" | custom-call | flops 1 | bytes 1 | tf_op jit(solution)/shard_map/pallas_call | solution.py:372
  628.8 5.3 collective-permute-start.39
  636.6 20.8 %all_to_all.34 = f32[8,2,192]{2,1,0:T(2,128)S(1)} all-to-all(f32[8,2,192]{2,1,0:T(2,128)S(1)} %bitcast.337), channel_id=1, replica_groups=mesh['q'=4,'c'=2,'z'=4] {'c','z'}, dimensions={0} | all-to-all | bytes 24576 | tf_op jit(solution)/shard_map/all_to_all | solution.py:620
  662.8 13.8 %collective-permute-done.49 = bf16[192,1024]{1,0:T(8,128)(2,1)S(1)} collective-permute-done((bf16[192,1024]{1,0:T(8,128)(2,1)S(1)}, bf16[192,1024]{1,0:T(8,128)(2,1)S(1)}, u32[]{:S(2)}, u32[]{:S(2)}) %collective-permute-start.49) | collective-permute-done | bytes 393248 | tf_op jit(solution)/shard_map/ppermute | solution.py:52
  683.9 12.2 %collective-permute-done.50 = bf16[2,192,1024]{2,1,0:T(8,128)(2,1)S(1)} collective-permute-done((bf16[2,192,1024]{2,1,0:T(8,128)(2,1)S(1)}, bf16[2,192,1024]{2,1,0:T(8,128)(2,1)S(1)}, u32[]{:S(2)}, u32[]{:S(2)}) %collective-permute-start.50) | collective-permute-done | bytes 786464 | tf_op jit(solution)/shard_map/ppermute | solution.py:52
  698.3 4.2 collective-permute-done.42
  711.3 4.4 collective-permute-start.43
  717.0 26.7 %shard_map.192 = (f32[1536,512]{1,0:T(8,128)}, bf16[1536,256]{1,0:T(8,128)(2,1)}, f32[8,1536]{1,0:T(8,128)}, f32[8,256]{1,0:T(8,128)}, f32[2048,256]{1,0:T(8,128)}) custom-call(f32[1536,768]{1,0:T(8,128)} %get-tuple-element.71.raw_ref, f32[8,1536]{1,0:T(8,128)} %pad.11.sum_ref, f32[8,256]{1,0:T(8,128)} %pad.12.gain_ref, f32[384,128]{1,0:T(8,128)} %bitcast.311, ...), custom_call_target="tpu_custom_call" | custom-call | flops 1 | bytes 1 | tf_op jit(solution)/shard_map/pallas_call | solution.py:349
  746.1 4.0 collective-permute-done.54
  753.7 5.7 collective-permute-start.45
  761.4 12.8 %shard_map.193 = (bf16[1536,768]{1,0:T(8,128)(2,1)}, bf16[768,2048]{1,0:T(8,128)(2,1)}, bf16[768,2048]{1,0:T(8,128)(2,1)}) custom-call(f32[1536,768]{1,0:T(8,128)} %get-tuple-element.71.raw_ref, f32[8,1536]{1,0:T(8,128)} %pad.11.sum_ref, f32[1536,512]{1,0:T(8,128)} %get-tuple-element.99.back_ref, bf16[1536,256]{1,0:T(8,128)(2,1)} %get-tuple-element.100.dv_ref, ...), custom_call_target="tpu_custom_call" | custom-call | flops 1 | bytes 1 | tf_op jit(solution)/shard_map/pallas_call | solution.py:349
  774.9 5.0 collective-permute-done.46
  781.8 8.0 convolution_convert_fusion.6
  808.1 16.2 %collective-permute-done.61 = bf16[256,2048]{1,0:T(8,128)(2,1)S(1)} collective-permute-done((bf16[256,2048]{1,0:T(8,128)(2,1)S(1)}, bf16[256,2048]{1,0:T(8,128)(2,1)S(1)}, u32[]{:S(2)}, u32[]{:S(2)}) %collective-permute-start.61) | collective-permute-done | bytes 1048608 | tf_op jit(solution)/shard_map/ppermute | solution.py:111
  824.2 4.2 collective-permute-done.62
  832.3 4.6 collective-permute-start.63
  840.7 14.1 %collective-permute-done.64 = bf16[256,2048]{1,0:T(8,128)(2,1)S(1)} collective-permute-done((bf16[256,2048]{1,0:T(8,128)(2,1)S(1)}, bf16[256,2048]{1,0:T(8,128)(2,1)S(1)}, u32[]{:S(2)}, u32[]{:S(2)}) %collective-permute-start.64) | collective-permute-done | bytes 1048608 | tf_op jit(solution)/shard_map/ppermute | solution.py:111
  859.0 5.4 collective-permute-start.65
  878.1 6.8 collective-permute-done.65
  884.9 5.4 collective-permute-done.66
  893.3 3.7 collective-permute-start.68
  897.0 3.6 collective-permute-start.69
  909.1 5.0 fusion.40
  921.8 3.9 maximum_convert_fusion
  (508 shorter events, 244.4 us)
Async XLA Ops:
  7.2 133.3 %all-gather.7.cloned.1.call-start = ((), (), s32[]{:S(2)}) async-start(), calls=%async_computation.9 | async-start | bytes 5242880 | tf_op jit(solution)/shard_map/all_gather | solution.py:496
  15.0 22.9 %collective-permute-start.6 = (bf16[64,2048]{1,0:T(8,128)(2,1)}, bf16[64,2048]{1,0:T(8,128)(2,1)S(1)}, u32[]{:S(2)}, u32[]{:S(2)}) collective-permute-start(bf16[64,2048]{1,0:T(8,128)(2,1)} %get-tuple-element.246), channel_id=1, source_target_pairs={{0,0},{1,1},{2,6},{3,11},{4,12},{5,13},{6,18},{7,23},{8,24},{9,25}... | collective-permute-start | bytes 786440 | tf_op jit(solution)/shard_map/ppermute | solution.py:418
  16.6 21.3 %collective-permute-start.7 = (bf16[64,2048]{1,0:T(8,128)(2,1)}, bf16[64,2048]{1,0:T(8,128)(2,1)}, u32[]{:S(2)}, u32[]{:S(2)}) collective-permute-start(bf16[64,2048]{1,0:T(8,128)(2,1)} %get-tuple-element.248), channel_id=1, source_target_pairs={{0,0},{1,5},{2,6},{3,11},{4,12},{5,17},{6,18},{7,23},{8,24},{9,29}... | collective-permute-start | bytes 786440 | tf_op jit(solution)/shard_map/ppermute | solution.py:418
  20.2 17.7 %collective-permute-start.8 = (bf16[64,2048]{1,0:T(8,128)(2,1)S(1)}, bf16[64,2048]{1,0:T(8,128)(2,1)}, u32[]{:S(2)}, u32[]{:S(2)}) collective-permute-start(bf16[64,2048]{1,0:T(8,128)(2,1)S(1)} %get-tuple-element.247), channel_id=1, source_target_pairs={{0,0},{1,5},{2,10},{3,11},{4,12},{5,17},{6,22},{7,23},{8,24},{9,29... | collective-permute-start | bytes 786440 | tf_op jit(solution)/shard_map/ppermute | solution.py:418
  25.9 18.4 %all-to-all-start = ((bf16[32,2,1504]{2,1,0:T(2,128)(2,1)}), bf16[32,2,1504]{2,1,0:T(2,128)(2,1)}, u32[]{:S(2)}, u32[]{:S(2)}) async-start(bf16[32,2,1504]{2,1,0:T(2,128)(2,1)} %reshape.529), calls=%async_computation | async-start | bytes 393216 | tf_op jit(solution)/shard_map/all_to_all | solution.py:441
  47.9 27.5 %collective-permute-start.10 = (bf16[192,2048]{1,0:T(8,128)(2,1)S(1)}, bf16[192,2048]{1,0:T(8,128)(2,1)}, u32[]{:S(2)}, u32[]{:S(2)}) collective-permute-start(bf16[192,2048]{1,0:T(8,128)(2,1)S(1)} %pad_maximum_fusion.15), channel_id=1, source_target_pairs={{0,1},{1,2},{2,3},{4,5},{5,6},{6,7},{8,9},{9,10},{10,11},{12,13},{... | collective-permute-start | bytes 2359304 | tf_op jit(solution)/shard_map/ppermute | solution.py:111
  50.4 25.0 %collective-permute-start.11 = (bf16[192,2048]{1,0:T(8,128)(2,1)S(1)}, bf16[192,2048]{1,0:T(8,128)(2,1)}, u32[]{:S(2)}, u32[]{:S(2)}) collective-permute-start(bf16[192,2048]{1,0:T(8,128)(2,1)S(1)} %pad_maximum_fusion.15), channel_id=1, source_target_pairs={{1,0},{2,1},{3,2},{5,4},{6,5},{7,6},{9,8},{10,9},{11,10},{13,12},{... | collective-permute-start | bytes 2359304 | tf_op jit(solution)/shard_map/ppermute | solution.py:111
  51.7 20.5 %collective-permute-start = (bf16[192,1024]{1,0:T(8,128)(2,1)}, bf16[192,1024]{1,0:T(8,128)(2,1)S(1)}, u32[]{:S(2)}, u32[]{:S(2)}) collective-permute-start(bf16[192,1024]{1,0:T(8,128)(2,1)} %get-tuple-element.254), channel_id=1, source_target_pairs={{0,8},{4,12},{8,0},{12,4},{16,24},{20,28},{24,16},{28,20},{1,9},{5... | collective-permute-start | bytes 1179656 | tf_op jit(solution)/shard_map/ppermute | solution.py:52
  55.0 47.3 %collective-permute-start.3 = (bf16[2,192,1024]{2,1,0:T(8,128)(2,1)}, bf16[2,192,1024]{2,1,0:T(8,128)(2,1)}, u32[]{:S(2)}, u32[]{:S(2)}) collective-permute-start(bf16[2,192,1024]{2,1,0:T(8,128)(2,1)} %get-tuple-element.250), channel_id=1, source_target_pairs={{0,8},{4,12},{8,0},{12,4},{16,24},{20,28},{24,16},{28,20},{1,9},{5... | collective-permute-start | bytes 2359304 | tf_op jit(solution)/shard_map/ppermute | solution.py:52
  74.2 30.6 %collective-permute-start.1 = (bf16[2,192,1024]{2,1,0:T(8,128)(2,1)}, bf16[2,192,1024]{2,1,0:T(8,128)(2,1)}, u32[]{:S(2)}, u32[]{:S(2)}) collective-permute-start(bf16[2,192,1024]{2,1,0:T(8,128)(2,1)} %get-tuple-element.256), channel_id=1, source_target_pairs={{0,16},{4,20},{8,24},{12,28},{16,0},{20,4},{24,8},{28,12},{1,17},{... | collective-permute-start | bytes 2359304 | tf_op jit(solution)/shard_map/ppermute | solution.py:52
  75.4 31.9 %collective-permute-start.12 = (bf16[192,2048]{1,0:T(8,128)(2,1)}, bf16[192,2048]{1,0:T(8,128)(2,1)}, u32[]{:S(2)}, u32[]{:S(2)}) collective-permute-start(bf16[192,2048]{1,0:T(8,128)(2,1)} %collective-permute-done.10), channel_id=1, source_target_pairs={{0,1},{1,2},{2,3},{4,5},{5,6},{6,7},{8,9},{9,10},{10,11},{12,13},{... | collective-permute-start | bytes 2359304 | tf_op jit(solution)/shard_map/ppermute | solution.py:111
  81.1 26.2 %collective-permute-start.13 = (bf16[192,2048]{1,0:T(8,128)(2,1)}, bf16[192,2048]{1,0:T(8,128)(2,1)}, u32[]{:S(2)}, u32[]{:S(2)}) collective-permute-start(bf16[192,2048]{1,0:T(8,128)(2,1)} %collective-permute-done.11), channel_id=1, source_target_pairs={{1,0},{2,1},{3,2},{5,4},{6,5},{7,6},{9,8},{10,9},{11,10},{13,12},{... | collective-permute-start | bytes 2359304 | tf_op jit(solution)/shard_map/ppermute | solution.py:111
  107.3 22.1 %collective-permute-start.14 = (bf16[192,2048]{1,0:T(8,128)(2,1)}, bf16[192,2048]{1,0:T(8,128)(2,1)}, u32[]{:S(2)}, u32[]{:S(2)}) collective-permute-start(bf16[192,2048]{1,0:T(8,128)(2,1)} %collective-permute-done.13), channel_id=1, source_target_pairs={{1,0},{2,1},{3,2},{5,4},{6,5},{7,6},{9,8},{10,9},{11,10},{13,12},{... | collective-permute-start | bytes 2359304 | tf_op jit(solution)/shard_map/ppermute | solution.py:111
  114.9 41.8 %collective-permute-start.5 = (bf16[768,1024]{1,0:T(8,128)(2,1)}, bf16[768,1024]{1,0:T(8,128)(2,1)}, u32[]{:S(2)}, u32[]{:S(2)}) collective-permute-start(bf16[768,1024]{1,0:T(8,128)(2,1)} %bitcast.9.b_own), channel_id=1, source_target_pairs={{0,4},{4,0},{8,12},{12,8},{16,20},{20,16},{24,28},{28,24},{1,5},{5... | collective-permute-start | bytes 4718600 | tf_op jit(solution)/shard_map/ppermute | solution.py:52
  114.9 41.8 %collective-permute-start.4 = (bf16[768,1024]{1,0:T(8,128)(2,1)}, bf16[768,1024]{1,0:T(8,128)(2,1)}, u32[]{:S(2)}, u32[]{:S(2)}) collective-permute-start(bf16[768,1024]{1,0:T(8,128)(2,1)} %bitcast.4.a_own), channel_id=1, source_target_pairs={{0,4},{4,0},{8,12},{12,8},{16,20},{20,16},{24,28},{28,24},{1,5},{5... | collective-permute-start | bytes 4718600 | tf_op jit(solution)/shard_map/ppermute | solution.py:52
  115.4 22.8 %collective-permute-start.15 = (bf16[192,2048]{1,0:T(8,128)(2,1)}, bf16[192,2048]{1,0:T(8,128)(2,1)}, u32[]{:S(2)}, u32[]{:S(2)}) collective-permute-start(bf16[192,2048]{1,0:T(8,128)(2,1)} %collective-permute-done.12), channel_id=1, source_target_pairs={{0,1},{1,2},{2,3},{4,5},{5,6},{6,7},{8,9},{9,10},{10,11},{12,13},{... | collective-permute-start | bytes 2359304 | tf_op jit(solution)/shard_map/ppermute | solution.py:111
  122.0 34.6 %all-to-all-start.1 = ((bf16[32,64,256]{2,1,0:T(8,128)(2,1)}), bf16[32,64,256]{2,1,0:T(8,128)(2,1)S(1)}, u32[]{:S(2)}, u32[]{:S(2)}) async-start(bf16[32,64,256]{2,1,0:T(8,128)(2,1)} %bitcast.296), calls=%async_computation.1 | async-start | bytes 2097152 | tf_op jit(solution)/shard_map/all_to_all | solution.py:493
  125.4 145.4 %all-gather.15.cloned.1.call-start = ((), (), s32[]{:S(2)}) async-start(), calls=%async_computation.17 | async-start | bytes 3932160 | tf_op jit(solution)/shard_map/all_gather | solution.py:497
  140.5 245.2 %all-gather.9.cloned.1.call-start = ((), (), s32[]{:S(2)}) async-start(), calls=%async_computation.10 | async-start | bytes 10485760 | tf_op jit(solution)/shard_map/all_gather | solution.py:541
  179.3 273.3 %all-gather.11.cloned.1.call-start = ((), (), s32[]{:S(2)}) async-start(), calls=%async_computation.11 | async-start | bytes 10485760 | tf_op jit(solution)/shard_map/all_gather | solution.py:541
  219.8 34.6 %collective-permute-start.20 = (bf16[2,192,1024]{2,1,0:T(8,128)(2,1)S(1)}, bf16[2,192,1024]{2,1,0:T(8,128)(2,1)S(1)}, u32[]{:S(2)}, u32[]{:S(2)}) collective-permute-start(bf16[2,192,1024]{2,1,0:T(8,128)(2,1)S(1)} %slice_bitcast_fusion.6), channel_id=1, source_target_pairs={{0,8},{4,12},{8,0},{12,4},{16,24},{20,28},{24,16},{28,20},{1,9},{5... | collective-permute-start | bytes 2359304 | tf_op jit(solution)/shard_map/ppermute | solution.py:52
  220.1 36.0 %collective-permute-start.22 = (bf16[2,192,1024]{2,1,0:T(8,128)(2,1)S(1)}, bf16[2,192,1024]{2,1,0:T(8,128)(2,1)S(1)}, u32[]{:S(2)}, u32[]{:S(2)}) collective-permute-start(bf16[2,192,1024]{2,1,0:T(8,128)(2,1)S(1)} %bitcast.324), channel_id=1, source_target_pairs={{0,16},{4,20},{8,24},{12,28},{16,0},{20,4},{24,8},{28,12},{1,17},{... | collective-permute-start | bytes 2359304 | tf_op jit(solution)/shard_map/ppermute | solution.py:52
  270.7 201.1 %all-gather.13.cloned.1.call-start = ((), (), s32[]{:S(2)}) async-start(), calls=%async_computation.12 | async-start | bytes 5242880 | tf_op jit(solution)/shard_map/all_gather | solution.py:542
  278.1 28.3 %collective-permute-start.26 = (bf16[768,2048]{1,0:T(8,128)(2,1)}, bf16[768,2048]{1,0:T(8,128)(2,1)}, u32[]{:S(2)}, u32[]{:S(2)}) collective-permute-start(bf16[768,2048]{1,0:T(8,128)(2,1)} %pad_maximum_fusion.1), channel_id=1, source_target_pairs={{0,4},{4,0},{1,5},{5,1},{2,6},{6,2},{3,7},{7,3},{8,12},{12,8},{9,1... | collective-permute-start | bytes 9437192 | tf_op jit(solution)/shard_map/ppermute | solution.py:151
  283.5 37.2 %collective-permute-start.24 = (bf16[192,2048]{1,0:T(8,128)(2,1)S(1)}, bf16[192,2048]{1,0:T(8,128)(2,1)S(1)}, u32[]{:S(2)}, u32[]{:S(2)}) collective-permute-start(bf16[192,2048]{1,0:T(8,128)(2,1)S(1)} %get-tuple-element.179), channel_id=1, source_target_pairs={{0,1},{1,2},{2,3},{4,5},{5,6},{6,7},{8,9},{9,10},{10,11},{12,13},{... | collective-permute-start | bytes 2359304 | tf_op jit(solution)/shard_map/ppermute | solution.py:111
  303.3 21.6 %collective-permute-start.25 = (bf16[192,2048]{1,0:T(8,128)(2,1)S(1)}, bf16[192,2048]{1,0:T(8,128)(2,1)S(1)}, u32[]{:S(2)}, u32[]{:S(2)}) collective-permute-start(bf16[192,2048]{1,0:T(8,128)(2,1)S(1)} %get-tuple-element.179), channel_id=1, source_target_pairs={{1,0},{2,1},{3,2},{5,4},{6,5},{7,6},{9,8},{10,9},{11,10},{13,12},{... | collective-permute-start | bytes 2359304 | tf_op jit(solution)/shard_map/ppermute | solution.py:111
  324.9 20.7 %collective-permute-start.27 = (bf16[192,2048]{1,0:T(8,128)(2,1)S(1)}, bf16[192,2048]{1,0:T(8,128)(2,1)S(1)}, u32[]{:S(2)}, u32[]{:S(2)}) collective-permute-start(bf16[192,2048]{1,0:T(8,128)(2,1)S(1)} %collective-permute-done.25), channel_id=1, source_target_pairs={{1,0},{2,1},{3,2},{5,4},{6,5},{7,6},{9,8},{10,9},{11,10},{13,12},{... | collective-permute-start | bytes 2359304 | tf_op jit(solution)/shard_map/ppermute | solution.py:111
  326.2 20.7 %collective-permute-start.29 = (bf16[192,2048]{1,0:T(8,128)(2,1)S(1)}, bf16[192,2048]{1,0:T(8,128)(2,1)S(1)}, u32[]{:S(2)}, u32[]{:S(2)}) collective-permute-start(bf16[192,2048]{1,0:T(8,128)(2,1)S(1)} %collective-permute-done.24), channel_id=1, source_target_pairs={{0,1},{1,2},{2,3},{4,5},{5,6},{6,7},{8,9},{9,10},{10,11},{12,13},{... | collective-permute-start | bytes 2359304 | tf_op jit(solution)/shard_map/ppermute | solution.py:111
  345.6 20.2 %collective-permute-start.28 = (bf16[192,2048]{1,0:T(8,128)(2,1)S(1)}, bf16[192,2048]{1,0:T(8,128)(2,1)S(1)}, u32[]{:S(2)}, u32[]{:S(2)}) collective-permute-start(bf16[192,2048]{1,0:T(8,128)(2,1)S(1)} %collective-permute-done.27), channel_id=1, source_target_pairs={{1,0},{2,1},{3,2},{5,4},{6,5},{7,6},{9,8},{10,9},{11,10},{13,12},{... | collective-permute-start | bytes 2359304 | tf_op jit(solution)/shard_map/ppermute | solution.py:111
  346.9 20.1 %collective-permute-start.30 = (bf16[192,2048]{1,0:T(8,128)(2,1)S(1)}, bf16[192,2048]{1,0:T(8,128)(2,1)S(1)}, u32[]{:S(2)}, u32[]{:S(2)}) collective-permute-start(bf16[192,2048]{1,0:T(8,128)(2,1)S(1)} %collective-permute-done.29), channel_id=1, source_target_pairs={{0,1},{1,2},{2,3},{4,5},{5,6},{6,7},{8,9},{9,10},{10,11},{12,13},{... | collective-permute-start | bytes 2359304 | tf_op jit(solution)/shard_map/ppermute | solution.py:111
  375.2 406.6 %reduce-scatter.5.cloned.1.call-start = ((), (), s32[]{:S(2)}) async-start(), calls=%async_computation.13 | async-start | bytes 5242880 | tf_op jit(solution)/shard_map/reduce_scatter | solution.py:595
  452.5 339.1 %reduce-scatter.7.cloned.1.call-start = ((), (), s32[]{:S(2)}) async-start(), calls=%async_computation.14 | async-start | bytes 5242880 | tf_op jit(solution)/shard_map/reduce_scatter | solution.py:595
  504.8 369.9 %reduce-scatter.9.cloned.1.call-start = ((), (), s32[]{:S(2)}) async-start(), calls=%async_computation.15 | async-start | bytes 10485760 | tf_op jit(solution)/shard_map/reduce_scatter | solution.py:655
  531.6 28.5 %collective-permute-start.35 = (bf16[192,2048]{1,0:T(8,128)(2,1)}, bf16[192,2048]{1,0:T(8,128)(2,1)}, u32[]{:S(2)}, u32[]{:S(2)}) collective-permute-start(bf16[192,2048]{1,0:T(8,128)(2,1)} %get-tuple-element.215), channel_id=1, source_target_pairs={{0,1},{1,2},{2,3},{4,5},{5,6},{6,7},{8,9},{9,10},{10,11},{12,13},{... | collective-permute-start | bytes 2359304 | tf_op jit(solution)/shard_map/ppermute | solution.py:111
  537.8 22.3 %collective-permute-start.36 = (bf16[192,2048]{1,0:T(8,128)(2,1)}, bf16[192,2048]{1,0:T(8,128)(2,1)}, u32[]{:S(2)}, u32[]{:S(2)}) collective-permute-start(bf16[192,2048]{1,0:T(8,128)(2,1)} %get-tuple-element.214), channel_id=1, source_target_pairs={{1,0},{2,1},{3,2},{5,4},{6,5},{7,6},{9,8},{10,9},{11,10},{13,12},{... | collective-permute-start | bytes 2359304 | tf_op jit(solution)/shard_map/ppermute | solution.py:111
  560.1 314.6 %reduce-scatter.11.cloned.1.call-start = ((), (), s32[]{:S(2)}) async-start(), calls=%async_computation.16 | async-start | bytes 10485760 | tf_op jit(solution)/shard_map/reduce_scatter | solution.py:655
  592.3 32.9 %collective-permute-start.37 = (bf16[192,2048]{1,0:T(8,128)(2,1)}, bf16[192,2048]{1,0:T(8,128)(2,1)S(1)}, u32[]{:S(2)}, u32[]{:S(2)}) collective-permute-start(bf16[192,2048]{1,0:T(8,128)(2,1)} %get-tuple-element.85), channel_id=1, source_target_pairs={{0,1},{1,2},{2,3},{4,5},{5,6},{6,7},{8,9},{9,10},{10,11},{12,13},{... | collective-permute-start | bytes 2359304 | tf_op jit(solution)/shard_map/ppermute | solution.py:111
  596.6 28.7 %collective-permute-start.38 = (bf16[192,2048]{1,0:T(8,128)(2,1)}, bf16[192,2048]{1,0:T(8,128)(2,1)}, u32[]{:S(2)}, u32[]{:S(2)}) collective-permute-start(bf16[192,2048]{1,0:T(8,128)(2,1)} %get-tuple-element.86), channel_id=1, source_target_pairs={{1,0},{2,1},{3,2},{5,4},{6,5},{7,6},{9,8},{10,9},{11,10},{13,12},{... | collective-permute-start | bytes 2359304 | tf_op jit(solution)/shard_map/ppermute | solution.py:111
  628.8 28.6 %collective-permute-start.39 = (bf16[192,2048]{1,0:T(8,128)(2,1)}, bf16[192,2048]{1,0:T(8,128)(2,1)}, u32[]{:S(2)}, u32[]{:S(2)}) collective-permute-start(bf16[192,2048]{1,0:T(8,128)(2,1)} %get-tuple-element.89), channel_id=1, source_target_pairs={{0,1},{1,2},{2,3},{4,5},{5,6},{6,7},{8,9},{9,10},{10,11},{12,13},{... | collective-permute-start | bytes 2359304 | tf_op jit(solution)/shard_map/ppermute | solution.py:111
  634.2 23.3 %collective-permute-start.40 = (bf16[192,2048]{1,0:T(8,128)(2,1)}, bf16[192,2048]{1,0:T(8,128)(2,1)}, u32[]{:S(2)}, u32[]{:S(2)}) collective-permute-start(bf16[192,2048]{1,0:T(8,128)(2,1)} %get-tuple-element.90), channel_id=1, source_target_pairs={{1,0},{2,1},{3,2},{5,4},{6,5},{7,6},{9,8},{10,9},{11,10},{13,12},{... | collective-permute-start | bytes 2359304 | tf_op jit(solution)/shard_map/ppermute | solution.py:111
  661.9 21.2 %collective-permute-start.47 = (bf16[192,1024]{1,0:T(8,128)(2,1)S(1)}, bf16[192,1024]{1,0:T(8,128)(2,1)S(1)}, u32[]{:S(2)}, u32[]{:S(2)}) collective-permute-start(bf16[192,1024]{1,0:T(8,128)(2,1)S(1)} %get-tuple-element.243), channel_id=1, source_target_pairs={{0,8},{4,12},{8,0},{12,4},{16,24},{20,28},{24,16},{28,20},{1,9},{5... | collective-permute-start | bytes 1179656 | tf_op jit(solution)/shard_map/ppermute | solution.py:52
  676.7 19.4 %collective-permute-start.50 = (bf16[2,192,1024]{2,1,0:T(8,128)(2,1)S(1)}, bf16[2,192,1024]{2,1,0:T(8,128)(2,1)S(1)}, u32[]{:S(2)}, u32[]{:S(2)}) collective-permute-start(bf16[2,192,1024]{2,1,0:T(8,128)(2,1)S(1)} %get-tuple-element.239), channel_id=1, source_target_pairs={{0,8},{4,12},{8,0},{12,4},{16,24},{20,28},{24,16},{28,20},{1,9},{5... | collective-permute-start | bytes 2359304 | tf_op jit(solution)/shard_map/ppermute | solution.py:52
  678.4 19.9 %collective-permute-start.41 = (bf16[192,2048]{1,0:T(8,128)(2,1)S(1)}, bf16[192,2048]{1,0:T(8,128)(2,1)S(1)}, u32[]{:S(2)}, u32[]{:S(2)}) collective-permute-start(bf16[192,2048]{1,0:T(8,128)(2,1)S(1)} %get-tuple-element.209), channel_id=1, source_target_pairs={{0,1},{1,2},{2,3},{4,5},{5,6},{6,7},{8,9},{9,10},{10,11},{12,13},{... | collective-permute-start | bytes 2359304 | tf_op jit(solution)/shard_map/ppermute | solution.py:111
  681.9 20.6 %collective-permute-start.42 = (bf16[192,2048]{1,0:T(8,128)(2,1)S(1)}, bf16[192,2048]{1,0:T(8,128)(2,1)S(1)}, u32[]{:S(2)}, u32[]{:S(2)}) collective-permute-start(bf16[192,2048]{1,0:T(8,128)(2,1)S(1)} %get-tuple-element.208), channel_id=1, source_target_pairs={{1,0},{2,1},{3,2},{5,4},{6,5},{7,6},{9,8},{10,9},{11,10},{13,12},{... | collective-permute-start | bytes 2359304 | tf_op jit(solution)/shard_map/ppermute | solution.py:111
  683.3 19.2 %collective-permute-start.48 = (bf16[2,192,1024]{2,1,0:T(8,128)(2,1)S(1)}, bf16[2,192,1024]{2,1,0:T(8,128)(2,1)S(1)}, u32[]{:S(2)}, u32[]{:S(2)}) collective-permute-start(bf16[2,192,1024]{2,1,0:T(8,128)(2,1)S(1)} %get-tuple-element.245), channel_id=1, source_target_pairs={{0,16},{4,20},{8,24},{12,28},{16,0},{20,4},{24,8},{28,12},{1,17},{... | collective-permute-start | bytes 2359304 | tf_op jit(solution)/shard_map/ppermute | solution.py:52
  711.3 32.4 %collective-permute-start.43 = (bf16[192,2048]{1,0:T(8,128)(2,1)}, bf16[192,2048]{1,0:T(8,128)(2,1)}, u32[]{:S(2)}, u32[]{:S(2)}) collective-permute-start(bf16[192,2048]{1,0:T(8,128)(2,1)} %get-tuple-element.92), channel_id=1, source_target_pairs={{0,1},{1,2},{2,3},{4,5},{5,6},{6,7},{8,9},{9,10},{10,11},{12,13},{... | collective-permute-start | bytes 2359304 | tf_op jit(solution)/shard_map/ppermute | solution.py:111
  715.7 28.0 %collective-permute-start.44 = (bf16[192,2048]{1,0:T(8,128)(2,1)}, bf16[192,2048]{1,0:T(8,128)(2,1)}, u32[]{:S(2)}, u32[]{:S(2)}) collective-permute-start(bf16[192,2048]{1,0:T(8,128)(2,1)} %get-tuple-element.93), channel_id=1, source_target_pairs={{1,0},{2,1},{3,2},{5,4},{6,5},{7,6},{9,8},{10,9},{11,10},{13,12},{... | collective-permute-start | bytes 2359304 | tf_op jit(solution)/shard_map/ppermute | solution.py:111
  753.7 21.2 %collective-permute-start.45 = (bf16[192,2048]{1,0:T(8,128)(2,1)}, bf16[192,2048]{1,0:T(8,128)(2,1)}, u32[]{:S(2)}, u32[]{:S(2)}) collective-permute-start(bf16[192,2048]{1,0:T(8,128)(2,1)} %get-tuple-element.94), channel_id=1, source_target_pairs={{0,1},{1,2},{2,3},{4,5},{5,6},{6,7},{8,9},{9,10},{10,11},{12,13},{... | collective-permute-start | bytes 2359304 | tf_op jit(solution)/shard_map/ppermute | solution.py:111
  759.4 20.5 %collective-permute-start.46 = (bf16[192,2048]{1,0:T(8,128)(2,1)}, bf16[192,2048]{1,0:T(8,128)(2,1)}, u32[]{:S(2)}, u32[]{:S(2)}) collective-permute-start(bf16[192,2048]{1,0:T(8,128)(2,1)} %get-tuple-element.95), channel_id=1, source_target_pairs={{1,0},{2,1},{3,2},{5,4},{6,5},{7,6},{9,8},{10,9},{11,10},{13,12},{... | collective-permute-start | bytes 2359304 | tf_op jit(solution)/shard_map/ppermute | solution.py:111
  774.3 20.8 %collective-permute-start.56 = (bf16[768,2048]{1,0:T(8,128)(2,1)}, bf16[768,2048]{1,0:T(8,128)(2,1)}, u32[]{:S(2)}, u32[]{:S(2)}) collective-permute-start(bf16[768,2048]{1,0:T(8,128)(2,1)} %get-tuple-element.104), channel_id=1, source_target_pairs={{0,4},{4,0},{8,12},{12,8},{16,20},{20,16},{24,28},{28,24},{1,5},{5... | collective-permute-start | bytes 9437192 | tf_op jit(solution)/shard_map/ppermute | solution.py:52
  800.2 24.0 %collective-permute-start.61 = (bf16[256,2048]{1,0:T(8,128)(2,1)S(1)}, bf16[256,2048]{1,0:T(8,128)(2,1)S(1)}, u32[]{:S(2)}, u32[]{:S(2)}) collective-permute-start(bf16[256,2048]{1,0:T(8,128)(2,1)S(1)} %get-tuple-element.108), channel_id=1, source_target_pairs={{0,1},{1,2},{2,3},{4,5},{5,6},{6,7},{8,9},{9,10},{10,11},{12,13},{... | collective-permute-start | bytes 3145736 | tf_op jit(solution)/shard_map/ppermute | solution.py:111
  801.9 26.5 %collective-permute-start.62 = (bf16[256,2048]{1,0:T(8,128)(2,1)S(1)}, bf16[256,2048]{1,0:T(8,128)(2,1)S(1)}, u32[]{:S(2)}, u32[]{:S(2)}) collective-permute-start(bf16[256,2048]{1,0:T(8,128)(2,1)S(1)} %get-tuple-element.109), channel_id=1, source_target_pairs={{1,0},{2,1},{3,2},{5,4},{6,5},{7,6},{9,8},{10,9},{11,10},{13,12},{... | collective-permute-start | bytes 3145736 | tf_op jit(solution)/shard_map/ppermute | solution.py:111
  805.8 24.5 %collective-permute-start.57 = (bf16[2,192,1024]{2,1,0:T(8,128)(2,1)S(1)}, bf16[2,192,1024]{2,1,0:T(8,128)(2,1)S(1)}, u32[]{:S(2)}, u32[]{:S(2)}) collective-permute-start(bf16[2,192,1024]{2,1,0:T(8,128)(2,1)S(1)} %slice_bitcast_fusion.4), channel_id=1, source_target_pairs={{0,8},{4,12},{8,0},{12,4},{16,24},{20,28},{24,16},{28,20},{1,9},{5... | collective-permute-start | bytes 2359304 | tf_op jit(solution)/shard_map/ppermute | solution.py:52
  806.5 30.4 %collective-permute-start.59 = (bf16[2,192,1024]{2,1,0:T(8,128)(2,1)S(1)}, bf16[2,192,1024]{2,1,0:T(8,128)(2,1)S(1)}, u32[]{:S(2)}, u32[]{:S(2)}) collective-permute-start(bf16[2,192,1024]{2,1,0:T(8,128)(2,1)S(1)} %bitcast.321), channel_id=1, source_target_pairs={{0,16},{4,20},{8,24},{12,28},{16,0},{20,4},{24,8},{28,12},{1,17},{... | collective-permute-start | bytes 2359304 | tf_op jit(solution)/shard_map/ppermute | solution.py:52
  829.1 25.7 %collective-permute-start.64 = (bf16[256,2048]{1,0:T(8,128)(2,1)S(1)}, bf16[256,2048]{1,0:T(8,128)(2,1)S(1)}, u32[]{:S(2)}, u32[]{:S(2)}) collective-permute-start(bf16[256,2048]{1,0:T(8,128)(2,1)S(1)} %get-tuple-element.111), channel_id=1, source_target_pairs={{1,0},{2,1},{3,2},{5,4},{6,5},{7,6},{9,8},{10,9},{11,10},{13,12},{... | collective-permute-start | bytes 3145736 | tf_op jit(solution)/shard_map/ppermute | solution.py:111
  832.3 25.3 %collective-permute-start.63 = (bf16[256,2048]{1,0:T(8,128)(2,1)S(1)}, bf16[256,2048]{1,0:T(8,128)(2,1)S(1)}, u32[]{:S(2)}, u32[]{:S(2)}) collective-permute-start(bf16[256,2048]{1,0:T(8,128)(2,1)S(1)} %get-tuple-element.110), channel_id=1, source_target_pairs={{0,1},{1,2},{2,3},{4,5},{5,6},{6,7},{8,9},{9,10},{10,11},{12,13},{... | collective-permute-start | bytes 3145736 | tf_op jit(solution)/shard_map/ppermute | solution.py:111
  837.3 28.6 %collective-permute-start.60 = (bf16[192,1024]{1,0:T(8,128)(2,1)S(1)}, bf16[192,1024]{1,0:T(8,128)(2,1)S(1)}, u32[]{:S(2)}, u32[]{:S(2)}) collective-permute-start(bf16[192,1024]{1,0:T(8,128)(2,1)S(1)} %slice_bitcast_fusion.12), channel_id=1, source_target_pairs={{0,8},{4,12},{8,0},{12,4},{16,24},{20,28},{24,16},{28,20},{1,9},{5... | collective-permute-start | bytes 1179656 | tf_op jit(solution)/shard_map/ppermute | solution.py:52
  859.0 25.9 %collective-permute-start.65 = (bf16[256,2048]{1,0:T(8,128)(2,1)}, bf16[256,2048]{1,0:T(8,128)(2,1)}, u32[]{:S(2)}, u32[]{:S(2)}) collective-permute-start(bf16[256,2048]{1,0:T(8,128)(2,1)} %add_convert_fusion.6), channel_id=1, source_target_pairs={{0,1},{1,2},{2,3},{4,5},{5,6},{6,7},{8,9},{9,10},{10,11},{12,13},{... | collective-permute-start | bytes 3145736 | tf_op jit(solution)/shard_map/ppermute | solution.py:111
  864.4 25.9 %collective-permute-start.66 = (bf16[256,2048]{1,0:T(8,128)(2,1)}, bf16[256,2048]{1,0:T(8,128)(2,1)}, u32[]{:S(2)}, u32[]{:S(2)}) collective-permute-start(bf16[256,2048]{1,0:T(8,128)(2,1)} %add_convert_fusion.5), channel_id=1, source_target_pairs={{1,0},{2,1},{3,2},{5,4},{6,5},{7,6},{9,8},{10,9},{11,10},{13,12},{... | collective-permute-start | bytes 3145736 | tf_op jit(solution)/shard_map/ppermute | solution.py:111
  871.3 33.7 %all-to-all-start.4 = ((f32[32,1,1280]{2,1,0:T(1,128)}), f32[32,1,1280]{2,1,0:T(1,128)S(1)}, u32[]{:S(2)}, u32[]{:S(2)}) async-start(f32[32,1,1280]{2,1,0:T(1,128)} %all_to_all.28), calls=%async_computation.6 | async-start | bytes 327680 | tf_op jit(solution)/shard_map/all_to_all | solution.py:729
  877.9 42.2 %collective-permute-start.71 = (bf16[2,256,2048]{2,1,0:T(8,128)(2,1)}, bf16[2,256,2048]{2,1,0:T(8,128)(2,1)}, u32[]{:S(2)}, u32[]{:S(2)}) collective-permute-start(bf16[2,256,2048]{2,1,0:T(8,128)(2,1)} %fusion.28), channel_id=1, source_target_pairs={{0,4},{4,0},{1,5},{5,1},{2,6},{6,2},{3,7},{7,3},{8,12},{12,8},{9,1... | collective-permute-start | bytes 6291464 | tf_op jit(solution)/shard_map/ppermute | solution.py:151
  893.3 24.3 %collective-permute-start.68 = (bf16[64,2048]{1,0:T(8,128)(2,1)}, bf16[64,2048]{1,0:T(8,128)(2,1)}, u32[]{:S(2)}, u32[]{:S(2)}) collective-permute-start(bf16[64,2048]{1,0:T(8,128)(2,1)} %get-tuple-element.232), channel_id=1, source_target_pairs={{0,0},{1,1},{6,2},{11,3},{12,4},{13,5},{18,6},{23,7},{24,8},{25,9}... | collective-permute-start | bytes 786440 | tf_op jit(solution)/shard_map/ppermute | solution.py:711
  897.0 20.6 %collective-permute-start.69 = (bf16[64,2048]{1,0:T(8,128)(2,1)}, bf16[64,2048]{1,0:T(8,128)(2,1)}, u32[]{:S(2)}, u32[]{:S(2)}) collective-permute-start(bf16[64,2048]{1,0:T(8,128)(2,1)} %get-tuple-element.231), channel_id=1, source_target_pairs={{0,0},{5,1},{6,2},{11,3},{12,4},{17,5},{18,6},{23,7},{24,8},{29,9}... | collective-permute-start | bytes 786440 | tf_op jit(solution)/shard_map/ppermute | solution.py:711
  900.6 17.0 %collective-permute-start.70 = (bf16[64,2048]{1,0:T(8,128)(2,1)}, bf16[64,2048]{1,0:T(8,128)(2,1)}, u32[]{:S(2)}, u32[]{:S(2)}) collective-permute-start(bf16[64,2048]{1,0:T(8,128)(2,1)} %get-tuple-element.230), channel_id=1, source_target_pairs={{0,0},{5,1},{10,2},{11,3},{12,4},{17,5},{22,6},{23,7},{24,8},{29,9... | collective-permute-start | bytes 786440 | tf_op jit(solution)/shard_map/ppermute | solution.py:711
  (103 other events, 1589.3 us)
Sparse Core Ops, SparseCore 0:
  14.3 85.1 all-gather.6
  140.6 66.5 all-gather.14
  209.1 110.4 all-gather.8
  321.3 92.4 all-gather.10
  415.5 52.5 all-gather.12
  471.5 52.5 reduce-scatter.4
  527.1 52.5 reduce-scatter.6
  583.3 89.7 reduce-scatter.8
  708.4 84.3 reduce-scatter.10
